TPU v7x, 32 devices: a whole 2x2x4 slice. The times are simulated.
32 devices in a mesh: dp: 4 (over x, core), fsdp: 8 (over z, y).
Axes of the slice: x: 2, y: 2, z: 4, core: 2. Of those that a mesh axis runs over, the one named last changes fastest.
Arguments:
- tokens: bfloat16 [32, 512, 1024], P(('dp', 'fsdp')), may hold values from -6 to 6
- ln1_gain: bfloat16 [1024], P(('dp', 'fsdp')), may hold values from 0.5 to 1.5
- ln1_bias: bfloat16 [1024], P(('dp', 'fsdp')), may hold values from -1.796875 to 1.796875
- w_qkv: bfloat16 [1024, 3072], P(('dp', 'fsdp')), may hold values from -0.1875 to 0.1875
- bias_q: bfloat16 [1024], P(('dp', 'fsdp')), may hold values from -3 to 3
- bias_v: bfloat16 [1024], P(('dp', 'fsdp')), may hold values from -3 to 3
- w_out: bfloat16 [1024, 1024], P(('dp', 'fsdp')), may hold values from -1 to 1
- bias_out: bfloat16 [1024], P(('dp', 'fsdp')), may hold values from -1.796875 to 1.796875
- ln2_gain: bfloat16 [1024], P(('dp', 'fsdp')), may hold values from 0.5 to 1.5
- ln2_bias: bfloat16 [1024], P(('dp', 'fsdp')), may hold values from -1.796875 to 1.796875
- w_up: bfloat16 [1024, 4096], P(('dp', 'fsdp')), may hold values from -0.1875 to 0.1875
- bias_up: bfloat16 [4096], P(('dp', 'fsdp')), may hold values from -1.796875 to 1.796875
- w_down: bfloat16 [4096, 1024], P(('dp', 'fsdp')), may hold values from -0.09375 to 0.09375
- bias_down: bfloat16 [1024], P(('dp', 'fsdp')), may hold values from -1.796875 to 1.796875
- cot_first: bfloat16 [32, 512, 1024], P(('dp', 'fsdp')), may hold values from -6 to 6
- cot_second: bfloat16 [32, 512, 1024], P(('dp', 'fsdp')), may hold values from -6 to 6
- valid: int32 [32, 512], P(('dp', 'fsdp')), may hold values from 0 to 1, as said below
Outputs:
- out_first: bfloat16 [32, 512, 1024], P(('dp', 'fsdp'))
- out_second: bfloat16 [32, 512, 1024], P(('dp', 'fsdp'))
- grad_tokens: bfloat16 [32, 512, 1024], P(('dp', 'fsdp'))
- grad_ln1_gain: float32 [1024], P(('dp', 'fsdp'))
- grad_ln1_bias: float32 [1024], P(('dp', 'fsdp'))
- grad_w_qkv: float32 [1024, 3072], P(('dp', 'fsdp'))
- grad_bias_q: float32 [1024], P(('dp', 'fsdp'))
- grad_bias_v: float32 [1024], P(('dp', 'fsdp'))
- grad_w_out: float32 [1024, 1024], P(('dp', 'fsdp'))
- grad_bias_out: float32 [1024], P(('dp', 'fsdp'))
- grad_ln2_gain: float32 [1024], P(('dp', 'fsdp'))
- grad_ln2_bias: float32 [1024], P(('dp', 'fsdp'))
- grad_w_up: float32 [1024, 4096], P(('dp', 'fsdp'))
- grad_bias_up: float32 [4096], P(('dp', 'fsdp'))
- grad_w_down: float32 [4096, 1024], P(('dp', 'fsdp'))
- grad_bias_down: float32 [1024], P(('dp', 'fsdp'))
Inputs may be any that keep to these rules, and one draw needn't show every extreme that they name: `valid`: the share of present cells differs from sample to sample.
All inputs are finite; a program needn't handle non-finite values.
Results may differ from a plain program's by a relative error of at most 0.02.
Values may be sent and summed in bfloat16 or wider, within the bound.
No kernel may reach another device: no remote copies, remote signals or barrier semaphores. Data moves between devices by JAX's collectives and lax.ppermute only.
A program may use at most 152 MiB of HBM per device.

v0:
```python
from functools import partial

import jax
import jax.numpy as jnp
from jax import lax
from jax.sharding import PartitionSpec as P

HEAD_DIM = 64


EPSILON = 1e-06


def norm_affine(values, gain_vec, shift_vec):
    centre = values - jnp.mean(values, axis=-1, keepdims=True)
    spread = jnp.mean(centre * centre, axis=-1, keepdims=True)
    return centre * lax.rsqrt(spread + EPSILON) * gain_vec + shift_vec


def exact_gelu(values):
    return jax.nn.gelu(values, approximate=False)


def attend_block(query_blk, keys_all, values_all):
    scores = (
        jnp.einsum("qhd,khd->hqk", query_blk, keys_all, preferred_element_type=jnp.float32) * 0.125
    )
    top_score = jnp.max(scores, axis=-1, keepdims=True)
    shifted = jnp.exp(scores - top_score)
    total = jnp.sum(shifted, axis=-1, keepdims=True)
    attn_probs = (shifted / total).astype(jnp.bfloat16)
    mixed_blk = jnp.einsum(
        "hqk,khd->qhd", attn_probs, values_all, preferred_element_type=jnp.float32
    )
    return (mixed_blk, top_score[..., 0] + jnp.log(total[..., 0]))


def attend_back(carry, block, keys_all, values_all):
    grad_keys, grad_values = carry
    query_blk, grad_mixed, log_total = block
    scores = (
        jnp.einsum("qhd,khd->hqk", query_blk, keys_all, preferred_element_type=jnp.float32) * 0.125
    )
    attn_probs = jnp.exp(scores - log_total[..., None])
    grad_probs = jnp.einsum(
        "qhd,khd->hqk", grad_mixed, values_all, preferred_element_type=jnp.float32
    )
    grad_values = grad_values + jnp.einsum(
        "hqk,qhd->khd",
        attn_probs.astype(jnp.bfloat16),
        grad_mixed,
        preferred_element_type=jnp.float32,
    )
    inner_sum = jnp.sum(attn_probs * grad_probs, axis=-1, keepdims=True)
    grad_scores = (attn_probs * (grad_probs - inner_sum)).astype(jnp.bfloat16)
    grad_queries = (
        jnp.einsum("hqk,khd->qhd", grad_scores, keys_all, preferred_element_type=jnp.float32)
        * 0.125
    )
    grad_keys = (
        grad_keys
        + jnp.einsum("hqk,qhd->khd", grad_scores, query_blk, preferred_element_type=jnp.float32)
        * 0.125
    )
    return ((grad_keys, grad_values), grad_queries)


def forward_pass(inputs, weights):
    (
        gain_one,
        shift_one,
        weight_qkv,
        query_bias,
        value_bias,
        weight_out,
        out_bias,
        gain_two,
        shift_two,
        weight_up,
        up_bias,
        weight_down,
        down_bias,
    ) = weights
    length, model_width = inputs.shape
    head_count = model_width // HEAD_DIM
    block_rows = min(512, length)
    block_count = length // block_rows
    normed = norm_affine(
        inputs, gain_one.astype(jnp.float32), shift_one.astype(jnp.float32)
    ).astype(jnp.bfloat16)
    projected = jnp.dot(normed, weight_qkv, preferred_element_type=jnp.float32)
    queries = (projected[:, :model_width] + query_bias.astype(jnp.float32)).astype(jnp.bfloat16)
    keys_all = projected[:, model_width : 2 * model_width].astype(jnp.bfloat16)
    values_all = (projected[:, 2 * model_width :] + value_bias.astype(jnp.float32)).astype(
        jnp.bfloat16
    )
    queries = queries.reshape(length, head_count, HEAD_DIM)
    keys_all = keys_all.reshape(length, head_count, HEAD_DIM)
    values_all = values_all.reshape(length, head_count, HEAD_DIM)
    query_blocks = queries.reshape(block_count, block_rows, head_count, HEAD_DIM)
    mixed_blocks, log_totals = lax.map(
        partial(attend_block, keys_all=keys_all, values_all=values_all), query_blocks
    )
    mixed_heads = mixed_blocks.reshape(length, model_width).astype(jnp.bfloat16)
    middle = (
        inputs
        + jnp.dot(mixed_heads, weight_out, preferred_element_type=jnp.float32)
        + out_bias.astype(jnp.float32)
    )
    normed_two = norm_affine(
        middle, gain_two.astype(jnp.float32), shift_two.astype(jnp.float32)
    ).astype(jnp.bfloat16)
    hidden = jnp.dot(normed_two, weight_up, preferred_element_type=jnp.float32) + up_bias.astype(
        jnp.float32
    )
    active = exact_gelu(hidden).astype(jnp.bfloat16)
    result = (
        middle
        + jnp.dot(active, weight_down, preferred_element_type=jnp.float32)
        + down_bias.astype(jnp.float32)
    )
    saved = (
        inputs,
        normed,
        queries,
        keys_all,
        values_all,
        log_totals,
        mixed_heads,
        middle,
        normed_two,
        hidden,
        active,
    )
    return (result, saved)


def backward_pass(grad_result, saved, weights):
    (
        gain_one,
        shift_one,
        weight_qkv,
        query_bias,
        value_bias,
        weight_out,
        out_bias,
        gain_two,
        shift_two,
        weight_up,
        up_bias,
        weight_down,
        down_bias,
    ) = weights
    (
        inputs,
        normed,
        queries,
        keys_all,
        values_all,
        log_totals,
        mixed_heads,
        middle,
        normed_two,
        hidden,
        active,
    ) = saved
    length, model_width = inputs.shape
    head_count = model_width // HEAD_DIM
    block_rows = min(512, length)
    block_count = length // block_rows
    grad_down_out = grad_result.astype(jnp.bfloat16)
    grad_w_down = jnp.einsum("sf,sd->fd", active, grad_down_out, preferred_element_type=jnp.float32)
    grad_b_down = jnp.sum(grad_down_out.astype(jnp.float32), axis=0)
    grad_active = jnp.einsum(
        "sd,fd->sf", grad_down_out, weight_down, preferred_element_type=jnp.float32
    )
    _, gelu_pullback = jax.vjp(exact_gelu, hidden)
    grad_hidden = gelu_pullback(grad_active)[0].astype(jnp.bfloat16)
    grad_w_up = jnp.einsum("sd,sf->df", normed_two, grad_hidden, preferred_element_type=jnp.float32)
    grad_b_up = jnp.sum(grad_hidden.astype(jnp.float32), axis=0)
    grad_normed_two = jnp.einsum(
        "sf,df->sd", grad_hidden, weight_up, preferred_element_type=jnp.float32
    )
    _, norm_two_pullback = jax.vjp(
        norm_affine, middle, gain_two.astype(jnp.float32), shift_two.astype(jnp.float32)
    )
    grad_mid_norm, grad_gain_two, grad_shift_two = norm_two_pullback(grad_normed_two)
    grad_middle = grad_result + grad_mid_norm
    grad_att = grad_middle.astype(jnp.bfloat16)
    grad_w_out = jnp.einsum("sd,se->de", mixed_heads, grad_att, preferred_element_type=jnp.float32)
    grad_b_out = jnp.sum(grad_att.astype(jnp.float32), axis=0)
    grad_mixed = jnp.einsum("se,de->sd", grad_att, weight_out, preferred_element_type=jnp.float32)
    grad_mixed = grad_mixed.astype(jnp.bfloat16).reshape(
        block_count, block_rows, head_count, HEAD_DIM
    )
    query_blocks = queries.reshape(block_count, block_rows, head_count, HEAD_DIM)
    zeros_kv = jnp.zeros((length, head_count, HEAD_DIM), jnp.float32)
    (grad_keys, grad_values), grad_queries = lax.scan(
        partial(attend_back, keys_all=keys_all, values_all=values_all),
        (zeros_kv, zeros_kv),
        (query_blocks, grad_mixed, log_totals),
    )
    grad_queries = grad_queries.reshape(length, model_width).astype(jnp.bfloat16)
    grad_keys = grad_keys.reshape(length, model_width).astype(jnp.bfloat16)
    grad_values = grad_values.reshape(length, model_width).astype(jnp.bfloat16)
    grad_proj = jnp.concatenate([grad_queries, grad_keys, grad_values], axis=1)
    grad_w_qkv = jnp.einsum("sd,se->de", normed, grad_proj, preferred_element_type=jnp.float32)
    grad_b_query = jnp.sum(grad_queries.astype(jnp.float32), axis=0)
    grad_b_value = jnp.sum(grad_values.astype(jnp.float32), axis=0)
    grad_normed = jnp.einsum("se,de->sd", grad_proj, weight_qkv, preferred_element_type=jnp.float32)
    _, norm_one_pullback = jax.vjp(
        norm_affine, inputs, gain_one.astype(jnp.float32), shift_one.astype(jnp.float32)
    )
    grad_in_norm, grad_gain_one, grad_shift_one = norm_one_pullback(grad_normed)
    grad_inputs = grad_middle + grad_in_norm
    grads = (
        grad_gain_one,
        grad_shift_one,
        grad_w_qkv,
        grad_b_query,
        grad_b_value,
        grad_w_out,
        grad_b_out,
        grad_gain_two,
        grad_shift_two,
        grad_w_up,
        grad_b_up,
        grad_w_down,
        grad_b_down,
    )
    return (grad_inputs, grads)


def per_device(
    tokens,
    ln1_gain,
    ln1_bias,
    w_qkv,
    bias_q,
    bias_v,
    w_out,
    bias_out,
    ln2_gain,
    ln2_bias,
    w_up,
    bias_up,
    w_down,
    bias_down,
    cot_first,
    cot_second,
    valid,
):
    gathered = (
        lax.all_gather(ln1_gain, ("dp", "fsdp"), axis=0, tiled=True),
        lax.all_gather(ln1_bias, ("dp", "fsdp"), axis=0, tiled=True),
        lax.all_gather(w_qkv, ("dp", "fsdp"), axis=0, tiled=True),
        lax.all_gather(bias_q, ("dp", "fsdp"), axis=0, tiled=True),
        lax.all_gather(bias_v, ("dp", "fsdp"), axis=0, tiled=True),
        lax.all_gather(w_out, ("dp", "fsdp"), axis=0, tiled=True),
        lax.all_gather(bias_out, ("dp", "fsdp"), axis=0, tiled=True),
        lax.all_gather(ln2_gain, ("dp", "fsdp"), axis=0, tiled=True),
        lax.all_gather(ln2_bias, ("dp", "fsdp"), axis=0, tiled=True),
        lax.all_gather(w_up, ("dp", "fsdp"), axis=0, tiled=True),
        lax.all_gather(bias_up, ("dp", "fsdp"), axis=0, tiled=True),
        lax.all_gather(w_down, ("dp", "fsdp"), axis=0, tiled=True),
        lax.all_gather(bias_down, ("dp", "fsdp"), axis=0, tiled=True),
    )
    start_rows = tokens[0].astype(jnp.float32)
    first_out, saved_first = forward_pass(start_rows, gathered)
    first_low = first_out.astype(jnp.bfloat16)
    second_in = lax.optimization_barrier(first_low).astype(jnp.float32)
    second_out, saved_second = forward_pass(second_in, gathered)
    back_weights = (
        lax.all_gather(ln1_gain, ("dp", "fsdp"), axis=0, tiled=True),
        lax.all_gather(ln1_bias, ("dp", "fsdp"), axis=0, tiled=True),
        lax.all_gather(w_qkv, ("dp", "fsdp"), axis=0, tiled=True),
        lax.all_gather(bias_q, ("dp", "fsdp"), axis=0, tiled=True),
        lax.all_gather(bias_v, ("dp", "fsdp"), axis=0, tiled=True),
        lax.all_gather(w_out, ("dp", "fsdp"), axis=0, tiled=True),
        lax.all_gather(bias_out, ("dp", "fsdp"), axis=0, tiled=True),
        lax.all_gather(ln2_gain, ("dp", "fsdp"), axis=0, tiled=True),
        lax.all_gather(ln2_bias, ("dp", "fsdp"), axis=0, tiled=True),
        lax.all_gather(w_up, ("dp", "fsdp"), axis=0, tiled=True),
        lax.all_gather(bias_up, ("dp", "fsdp"), axis=0, tiled=True),
        lax.all_gather(w_down, ("dp", "fsdp"), axis=0, tiled=True),
        lax.all_gather(bias_down, ("dp", "fsdp"), axis=0, tiled=True),
    )
    keep_mask = valid[0].astype(jnp.float32)[:, None]
    grad_second = cot_second[0].astype(jnp.float32) * keep_mask
    grad_between, grads_second = backward_pass(grad_second, saved_second, back_weights)
    grad_first = cot_first[0].astype(jnp.float32) * keep_mask + grad_between
    grad_inputs, grads_first = backward_pass(grad_first, saved_first, back_weights)
    totals = tuple((left + right for left, right in zip(grads_first, grads_second)))
    partial_sums = (
        lax.psum_scatter(
            totals[0].astype(jnp.bfloat16), "dp", scatter_dimension=0, tiled=True
        ).astype(jnp.float32),
        lax.psum_scatter(
            totals[1].astype(jnp.bfloat16), "dp", scatter_dimension=0, tiled=True
        ).astype(jnp.float32),
        lax.psum_scatter(
            totals[2].astype(jnp.bfloat16), "dp", scatter_dimension=0, tiled=True
        ).astype(jnp.float32),
        lax.psum_scatter(
            totals[3].astype(jnp.bfloat16), "dp", scatter_dimension=0, tiled=True
        ).astype(jnp.float32),
        lax.psum_scatter(
            totals[4].astype(jnp.bfloat16), "dp", scatter_dimension=0, tiled=True
        ).astype(jnp.float32),
        lax.psum_scatter(
            totals[5].astype(jnp.bfloat16), "dp", scatter_dimension=0, tiled=True
        ).astype(jnp.float32),
        lax.psum_scatter(
            totals[6].astype(jnp.bfloat16), "dp", scatter_dimension=0, tiled=True
        ).astype(jnp.float32),
        lax.psum_scatter(
            totals[7].astype(jnp.bfloat16), "dp", scatter_dimension=0, tiled=True
        ).astype(jnp.float32),
        lax.psum_scatter(
            totals[8].astype(jnp.bfloat16), "dp", scatter_dimension=0, tiled=True
        ).astype(jnp.float32),
        lax.psum_scatter(
            totals[9].astype(jnp.bfloat16), "dp", scatter_dimension=0, tiled=True
        ).astype(jnp.float32),
        lax.psum_scatter(
            totals[10].astype(jnp.bfloat16), "dp", scatter_dimension=0, tiled=True
        ).astype(jnp.float32),
        lax.psum_scatter(
            totals[11].astype(jnp.bfloat16), "dp", scatter_dimension=0, tiled=True
        ).astype(jnp.float32),
        lax.psum_scatter(
            totals[12].astype(jnp.bfloat16), "dp", scatter_dimension=0, tiled=True
        ).astype(jnp.float32),
    )
    shares = (
        lax.psum_scatter(
            partial_sums[0].astype(jnp.bfloat16), "fsdp", scatter_dimension=0, tiled=True
        ).astype(jnp.float32),
        lax.psum_scatter(
            partial_sums[1].astype(jnp.bfloat16), "fsdp", scatter_dimension=0, tiled=True
        ).astype(jnp.float32),
        lax.psum_scatter(
            partial_sums[2].astype(jnp.bfloat16), "fsdp", scatter_dimension=0, tiled=True
        ).astype(jnp.float32),
        lax.psum_scatter(
            partial_sums[3].astype(jnp.bfloat16), "fsdp", scatter_dimension=0, tiled=True
        ).astype(jnp.float32),
        lax.psum_scatter(
            partial_sums[4].astype(jnp.bfloat16), "fsdp", scatter_dimension=0, tiled=True
        ).astype(jnp.float32),
        lax.psum_scatter(
            partial_sums[5].astype(jnp.bfloat16), "fsdp", scatter_dimension=0, tiled=True
        ).astype(jnp.float32),
        lax.psum_scatter(
            partial_sums[6].astype(jnp.bfloat16), "fsdp", scatter_dimension=0, tiled=True
        ).astype(jnp.float32),
        lax.psum_scatter(
            partial_sums[7].astype(jnp.bfloat16), "fsdp", scatter_dimension=0, tiled=True
        ).astype(jnp.float32),
        lax.psum_scatter(
            partial_sums[8].astype(jnp.bfloat16), "fsdp", scatter_dimension=0, tiled=True
        ).astype(jnp.float32),
        lax.psum_scatter(
            partial_sums[9].astype(jnp.bfloat16), "fsdp", scatter_dimension=0, tiled=True
        ).astype(jnp.float32),
        lax.psum_scatter(
            partial_sums[10].astype(jnp.bfloat16), "fsdp", scatter_dimension=0, tiled=True
        ).astype(jnp.float32),
        lax.psum_scatter(
            partial_sums[11].astype(jnp.bfloat16), "fsdp", scatter_dimension=0, tiled=True
        ).astype(jnp.float32),
        lax.psum_scatter(
            partial_sums[12].astype(jnp.bfloat16), "fsdp", scatter_dimension=0, tiled=True
        ).astype(jnp.float32),
    )
    return (
        first_low[None],
        second_out.astype(jnp.bfloat16)[None],
        grad_inputs.astype(jnp.bfloat16)[None],
        shares[0],
        shares[1],
        shares[2],
        shares[3],
        shares[4],
        shares[5],
        shares[6],
        shares[7],
        shares[8],
        shares[9],
        shares[10],
        shares[11],
        shares[12],
    )


def solution(mesh):
    return jax.shard_map(
        per_device,
        mesh=mesh,
        in_specs=(
            P(("dp", "fsdp"), None, None),
            P(("dp", "fsdp")),
            P(("dp", "fsdp")),
            P(("dp", "fsdp"), None),
            P(("dp", "fsdp")),
            P(("dp", "fsdp")),
            P(("dp", "fsdp"), None),
            P(("dp", "fsdp")),
            P(("dp", "fsdp")),
            P(("dp", "fsdp")),
            P(("dp", "fsdp"), None),
            P(("dp", "fsdp")),
            P(("dp", "fsdp"), None),
            P(("dp", "fsdp")),
            P(("dp", "fsdp"), None, None),
            P(("dp", "fsdp"), None, None),
            P(("dp", "fsdp"), None),
        ),
        out_specs=(
            P(("dp", "fsdp"), None, None),
            P(("dp", "fsdp"), None, None),
            P(("dp", "fsdp"), None, None),
            P(("dp", "fsdp")),
            P(("dp", "fsdp")),
            P(("dp", "fsdp"), None),
            P(("dp", "fsdp")),
            P(("dp", "fsdp")),
            P(("dp", "fsdp"), None),
            P(("dp", "fsdp")),
            P(("dp", "fsdp")),
            P(("dp", "fsdp")),
            P(("dp", "fsdp"), None),
            P(("dp", "fsdp")),
            P(("dp", "fsdp"), None),
            P(("dp", "fsdp")),
        ),
        check_vma=False,
    )
```

profile of v0, /device:TPU:0, one launch (start us, length us, event | category | flops | bytes accessed | tf_op | source)
XLA Modules:
  0.0 1061.5 jit_solution(16335738854915446491)
XLA Ops:
  16.7 42.4 %all-reduce.26 = (bf16[1024]{0:T(1024)(128)(2,1)S(1)}, bf16[1024]{0:T(1024)(128)(2,1)S(1)}, bf16[1024]{0:T(1024)(128)(2,1)S(1)}, bf16[1024]{0:T(1024)(128)(2,1)S...) all-reduce(bf16[1024]{0:T(1024)(128)(2,1)S(1)} %dynamic-update-slic, ...), channel_id=1, replica_groups=mesh['dp'=4,'fsdp'=8] {'dp','fsdp'}, use_global_device_ids=true, to_apply=%add.1 | all-reduce | flops 8192 | bytes 32768
  59.2 65.8 %all-gather = bf16[32,1,128]{2,1,0:T(2,128)(2,1)S(1)} all-gather(bf16[1,1,128]{2,1,0:T(2,128)(2,1)} %bitcast.196), channel_id=1, replica_groups=mesh['dp'=4,'fsdp'=8] {'dp','fsdp'}, dimensions={0}, use_global_device_ids=true | all-gather | bytes 8448 | tf_op jit(solution)/shard_map/all_gather | solution.py:264
  128.4 1.6 fusion.46
  130.1 6.6 fusion.98
  136.8 1.6 fusion.54
  139.5 1.9 copy.73
  141.4 8.2 multiply_reduce_fusion.3
  149.6 8.9 fusion
  158.5 8.8 fusion.60
  167.3 3.3 fusion.117
  171.9 48.7 %all-gather.10.cloned.1.call-done = bf16[1024,4096]{1,0:T(8,128)(2,1)} async-done(((bf16[32,4096]{1,0:T(8,128)(2,1)}), bf16[1024,4096]{1,0:T(8,128)(2,1)}) %all-gather.10.cloned.1.call-update) | async-done | bytes 8388624 | tf_op jit(solution)/shard_map/all_gather | solution.py:263
  220.7 27.7 %multiply_convert_fusion.3 = (bf16[512,4096]{1,0:T(8,128)(2,1)}, f32[512,4096]{1,0:T(8,128)}, f32[512,4096]{1,0:T(8,128)}) fusion(f32[4096]{0:T(1024)S(1)} %bitcast.192, bf16[1024,4096]{1,0:T(8,128)(2,1)} %all-gather.10.cloned.1.call-done, f32[512,1024]{1,0:T(8,128)S(1)} %get-tuple-element.168, f32[1024]{0:T(1024)S(1)} %convert_element_type.403, ...), kind=kOutput, calls=%fused_computation.44 | convolution fusion | flops 4436000768 | bytes 31485952 | tf_op jit(solution)/shard_map/dot_general | solution.py:113
  248.5 51.1 %all-gather.12.cloned.1.call-done = bf16[4096,1024]{1,0:T(8,128)(2,1)} async-done(((bf16[128,1024]{1,0:T(8,128)(2,1)}), bf16[4096,1024]{1,0:T(8,128)(2,1)}) %all-gather.12.cloned.1.call-update) | async-done | bytes 8388624 | tf_op jit(solution)/shard_map/all_gather | solution.py:265
  299.5 9.9 add_convert_fusion.9
  310.2 5.8 fusion.101
  316.0 1.6 fusion.52
  319.3 2.1 copy.79
  321.4 8.2 multiply_reduce_fusion.2
  329.6 8.7 fusion.1
  339.4 8.2 fusion.59
  349.5 28.3 %multiply_convert_fusion.2 = (bf16[512,4096]{1,0:T(8,128)(2,1)}, f32[512,4096]{1,0:T(8,128)}, f32[512,4096]{1,0:T(8,128)}) fusion(f32[4096]{0:T(1024)S(1)} %bitcast.193, bf16[1024,4096]{1,0:T(8,128)(2,1)} %all-gather.10.cloned.1.call-done, f32[512,1024]{1,0:T(8,128)S(1)} %get-tuple-element.173, f32[512]{0:T(512)S(1)} %fusion.77, ...), kind=kOutput, calls=%fused_computation.31 | convolution fusion | flops 4436000768 | bytes 31485952 | tf_op jit(solution)/shard_map/dot_general | solution.py:113
  377.8 15.5 %convert_reduce_fusion = (f32[4096]{0:T(1024)}, bf16[512,4096]{1,0:T(8,128)(2,1)}) fusion(f32[512,4096]{1,0:T(8,128)} %get-tuple-element.157, bf16[4096,1024]{1,0:T(8,128)(2,1)} %all-gather.12.cloned.1.call-done, bf16[1,512,1024]{2,1,0:T(8,128)(2,1)S(1)} %copy-done.28, f32[512]{0:T(512)S(1)} %bitcast.188, f32[512,4096]{1,0:T(8,128)} %get-tuple-element.174, ...), kind=kOutput, calls=%fused_computation.25 | convolution fusion | flops 4332187648 | bytes 30443520 | tf_op jit(solution)/shard_map/sd,fd->sf/dot_general | solution.py:174
  393.3 9.5 multiply_reduce_fusion.4
  409.7 16.5 %multiply_reduce_fusion.1 = (f32[16,512]{1,0:T(8,128)}, f32[16,512,512]{1,2,0:T(8,128)}) fusion(f32[16,512,512]{1,2,0:T(8,128)} %get-tuple-element.171, f32[16,512]{1,0:T(8,128)} %log_add_fusion.1, bf16[512,16,64]{0,2,1:T(8,128)(2,1)} %bitcast.164, bf16[512,16,64]{0,2,1:T(8,128)(2,1)} %bitcast.171), kind=kOutput, calls=%fused_computation.6 | convolution fusion | flops 553639936 | bytes 35717120 | tf_op jit(solution)/shard_map/while/body/eval_jaxpr/qhd,khd->hqk/dot_general | solution.py:45
  426.3 8.1 multiply_convert_fusion.1
  434.4 3.2 copy-done
  437.7 2.1 convert_reduce_fusion.10
  439.7 6.4 multiply_convert_fusion.6
  446.2 9.0 convert_reduce_fusion.8
  455.3 7.7 fusion.108
  464.6 2.0 convert_reduce_fusion.5
  466.6 16.1 %convert_reduce_fusion.1 = (f32[4096]{0:T(1024)}, bf16[512,4096]{1,0:T(8,128)(2,1)}) fusion(f32[512,4096]{1,0:T(8,128)} %get-tuple-element.159, bf16[4096,1024]{1,0:T(8,128)(2,1)} %all-gather.12.cloned.1.call-done, f32[512,1024]{1,0:T(8,128)S(1)} %get-tuple-element.147, f32[512,4096]{1,0:T(8,128)} %get-tuple-element.169, f32[4096]{0:T(1024)S(1)} %bitcast.195), kind=kOutput, calls=%fused_computation.26 | convolution fusion | flops 4331139072 | bytes 31490048 | tf_op jit(solution)/shard_map/sd,fd->sf/dot_general | solution.py:174
  482.8 9.5 multiply_reduce_fusion.5
  495.8 2.6 add_convert_fusion.5
  498.5 3.5 convolution_convert_fusion
  502.0 2.3 copy.85
  504.4 17.1 %multiply_reduce_fusion = (f32[16,512]{1,0:T(8,128)}, f32[16,512,512]{1,2,0:T(8,128)}) fusion(f32[16,512,512]{1,2,0:T(8,128)} %get-tuple-element.166, f32[16,512]{1,0:T(8,128)} %log_add_fusion, bf16[512,16,64]{0,2,1:T(8,128)(2,1)} %bitcast.166, bf16[512,16,64]{0,2,1:T(8,128)(2,1)} %bitcast.169), kind=kOutput, calls=%fused_computation.3 | convolution fusion | flops 553639936 | bytes 35717120 | tf_op jit(solution)/shard_map/while/body/eval_jaxpr/qhd,khd->hqk/dot_general | solution.py:45
  521.5 8.1 multiply_convert_fusion
  529.6 3.3 copy-done.1
  532.9 2.1 convert_reduce_fusion.11
  535.0 6.4 multiply_convert_fusion.4
  541.5 8.6 convert_reduce_fusion.9
  551.2 9.7 fusion.68
  560.9 11.8 %add_convert_fusion.2 = bf16[1024,3072]{1,0:T(8,128)(2,1)} fusion(f32[1024,3072]{1,0:T(8,128)} %fusion.68, bf16[512,1024]{0,1:T(8,128)(2,1)S(1)} %bitcast.185, bf16[512,1024]{0,1:T(8,128)(2,1)S(1)} %bitcast.183, bf16[512,1024]{0,1:T(8,128)(2,1)S(1)} %bitcast.177, bf16[512,1024]{1,0:T(8,128)(2,1)S(1)} %add_convert_fusion.9, f32[512]{0:T(512)S(1)} %copy-done.80, ...), kind=kOutput, calls=%fused_computation.16 | convolution fusion | flops 3240099840 | bytes 23080960 | tf_op jit(solution)/shard_map/sd,se->de/dot_general | solution.py:207
  574.4 12.1 %fusion.82 = f32[4096,1024]{1,0:T(8,128)} fusion(bf16[512,4096]{1,0:T(8,128)(2,1)} %get-tuple-element.158, f32[512,1024]{1,0:T(8,128)S(1)} %copy-done.11), kind=kOutput, calls=%fused_computation.197 | convolution fusion | flops 4295491584 | bytes 23068672 | tf_op jit(solution)/shard_map/sf,sd->fd/dot_general | solution.py:172
  586.5 12.0 %add_convert_fusion = bf16[4096,1024]{1,0:T(8,128)(2,1)} fusion(f32[4096,1024]{1,0:T(8,128)} %fusion.82, bf16[512,4096]{1,0:T(8,128)(2,1)} %get-tuple-element.156, bf16[1,512,1024]{2,1,0:T(8,128)(2,1)S(1)} %copy-done.30, f32[512]{0:T(512)S(1)} %bitcast.191), kind=kOutput, calls=%fused_computation | convolution fusion | flops 4304928768 | bytes 30410752 | tf_op jit(solution)/shard_map/sf,sd->fd/dot_general | solution.py:172
  599.1 13.3 %fusion.105 = f32[1024,4096]{1,0:T(8,128)} fusion(bf16[512,4096]{1,0:T(8,128)(2,1)} %get-tuple-element.192, f32[512,1024]{1,0:T(8,128)} %copy-done.12, f32[1024]{0:T(1024)S(1)} %copy-done.116, f32[1024]{0:T(1024)S(1)} %copy-done.59, f32[512]{0:T(512)S(1)} %copy-done.104, f32[512]{0:T(512)S(1)} %copy-done.87), kind=kOutput, calls=%fused_computation.210 | convolution fusion | flops 4297588736 | bytes 23080960 | tf_op jit(solution)/shard_map/sd,sf->df/dot_general | solution.py:179
  612.5 11.8 %add_convert_fusion.1 = bf16[1024,4096]{1,0:T(8,128)(2,1)} fusion(f32[1024,4096]{1,0:T(8,128)} %fusion.105, bf16[512,4096]{1,0:T(8,128)(2,1)} %get-tuple-element.194, f32[512,1024]{1,0:T(8,128)S(1)} %copy-done.8, f32[512]{0:T(512)S(1)} %copy-done.106, f32[512]{0:T(512)S(1)} %copy-done.89, f32[1024]{0:T(1024)S(1)} %copy-done.116, f32[1024]{0:T(1024)S(1)} %copy-done.59), kind=kOutput, calls=%fused_computation.1 | convolution fusion | flops 4305977344 | bytes 31469568 | tf_op jit(solution)/shard_map/sd,sf->df/dot_general | solution.py:179
  625.2 5.2 reduce-scatter.9.cloned.1.call-done
  630.5 74.3 %reduce-scatter.21.cloned.1.call-done = bf16[1024,1024]{1,0:T(8,128)(2,1)} async-done(((bf16[4096,1024]{1,0:T(8,128)(2,1)}), bf16[1024,1024]{1,0:T(8,128)(2,1)}) %reduce-scatter.21.cloned.1.call-update) | async-done | bytes 2097168 | tf_op jit(solution)/shard_map/reduce_scatter | solution.py:328
  709.1 8.2 fusion.109
  717.3 62.0 %reduce-scatter.17.cloned.1.call-done = bf16[256,4096]{1,0:T(8,128)(2,1)} async-done(((bf16[1024,4096]{1,0:T(8,128)(2,1)}), bf16[256,4096]{1,0:T(8,128)(2,1)}) %reduce-scatter.17.cloned.1.call-update) | async-done | bytes 2097168 | tf_op jit(solution)/shard_map/reduce_scatter | solution.py:322
  779.5 2.6 fusion.45
  782.2 10.3 all-reduce.28
  793.0 21.8 %all-reduce.27 = (bf16[256]{0:T(256)(128)(2,1)S(1)}, bf16[256]{0:T(256)(128)(2,1)S(1)}, bf16[256]{0:T(256)(128)(2,1)S(1)}, bf16[256]{0:T(256)(128)(2,1)S(1)}, bf...) all-reduce(bf16[256]{0:T(256)(128)(2,1)S(1)} %dynamic-slice.3, ...), channel_id=3, replica_groups=mesh['dp'=4,'fsdp'=8] {'fsdp'}, use_global_device_ids=true, to_apply=%region_25.26.clone | all-reduce | flops 3072 | bytes 12288
  820.1 3.5 fusion.72
  823.5 9.0 fusion.67
  832.5 12.2 %reduce-scatter.15.cloned.1.call-done = bf16[32,1024]{1,0:T(8,128)(2,1)} async-done(((bf16[256,1024]{1,0:T(8,128)(2,1)}), bf16[32,1024]{1,0:T(8,128)(2,1)}) %reduce-scatter.15.cloned.1.call-update) | async-done | bytes 65552 | tf_op jit(solution)/shard_map/reduce_scatter | solution.py:351
  846.2 66.0 %reduce-scatter.11.cloned.1.call-done = bf16[32,3072]{1,0:T(8,128)(2,1)} async-done(((bf16[256,3072]{1,0:T(8,128)(2,1)}), bf16[32,3072]{1,0:T(8,128)(2,1)}) %reduce-scatter.11.cloned.1.call-update) | async-done | bytes 196624 | tf_op jit(solution)/shard_map/reduce_scatter | solution.py:342
  912.2 1.7 convert_element_type.462
  913.9 68.6 %reduce-scatter.23.cloned.1.call-done = bf16[128,1024]{1,0:T(8,128)(2,1)} async-done(((bf16[1024,1024]{1,0:T(8,128)(2,1)}), bf16[128,1024]{1,0:T(8,128)(2,1)}) %reduce-scatter.23.cloned.1.call-update) | async-done | bytes 262160 | tf_op jit(solution)/shard_map/reduce_scatter | solution.py:369
  982.5 1.8 convert_element_type.490
  984.3 68.4 %reduce-scatter.19.cloned.1.call-done = bf16[32,4096]{1,0:T(8,128)(2,1)} async-done(((bf16[256,4096]{1,0:T(8,128)(2,1)}), bf16[32,4096]{1,0:T(8,128)(2,1)}) %reduce-scatter.19.cloned.1.call-update) | async-done | bytes 262160 | tf_op jit(solution)/shard_map/reduce_scatter | solution.py:363
  1052.7 1.8 convert_element_type.484
  (383 shorter events, 45.9 us)
Async XLA Ops:
  7.2 122.9 %all-gather.6.cloned.1.call-start = ((), (), s32[]{:S(2)}) async-start(), calls=%async_computation.8 | async-start | bytes 6488064 | tf_op jit(solution)/shard_map/all_gather | solution.py:256
  7.9 159.4 %all-gather.8.cloned.1.call-start = ((), (), s32[]{:S(2)}) async-start(), calls=%async_computation.9 | async-start | bytes 2162688 | tf_op jit(solution)/shard_map/all_gather | solution.py:259
  8.7 212.0 %all-gather.10.cloned.1.call-start = ((), (), s32[]{:S(2)}) async-start(), calls=%async_computation.10 | async-start | bytes 8650752 | tf_op jit(solution)/shard_map/all_gather | solution.py:263
  9.4 290.1 %all-gather.12.cloned.1.call-start = ((), (), s32[]{:S(2)}) async-start(), calls=%async_computation.11 | async-start | bytes 8650752 | tf_op jit(solution)/shard_map/all_gather | solution.py:265
  10.0 614.5 %reduce-scatter.13.cloned.1.call-start = ((), (), s32[]{:S(2)}) async-start(), calls=%async_computation.14 | async-start | bytes 2621440 | tf_op jit(solution)/shard_map/reduce_scatter | solution.py:310
  59.1 251.0 %copy-start.54 = (f32[1024]{0:T(1024)}, f32[1024]{0:T(1024)S(1)}, u32[]{:S(2)}) copy-start(f32[1024]{0:T(1024)S(1)} %convert_element_type.390) | copy-start | bytes 12292
  59.1 77.5 %copy-start.117 = (f32[1024]{0:T(1024)}, f32[1024]{0:T(1024)S(1)}, u32[]{:S(2)}) copy-start(f32[1024]{0:T(1024)S(1)} %convert_element_type.391) | copy-start | bytes 12292
  59.2 77.7 %copy-start.56 = (f32[1024]{0:T(1024)}, f32[1024]{0:T(1024)S(1)}, u32[]{:S(2)}) copy-start(f32[1024]{0:T(1024)S(1)} %convert_element_type.395) | copy-start | bytes 12292
  59.2 161.5 %copy-start.58 = (f32[1024]{0:T(1024)}, f32[1024]{0:T(1024)S(1)}, u32[]{:S(2)}) copy-start(f32[1024]{0:T(1024)S(1)} %convert_element_type.402) | copy-start | bytes 12292
  59.2 161.5 %copy-start.114 = (f32[1024]{0:T(1024)}, f32[1024]{0:T(1024)S(1)}, u32[]{:S(2)}) copy-start(f32[1024]{0:T(1024)S(1)} %convert_element_type.403) | copy-start | bytes 12292
  125.1 95.6 %copy-start.98 = (f32[32,1,128]{2,1,0:T(1,128)}, f32[32,1,128]{2,1,0:T(1,128)S(1)}, u32[]{:S(2)}) copy-start(f32[32,1,128]{2,1,0:T(1,128)S(1)} %convert_element_type.497) | copy-start | bytes 49156
  141.4 17.1 %copy-start.31 = (bf16[512,1024]{0,1:T(8,128)(2,1)}, bf16[512,1024]{0,1:T(8,128)(2,1)S(1)}, u32[]{:S(2)}) copy-start(bf16[512,1024]{0,1:T(8,128)(2,1)S(1)} %copy.73) | copy-start | bytes 3145732
  170.6 77.8 %copy-start.12 = (f32[512,1024]{1,0:T(8,128)}, f32[512,1024]{1,0:T(8,128)S(1)}, u32[]{:S(2)}) copy-start(f32[512,1024]{1,0:T(8,128)S(1)} %get-tuple-element.168) | copy-start | bytes 6291460
  170.6 77.8 %copy-start.85 = (f32[512]{0:T(512)}, f32[512]{0:T(512)S(1)}, u32[]{:S(2)}) copy-start(f32[512]{0:T(512)S(1)} %broadcast_multiply_fusion.2) | copy-start | bytes 6148
  171.0 77.5 %copy-start.90 = (f32[512]{0:T(512)}, f32[512]{0:T(512)S(1)}, u32[]{:S(2)}) copy-start(f32[512]{0:T(512)S(1)} %multiply_reduce_fusion.9) | copy-start | bytes 6148
  171.0 77.4 %copy-start.102 = (f32[512]{0:T(512)}, f32[512]{0:T(512)S(1)}, u32[]{:S(2)}) copy-start(f32[512]{0:T(512)S(1)} %fusion.75) | copy-start | bytes 6148
  220.7 78.9 %copy-start.112 = (f32[1024]{0:T(1024)S(1)}, f32[1024]{0:T(1024)}, u32[]{:S(2)}) copy-start(f32[1024]{0:T(1024)} %convert_element_type.407) | copy-start | bytes 12292
  309.5 251.5 %copy-start.4 = (bf16[512,1024]{1,0:T(8,128)(2,1)}, bf16[512,1024]{1,0:T(8,128)(2,1)S(1)}, u32[]{:S(2)}) copy-start(bf16[512,1024]{1,0:T(8,128)(2,1)S(1)} %add_convert_fusion.9) | copy-start | bytes 3145732
  347.6 30.2 %copy-start.36 = (bf16[16,64,512]{2,1,0:T(8,128)(2,1)}, bf16[16,64,512]{2,1,0:T(8,128)(2,1)S(1)}, u32[]{:S(2)}) copy-start(bf16[16,64,512]{2,1,0:T(8,128)(2,1)S(1)} %fusion.59) | copy-start | bytes 3145732
  349.1 53.8 %copy-start.7 = (f32[512,1024]{1,0:T(8,128)}, f32[512,1024]{1,0:T(8,128)S(1)}, u32[]{:S(2)}) copy-start(f32[512,1024]{1,0:T(8,128)S(1)} %get-tuple-element.173) | copy-start | bytes 6291460
  349.1 53.8 %copy-start.88 = (f32[512]{0:T(512)}, f32[512]{0:T(512)S(1)}, u32[]{:S(2)}) copy-start(f32[512]{0:T(512)S(1)} %broadcast_multiply_fusion) | copy-start | bytes 6148
  349.5 53.4 %copy-start.105 = (f32[512]{0:T(512)}, f32[512]{0:T(512)S(1)}, u32[]{:S(2)}) copy-start(f32[512]{0:T(512)S(1)} %fusion.77) | copy-start | bytes 6148
  349.5 28.3 %copy-start.28 = (bf16[1,512,1024]{2,1,0:T(8,128)(2,1)S(1)}, bf16[1,512,1024]{2,1,0:T(8,128)(2,1)}, u32[]{:S(2)}) copy-start(bf16[1,512,1024]{2,1,0:T(8,128)(2,1)} %param.32) | copy-start | bytes 3145732
  349.5 28.3 %copy-start.69 = (f32[1,512]{1,0:T(1,128)S(1)}, f32[1,512]{1,0:T(1,128)}, u32[]{:S(2)}) copy-start(f32[1,512]{1,0:T(1,128)} %convert_element_type.422) | copy-start | bytes 6148
  409.7 16.6 %slice-start.5 = ((s8[16777216]{0:T(1024)(128)(4,1)}), s8[4194304]{0:T(1024)(128)(4,1)S(1)}, s32[]{:S(2)}) async-start(s8[16777216]{0:T(1024)(128)(4,1)} %bitcast.153), calls=%async_computation.25 | async-start | bytes 8388608
  409.7 16.6 %slice-start.6 = ((s8[16777216]{0:T(1024)(128)(4,1)}), s8[4194304]{0:T(1024)(128)(4,1)S(1)}, s32[]{:S(2)}) async-start(s8[16777216]{0:T(1024)(128)(4,1)} %bitcast.153), calls=%async_computation.26 | async-start | bytes 8388608
  409.7 16.6 %slice-start.7 = ((s8[16777216]{0:T(1024)(128)(4,1)}), s8[4194304]{0:T(1024)(128)(4,1)S(1)}, s32[]{:S(2)}) async-start(s8[16777216]{0:T(1024)(128)(4,1)} %bitcast.153), calls=%async_computation.27 | async-start | bytes 8388608
  466.6 26.5 %copy-start.10 = (f32[512,1024]{1,0:T(8,128)}, f32[512,1024]{1,0:T(8,128)S(1)}, u32[]{:S(2)}) copy-start(f32[512,1024]{1,0:T(8,128)S(1)} %get-tuple-element.147) | copy-start | bytes 6291460
  498.5 132.0 %reduce-scatter.9.cloned.1.call-start = ((), (), s32[]{:S(2)}) async-start(), calls=%async_computation.12 | async-start | bytes 7864320 | tf_op jit(solution)/shard_map/reduce_scatter | solution.py:301
  504.3 17.1 %slice-start = ((s8[16777216]{0:T(1024)(128)(4,1)}), s8[4194304]{0:T(1024)(128)(4,1)S(1)}, s32[]{:S(2)}) async-start(s8[16777216]{0:T(1024)(128)(4,1)} %bitcast.151), calls=%async_computation.20 | async-start | bytes 8388608
  504.3 17.1 %slice-start.1 = ((s8[16777216]{0:T(1024)(128)(4,1)}), s8[4194304]{0:T(1024)(128)(4,1)S(1)}, s32[]{:S(2)}) async-start(s8[16777216]{0:T(1024)(128)(4,1)} %bitcast.151), calls=%async_computation.21 | async-start | bytes 8388608
  504.3 17.1 %slice-start.2 = ((s8[16777216]{0:T(1024)(128)(4,1)}), s8[4194304]{0:T(1024)(128)(4,1)S(1)}, s32[]{:S(2)}) async-start(s8[16777216]{0:T(1024)(128)(4,1)} %bitcast.151), calls=%async_computation.22 | async-start | bytes 8388608
  504.3 17.1 %slice-start.3 = ((s8[16777216]{0:T(1024)(128)(4,1)}), s8[4194304]{0:T(1024)(128)(4,1)S(1)}, s32[]{:S(2)}) async-start(s8[16777216]{0:T(1024)(128)(4,1)} %bitcast.151), calls=%async_computation.23 | async-start | bytes 8388608
  572.8 132.0 %reduce-scatter.21.cloned.1.call-start = ((), (), s32[]{:S(2)}) async-start(), calls=%async_computation.18 | async-start | bytes 10485760 | tf_op jit(solution)/shard_map/reduce_scatter | solution.py:328
  598.5 180.8 %reduce-scatter.17.cloned.1.call-start = ((), (), s32[]{:S(2)}) async-start(), calls=%async_computation.16 | async-start | bytes 10485760 | tf_op jit(solution)/shard_map/reduce_scatter | solution.py:322
  624.3 80.8 %copy-start.121 = (u32[32]{0:T(128)S(1)}, u32[32]{0:T(128)}, u32[]{:S(2)}) copy-start(u32[32]{0:T(128)} %constant.185) | copy-start | bytes 388
  624.3 82.7 %copy-start.120 = (u32[32]{0:T(128)S(1)}, u32[32]{0:T(128)}, u32[]{:S(2)}) copy-start(u32[32]{0:T(128)} %constant.189) | copy-start | bytes 388
  624.3 84.6 %copy-start.94 = (f32[1024]{0:T(1024)S(1)}, f32[1024]{0:T(1024)}, u32[]{:S(2)}) copy-start(f32[1024]{0:T(1024)} %get-tuple-element.164) | copy-start | bytes 12292
  624.3 84.6 %copy-start.95 = (f32[1024]{0:T(1024)S(1)}, f32[1024]{0:T(1024)}, u32[]{:S(2)}) copy-start(f32[1024]{0:T(1024)} %get-tuple-element.146) | copy-start | bytes 12292
  624.3 84.6 %copy-start.93 = (f32[1024]{0:T(1024)S(1)}, f32[1024]{0:T(1024)}, u32[]{:S(2)}) copy-start(f32[1024]{0:T(1024)} %get-tuple-element.148) | copy-start | bytes 12292
  624.3 84.6 %copy-start.101 = (f32[1024]{0:T(1024)S(1)}, f32[1024]{0:T(1024)}, u32[]{:S(2)}) copy-start(f32[1024]{0:T(1024)} %get-tuple-element.150) | copy-start | bytes 12292
  624.3 84.6 %copy-start.66 = (f32[16,64]{1,0:T(8,128)S(1)}, f32[16,64]{1,0:T(8,128)}, u32[]{:S(2)}) copy-start(f32[16,64]{1,0:T(8,128)} %get-tuple-element.189) | copy-start | bytes 12292
  624.3 84.6 %copy-start.68 = (f32[16,64]{1,0:T(8,128)S(1)}, f32[16,64]{1,0:T(8,128)}, u32[]{:S(2)}) copy-start(f32[16,64]{1,0:T(8,128)} %get-tuple-element.187) | copy-start | bytes 12292
  624.3 84.6 %copy-start.65 = (f32[16,64]{1,0:T(8,128)S(1)}, f32[16,64]{1,0:T(8,128)}, u32[]{:S(2)}) copy-start(f32[16,64]{1,0:T(8,128)} %get-tuple-element.185) | copy-start | bytes 12292
  624.3 84.6 %copy-start.67 = (f32[16,64]{1,0:T(8,128)S(1)}, f32[16,64]{1,0:T(8,128)}, u32[]{:S(2)}) copy-start(f32[16,64]{1,0:T(8,128)} %get-tuple-element.183) | copy-start | bytes 12292
  624.3 84.6 %copy-start.107 = (f32[1024]{0:T(1024)S(1)}, f32[1024]{0:T(1024)}, u32[]{:S(2)}) copy-start(f32[1024]{0:T(1024)} %get-tuple-element.88) | copy-start | bytes 12292
  624.3 84.6 %copy-start.108 = (f32[1024]{0:T(1024)S(1)}, f32[1024]{0:T(1024)}, u32[]{:S(2)}) copy-start(f32[1024]{0:T(1024)} %get-tuple-element.105) | copy-start | bytes 12292
  624.4 84.6 %copy-start.110 = (f32[1024]{0:T(1024)S(1)}, f32[1024]{0:T(1024)}, u32[]{:S(2)}) copy-start(f32[1024]{0:T(1024)} %get-tuple-element.90) | copy-start | bytes 12292
  624.4 84.6 %copy-start.111 = (f32[1024]{0:T(1024)S(1)}, f32[1024]{0:T(1024)}, u32[]{:S(2)}) copy-start(f32[1024]{0:T(1024)} %get-tuple-element.106) | copy-start | bytes 12292
  624.4 84.7 %copy-start.39 = (bf16[16,64,512]{2,1,0:T(8,128)(2,1)S(1)}, bf16[16,64,512]{2,1,0:T(8,128)(2,1)}, u32[]{:S(2)}) copy-start(bf16[16,64,512]{2,1,0:T(8,128)(2,1)} %copy-done.38) | copy-start | bytes 3145732
  624.4 84.7 %copy-start.44 = (bf16[16,64,512]{2,1,0:T(8,128)(2,1)S(1)}, bf16[16,64,512]{2,1,0:T(8,128)(2,1)}, u32[]{:S(2)}) copy-start(bf16[16,64,512]{2,1,0:T(8,128)(2,1)} %copy-done.43) | copy-start | bytes 3145732
  624.4 220.3 %reduce-scatter.15.cloned.1.call-start = ((), (), s32[]{:S(2)}) async-start(), calls=%async_computation.15 | async-start | bytes 589824 | tf_op jit(solution)/shard_map/reduce_scatter | solution.py:351
  625.2 287.0 %reduce-scatter.11.cloned.1.call-start = ((), (), s32[]{:S(2)}) async-start(), calls=%async_computation.13 | async-start | bytes 1769472 | tf_op jit(solution)/shard_map/reduce_scatter | solution.py:342
  630.5 352.1 %reduce-scatter.23.cloned.1.call-start = ((), (), s32[]{:S(2)}) async-start(), calls=%async_computation.19 | async-start | bytes 2359296 | tf_op jit(solution)/shard_map/reduce_scatter | solution.py:369
  704.8 347.9 %reduce-scatter.19.cloned.1.call-start = ((), (), s32[]{:S(2)}) async-start(), calls=%async_computation.17 | async-start | bytes 2359296 | tf_op jit(solution)/shard_map/reduce_scatter | solution.py:363
  709.0 70.3 %copy-start.82 = (f32[512]{0:T(512)S(1)}, f32[512]{0:T(512)}, u32[]{:S(2)}) copy-start(f32[512]{0:T(512)} %copy-done.81) | copy-start | bytes 6148
  709.1 70.5 %copy-start.75 = (f32[512]{0:T(512)S(1)}, f32[512]{0:T(512)}, u32[]{:S(2)}) copy-start(f32[512]{0:T(512)} %copy-done.73) | copy-start | bytes 6148
  709.1 73.0 %copy-start.92 = (f32[1024]{0:T(1024)S(1)}, f32[1024]{0:T(1024)}, u32[]{:S(2)}) copy-start(f32[1024]{0:T(1024)} %get-tuple-element.92) | copy-start | bytes 12292
  709.1 73.0 %copy-start.109 = (f32[1024]{0:T(1024)S(1)}, f32[1024]{0:T(1024)}, u32[]{:S(2)}) copy-start(f32[1024]{0:T(1024)} %get-tuple-element.107) | copy-start | bytes 12292
  709.1 73.0 %copy-start.96 = (f32[4096]{0:T(1024)S(1)}, f32[4096]{0:T(1024)}, u32[]{:S(2)}) copy-start(f32[4096]{0:T(1024)} %get-tuple-element.193) | copy-start | bytes 49156
  709.1 73.0 %copy-start.97 = (f32[4096]{0:T(1024)S(1)}, f32[4096]{0:T(1024)}, u32[]{:S(2)}) copy-start(f32[4096]{0:T(1024)} %get-tuple-element.191) | copy-start | bytes 49156
  709.1 110.9 %copy-start.77 = (f32[512]{0:T(512)S(1)}, f32[512]{0:T(512)}, u32[]{:S(2)}) copy-start(f32[512]{0:T(512)} %copy-done.76) | copy-start | bytes 6148
  717.3 102.8 %copy-start.6 = (f32[512,1024]{1,0:T(8,128)S(1)}, f32[512,1024]{1,0:T(8,128)}, u32[]{:S(2)}) copy-start(f32[512,1024]{1,0:T(8,128)} %copy-done.5) | copy-start | bytes 6291460
  779.3 44.2 %copy-start.113 = (f32[1024]{0:T(1024)S(1)}, f32[1024]{0:T(1024)}, u32[]{:S(2)}) copy-start(f32[1024]{0:T(1024)} %convert_element_type.407) | copy-start | bytes 12292
  (79 other events, 599.3 us)
Sparse Core Ops, SparseCore 0:
  10.9 72.3 all-gather.5
  86.3 55.0 all-gather.7
  144.4 76.2 all-gather.9
  223.5 75.9 all-gather.11
  498.6 29.9 reduce-scatter.12
  572.9 57.4 reduce-scatter.8
  633.0 71.7 reduce-scatter.20
  707.6 71.6 reduce-scatter.16
  782.7 62.0 reduce-scatter.14
  848.4 63.7 reduce-scatter.10
  915.7 66.7 reduce-scatter.22
  985.9 66.7 reduce-scatter.18
where the time goes:
time: 1070 us; the launch traced here: 1060 us
  waiting for transfers between devices  460 us (43%)
  matrix products  339 us (32%)
  blocking collectives  140 us (13%)
  other arithmetic  70 us (7%)
  local copies, waits for them, and re-layouts  32.2 us (3%)
  between operations  18.6 us (2%)
    unnamed x3, blocking collectives  74.4 us
    reduce_scatter x1, waiting for transfers between devices, per_device(): lax.psum_scatter(totals[11].astype(jnp.bfloat16), 'dp', scatter_dimension...  74.3 us
    reduce_scatter x1, waiting for transfers between devices, per_device(): lax.psum_scatter(partial_sums[11].astype(jnp.bfloat16), 'fsdp', scatter_d...  68.6 us
    reduce_scatter x1, waiting for transfers between devices, per_device(): lax.psum_scatter(partial_sums[9].astype(jnp.bfloat16), 'fsdp', scatter_di...  68.4 us
    reduce_scatter x1, waiting for transfers between devices, per_device(): lax.psum_scatter(partial_sums[2].astype(jnp.bfloat16), 'fsdp', scatter_di...  66 us
    all_gather x1, blocking collectives, per_device(): lax.all_gather(bias_up, ('dp', 'fsdp'), axis=0, tiled=True)  65.8 us
    reduce_scatter x1, waiting for transfers between devices, per_device(): lax.psum_scatter(totals[9].astype(jnp.bfloat16), 'dp', scatter_dimension=...  62 us
    dot_general x2, matrix products, forward_pass(): jnp.dot(normed_two, weight_up, preferred_element_type=jnp.float32)  56 us
  transfers between devices with their start and end apart: 12, of which 9 were waited for; matrix products, arithmetic and copies ran while one was open for 22% of the time, Pallas kernels for 0%

commit v1 on v0

--- a/solution.py
+++ b/solution.py
@@ -1,8 +1,12 @@
 from functools import partial
+
+import numpy as np
 
 import jax
 import jax.numpy as jnp
 from jax import lax
+from jax.experimental import pallas as pl
+from jax.experimental.pallas import tpu as pltpu
 from jax.sharding import PartitionSpec as P
 
 HEAD_DIM = 64
@@ -231,7 +235,94 @@
     return (grad_inputs, grads)
 
 
-def per_device(
+def bits_of(ndp, nfs):
+    core = nfs
+    outer = [nfs << i for i in range(1, ndp.bit_length() - 1)]
+    inner = [1 << i for i in range(nfs.bit_length() - 1)]
+    return core, outer, inner
+
+
+def stage_orders(ndp, nfs):
+    core, outer, inner = bits_of(ndp, nfs)
+    first, second = outer[0], inner[0]
+    tail = outer[1:] + inner[1:]
+    return core, ([first, second] + tail, [second, first] + tail)
+
+
+def shard_table(ndp, nfs):
+    n = ndp * nfs
+    core, orders = stage_orders(ndp, nfs)
+    table = np.zeros((n, n), np.int32)
+    for me in range(n):
+        for p in range(n):
+            rel = core if p >= n // 2 else 0
+            owner = 1 if (me ^ rel) & core else 0
+            for i, mask in enumerate(orders[owner]):
+                if p & (n >> (i + 2)):
+                    rel ^= mask
+            table[me, p] = me ^ rel
+    return table
+
+
+def stage_perms(ndp, nfs):
+    n = ndp * nfs
+    core, orders = stage_orders(ndp, nfs)
+    perms = [[(i, i ^ core) for i in range(n)]]
+    for a, b in zip(*orders):
+        perms.append([(i, i ^ (b if i & core else a)) for i in range(n)])
+    return perms
+
+
+def place_blocks(pieces, table_row, scatter):
+    n = pieces[0].shape[0]
+
+    def body(t_ref, *refs):
+        ins, outs, sem = refs[: len(pieces)], refs[len(pieces) : -1], refs[-1]
+        copies = []
+        for src, dst in zip(ins, outs):
+            for i in range(n):
+                j = t_ref[i]
+                s, d = (i, j) if scatter else (j, i)
+                copies.append(pltpu.make_async_copy(src.at[s], dst.at[d], sem))
+        for c in copies:
+            c.start()
+        for c in copies:
+            c.wait()
+
+    return pl.pallas_call(
+        body,
+        out_shape=[jax.ShapeDtypeStruct(p.shape, p.dtype) for p in pieces],
+        grid_spec=pltpu.PrefetchScalarGridSpec(
+            num_scalar_prefetch=1,
+            in_specs=[pl.BlockSpec(memory_space=pl.ANY)] * len(pieces),
+            out_specs=[pl.BlockSpec(memory_space=pl.ANY)] * len(pieces),
+            scratch_shapes=[pltpu.SemaphoreType.DMA],
+        ),
+        name="place",
+    )(table_row, *pieces)
+
+
+AXES = ("dp", "fsdp")
+
+
+def gather_relative(shard, perms):
+    cur = shard[None]
+    for perm in perms[:0:-1]:
+        cur = jnp.concatenate([cur, lax.ppermute(cur, AXES, perm)], axis=0)
+    return jnp.concatenate([cur, lax.ppermute(cur, AXES, perms[0])], axis=0)
+
+
+def reduce_relative(rel, perms, wide=jnp.bfloat16):
+    cur = rel
+    for i, perm in enumerate(perms):
+        half = cur.shape[0] // 2
+        got = lax.ppermute(cur[half:], AXES, perm)
+        total = cur[:half].astype(jnp.float32) + got.astype(jnp.float32)
+        cur = total if i == len(perms) - 1 else total.astype(wide)
+    return cur[0]
+
+
+def per_device(ndp, nfs,
     tokens,
     ln1_gain,
     ln1_bias,
@@ -250,152 +341,103 @@
     cot_second,
     valid,
 ):
+    n = ndp * nfs
+    perms = stage_perms(ndp, nfs)
+    me = lax.axis_index("dp") * nfs + lax.axis_index("fsdp")
+    row = lax.dynamic_slice(jnp.asarray(shard_table(ndp, nfs)), (me, 0), (1, n))[0]
+    vectors = (ln1_gain, ln1_bias, bias_q, bias_v, bias_out, ln2_gain, ln2_bias, bias_down, bias_up)
+    sizes = [v.shape[0] for v in vectors]
+    width = -(-sum(sizes) // 128) * 128
+    packed = jnp.pad(jnp.concatenate(vectors), (0, width - sum(sizes)))[None]
+    got_small = gather_relative(packed, perms)
+    got_qkv = gather_relative(w_qkv, perms)
+    got_out = gather_relative(w_out, perms)
+    got_up = gather_relative(w_up, perms)
+    got_down = gather_relative(w_down, perms)
+    full_small = jnp.zeros_like(got_small).at[row].set(got_small)[:, 0]
+    parts = []
+    offset = 0
+    for size in sizes:
+        parts.append(full_small[:, offset : offset + size].reshape(-1))
+        offset += size
+    g1, s1, bq, bv, bo, g2, s2, bd, bu = parts
+    (full_qkv,) = place_blocks([got_qkv], row, True)
+    (full_out,) = place_blocks([got_out], row, True)
+    (full_up,) = place_blocks([got_up], row, True)
+    (full_down,) = place_blocks([got_down], row, True)
+    flat = lambda w: w.reshape(-1, w.shape[-1])
     gathered = (
-        lax.all_gather(ln1_gain, ("dp", "fsdp"), axis=0, tiled=True),
-        lax.all_gather(ln1_bias, ("dp", "fsdp"), axis=0, tiled=True),
-        lax.all_gather(w_qkv, ("dp", "fsdp"), axis=0, tiled=True),
-        lax.all_gather(bias_q, ("dp", "fsdp"), axis=0, tiled=True),
-        lax.all_gather(bias_v, ("dp", "fsdp"), axis=0, tiled=True),
-        lax.all_gather(w_out, ("dp", "fsdp"), axis=0, tiled=True),
-        lax.all_gather(bias_out, ("dp", "fsdp"), axis=0, tiled=True),
-        lax.all_gather(ln2_gain, ("dp", "fsdp"), axis=0, tiled=True),
-        lax.all_gather(ln2_bias, ("dp", "fsdp"), axis=0, tiled=True),
-        lax.all_gather(w_up, ("dp", "fsdp"), axis=0, tiled=True),
-        lax.all_gather(bias_up, ("dp", "fsdp"), axis=0, tiled=True),
-        lax.all_gather(w_down, ("dp", "fsdp"), axis=0, tiled=True),
-        lax.all_gather(bias_down, ("dp", "fsdp"), axis=0, tiled=True),
+        g1,
+        s1,
+        flat(full_qkv),
+        bq,
+        bv,
+        flat(full_out),
+        bo,
+        g2,
+        s2,
+        flat(full_up),
+        bu,
+        flat(full_down),
+        bd,
     )
     start_rows = tokens[0].astype(jnp.float32)
     first_out, saved_first = forward_pass(start_rows, gathered)
     first_low = first_out.astype(jnp.bfloat16)
     second_in = lax.optimization_barrier(first_low).astype(jnp.float32)
     second_out, saved_second = forward_pass(second_in, gathered)
-    back_weights = (
-        lax.all_gather(ln1_gain, ("dp", "fsdp"), axis=0, tiled=True),
-        lax.all_gather(ln1_bias, ("dp", "fsdp"), axis=0, tiled=True),
-        lax.all_gather(w_qkv, ("dp", "fsdp"), axis=0, tiled=True),
-        lax.all_gather(bias_q, ("dp", "fsdp"), axis=0, tiled=True),
-        lax.all_gather(bias_v, ("dp", "fsdp"), axis=0, tiled=True),
-        lax.all_gather(w_out, ("dp", "fsdp"), axis=0, tiled=True),
-        lax.all_gather(bias_out, ("dp", "fsdp"), axis=0, tiled=True),
-        lax.all_gather(ln2_gain, ("dp", "fsdp"), axis=0, tiled=True),
-        lax.all_gather(ln2_bias, ("dp", "fsdp"), axis=0, tiled=True),
-        lax.all_gather(w_up, ("dp", "fsdp"), axis=0, tiled=True),
-        lax.all_gather(bias_up, ("dp", "fsdp"), axis=0, tiled=True),
-        lax.all_gather(w_down, ("dp", "fsdp"), axis=0, tiled=True),
-        lax.all_gather(bias_down, ("dp", "fsdp"), axis=0, tiled=True),
-    )
     keep_mask = valid[0].astype(jnp.float32)[:, None]
     grad_second = cot_second[0].astype(jnp.float32) * keep_mask
-    grad_between, grads_second = backward_pass(grad_second, saved_second, back_weights)
+    grad_between, grads_second = backward_pass(grad_second, saved_second, gathered)
     grad_first = cot_first[0].astype(jnp.float32) * keep_mask + grad_between
-    grad_inputs, grads_first = backward_pass(grad_first, saved_first, back_weights)
+    grad_inputs, grads_first = backward_pass(grad_first, saved_first, gathered)
     totals = tuple((left + right for left, right in zip(grads_first, grads_second)))
-    partial_sums = (
-        lax.psum_scatter(
-            totals[0].astype(jnp.bfloat16), "dp", scatter_dimension=0, tiled=True
-        ).astype(jnp.float32),
-        lax.psum_scatter(
-            totals[1].astype(jnp.bfloat16), "dp", scatter_dimension=0, tiled=True
-        ).astype(jnp.float32),
-        lax.psum_scatter(
-            totals[2].astype(jnp.bfloat16), "dp", scatter_dimension=0, tiled=True
-        ).astype(jnp.float32),
-        lax.psum_scatter(
-            totals[3].astype(jnp.bfloat16), "dp", scatter_dimension=0, tiled=True
-        ).astype(jnp.float32),
-        lax.psum_scatter(
-            totals[4].astype(jnp.bfloat16), "dp", scatter_dimension=0, tiled=True
-        ).astype(jnp.float32),
-        lax.psum_scatter(
-            totals[5].astype(jnp.bfloat16), "dp", scatter_dimension=0, tiled=True
-        ).astype(jnp.float32),
-        lax.psum_scatter(
-            totals[6].astype(jnp.bfloat16), "dp", scatter_dimension=0, tiled=True
-        ).astype(jnp.float32),
-        lax.psum_scatter(
-            totals[7].astype(jnp.bfloat16), "dp", scatter_dimension=0, tiled=True
-        ).astype(jnp.float32),
-        lax.psum_scatter(
-            totals[8].astype(jnp.bfloat16), "dp", scatter_dimension=0, tiled=True
-        ).astype(jnp.float32),
-        lax.psum_scatter(
-            totals[9].astype(jnp.bfloat16), "dp", scatter_dimension=0, tiled=True
-        ).astype(jnp.float32),
-        lax.psum_scatter(
-            totals[10].astype(jnp.bfloat16), "dp", scatter_dimension=0, tiled=True
-        ).astype(jnp.float32),
-        lax.psum_scatter(
-            totals[11].astype(jnp.bfloat16), "dp", scatter_dimension=0, tiled=True
-        ).astype(jnp.float32),
-        lax.psum_scatter(
-            totals[12].astype(jnp.bfloat16), "dp", scatter_dimension=0, tiled=True
-        ).astype(jnp.float32),
-    )
-    shares = (
-        lax.psum_scatter(
-            partial_sums[0].astype(jnp.bfloat16), "fsdp", scatter_dimension=0, tiled=True
-        ).astype(jnp.float32),
-        lax.psum_scatter(
-            partial_sums[1].astype(jnp.bfloat16), "fsdp", scatter_dimension=0, tiled=True
-        ).astype(jnp.float32),
-        lax.psum_scatter(
-            partial_sums[2].astype(jnp.bfloat16), "fsdp", scatter_dimension=0, tiled=True
-        ).astype(jnp.float32),
-        lax.psum_scatter(
-            partial_sums[3].astype(jnp.bfloat16), "fsdp", scatter_dimension=0, tiled=True
-        ).astype(jnp.float32),
-        lax.psum_scatter(
-            partial_sums[4].astype(jnp.bfloat16), "fsdp", scatter_dimension=0, tiled=True
-        ).astype(jnp.float32),
-        lax.psum_scatter(
-            partial_sums[5].astype(jnp.bfloat16), "fsdp", scatter_dimension=0, tiled=True
-        ).astype(jnp.float32),
-        lax.psum_scatter(
-            partial_sums[6].astype(jnp.bfloat16), "fsdp", scatter_dimension=0, tiled=True
-        ).astype(jnp.float32),
-        lax.psum_scatter(
-            partial_sums[7].astype(jnp.bfloat16), "fsdp", scatter_dimension=0, tiled=True
-        ).astype(jnp.float32),
-        lax.psum_scatter(
-            partial_sums[8].astype(jnp.bfloat16), "fsdp", scatter_dimension=0, tiled=True
-        ).astype(jnp.float32),
-        lax.psum_scatter(
-            partial_sums[9].astype(jnp.bfloat16), "fsdp", scatter_dimension=0, tiled=True
-        ).astype(jnp.float32),
-        lax.psum_scatter(
-            partial_sums[10].astype(jnp.bfloat16), "fsdp", scatter_dimension=0, tiled=True
-        ).astype(jnp.float32),
-        lax.psum_scatter(
-            partial_sums[11].astype(jnp.bfloat16), "fsdp", scatter_dimension=0, tiled=True
-        ).astype(jnp.float32),
-        lax.psum_scatter(
-            partial_sums[12].astype(jnp.bfloat16), "fsdp", scatter_dimension=0, tiled=True
-        ).astype(jnp.float32),
-    )
+    (t_g1, t_s1, t_qkv, t_bq, t_bv, t_out, t_bo, t_g2, t_s2, t_up, t_bu, t_down, t_bd) = totals
+
+    def reduce_matrix(total):
+        low = total.astype(jnp.bfloat16).reshape(n, total.shape[0] // n, total.shape[1])
+        (rel,) = place_blocks([low], row, False)
+        return reduce_relative(rel, perms)
+
+    d_down = reduce_matrix(t_down)
+    d_up = reduce_matrix(t_up)
+    d_out = reduce_matrix(t_out)
+    d_qkv = reduce_matrix(t_qkv)
+    small = jnp.concatenate(
+        [v.reshape(n, -1) for v in (t_g1, t_s1, t_bq, t_bv, t_bo, t_g2, t_s2, t_bd, t_bu)], axis=1
+    )
+    small = jnp.pad(small, ((0, 0), (0, width - small.shape[1])))[:, None]
+    small = reduce_relative(small[row], perms, jnp.float32)[0]
+    outs = []
+    offset = 0
+    for size in sizes:
+        outs.append(small[offset : offset + size])
+        offset += size
+    o_g1, o_s1, o_bq, o_bv, o_bo, o_g2, o_s2, o_bd, o_bu = outs
     return (
         first_low[None],
         second_out.astype(jnp.bfloat16)[None],
         grad_inputs.astype(jnp.bfloat16)[None],
-        shares[0],
-        shares[1],
-        shares[2],
-        shares[3],
-        shares[4],
-        shares[5],
-        shares[6],
-        shares[7],
-        shares[8],
-        shares[9],
-        shares[10],
-        shares[11],
-        shares[12],
+        o_g1,
+        o_s1,
+        d_qkv,
+        o_bq,
+        o_bv,
+        d_out,
+        o_bo,
+        o_g2,
+        o_s2,
+        d_up,
+        o_bu,
+        d_down,
+        o_bd,
     )
 
 
 def solution(mesh):
+    ndp, nfs = mesh.shape["dp"], mesh.shape["fsdp"]
     return jax.shard_map(
-        per_device,
+        partial(per_device, ndp, nfs),
         mesh=mesh,
         in_specs=(
             P(("dp", "fsdp"), None, None),

time: 1070 us -> 2300 us (2.15)
  Pallas kernels: 0 us -> 1540 us
  waiting for transfers between devices: 460 us -> 182 us
  blocking collectives: 140 us -> 0 us
  local copies, waits for them, and re-layouts: 32.2 us -> 99.2 us
  starting transfers between devices: 1.05 us -> 59.6 us
    pallas_call x0 -> x8, Pallas kernels: none -> 1540 us  [place_blocks(): pl.pallas_call(body, out_shape=[jax.ShapeDtypeStruct(p.shape, p.dtype) fo...]
    reduce_scatter x8 -> x0, waiting for transfers between devices: 357 us -> none  [the longest x1 74.3 us: per_device(): lax.psum_scatter(totals[11].astype(jnp.bfloat16), 'dp', scatter_dimension...]
    ppermute x0 -> x50, waiting for transfers between devices: none -> 182 us  [the longest x25 111 us: reduce_relative(): got = lax.ppermute(cur[half:], AXES, perm)]
    all_gather x4 -> x0, waiting for transfers between devices: 99.8 us -> none  [the longest x1 51.1 us: per_device(): lax.all_gather(w_down, ('dp', 'fsdp'), axis=0, tiled=True)]
    unnamed x3 -> x0, blocking collectives: 74.4 us -> none
    all_gather x1 -> x0, blocking collectives: 65.8 us -> none  [per_device(): lax.all_gather(bias_up, ('dp', 'fsdp'), axis=0, tiled=True)]
    ppermute x0 -> x50, starting transfers between devices: none -> 59.6 us  [the longest x20 30.4 us: gather_relative(): cur = jnp.concatenate([cur, lax.ppermute(cur, AXES, perm)], axis=0)]
    concatenate x0 -> x12, local copies, waits for them, and re-layouts: none -> 30.1 us  [the longest x5 13.4 us: gather_relative(): return jnp.concatenate([cur, lax.ppermute(cur, AXES, perms[0])], axis=0)]
  transfers between devices with their start and end apart: 12 -> 50, of which waited for: 9 -> 19; matrix products, arithmetic and copies ran while one was open for 22% -> 8% of each run, Pallas kernels for 0% -> 45%
where the time goes in v1:
time: 2300 us; the launch traced here: 2290 us
  Pallas kernels  1540 us (67%)
  matrix products  325 us (14%)
  waiting for transfers between devices  182 us (8%)
  local copies, waits for them, and re-layouts  99.2 us (4%)
  other arithmetic  83.2 us (4%)
  starting transfers between devices  59.6 us (3%)
    pallas_call x8, Pallas kernels, place_blocks(): pl.pallas_call(body, out_shape=[jax.ShapeDtypeStruct(p.shape, p.dtype) fo...  1540 us
    ppermute x25, waiting for transfers between devices, reduce_relative(): got = lax.ppermute(cur[half:], AXES, perm)  111 us
    ppermute x20, waiting for transfers between devices, gather_relative(): cur = jnp.concatenate([cur, lax.ppermute(cur, AXES, perm)], axis=0)  70.9 us
    dot_general x2, matrix products, forward_pass(): jnp.dot(normed_two, weight_up, preferred_element_type=jnp.float32)  55.7 us
  transfers between devices with their start and end apart: 50, of which 19 were waited for; matrix products, arithmetic and copies ran while one was open for 8% of the time, Pallas kernels for 45%

profile of v1, /device:TPU:0, one launch (start us, length us, event | category | flops | bytes accessed | tf_op | source)
XLA Modules:
  0.0 2292.0 jit_solution(17932859499288428252)
XLA Ops:
  0.7 4.1 collective-permute-start.5
  4.8 6.1 concatenate.107
  49.6 5.6 collective-permute-done.6
  59.9 7.4 collective-permute-done.7
  74.2 8.1 collective-permute-done.21
  85.3 18.4 collective-permute-done.8
  115.5 24.1 %collective-permute-done.13 = bf16[8,32,1024]{2,1,0:T(8,128)(2,1)S(1)} collective-permute-done((bf16[8,32,1024]{2,1,0:T(8,128)(2,1)S(1)}, bf16[8,32,1024]{2,1,0:T(8,128)(2,1)S(1)}, u32[]{:S(2)}, u32[]{:S(2)}) %collective-permute-start.13) | collective-permute-done | bytes 524320 | tf_op jit(solution)/shard_map/ppermute | solution.py:311
  145.4 65.3 %place.9 = bf16[32,32,1024]{2,1,0:T(8,128)(2,1)} custom-call(s32[32]{0:T(128)} %dynamic-slice_bitcast_fusion.t_ref, bf16[32,32,1024]{2,1,0:T(8,128)(2,1)} %copy-done.48), custom_call_target="tpu_custom_call" | custom-call | tf_op jit(solution)/shard_map/place/pallas_call | solution.py:292
  210.8 4.2 constant_dynamic-update-slice_fusion.22
  215.4 4.2 constant_dynamic-update-slice_fusion.33
  219.6 3.8 constant_dynamic-update-slice_fusion.5.refs_0_
  223.4 192.5 %place.8 = bf16[32,32,3072]{2,1,0:T(8,128)(2,1)} custom-call(s32[32]{0:T(128)} %dynamic-slice_bitcast_fusion.t_ref, bf16[32,32,3072]{2,1,0:T(8,128)(2,1)} %constant_dynamic-update-slice_fusion.5.refs_0_), custom_call_target="tpu_custom_call" | custom-call | tf_op jit(solution)/shard_map/place/pallas_call | solution.py:292
  416.0 6.2 fusion.80
  430.0 8.2 multiply_reduce_fusion.3
  438.3 8.7 fusion
  447.0 8.1 fusion.66
  457.8 4.7 constant_dynamic-update-slice_fusion.27.refs_0_
  462.5 255.9 %place.10 = bf16[32,32,4096]{2,1,0:T(8,128)(2,1)} custom-call(s32[32]{0:T(128)} %dynamic-slice_bitcast_fusion.t_ref, bf16[32,32,4096]{2,1,0:T(8,128)(2,1)} %constant_dynamic-update-slice_fusion.27.refs_0_), custom_call_target="tpu_custom_call" | custom-call | tf_op jit(solution)/shard_map/place/pallas_call | solution.py:292
  718.4 4.8 constant_dynamic-update-slice_fusion.38.refs_0_
  723.2 256.0 %place.11 = bf16[32,128,1024]{2,1,0:T(8,128)(2,1)} custom-call(s32[32]{0:T(128)} %dynamic-slice_bitcast_fusion.t_ref, bf16[32,128,1024]{2,1,0:T(8,128)(2,1)} %constant_dynamic-update-slice_fusion.38.refs_0_), custom_call_target="tpu_custom_call" | custom-call | tf_op jit(solution)/shard_map/place/pallas_call | solution.py:292
  979.3 27.4 %multiply_convert_fusion.3 = (bf16[512,4096]{1,0:T(8,128)(2,1)S(1)}, f32[512,4096]{1,0:T(8,128)}, f32[512,4096]{1,0:T(8,128)}) fusion(f32[4096]{0:T(1024)S(1)} %copy-done.97, bf16[1024,4096]{1,0:T(8,128)(2,1)} %bitcast.257, f32[512,1024]{1,0:T(8,128)S(1)} %get-tuple-element.198, f32[1024]{0:T(1024)S(1)} %copy-done.111, f32[1024]{0:T(1024)S(1)} %copy-done.60, ...), kind=kOutput, calls=%fused_computation.48 | convolution fusion | flops 4436000768 | bytes 31485952 | tf_op jit(solution)/shard_map/dot_general | solution.py:117
  1006.7 6.8 add_convert_fusion.18
  1014.2 6.0 fusion.124
  1025.4 8.2 multiply_reduce_fusion.2
  1033.6 8.7 fusion.1
  1043.5 8.2 fusion.65
  1053.6 28.3 %multiply_convert_fusion.2 = (bf16[512,4096]{1,0:T(8,128)(2,1)}, f32[512,4096]{1,0:T(8,128)}, f32[512,4096]{1,0:T(8,128)}) fusion(f32[4096]{0:T(1024)S(1)} %copy-done.98, bf16[1024,4096]{1,0:T(8,128)(2,1)} %bitcast.258, f32[512,1024]{1,0:T(8,128)S(1)} %get-tuple-element.203, f32[512]{0:T(512)S(1)} %fusion.107, f32[512]{0:T(512)S(1)} %broadcast_multiply_fusion, ...), kind=kOutput, calls=%fused_computation.35 | convolution fusion | flops 4436000768 | bytes 31485952 | tf_op jit(solution)/shard_map/dot_general | solution.py:117
  1081.9 15.5 convert_reduce_fusion
  1097.4 9.5 multiply_reduce_fusion.4
  1113.8 16.5 multiply_reduce_fusion.1
  1130.3 8.1 multiply_convert_fusion.1
  1143.9 6.4 multiply_convert_fusion.6
  1150.4 9.8 convert_reduce_fusion.8
  1160.3 5.8 fusion.131
  1169.9 8.2 fusion.113
  1178.1 15.5 convert_reduce_fusion.1
  1193.6 11.2 fusion.128
  1204.9 8.1 multiply_reduce_fusion.5
  1221.6 16.5 multiply_reduce_fusion
  1238.1 8.3 multiply_convert_fusion
  1251.3 6.1 multiply_convert_fusion.4
  1257.4 7.8 convert_reduce_fusion.9
  1265.3 9.8 fusion.74
  1275.1 5.1 fusion.132
  1280.2 12.0 add_convert_fusion
  1292.2 255.9 %place.15 = bf16[32,128,1024]{2,1,0:T(8,128)(2,1)} custom-call(s32[32]{0:T(128)} %dynamic-slice_bitcast_fusion.t_ref, bf16[32,128,1024]{2,1,0:T(8,128)(2,1)} %bitcast.262), custom_call_target="tpu_custom_call" | custom-call | tf_op jit(solution)/shard_map/place/pallas_call | solution.py:292
  1548.1 4.8 slice.402
  1553.4 15.7 add_convert_fusion.1
  1569.1 255.9 %place.14 = bf16[32,32,4096]{2,1,0:T(8,128)(2,1)} custom-call(s32[32]{0:T(128)} %dynamic-slice_bitcast_fusion.t_ref, bf16[32,32,4096]{2,1,0:T(8,128)(2,1)} %bitcast.261), custom_call_target="tpu_custom_call" | custom-call | tf_op jit(solution)/shard_map/place/pallas_call | solution.py:292
  1825.2 4.7 slice.391
  1834.5 5.1 add_convert_fusion.10
  1839.7 65.4 %place.13 = bf16[32,32,1024]{2,1,0:T(8,128)(2,1)} custom-call(s32[32]{0:T(128)} %dynamic-slice_bitcast_fusion.t_ref, bf16[32,32,1024]{2,1,0:T(8,128)(2,1)} %bitcast.263), custom_call_target="tpu_custom_call" | custom-call | tf_op jit(solution)/shard_map/place/pallas_call | solution.py:292
  1909.6 11.9 add_convert_fusion.2
  1921.5 192.4 %place.12 = bf16[32,32,3072]{2,1,0:T(8,128)(2,1)} custom-call(s32[32]{0:T(128)} %dynamic-slice_bitcast_fusion.t_ref, bf16[32,32,3072]{2,1,0:T(8,128)(2,1)} %bitcast.272), custom_call_target="tpu_custom_call" | custom-call | tf_op jit(solution)/shard_map/place/pallas_call | solution.py:292
  2117.7 9.1 fusion.73
  2135.4 6.3 collective-permute-done.36
  2146.4 5.1 add_convert_fusion.3
  2154.0 3.7 add_convert_fusion.4
  2171.8 25.1 %collective-permute-done.46 = bf16[8,128,1024]{2,1,0:T(8,128)(2,1)} collective-permute-done((bf16[8,128,1024]{2,1,0:T(8,128)(2,1)}, bf16[8,128,1024]{2,1,0:T(8,128)(2,1)}, u32[]{:S(2)}, u32[]{:S(2)}) %collective-permute-start.46) | collective-permute-done | bytes 2097184 | tf_op jit(solution)/shard_map/ppermute | solution.py:319
  2200.8 29.7 %collective-permute-done.41 = bf16[8,32,4096]{2,1,0:T(8,128)(2,1)S(1)} collective-permute-done((bf16[8,32,4096]{2,1,0:T(8,128)(2,1)S(1)}, bf16[8,32,4096]{2,1,0:T(8,128)(2,1)S(1)}, u32[]{:S(2)}, u32[]{:S(2)}) %collective-permute-start.41) | collective-permute-done | bytes 2097184 | tf_op jit(solution)/shard_map/ppermute | solution.py:319
  2236.4 10.0 collective-permute-done.42
  2251.1 13.0 collective-permute-done.48
  2266.1 7.7 collective-permute-done.43
  2275.5 11.6 collective-permute-done.49
  (550 shorter events, 185.6 us)
Async XLA Ops:
  0.7 41.7 %collective-permute-start.5 = (bf16[1,32,3072]{2,1,0:T(8,128)(2,1)}, bf16[1,32,3072]{2,1,0:T(8,128)(2,1)S(1)}, u32[]{:S(2)}, u32[]{:S(2)}) collective-permute-start(bf16[1,32,3072]{2,1,0:T(8,128)(2,1)} %bitcast.291), channel_id=1, source_target_pairs={{0,4},{1,5},{2,6},{3,7},{4,0},{5,1},{6,2},{7,3},{8,12},{9,13},{10,... | collective-permute-start | bytes 589832 | tf_op jit(solution)/shard_map/ppermute | solution.py:311
  10.9 15.9 collective-permute-start
  11.0 29.8 %collective-permute-start.10 = (bf16[1,32,1024]{2,1,0:T(8,128)(2,1)}, bf16[1,32,1024]{2,1,0:T(8,128)(2,1)S(1)}, u32[]{:S(2)}, u32[]{:S(2)}) collective-permute-start(bf16[1,32,1024]{2,1,0:T(8,128)(2,1)} %bitcast.303), channel_id=1, source_target_pairs={{0,4},{1,5},{2,6},{3,7},{4,0},{5,1},{6,2},{7,3},{8,12},{9,13},{10,... | collective-permute-start | bytes 196616 | tf_op jit(solution)/shard_map/ppermute | solution.py:311
  13.9 43.8 %collective-permute-start.15 = (bf16[1,32,4096]{2,1,0:T(8,128)(2,1)}, bf16[1,32,4096]{2,1,0:T(8,128)(2,1)S(1)}, u32[]{:S(2)}, u32[]{:S(2)}) collective-permute-start(bf16[1,32,4096]{2,1,0:T(8,128)(2,1)} %bitcast.277), channel_id=1, source_target_pairs={{0,4},{1,5},{2,6},{3,7},{4,0},{5,1},{6,2},{7,3},{8,12},{9,13},{10,... | collective-permute-start | bytes 786440 | tf_op jit(solution)/shard_map/ppermute | solution.py:311
  13.9 45.3 %collective-permute-start.20 = (bf16[1,128,1024]{2,1,0:T(8,128)(2,1)}, bf16[1,128,1024]{2,1,0:T(8,128)(2,1)S(1)}, u32[]{:S(2)}, u32[]{:S(2)}) collective-permute-start(bf16[1,128,1024]{2,1,0:T(8,128)(2,1)} %bitcast.281), channel_id=1, source_target_pairs={{0,4},{1,5},{2,6},{3,7},{4,0},{5,1},{6,2},{7,3},{8,12},{9,13},{10,... | collective-permute-start | bytes 786440 | tf_op jit(solution)/shard_map/ppermute | solution.py:311
  26.8 3.8 collective-permute-start.1
  30.6 3.7 collective-permute-start.2
  34.3 3.7 collective-permute-start.3
  38.1 1.9 collective-permute-start.4
  40.8 6.4 collective-permute-start.11
  42.4 12.8 collective-permute-start.6
  43.7 970.5 %copy-start.56 = (f32[1024]{0:T(1024)}, f32[1024]{0:T(1024)S(1)}, u32[]{:S(2)}) copy-start(f32[1024]{0:T(1024)S(1)} %reshape.441) | copy-start | bytes 12292
  44.5 378.8 %copy-start.58 = (f32[1024]{0:T(1024)}, f32[1024]{0:T(1024)S(1)}, u32[]{:S(2)}) copy-start(f32[1024]{0:T(1024)S(1)} %reshape.444) | copy-start | bytes 12292
  47.3 62.5 %collective-permute-start.12 = (bf16[4,32,1024]{2,1,0:T(8,128)(2,1)S(1)}, bf16[4,32,1024]{2,1,0:T(8,128)(2,1)S(1)}, u32[]{:S(2)}, u32[]{:S(2)}) collective-permute-start(bf16[4,32,1024]{2,1,0:T(8,128)(2,1)S(1)} %pad_maximum_fusion.16), channel_id=1, source_target_pairs={{0,1},{1,0},{2,3},{3,2},{4,5},{5,4},{6,7},{7,6},{8,24},{9,25},{10,... | collective-permute-start | bytes 786440 | tf_op jit(solution)/shard_map/ppermute | solution.py:311
  55.3 12.1 collective-permute-start.7
  57.7 14.9 collective-permute-start.16
  59.3 23.0 %collective-permute-start.21 = (bf16[2,128,1024]{2,1,0:T(8,128)(2,1)S(1)}, bf16[2,128,1024]{2,1,0:T(8,128)(2,1)S(1)}, u32[]{:S(2)}, u32[]{:S(2)}) collective-permute-start(bf16[2,128,1024]{2,1,0:T(8,128)(2,1)S(1)} %pad_maximum_fusion.14), channel_id=1, source_target_pairs={{0,2},{1,3},{2,0},{3,1},{4,6},{5,7},{6,4},{7,5},{8,10},{9,11},{10,... | collective-permute-start | bytes 1572872 | tf_op jit(solution)/shard_map/ppermute | solution.py:311
  67.5 36.2 %collective-permute-start.8 = (bf16[8,32,3072]{2,1,0:T(8,128)(2,1)S(1)}, bf16[8,32,3072]{2,1,0:T(8,128)(2,1)S(1)}, u32[]{:S(2)}, u32[]{:S(2)}) collective-permute-start(bf16[8,32,3072]{2,1,0:T(8,128)(2,1)S(1)} %pad_maximum_fusion.4), channel_id=1, source_target_pairs={{0,16},{1,17},{2,18},{3,19},{4,20},{5,21},{6,22},{7,23},{8,9},{9,8... | collective-permute-start | bytes 4718600 | tf_op jit(solution)/shard_map/ppermute | solution.py:311
  72.8 33.0 %collective-permute-start.17 = (bf16[4,32,4096]{2,1,0:T(8,128)(2,1)S(1)}, bf16[4,32,4096]{2,1,0:T(8,128)(2,1)S(1)}, u32[]{:S(2)}, u32[]{:S(2)}) collective-permute-start(bf16[4,32,4096]{2,1,0:T(8,128)(2,1)S(1)} %pad_maximum_fusion.9), channel_id=1, source_target_pairs={{0,1},{1,0},{2,3},{3,2},{4,5},{5,4},{6,7},{7,6},{8,24},{9,25},{10,... | collective-permute-start | bytes 3145736 | tf_op jit(solution)/shard_map/ppermute | solution.py:311
  82.4 28.5 %collective-permute-start.22 = (bf16[4,128,1024]{2,1,0:T(8,128)(2,1)S(1)}, bf16[4,128,1024]{2,1,0:T(8,128)(2,1)S(1)}, u32[]{:S(2)}, u32[]{:S(2)}) collective-permute-start(bf16[4,128,1024]{2,1,0:T(8,128)(2,1)S(1)} %pad_maximum_fusion.10), channel_id=1, source_target_pairs={{0,1},{1,0},{2,3},{3,2},{4,5},{5,4},{6,7},{7,6},{8,24},{9,25},{10,... | collective-permute-start | bytes 3145736 | tf_op jit(solution)/shard_map/ppermute | solution.py:311
  105.8 113.8 %collective-permute-start.9 = (bf16[16,32,3072]{2,1,0:T(8,128)(2,1)}, bf16[16,32,3072]{2,1,0:T(8,128)(2,1)}, u32[]{:S(2)}, u32[]{:S(2)}) collective-permute-start(bf16[16,32,3072]{2,1,0:T(8,128)(2,1)} %get-tuple-element.142), channel_id=1, source_target_pairs={{0,8},{1,9},{2,10},{3,11},{4,12},{5,13},{6,14},{7,15},{8,0},{9,1},... | collective-permute-start | bytes 9437192 | tf_op jit(solution)/shard_map/ppermute | solution.py:312
  107.3 103.5 %collective-permute-start.18 = (bf16[8,32,4096]{2,1,0:T(8,128)(2,1)}, bf16[8,32,4096]{2,1,0:T(8,128)(2,1)}, u32[]{:S(2)}, u32[]{:S(2)}) collective-permute-start(bf16[8,32,4096]{2,1,0:T(8,128)(2,1)} %pad_maximum_fusion.2), channel_id=1, source_target_pairs={{0,16},{1,17},{2,18},{3,19},{4,20},{5,21},{6,22},{7,23},{8,9},{9,8... | collective-permute-start | bytes 6291464 | tf_op jit(solution)/shard_map/ppermute | solution.py:311
  109.9 29.8 %collective-permute-start.13 = (bf16[8,32,1024]{2,1,0:T(8,128)(2,1)S(1)}, bf16[8,32,1024]{2,1,0:T(8,128)(2,1)S(1)}, u32[]{:S(2)}, u32[]{:S(2)}) collective-permute-start(bf16[8,32,1024]{2,1,0:T(8,128)(2,1)S(1)} %pad_maximum_fusion.12), channel_id=1, source_target_pairs={{0,16},{1,17},{2,18},{3,19},{4,20},{5,21},{6,22},{7,23},{8,9},{9,8... | collective-permute-start | bytes 1572872 | tf_op jit(solution)/shard_map/ppermute | solution.py:311
  112.5 103.0 %collective-permute-start.23 = (bf16[8,128,1024]{2,1,0:T(8,128)(2,1)}, bf16[8,128,1024]{2,1,0:T(8,128)(2,1)}, u32[]{:S(2)}, u32[]{:S(2)}) collective-permute-start(bf16[8,128,1024]{2,1,0:T(8,128)(2,1)} %pad_maximum_fusion.3), channel_id=1, source_target_pairs={{0,16},{1,17},{2,18},{3,19},{4,20},{5,21},{6,22},{7,23},{8,9},{9,8... | collective-permute-start | bytes 6291464 | tf_op jit(solution)/shard_map/ppermute | solution.py:311
  139.7 4.3 collective-permute-start.14
  214.9 242.8 %collective-permute-start.19 = (bf16[16,32,4096]{2,1,0:T(8,128)(2,1)}, bf16[16,32,4096]{2,1,0:T(8,128)(2,1)}, u32[]{:S(2)}, u32[]{:S(2)}) collective-permute-start(bf16[16,32,4096]{2,1,0:T(8,128)(2,1)} %get-tuple-element.140), channel_id=1, source_target_pairs={{0,8},{1,9},{2,10},{3,11},{4,12},{5,13},{6,14},{7,15},{8,0},{9,1},... | collective-permute-start | bytes 12582920 | tf_op jit(solution)/shard_map/ppermute | solution.py:312
  219.6 498.8 %collective-permute-start.24 = (bf16[16,128,1024]{2,1,0:T(8,128)(2,1)}, bf16[16,128,1024]{2,1,0:T(8,128)(2,1)}, u32[]{:S(2)}, u32[]{:S(2)}) collective-permute-start(bf16[16,128,1024]{2,1,0:T(8,128)(2,1)} %get-tuple-element.138), channel_id=1, source_target_pairs={{0,8},{1,9},{2,10},{3,11},{4,12},{5,13},{6,14},{7,15},{8,0},{9,1},... | collective-permute-start | bytes 12582920 | tf_op jit(solution)/shard_map/ppermute | solution.py:312
  223.4 192.5 %copy-start.2 = (bf16[1,512,1024]{2,1,0:T(8,128)(2,1)S(1)}, bf16[1,512,1024]{2,1,0:T(8,128)(2,1)}, u32[]{:S(2)}) copy-start(bf16[1,512,1024]{2,1,0:T(8,128)(2,1)} %param.18) | copy-start | bytes 3145732
  223.4 192.5 %copy-start.63 = (f32[512]{0:T(512)S(1)}, f32[512]{0:T(512)}, u32[]{:S(2)}) copy-start(f32[512]{0:T(512)} %copy-done.62) | copy-start | bytes 6148
  223.4 192.5 %copy-start.74 = (f32[512]{0:T(512)S(1)}, f32[512]{0:T(512)}, u32[]{:S(2)}) copy-start(f32[512]{0:T(512)} %fusion.104) | copy-start | bytes 6148
  223.4 192.5 %copy-start.108 = (f32[1024]{0:T(1024)S(1)}, f32[1024]{0:T(1024)}, u32[]{:S(2)}) copy-start(f32[1024]{0:T(1024)} %reshape.442) | copy-start | bytes 12292
  456.5 522.8 %copy-start.14 = (f32[512,1024]{1,0:T(8,128)}, f32[512,1024]{1,0:T(8,128)S(1)}, u32[]{:S(2)}) copy-start(f32[512,1024]{1,0:T(8,128)S(1)} %get-tuple-element.198) | copy-start | bytes 6291460
  456.5 522.7 %copy-start.85 = (f32[512]{0:T(512)}, f32[512]{0:T(512)S(1)}, u32[]{:S(2)}) copy-start(f32[512]{0:T(512)S(1)} %broadcast_multiply_fusion.2) | copy-start | bytes 6148
  456.9 522.4 %copy-start.101 = (f32[512]{0:T(512)}, f32[512]{0:T(512)S(1)}, u32[]{:S(2)}) copy-start(f32[512]{0:T(512)S(1)} %fusion.105) | copy-start | bytes 6148
  723.2 256.1 %copy-start.60 = (f32[1024]{0:T(1024)S(1)}, f32[1024]{0:T(1024)}, u32[]{:S(2)}) copy-start(f32[1024]{0:T(1024)} %reshape.446) | copy-start | bytes 12292
  723.2 256.1 %copy-start.97 = (f32[4096]{0:T(1024)S(1)}, f32[4096]{0:T(1024)}, u32[]{:S(2)}) copy-start(f32[4096]{0:T(1024)} %fusion.103) | copy-start | bytes 49156
  723.2 256.1 %copy-start.111 = (f32[1024]{0:T(1024)S(1)}, f32[1024]{0:T(1024)}, u32[]{:S(2)}) copy-start(f32[1024]{0:T(1024)} %reshape.447) | copy-start | bytes 12292
  1013.5 896.1 %copy-start.4 = (bf16[512,1024]{1,0:T(8,128)(2,1)}, bf16[512,1024]{1,0:T(8,128)(2,1)S(1)}, u32[]{:S(2)}) copy-start(bf16[512,1024]{1,0:T(8,128)(2,1)S(1)} %add_convert_fusion.18) | copy-start | bytes 3145732
  1552.9 593.5 %collective-permute-start.45 = (bf16[16,128,1024]{2,1,0:T(8,128)(2,1)}, bf16[16,128,1024]{2,1,0:T(8,128)(2,1)}, u32[]{:S(2)}, u32[]{:S(2)}) collective-permute-start(bf16[16,128,1024]{2,1,0:T(8,128)(2,1)} %slice.402), channel_id=1, source_target_pairs={{0,8},{1,9},{2,10},{3,11},{4,12},{5,13},{6,14},{7,15},{8,0},{9,1},... | collective-permute-start | bytes 12582920 | tf_op jit(solution)/shard_map/ppermute | solution.py:319
  1829.9 324.1 %collective-permute-start.40 = (bf16[16,32,4096]{2,1,0:T(8,128)(2,1)}, bf16[16,32,4096]{2,1,0:T(8,128)(2,1)}, u32[]{:S(2)}, u32[]{:S(2)}) collective-permute-start(bf16[16,32,4096]{2,1,0:T(8,128)(2,1)} %slice.391), channel_id=1, source_target_pairs={{0,8},{1,9},{2,10},{3,11},{4,12},{5,13},{6,14},{7,15},{8,0},{9,1},... | collective-permute-start | bytes 12582920 | tf_op jit(solution)/shard_map/ppermute | solution.py:319
  1834.0 73.5 %collective-permute-start.25 = (f32[16,1,384]{2,0,1:T(8,128)S(1)}, f32[16,1,384]{2,0,1:T(8,128)S(1)}, u32[]{:S(2)}, u32[]{:S(2)}) collective-permute-start(f32[16,1,384]{2,0,1:T(8,128)S(1)} %slice_bitcast_fusion), channel_id=1, source_target_pairs={{0,8},{1,9},{2,10},{3,11},{4,12},{5,13},{6,14},{7,15},{8,0},{9,1},... | collective-permute-start | bytes 73736 | tf_op jit(solution)/shard_map/ppermute | solution.py:319
  1839.7 69.9 %copy-start.78 = (f32[512]{0:T(512)S(1)}, f32[512]{0:T(512)}, u32[]{:S(2)}) copy-start(f32[512]{0:T(512)} %copy-done.76) | copy-start | bytes 6148
  1907.5 223.3 %collective-permute-start.35 = (bf16[16,32,1024]{2,1,0:T(8,128)(2,1)}, bf16[16,32,1024]{2,1,0:T(8,128)(2,1)}, u32[]{:S(2)}, u32[]{:S(2)}) collective-permute-start(bf16[16,32,1024]{2,1,0:T(8,128)(2,1)} %slice.378), channel_id=1, source_target_pairs={{0,8},{1,9},{2,10},{3,11},{4,12},{5,13},{6,14},{7,15},{8,0},{9,1},... | collective-permute-start | bytes 3145736 | tf_op jit(solution)/shard_map/ppermute | solution.py:319
  1907.5 208.8 %collective-permute-start.26 = (f32[8,1,384]{2,0,1:T(8,128)S(1)}, f32[8,1,384]{2,0,1:T(8,128)S(1)}, u32[]{:S(2)}, u32[]{:S(2)}) collective-permute-start(f32[8,1,384]{2,0,1:T(8,128)S(1)} %slice.356), channel_id=1, source_target_pairs={{0,16},{1,17},{2,18},{3,19},{4,20},{5,21},{6,22},{7,23},{8,9},{9,8... | collective-permute-start | bytes 36872 | tf_op jit(solution)/shard_map/ppermute | solution.py:319
  2116.3 26.5 %collective-permute-start.30 = (bf16[16,32,3072]{2,1,0:T(8,128)(2,1)S(1)}, bf16[16,32,3072]{2,1,0:T(8,128)(2,1)S(1)}, u32[]{:S(2)}, u32[]{:S(2)}) collective-permute-start(bf16[16,32,3072]{2,1,0:T(8,128)(2,1)S(1)} %slice.366), channel_id=1, source_target_pairs={{0,8},{1,9},{2,10},{3,11},{4,12},{5,13},{6,14},{7,15},{8,0},{9,1},... | collective-permute-start | bytes 9437192 | tf_op jit(solution)/shard_map/ppermute | solution.py:319
  2116.4 10.4 collective-permute-start.27
  2126.8 3.7 collective-permute-start.28
  2130.5 4.9 collective-permute-start.29
  2132.4 9.2 collective-permute-start.36
  2141.9 17.8 collective-permute-start.37
  2145.3 23.1 %collective-permute-start.31 = (bf16[8,32,3072]{2,1,0:T(8,128)(2,1)}, bf16[8,32,3072]{2,1,0:T(8,128)(2,1)}, u32[]{:S(2)}, u32[]{:S(2)}) collective-permute-start(bf16[8,32,3072]{2,1,0:T(8,128)(2,1)} %slice.368), channel_id=1, source_target_pairs={{0,16},{1,17},{2,18},{3,19},{4,20},{5,21},{6,22},{7,23},{8,9},{9,8... | collective-permute-start | bytes 4718600 | tf_op jit(solution)/shard_map/ppermute | solution.py:319
  2153.0 43.9 %collective-permute-start.46 = (bf16[8,128,1024]{2,1,0:T(8,128)(2,1)}, bf16[8,128,1024]{2,1,0:T(8,128)(2,1)}, u32[]{:S(2)}, u32[]{:S(2)}) collective-permute-start(bf16[8,128,1024]{2,1,0:T(8,128)(2,1)} %slice.404), channel_id=1, source_target_pairs={{0,16},{1,17},{2,18},{3,19},{4,20},{5,21},{6,22},{7,23},{8,9},{9,8... | collective-permute-start | bytes 6291464 | tf_op jit(solution)/shard_map/ppermute | solution.py:319
  2158.0 72.6 %collective-permute-start.41 = (bf16[8,32,4096]{2,1,0:T(8,128)(2,1)S(1)}, bf16[8,32,4096]{2,1,0:T(8,128)(2,1)S(1)}, u32[]{:S(2)}, u32[]{:S(2)}) collective-permute-start(bf16[8,32,4096]{2,1,0:T(8,128)(2,1)S(1)} %slice.393), channel_id=1, source_target_pairs={{0,16},{1,17},{2,18},{3,19},{4,20},{5,21},{6,22},{7,23},{8,9},{9,8... | collective-permute-start | bytes 6291464 | tf_op jit(solution)/shard_map/ppermute | solution.py:319
  2159.8 5.0 collective-permute-start.38
  2164.9 67.9 %collective-permute-start.39 = (bf16[1,32,1024]{2,1,0:T(8,128)(2,1)S(1)}, bf16[1,32,1024]{2,1,0:T(8,128)(2,1)S(1)}, u32[]{:S(2)}, u32[]{:S(2)}) collective-permute-start(bf16[1,32,1024]{2,1,0:T(8,128)(2,1)S(1)} %slice.386), channel_id=1, source_target_pairs={{0,4},{1,5},{2,6},{3,7},{4,0},{5,1},{6,2},{7,3},{8,12},{9,13},{10,... | collective-permute-start | bytes 196616 | tf_op jit(solution)/shard_map/ppermute | solution.py:319
  2170.5 63.0 %collective-permute-start.32 = (bf16[4,32,3072]{2,1,0:T(8,128)(2,1)S(1)}, bf16[4,32,3072]{2,1,0:T(8,128)(2,1)S(1)}, u32[]{:S(2)}, u32[]{:S(2)}) collective-permute-start(bf16[4,32,3072]{2,1,0:T(8,128)(2,1)S(1)} %slice.370), channel_id=1, source_target_pairs={{0,1},{1,0},{2,3},{3,2},{4,5},{5,4},{6,7},{7,6},{8,24},{9,25},{10,... | collective-permute-start | bytes 2359304 | tf_op jit(solution)/shard_map/ppermute | solution.py:319
  2199.6 36.0 %collective-permute-start.47 = (bf16[4,128,1024]{2,1,0:T(8,128)(2,1)S(1)}, bf16[4,128,1024]{2,1,0:T(8,128)(2,1)S(1)}, u32[]{:S(2)}, u32[]{:S(2)}) collective-permute-start(bf16[4,128,1024]{2,1,0:T(8,128)(2,1)S(1)} %slice.406), channel_id=1, source_target_pairs={{0,1},{1,0},{2,3},{3,2},{4,5},{5,4},{6,7},{7,6},{8,24},{9,25},{10,... | collective-permute-start | bytes 3145736 | tf_op jit(solution)/shard_map/ppermute | solution.py:319
  2231.5 14.9 collective-permute-start.42
  2233.7 14.8 collective-permute-start.33
  2236.0 28.1 %collective-permute-start.48 = (bf16[2,128,1024]{2,1,0:T(8,128)(2,1)S(1)}, bf16[2,128,1024]{2,1,0:T(8,128)(2,1)S(1)}, u32[]{:S(2)}, u32[]{:S(2)}) collective-permute-start(bf16[2,128,1024]{2,1,0:T(8,128)(2,1)S(1)} %slice.408), channel_id=1, source_target_pairs={{0,2},{1,3},{2,0},{3,1},{4,6},{5,7},{6,4},{7,5},{8,10},{9,11},{10,... | collective-permute-start | bytes 1572872 | tf_op jit(solution)/shard_map/ppermute | solution.py:319
  2246.7 27.1 %collective-permute-start.43 = (bf16[2,32,4096]{2,1,0:T(8,128)(2,1)S(1)}, bf16[2,32,4096]{2,1,0:T(8,128)(2,1)S(1)}, u32[]{:S(2)}, u32[]{:S(2)}) collective-permute-start(bf16[2,32,4096]{2,1,0:T(8,128)(2,1)S(1)} %slice.397), channel_id=1, source_target_pairs={{0,2},{1,3},{2,0},{3,1},{4,6},{5,7},{6,4},{7,5},{8,10},{9,11},{10,... | collective-permute-start | bytes 1572872 | tf_op jit(solution)/shard_map/ppermute | solution.py:319
  2248.6 26.1 %collective-permute-start.34 = (bf16[1,32,3072]{2,1,0:T(8,128)(2,1)S(1)}, bf16[1,32,3072]{2,1,0:T(8,128)(2,1)S(1)}, u32[]{:S(2)}, u32[]{:S(2)}) collective-permute-start(bf16[1,32,3072]{2,1,0:T(8,128)(2,1)S(1)} %slice.374), channel_id=1, source_target_pairs={{0,4},{1,5},{2,6},{3,7},{4,0},{5,1},{6,2},{7,3},{8,12},{9,13},{10,... | collective-permute-start | bytes 589832 | tf_op jit(solution)/shard_map/ppermute | solution.py:319
  2264.3 22.8 collective-permute-start.49
  2273.9 17.0 collective-permute-start.44
  (129 other events, 1470.9 us)

commit v2 on v1

--- a/solution.py
+++ b/solution.py
@@ -295,7 +295,7 @@
         grid_spec=pltpu.PrefetchScalarGridSpec(
             num_scalar_prefetch=1,
             in_specs=[pl.BlockSpec(memory_space=pl.ANY)] * len(pieces),
-            out_specs=[pl.BlockSpec(memory_space=pl.ANY)] * len(pieces),
+            out_specs=[pl.BlockSpec(memory_space=pltpu.VMEM)] * len(pieces),
             scratch_shapes=[pltpu.SemaphoreType.DMA],
         ),
         name="place",

time: 2300 us -> 817 us (0.36)
  Pallas kernels: 1540 us -> 49.2 us
    pallas_call x8, Pallas kernels: 1540 us -> 49.2 us  [place_blocks(): pl.pallas_call(body, out_shape=[jax.ShapeDtypeStruct(p.shape, p.dtype) fo...]
  transfers between devices with their start and end apart: 50 -> 50, of which waited for: 19 -> 20; matrix products, arithmetic and copies ran while one was open for 8% -> 23% of each run, Pallas kernels for 45% -> 4%
where the time goes in v2:
time: 817 us; the launch traced here: 810 us
  matrix products  325 us (40%)
  waiting for transfers between devices  191 us (23%)
  local copies, waits for them, and re-layouts  99.2 us (12%)
  other arithmetic  83.2 us (10%)
  starting transfers between devices  59.6 us (7%)
  Pallas kernels  49.2 us (6%)
    ppermute x25, waiting for transfers between devices, reduce_relative(): got = lax.ppermute(cur[half:], AXES, perm)  111 us
    ppermute x20, waiting for transfers between devices, gather_relative(): cur = jnp.concatenate([cur, lax.ppermute(cur, AXES, perm)], axis=0)  79.4 us
    dot_general x2, matrix products, forward_pass(): jnp.dot(normed_two, weight_up, preferred_element_type=jnp.float32)  55.7 us
    pallas_call x8, Pallas kernels, place_blocks(): pl.pallas_call(body, out_shape=[jax.ShapeDtypeStruct(p.shape, p.dtype) fo...  49.2 us
    dot_general x2, matrix products, attend_back(): jnp.einsum('qhd,khd->hqk', grad_mixed, values_all, preferred_element_type...  33.1 us
    unnamed x302, local copies, waits for them, and re-layouts  31.4 us
    dot_general x2, matrix products, backward_pass(): jnp.einsum('sd,fd->sf', grad_down_out, weight_down, preferred_element_typ...  31 us
    ppermute x20, starting transfers between devices, gather_relative(): cur = jnp.concatenate([cur, lax.ppermute(cur, AXES, perm)], axis=0)  30.4 us
  transfers between devices with their start and end apart: 50, of which 20 were waited for; matrix products, arithmetic and copies ran while one was open for 23% of the time, Pallas kernels for 4%

profile of v2, /device:TPU:0, one launch (start us, length us, event | category | flops | bytes accessed | tf_op | source)
XLA Modules:
  0.0 810.4 jit_solution(4689440798920462810)
XLA Ops:
  0.7 4.1 collective-permute-start.5
  4.8 6.1 concatenate.107
  49.6 5.6 collective-permute-done.6
  59.9 7.4 collective-permute-done.7
  74.2 8.1 collective-permute-done.21
  85.3 18.4 %collective-permute-done.8 = bf16[8,32,3072]{2,1,0:T(8,128)(2,1)S(1)} collective-permute-done((bf16[8,32,3072]{2,1,0:T(8,128)(2,1)S(1)}, bf16[8,32,3072]{2,1,0:T(8,128)(2,1)S(1)}, u32[]{:S(2)}, u32[]{:S(2)}) %collective-permute-start.8) | collective-permute-done | bytes 1572896 | tf_op jit(solution)/shard_map/ppermute | solution.py:311
  115.5 24.1 %collective-permute-done.13 = bf16[8,32,1024]{2,1,0:T(8,128)(2,1)S(1)} collective-permute-done((bf16[8,32,1024]{2,1,0:T(8,128)(2,1)S(1)}, bf16[8,32,1024]{2,1,0:T(8,128)(2,1)S(1)}, u32[]{:S(2)}, u32[]{:S(2)}) %collective-permute-start.13) | collective-permute-done | bytes 524320 | tf_op jit(solution)/shard_map/ppermute | solution.py:311
  149.1 4.2 constant_dynamic-update-slice_fusion.22
  153.7 8.5 %collective-permute-done.23 = bf16[8,128,1024]{2,1,0:T(8,128)(2,1)} collective-permute-done((bf16[8,128,1024]{2,1,0:T(8,128)(2,1)}, bf16[8,128,1024]{2,1,0:T(8,128)(2,1)}, u32[]{:S(2)}, u32[]{:S(2)}) %collective-permute-start.23) | collective-permute-done | bytes 2097184 | tf_op jit(solution)/shard_map/ppermute | solution.py:311
  162.2 4.2 constant_dynamic-update-slice_fusion.33
  166.4 3.8 constant_dynamic-update-slice_fusion.5.refs_0_
  170.2 6.3 place.8
  176.5 6.2 fusion.80
  190.6 8.2 %multiply_reduce_fusion.3 = (f32[16,512]{1,0:T(8,128)S(1)}, f32[16,512,512]{1,2,0:T(8,128)}) fusion(bf16[512,16,64]{0,2,1:T(8,128)(2,1)S(1)} %bitcast.245, bf16[512,16,64]{0,2,1:T(8,128)(2,1)S(1)} %bitcast.241), kind=kOutput, calls=%fused_computation.17 | convolution fusion | flops 545251328 | bytes 18907136 | tf_op jit(solution)/shard_map/while/body/eval_jaxpr/qhd,khd->hqk/dot_general | solution.py:30
  198.8 8.7 %fusion = f32[16,512]{1,0:T(8,128)S(1)} fusion(f32[16,512,512]{1,2,0:T(8,128)} %get-tuple-element.196, f32[16,512]{1,0:T(8,128)S(1)} %get-tuple-element.195), kind=kLoop, calls=%fused_computation.14 | loop fusion | flops 12574720 | bytes 16842752 | tf_op jit(solution)/shard_map/while/body/eval_jaxpr/reduce_sum | solution.py:34
  207.5 8.1 fusion.66
  218.3 4.7 constant_dynamic-update-slice_fusion.27.refs_0_
  223.0 7.4 place.10
  230.4 4.8 constant_dynamic-update-slice_fusion.38.refs_0_
  235.2 7.5 place.11
  242.8 27.4 %multiply_convert_fusion.3 = (bf16[512,4096]{1,0:T(8,128)(2,1)S(1)}, f32[512,4096]{1,0:T(8,128)}, f32[512,4096]{1,0:T(8,128)}) fusion(f32[4096]{0:T(1024)S(1)} %copy-done.97, bf16[1024,4096]{1,0:T(8,128)(2,1)} %bitcast.257, f32[512,1024]{1,0:T(8,128)S(1)} %get-tuple-element.198, f32[1024]{0:T(1024)S(1)} %copy-done.111, f32[1024]{0:T(1024)S(1)} %copy-done.60, ...), kind=kOutput, calls=%fused_computation.48 | convolution fusion | flops 4436000768 | bytes 31485952 | tf_op jit(solution)/shard_map/dot_general | solution.py:117
  270.1 6.8 add_convert_fusion.18
  277.7 6.0 fusion.124
  288.9 8.2 %multiply_reduce_fusion.2 = (f32[16,512]{1,0:T(8,128)S(1)}, f32[16,512,512]{1,2,0:T(8,128)}) fusion(bf16[512,16,64]{0,2,1:T(8,128)(2,1)S(1)} %bitcast.247, bf16[512,16,64]{0,2,1:T(8,128)(2,1)S(1)} %bitcast.243), kind=kOutput, calls=%fused_computation.16 | convolution fusion | flops 545251328 | bytes 18907136 | tf_op jit(solution)/shard_map/while/body/eval_jaxpr/qhd,khd->hqk/dot_general | solution.py:30
  297.1 8.7 %fusion.1 = f32[16,512]{1,0:T(8,128)S(1)} fusion(f32[16,512,512]{1,2,0:T(8,128)} %get-tuple-element.201, f32[16,512]{1,0:T(8,128)S(1)} %get-tuple-element.200), kind=kLoop, calls=%fused_computation.15 | loop fusion | flops 12574720 | bytes 16842752 | tf_op jit(solution)/shard_map/while/body/eval_jaxpr/reduce_sum | solution.py:34
  306.9 8.2 %fusion.65 = bf16[16,64,512]{2,1,0:T(8,128)(2,1)S(1)} fusion(bf16[512,16,64]{0,2,1:T(8,128)(2,1)S(1)} %bitcast.275, f32[16,512,512]{1,2,0:T(8,128)} %get-tuple-element.201, f32[16,512]{1,0:T(8,128)S(1)} %fusion.1, f32[16,512]{1,0:T(8,128)S(1)} %get-tuple-element.200), kind=kOutput, calls=%fused_computation.163 | convolution fusion | flops 554172416 | bytes 18939904 | tf_op jit(solution)/shard_map/while/body/eval_jaxpr/hqk,khd->qhd/dot_general | solution.py:36
  317.0 28.3 %multiply_convert_fusion.2 = (bf16[512,4096]{1,0:T(8,128)(2,1)}, f32[512,4096]{1,0:T(8,128)}, f32[512,4096]{1,0:T(8,128)}) fusion(f32[4096]{0:T(1024)S(1)} %copy-done.98, bf16[1024,4096]{1,0:T(8,128)(2,1)} %bitcast.258, f32[512,1024]{1,0:T(8,128)S(1)} %get-tuple-element.203, f32[512]{0:T(512)S(1)} %fusion.107, f32[512]{0:T(512)S(1)} %broadcast_multiply_fusion, ...), kind=kOutput, calls=%fused_computation.35 | convolution fusion | flops 4436000768 | bytes 31485952 | tf_op jit(solution)/shard_map/dot_general | solution.py:117
  345.4 15.5 %convert_reduce_fusion = (f32[4096]{0:T(1024)}, bf16[512,4096]{1,0:T(8,128)(2,1)}) fusion(f32[512,4096]{1,0:T(8,128)} %get-tuple-element.131, bf16[4096,1024]{1,0:T(8,128)(2,1)} %bitcast.253, bf16[1,512,1024]{2,1,0:T(8,128)(2,1)S(1)} %copy-done.33, f32[512]{0:T(512)S(1)} %bitcast.309, f32[512,4096]{1,0:T(8,128)} %get-tuple-element.204, f32[4096]{0:T(1024)S(1)} %copy-done.98), kind=kOutput, calls=%fused_computation.29 | convolution fusion | flops 4332187648 | bytes 30443520 | tf_op jit(solution)/shard_map/sd,fd->sf/dot_general | solution.py:178
  360.9 9.5 %multiply_reduce_fusion.4 = (f32[1024]{0:T(1024)}, f32[512]{0:T(512)S(1)}, f32[1024]{0:T(1024)}, f32[512,1024]{1,0:T(8,128)S(1)}) fusion(f32[512,1024]{1,0:T(8,128)S(1)} %get-tuple-element.203, f32[512]{0:T(512)S(1)} %fusion.107, f32[512]{0:T(512)S(1)} %broadcast_multiply_fusion, f32[1024]{0:T(1024)S(1)} %copy-done.61, ...), kind=kOutput, calls=%fused_computation.139 | convolution fusion | flops 4299159040 | bytes 16795648 | tf_op jit(solution)/shard_map/sf,df->sd/dot_general | solution.py:185
  377.2 16.5 %multiply_reduce_fusion.1 = (f32[16,512]{1,0:T(8,128)}, f32[16,512,512]{1,2,0:T(8,128)}) fusion(f32[16,512,512]{1,2,0:T(8,128)} %get-tuple-element.201, f32[16,512]{1,0:T(8,128)} %log_add_fusion.1, bf16[512,16,64]{0,2,1:T(8,128)(2,1)} %bitcast.249, bf16[512,16,64]{0,2,1:T(8,128)(2,1)} %bitcast.276), kind=kOutput, calls=%fused_computation.8 | convolution fusion | flops 553639936 | bytes 35717120 | tf_op jit(solution)/shard_map/while/body/eval_jaxpr/qhd,khd->hqk/dot_general | solution.py:49
  393.8 8.1 multiply_convert_fusion.1
  407.4 6.4 multiply_convert_fusion.6
  413.8 9.8 %convert_reduce_fusion.8 = (f32[16,64]{1,0:T(8,128)}, bf16[16,64,512]{2,1,0:T(8,128)(2,1)}) fusion(bf16[512,16,64]{0,2,1:T(8,128)(2,1)S(1)} %bitcast.250, f32[16,512,512]{1,2,0:T(8,128)} %get-tuple-element.201, f32[16,512]{1,0:T(8,128)S(1)} %copy-done.55), kind=kOutput, calls=%fused_computation.143 | convolution fusion | flops 551025664 | bytes 18911232 | tf_op jit(solution)/shard_map/while/body/eval_jaxpr/hqk,qhd->khd/dot_general | solution.py:52
  423.7 5.8 fusion.131
  433.4 8.2 %fusion.113 = f32[4096,1024]{1,0:T(8,128)} fusion(bf16[512,4096]{1,0:T(8,128)(2,1)S(1)} %copy-done.122, f32[512,1024]{1,0:T(8,128)S(1)} %get-tuple-element.121), kind=kOutput, calls=%fused_computation.315 | convolution fusion | flops 4295491584 | bytes 23068672 | tf_op jit(solution)/shard_map/sf,sd->fd/dot_general | solution.py:176
  441.6 15.5 %convert_reduce_fusion.1 = (f32[4096]{0:T(1024)}, bf16[512,4096]{1,0:T(8,128)(2,1)}) fusion(f32[512,4096]{1,0:T(8,128)} %get-tuple-element.133, bf16[4096,1024]{1,0:T(8,128)(2,1)} %bitcast.254, f32[512,1024]{1,0:T(8,128)S(1)} %get-tuple-element.121, f32[512,4096]{1,0:T(8,128)} %get-tuple-element.199, f32[4096]{0:T(1024)S(1)} %copy-done.99), kind=kOutput, calls=%fused_computation.30 | convolution fusion | flops 4331139072 | bytes 31490048 | tf_op jit(solution)/shard_map/sd,fd->sf/dot_general | solution.py:178
  457.1 11.2 %fusion.128 = f32[1024,4096]{1,0:T(8,128)} fusion(bf16[512,4096]{1,0:T(8,128)(2,1)} %get-tuple-element.222, f32[512,1024]{1,0:T(8,128)S(1)} %copy-done.15, f32[1024]{0:T(1024)S(1)} %copy-done.113, f32[1024]{0:T(1024)S(1)} %copy-done.61, f32[512]{0:T(512)S(1)} %copy-done.102, f32[512]{0:T(512)S(1)} %copy-done.86), kind=kOutput, calls=%fused_computation.326 | convolution fusion | flops 4297588736 | bytes 23080960 | tf_op jit(solution)/shard_map/sd,sf->df/dot_general | solution.py:183
  468.4 8.1 multiply_reduce_fusion.5
  485.0 16.5 %multiply_reduce_fusion = (f32[16,512]{1,0:T(8,128)}, f32[16,512,512]{1,2,0:T(8,128)}) fusion(f32[16,512,512]{1,2,0:T(8,128)} %get-tuple-element.196, f32[16,512]{1,0:T(8,128)} %log_add_fusion, bf16[512,16,64]{0,2,1:T(8,128)(2,1)} %bitcast.251, bf16[512,16,64]{0,2,1:T(8,128)(2,1)} %bitcast.273), kind=kOutput, calls=%fused_computation.5 | convolution fusion | flops 553639936 | bytes 35717120 | tf_op jit(solution)/shard_map/while/body/eval_jaxpr/qhd,khd->hqk/dot_general | solution.py:49
  501.6 8.3 %multiply_convert_fusion = bf16[16,512,512]{1,2,0:T(8,128)(2,1)S(1)} fusion(f32[16,512,512]{1,2,0:T(8,128)} %get-tuple-element.211, f32[16,512,512]{1,2,0:T(8,128)S(1)} %bitcast.227, f32[16,512]{1,0:T(8,128)} %get-tuple-element.210, f32[16,512]{1,0:T(8,128)} %log_add_fusion), kind=kLoop, calls=%fused_computation.4 | loop fusion | flops 20971520 | bytes 42008576 | tf_op jit(solution)/shard_map/while/body/eval_jaxpr/convert_element_type | solution.py:59
  514.7 6.1 multiply_convert_fusion.4
  520.9 7.8 convert_reduce_fusion.9
  528.8 9.8 %fusion.74 = f32[1024,3072]{1,0:T(8,128)} fusion(bf16[512,1024]{0,1:T(8,128)(2,1)S(1)} %bitcast.301, bf16[512,1024]{0,1:T(8,128)(2,1)S(1)} %bitcast.299, bf16[512,1024]{0,1:T(8,128)(2,1)S(1)} %bitcast.289, bf16[1,512,1024]{2,1,0:T(8,128)(2,1)S(1)} %copy-done.3, f32[512]{0:T(512)S(1)} %copy-done.75, f32[1024]{0:T(1024)S(1)} %copy-done.110, ...), kind=kOutput, calls=%fused_computation.170 | convolution fusion | flops 3233808384 | bytes 16789504 | tf_op jit(solution)/shard_map/sd,se->de/dot_general | solution.py:211
  538.6 5.1 fusion.132
  543.6 12.0 %add_convert_fusion = bf16[4096,1024]{1,0:T(8,128)(2,1)} fusion(f32[4096,1024]{1,0:T(8,128)} %fusion.113, bf16[512,4096]{1,0:T(8,128)(2,1)} %get-tuple-element.130, bf16[1,512,1024]{2,1,0:T(8,128)(2,1)S(1)} %copy-done.35, f32[512]{0:T(512)S(1)} %bitcast.312), kind=kOutput, calls=%fused_computation.2 | convolution fusion | flops 4304928768 | bytes 30410752 | tf_op jit(solution)/shard_map/sf,sd->fd/dot_general | solution.py:176
  555.7 7.4 place.15
  563.1 4.8 slice.402
  568.4 15.7 %add_convert_fusion.1 = bf16[1024,4096]{1,0:T(8,128)(2,1)} fusion(f32[1024,4096]{1,0:T(8,128)} %fusion.128, bf16[512,4096]{1,0:T(8,128)(2,1)} %get-tuple-element.224, f32[512,1024]{1,0:T(8,128)} %copy-done.7, f32[512]{0:T(512)S(1)} %copy-done.104, f32[512]{0:T(512)S(1)} %copy-done.88, f32[1024]{0:T(1024)S(1)} %copy-done.114, f32[1024]{0:T(1024)S(1)} %copy-done.61), kind=kOutput, calls=%fused_computation.3 | convolution fusion | flops 4305977344 | bytes 31469568 | tf_op jit(solution)/shard_map/sd,sf->df/dot_general | solution.py:183
  584.1 7.3 place.14
  591.6 4.7 slice.391
  600.9 5.1 add_convert_fusion.10
  606.0 3.7 place.13
  614.2 11.9 %add_convert_fusion.2 = bf16[1024,3072]{1,0:T(8,128)(2,1)} fusion(f32[1024,3072]{1,0:T(8,128)} %fusion.74, bf16[512,1024]{0,1:T(8,128)(2,1)} %bitcast.298, bf16[512,1024]{0,1:T(8,128)(2,1)} %bitcast.296, bf16[512,1024]{0,1:T(8,128)(2,1)S(1)} %bitcast.288, bf16[512,1024]{1,0:T(8,128)(2,1)S(1)} %add_convert_fusion.18, f32[1024]{0:T(1024)S(1)} %copy-done.110, ...), kind=kOutput, calls=%fused_computation.18 | convolution fusion | flops 3240099840 | bytes 23080960 | tf_op jit(solution)/shard_map/sd,se->de/dot_general | solution.py:211
  626.1 6.1 place.12
  636.1 9.1 %fusion.73 = bf16[1,512,1024]{2,1,0:T(8,128)(2,1)} fusion(f32[512,1024]{1,0:T(8,128)S(1)} %copy-done.8, bf16[512,4096]{1,0:T(8,128)(2,1)S(1)} %copy-done.124, bf16[4096,1024]{1,0:T(8,128)(2,1)} %bitcast.255, f32[1024]{0:T(1024)S(1)} %copy-done.107), kind=kOutput, calls=%fused_computation.169 | convolution fusion | flops 4296540160 | bytes 15732736 | tf_op jit(solution)/shard_map/dot_general | solution.py:123
  653.8 6.3 collective-permute-done.36
  664.8 5.1 add_convert_fusion.3
  672.4 3.7 add_convert_fusion.4
  690.2 25.1 %collective-permute-done.46 = bf16[8,128,1024]{2,1,0:T(8,128)(2,1)} collective-permute-done((bf16[8,128,1024]{2,1,0:T(8,128)(2,1)}, bf16[8,128,1024]{2,1,0:T(8,128)(2,1)}, u32[]{:S(2)}, u32[]{:S(2)}) %collective-permute-start.46) | collective-permute-done | bytes 2097184 | tf_op jit(solution)/shard_map/ppermute | solution.py:319
  719.2 29.7 %collective-permute-done.41 = bf16[8,32,4096]{2,1,0:T(8,128)(2,1)S(1)} collective-permute-done((bf16[8,32,4096]{2,1,0:T(8,128)(2,1)S(1)}, bf16[8,32,4096]{2,1,0:T(8,128)(2,1)S(1)}, u32[]{:S(2)}, u32[]{:S(2)}) %collective-permute-start.41) | collective-permute-done | bytes 2097184 | tf_op jit(solution)/shard_map/ppermute | solution.py:319
  754.8 10.0 %collective-permute-done.42 = bf16[4,32,4096]{2,1,0:T(8,128)(2,1)S(1)} collective-permute-done((bf16[4,32,4096]{2,1,0:T(8,128)(2,1)S(1)}, bf16[4,32,4096]{2,1,0:T(8,128)(2,1)S(1)}, u32[]{:S(2)}, u32[]{:S(2)}) %collective-permute-start.42) | collective-permute-done | bytes 1048608 | tf_op jit(solution)/shard_map/ppermute | solution.py:319
  769.5 13.0 %collective-permute-done.48 = bf16[2,128,1024]{2,1,0:T(8,128)(2,1)S(1)} collective-permute-done((bf16[2,128,1024]{2,1,0:T(8,128)(2,1)S(1)}, bf16[2,128,1024]{2,1,0:T(8,128)(2,1)S(1)}, u32[]{:S(2)}, u32[]{:S(2)}) %collective-permute-start.48) | collective-permute-done | bytes 524320 | tf_op jit(solution)/shard_map/ppermute | solution.py:319
  784.5 7.7 collective-permute-done.43
  793.9 11.6 %collective-permute-done.49 = bf16[1,128,1024]{2,1,0:T(8,128)(2,1)S(1)} collective-permute-done((bf16[1,128,1024]{2,1,0:T(8,128)(2,1)S(1)}, bf16[1,128,1024]{2,1,0:T(8,128)(2,1)S(1)}, u32[]{:S(2)}, u32[]{:S(2)}) %collective-permute-start.49) | collective-permute-done | bytes 262176 | tf_op jit(solution)/shard_map/ppermute | solution.py:319
  (550 shorter events, 189.2 us)
Async XLA Ops:
  0.7 41.7 %copy-start.46 = (bf16[32,3072]{1,0:T(8,128)(2,1)S(1)}, bf16[32,3072]{1,0:T(8,128)(2,1)}, u32[]{:S(2)}) copy-start(bf16[32,3072]{1,0:T(8,128)(2,1)} %param.21) | copy-start | bytes 589828
  0.7 40.2 %copy-start.51 = (bf16[32,1024]{1,0:T(8,128)(2,1)S(1)}, bf16[32,1024]{1,0:T(8,128)(2,1)}, u32[]{:S(2)}) copy-start(bf16[32,1024]{1,0:T(8,128)(2,1)} %param.24) | copy-start | bytes 196612
  0.7 38.7 %copy-start.120 = (s32[1,512]{1,0:T(1,128)S(1)}, s32[1,512]{1,0:T(1,128)}, u32[]{:S(2)}) copy-start(s32[1,512]{1,0:T(1,128)} %param.34) | copy-start | bytes 6148
  0.7 41.7 %collective-permute-start.5 = (bf16[1,32,3072]{2,1,0:T(8,128)(2,1)}, bf16[1,32,3072]{2,1,0:T(8,128)(2,1)S(1)}, u32[]{:S(2)}, u32[]{:S(2)}) collective-permute-start(bf16[1,32,3072]{2,1,0:T(8,128)(2,1)} %bitcast.291), channel_id=1, source_target_pairs={{0,4},{1,5},{2,6},{3,7},{4,0},{5,1},{6,2},{7,3},{8,12},{9,13},{10,... | collective-permute-start | bytes 589832 | tf_op jit(solution)/shard_map/ppermute | solution.py:311
  10.9 15.9 %collective-permute-start = (bf16[1,1,384]{2,0,1:T(2,128)(2,1)S(1)}, bf16[1,1,384]{2,0,1:T(2,128)(2,1)S(1)}, u32[]{:S(2)}, u32[]{:S(2)}) collective-permute-start(bf16[1,1,384]{2,0,1:T(2,128)(2,1)S(1)} %broadcast_in_dim_broadcast_in_dim.3), channel_id=1, source_target_pairs={{0,4},{1,5},{2,6},{3,7},{4,0},{5,1},{6,2},{7,3},{8,12},{9,13},{10,... | collective-permute-start | bytes 2312 | tf_op jit(solution)/shard_map/ppermute | solution.py:311
  11.0 29.8 %collective-permute-start.10 = (bf16[1,32,1024]{2,1,0:T(8,128)(2,1)}, bf16[1,32,1024]{2,1,0:T(8,128)(2,1)S(1)}, u32[]{:S(2)}, u32[]{:S(2)}) collective-permute-start(bf16[1,32,1024]{2,1,0:T(8,128)(2,1)} %bitcast.303), channel_id=1, source_target_pairs={{0,4},{1,5},{2,6},{3,7},{4,0},{5,1},{6,2},{7,3},{8,12},{9,13},{10,... | collective-permute-start | bytes 196616 | tf_op jit(solution)/shard_map/ppermute | solution.py:311
  13.9 43.8 %collective-permute-start.15 = (bf16[1,32,4096]{2,1,0:T(8,128)(2,1)}, bf16[1,32,4096]{2,1,0:T(8,128)(2,1)S(1)}, u32[]{:S(2)}, u32[]{:S(2)}) collective-permute-start(bf16[1,32,4096]{2,1,0:T(8,128)(2,1)} %bitcast.277), channel_id=1, source_target_pairs={{0,4},{1,5},{2,6},{3,7},{4,0},{5,1},{6,2},{7,3},{8,12},{9,13},{10,... | collective-permute-start | bytes 786440 | tf_op jit(solution)/shard_map/ppermute | solution.py:311
  13.9 45.3 %collective-permute-start.20 = (bf16[1,128,1024]{2,1,0:T(8,128)(2,1)}, bf16[1,128,1024]{2,1,0:T(8,128)(2,1)S(1)}, u32[]{:S(2)}, u32[]{:S(2)}) collective-permute-start(bf16[1,128,1024]{2,1,0:T(8,128)(2,1)} %bitcast.281), channel_id=1, source_target_pairs={{0,4},{1,5},{2,6},{3,7},{4,0},{5,1},{6,2},{7,3},{8,12},{9,13},{10,... | collective-permute-start | bytes 786440 | tf_op jit(solution)/shard_map/ppermute | solution.py:311
  20.0 37.7 %copy-start.39 = (bf16[32,4096]{1,0:T(8,128)(2,1)S(1)}, bf16[32,4096]{1,0:T(8,128)(2,1)}, u32[]{:S(2)}) copy-start(bf16[32,4096]{1,0:T(8,128)(2,1)} %param.28) | copy-start | bytes 786436
  23.7 35.6 %copy-start.40 = (bf16[128,1024]{1,0:T(8,128)(2,1)S(1)}, bf16[128,1024]{1,0:T(8,128)(2,1)}, u32[]{:S(2)}) copy-start(bf16[128,1024]{1,0:T(8,128)(2,1)} %param.30) | copy-start | bytes 786436
  26.8 3.8 collective-permute-start.1
  30.6 3.7 collective-permute-start.2
  34.3 3.7 collective-permute-start.3
  38.1 1.9 collective-permute-start.4
  40.8 6.4 collective-permute-start.11
  42.4 12.8 %collective-permute-start.6 = (bf16[2,32,3072]{2,1,0:T(8,128)(2,1)S(1)}, bf16[2,32,3072]{2,1,0:T(8,128)(2,1)S(1)}, u32[]{:S(2)}, u32[]{:S(2)}) collective-permute-start(bf16[2,32,3072]{2,1,0:T(8,128)(2,1)S(1)} %pad_maximum_fusion.15), channel_id=1, source_target_pairs={{0,2},{1,3},{2,0},{3,1},{4,6},{5,7},{6,4},{7,5},{8,10},{9,11},{10,... | collective-permute-start | bytes 1179656 | tf_op jit(solution)/shard_map/ppermute | solution.py:311
  43.7 233.9 %copy-start.56 = (f32[1024]{0:T(1024)}, f32[1024]{0:T(1024)S(1)}, u32[]{:S(2)}) copy-start(f32[1024]{0:T(1024)S(1)} %reshape.441) | copy-start | bytes 12292
  44.5 139.4 %copy-start.58 = (f32[1024]{0:T(1024)}, f32[1024]{0:T(1024)S(1)}, u32[]{:S(2)}) copy-start(f32[1024]{0:T(1024)S(1)} %reshape.444) | copy-start | bytes 12292
  47.3 62.5 %collective-permute-start.12 = (bf16[4,32,1024]{2,1,0:T(8,128)(2,1)S(1)}, bf16[4,32,1024]{2,1,0:T(8,128)(2,1)S(1)}, u32[]{:S(2)}, u32[]{:S(2)}) collective-permute-start(bf16[4,32,1024]{2,1,0:T(8,128)(2,1)S(1)} %pad_maximum_fusion.16), channel_id=1, source_target_pairs={{0,1},{1,0},{2,3},{3,2},{4,5},{5,4},{6,7},{7,6},{8,24},{9,25},{10,... | collective-permute-start | bytes 786440 | tf_op jit(solution)/shard_map/ppermute | solution.py:311
  55.3 12.1 %collective-permute-start.7 = (bf16[4,32,3072]{2,1,0:T(8,128)(2,1)S(1)}, bf16[4,32,3072]{2,1,0:T(8,128)(2,1)S(1)}, u32[]{:S(2)}, u32[]{:S(2)}) collective-permute-start(bf16[4,32,3072]{2,1,0:T(8,128)(2,1)S(1)} %pad_maximum_fusion.11), channel_id=1, source_target_pairs={{0,1},{1,0},{2,3},{3,2},{4,5},{5,4},{6,7},{7,6},{8,24},{9,25},{10,... | collective-permute-start | bytes 2359304 | tf_op jit(solution)/shard_map/ppermute | solution.py:311
  57.7 14.9 %collective-permute-start.16 = (bf16[2,32,4096]{2,1,0:T(8,128)(2,1)S(1)}, bf16[2,32,4096]{2,1,0:T(8,128)(2,1)S(1)}, u32[]{:S(2)}, u32[]{:S(2)}) collective-permute-start(bf16[2,32,4096]{2,1,0:T(8,128)(2,1)S(1)} %pad_maximum_fusion.13), channel_id=1, source_target_pairs={{0,2},{1,3},{2,0},{3,1},{4,6},{5,7},{6,4},{7,5},{8,10},{9,11},{10,... | collective-permute-start | bytes 1572872 | tf_op jit(solution)/shard_map/ppermute | solution.py:311
  59.3 23.0 %collective-permute-start.21 = (bf16[2,128,1024]{2,1,0:T(8,128)(2,1)S(1)}, bf16[2,128,1024]{2,1,0:T(8,128)(2,1)S(1)}, u32[]{:S(2)}, u32[]{:S(2)}) collective-permute-start(bf16[2,128,1024]{2,1,0:T(8,128)(2,1)S(1)} %pad_maximum_fusion.14), channel_id=1, source_target_pairs={{0,2},{1,3},{2,0},{3,1},{4,6},{5,7},{6,4},{7,5},{8,10},{9,11},{10,... | collective-permute-start | bytes 1572872 | tf_op jit(solution)/shard_map/ppermute | solution.py:311
  67.5 36.2 %collective-permute-start.8 = (bf16[8,32,3072]{2,1,0:T(8,128)(2,1)S(1)}, bf16[8,32,3072]{2,1,0:T(8,128)(2,1)S(1)}, u32[]{:S(2)}, u32[]{:S(2)}) collective-permute-start(bf16[8,32,3072]{2,1,0:T(8,128)(2,1)S(1)} %pad_maximum_fusion.4), channel_id=1, source_target_pairs={{0,16},{1,17},{2,18},{3,19},{4,20},{5,21},{6,22},{7,23},{8,9},{9,8... | collective-permute-start | bytes 4718600 | tf_op jit(solution)/shard_map/ppermute | solution.py:311
  72.8 33.0 %collective-permute-start.17 = (bf16[4,32,4096]{2,1,0:T(8,128)(2,1)S(1)}, bf16[4,32,4096]{2,1,0:T(8,128)(2,1)S(1)}, u32[]{:S(2)}, u32[]{:S(2)}) collective-permute-start(bf16[4,32,4096]{2,1,0:T(8,128)(2,1)S(1)} %pad_maximum_fusion.9), channel_id=1, source_target_pairs={{0,1},{1,0},{2,3},{3,2},{4,5},{5,4},{6,7},{7,6},{8,24},{9,25},{10,... | collective-permute-start | bytes 3145736 | tf_op jit(solution)/shard_map/ppermute | solution.py:311
  82.4 28.5 %collective-permute-start.22 = (bf16[4,128,1024]{2,1,0:T(8,128)(2,1)S(1)}, bf16[4,128,1024]{2,1,0:T(8,128)(2,1)S(1)}, u32[]{:S(2)}, u32[]{:S(2)}) collective-permute-start(bf16[4,128,1024]{2,1,0:T(8,128)(2,1)S(1)} %pad_maximum_fusion.10), channel_id=1, source_target_pairs={{0,1},{1,0},{2,3},{3,2},{4,5},{5,4},{6,7},{7,6},{8,24},{9,25},{10,... | collective-permute-start | bytes 3145736 | tf_op jit(solution)/shard_map/ppermute | solution.py:311
  105.8 60.6 %collective-permute-start.9 = (bf16[16,32,3072]{2,1,0:T(8,128)(2,1)}, bf16[16,32,3072]{2,1,0:T(8,128)(2,1)}, u32[]{:S(2)}, u32[]{:S(2)}) collective-permute-start(bf16[16,32,3072]{2,1,0:T(8,128)(2,1)} %get-tuple-element.142), channel_id=1, source_target_pairs={{0,8},{1,9},{2,10},{3,11},{4,12},{5,13},{6,14},{7,15},{8,0},{9,1},... | collective-permute-start | bytes 9437192 | tf_op jit(solution)/shard_map/ppermute | solution.py:312
  107.3 41.7 %collective-permute-start.18 = (bf16[8,32,4096]{2,1,0:T(8,128)(2,1)}, bf16[8,32,4096]{2,1,0:T(8,128)(2,1)}, u32[]{:S(2)}, u32[]{:S(2)}) collective-permute-start(bf16[8,32,4096]{2,1,0:T(8,128)(2,1)} %pad_maximum_fusion.2), channel_id=1, source_target_pairs={{0,16},{1,17},{2,18},{3,19},{4,20},{5,21},{6,22},{7,23},{8,9},{9,8... | collective-permute-start | bytes 6291464 | tf_op jit(solution)/shard_map/ppermute | solution.py:311
  109.9 29.8 %collective-permute-start.13 = (bf16[8,32,1024]{2,1,0:T(8,128)(2,1)S(1)}, bf16[8,32,1024]{2,1,0:T(8,128)(2,1)S(1)}, u32[]{:S(2)}, u32[]{:S(2)}) collective-permute-start(bf16[8,32,1024]{2,1,0:T(8,128)(2,1)S(1)} %pad_maximum_fusion.12), channel_id=1, source_target_pairs={{0,16},{1,17},{2,18},{3,19},{4,20},{5,21},{6,22},{7,23},{8,9},{9,8... | collective-permute-start | bytes 1572872 | tf_op jit(solution)/shard_map/ppermute | solution.py:311
  112.5 49.8 %collective-permute-start.23 = (bf16[8,128,1024]{2,1,0:T(8,128)(2,1)}, bf16[8,128,1024]{2,1,0:T(8,128)(2,1)}, u32[]{:S(2)}, u32[]{:S(2)}) collective-permute-start(bf16[8,128,1024]{2,1,0:T(8,128)(2,1)} %pad_maximum_fusion.3), channel_id=1, source_target_pairs={{0,16},{1,17},{2,18},{3,19},{4,20},{5,21},{6,22},{7,23},{8,9},{9,8... | collective-permute-start | bytes 6291464 | tf_op jit(solution)/shard_map/ppermute | solution.py:311
  139.7 4.3 collective-permute-start.14
  153.2 65.1 %collective-permute-start.19 = (bf16[16,32,4096]{2,1,0:T(8,128)(2,1)}, bf16[16,32,4096]{2,1,0:T(8,128)(2,1)}, u32[]{:S(2)}, u32[]{:S(2)}) collective-permute-start(bf16[16,32,4096]{2,1,0:T(8,128)(2,1)} %get-tuple-element.140), channel_id=1, source_target_pairs={{0,8},{1,9},{2,10},{3,11},{4,12},{5,13},{6,14},{7,15},{8,0},{9,1},... | collective-permute-start | bytes 12582920 | tf_op jit(solution)/shard_map/ppermute | solution.py:312
  166.4 64.0 %collective-permute-start.24 = (bf16[16,128,1024]{2,1,0:T(8,128)(2,1)}, bf16[16,128,1024]{2,1,0:T(8,128)(2,1)}, u32[]{:S(2)}, u32[]{:S(2)}) collective-permute-start(bf16[16,128,1024]{2,1,0:T(8,128)(2,1)} %get-tuple-element.138), channel_id=1, source_target_pairs={{0,8},{1,9},{2,10},{3,11},{4,12},{5,13},{6,14},{7,15},{8,0},{9,1},... | collective-permute-start | bytes 12582920 | tf_op jit(solution)/shard_map/ppermute | solution.py:312
  277.0 337.2 %copy-start.4 = (bf16[512,1024]{1,0:T(8,128)(2,1)}, bf16[512,1024]{1,0:T(8,128)(2,1)S(1)}, u32[]{:S(2)}) copy-start(bf16[512,1024]{1,0:T(8,128)(2,1)S(1)} %add_convert_fusion.18) | copy-start | bytes 3145732
  316.6 53.9 %copy-start.7 = (f32[512,1024]{1,0:T(8,128)}, f32[512,1024]{1,0:T(8,128)S(1)}, u32[]{:S(2)}) copy-start(f32[512,1024]{1,0:T(8,128)S(1)} %get-tuple-element.203) | copy-start | bytes 6291460
  316.6 53.8 %copy-start.87 = (f32[512]{0:T(512)}, f32[512]{0:T(512)S(1)}, u32[]{:S(2)}) copy-start(f32[512]{0:T(512)S(1)} %broadcast_multiply_fusion) | copy-start | bytes 6148
  317.0 53.5 %copy-start.103 = (f32[512]{0:T(512)}, f32[512]{0:T(512)S(1)}, u32[]{:S(2)}) copy-start(f32[512]{0:T(512)S(1)} %fusion.107) | copy-start | bytes 6148
  317.0 28.4 %copy-start.33 = (bf16[1,512,1024]{2,1,0:T(8,128)(2,1)S(1)}, bf16[1,512,1024]{2,1,0:T(8,128)(2,1)}, u32[]{:S(2)}) copy-start(bf16[1,512,1024]{2,1,0:T(8,128)(2,1)} %param.33) | copy-start | bytes 3145732
  317.0 28.4 %copy-start.69 = (f32[1,512]{1,0:T(1,128)S(1)}, f32[1,512]{1,0:T(1,128)}, u32[]{:S(2)}) copy-start(f32[1,512]{1,0:T(1,128)} %convert_element_type.583) | copy-start | bytes 6148
  433.2 44.0 %copy-start.9 = (f32[512,1024]{1,0:T(8,128)}, f32[512,1024]{1,0:T(8,128)S(1)}, u32[]{:S(2)}) copy-start(f32[512,1024]{1,0:T(8,128)S(1)} %get-tuple-element.121) | copy-start | bytes 6291460
  567.8 96.9 %collective-permute-start.45 = (bf16[16,128,1024]{2,1,0:T(8,128)(2,1)}, bf16[16,128,1024]{2,1,0:T(8,128)(2,1)}, u32[]{:S(2)}, u32[]{:S(2)}) collective-permute-start(bf16[16,128,1024]{2,1,0:T(8,128)(2,1)} %slice.402), channel_id=1, source_target_pairs={{0,8},{1,9},{2,10},{3,11},{4,12},{5,13},{6,14},{7,15},{8,0},{9,1},... | collective-permute-start | bytes 12582920 | tf_op jit(solution)/shard_map/ppermute | solution.py:319
  596.2 76.1 %collective-permute-start.40 = (bf16[16,32,4096]{2,1,0:T(8,128)(2,1)}, bf16[16,32,4096]{2,1,0:T(8,128)(2,1)}, u32[]{:S(2)}, u32[]{:S(2)}) collective-permute-start(bf16[16,32,4096]{2,1,0:T(8,128)(2,1)} %slice.391), channel_id=1, source_target_pairs={{0,8},{1,9},{2,10},{3,11},{4,12},{5,13},{6,14},{7,15},{8,0},{9,1},... | collective-permute-start | bytes 12582920 | tf_op jit(solution)/shard_map/ppermute | solution.py:319
  600.4 11.7 %collective-permute-start.25 = (f32[16,1,384]{2,0,1:T(8,128)S(1)}, f32[16,1,384]{2,0,1:T(8,128)S(1)}, u32[]{:S(2)}, u32[]{:S(2)}) collective-permute-start(f32[16,1,384]{2,0,1:T(8,128)S(1)} %slice_bitcast_fusion), channel_id=1, source_target_pairs={{0,8},{1,9},{2,10},{3,11},{4,12},{5,13},{6,14},{7,15},{8,0},{9,1},... | collective-permute-start | bytes 73736 | tf_op jit(solution)/shard_map/ppermute | solution.py:319
  612.1 37.0 %collective-permute-start.35 = (bf16[16,32,1024]{2,1,0:T(8,128)(2,1)}, bf16[16,32,1024]{2,1,0:T(8,128)(2,1)}, u32[]{:S(2)}, u32[]{:S(2)}) collective-permute-start(bf16[16,32,1024]{2,1,0:T(8,128)(2,1)} %slice.378), channel_id=1, source_target_pairs={{0,8},{1,9},{2,10},{3,11},{4,12},{5,13},{6,14},{7,15},{8,0},{9,1},... | collective-permute-start | bytes 3145736 | tf_op jit(solution)/shard_map/ppermute | solution.py:319
  612.1 22.6 %collective-permute-start.26 = (f32[8,1,384]{2,0,1:T(8,128)S(1)}, f32[8,1,384]{2,0,1:T(8,128)S(1)}, u32[]{:S(2)}, u32[]{:S(2)}) collective-permute-start(f32[8,1,384]{2,0,1:T(8,128)S(1)} %slice.356), channel_id=1, source_target_pairs={{0,16},{1,17},{2,18},{3,19},{4,20},{5,21},{6,22},{7,23},{8,9},{9,8... | collective-permute-start | bytes 36872 | tf_op jit(solution)/shard_map/ppermute | solution.py:319
  634.7 26.5 %collective-permute-start.30 = (bf16[16,32,3072]{2,1,0:T(8,128)(2,1)S(1)}, bf16[16,32,3072]{2,1,0:T(8,128)(2,1)S(1)}, u32[]{:S(2)}, u32[]{:S(2)}) collective-permute-start(bf16[16,32,3072]{2,1,0:T(8,128)(2,1)S(1)} %slice.366), channel_id=1, source_target_pairs={{0,8},{1,9},{2,10},{3,11},{4,12},{5,13},{6,14},{7,15},{8,0},{9,1},... | collective-permute-start | bytes 9437192 | tf_op jit(solution)/shard_map/ppermute | solution.py:319
  634.8 10.4 %collective-permute-start.27 = (f32[4,1,384]{2,0,1:T(4,128)S(1)}, f32[4,1,384]{2,0,1:T(4,128)S(1)}, u32[]{:S(2)}, u32[]{:S(2)}) collective-permute-start(f32[4,1,384]{2,0,1:T(4,128)S(1)} %slice.358), channel_id=1, source_target_pairs={{0,1},{1,0},{2,3},{3,2},{4,5},{5,4},{6,7},{7,6},{8,24},{9,25},{10,... | collective-permute-start | bytes 18440 | tf_op jit(solution)/shard_map/ppermute | solution.py:319
  645.2 3.7 collective-permute-start.28
  648.9 4.9 collective-permute-start.29
  650.8 9.2 %collective-permute-start.36 = (bf16[8,32,1024]{2,1,0:T(8,128)(2,1)S(1)}, bf16[8,32,1024]{2,1,0:T(8,128)(2,1)S(1)}, u32[]{:S(2)}, u32[]{:S(2)}) collective-permute-start(bf16[8,32,1024]{2,1,0:T(8,128)(2,1)S(1)} %slice.380), channel_id=1, source_target_pairs={{0,16},{1,17},{2,18},{3,19},{4,20},{5,21},{6,22},{7,23},{8,9},{9,8... | collective-permute-start | bytes 1572872 | tf_op jit(solution)/shard_map/ppermute | solution.py:319
  660.3 17.8 %collective-permute-start.37 = (bf16[4,32,1024]{2,1,0:T(8,128)(2,1)S(1)}, bf16[4,32,1024]{2,1,0:T(8,128)(2,1)S(1)}, u32[]{:S(2)}, u32[]{:S(2)}) collective-permute-start(bf16[4,32,1024]{2,1,0:T(8,128)(2,1)S(1)} %slice.382), channel_id=1, source_target_pairs={{0,1},{1,0},{2,3},{3,2},{4,5},{5,4},{6,7},{7,6},{8,24},{9,25},{10,... | collective-permute-start | bytes 786440 | tf_op jit(solution)/shard_map/ppermute | solution.py:319
  663.7 23.1 %collective-permute-start.31 = (bf16[8,32,3072]{2,1,0:T(8,128)(2,1)}, bf16[8,32,3072]{2,1,0:T(8,128)(2,1)}, u32[]{:S(2)}, u32[]{:S(2)}) collective-permute-start(bf16[8,32,3072]{2,1,0:T(8,128)(2,1)} %slice.368), channel_id=1, source_target_pairs={{0,16},{1,17},{2,18},{3,19},{4,20},{5,21},{6,22},{7,23},{8,9},{9,8... | collective-permute-start | bytes 4718600 | tf_op jit(solution)/shard_map/ppermute | solution.py:319
  671.4 43.9 %collective-permute-start.46 = (bf16[8,128,1024]{2,1,0:T(8,128)(2,1)}, bf16[8,128,1024]{2,1,0:T(8,128)(2,1)}, u32[]{:S(2)}, u32[]{:S(2)}) collective-permute-start(bf16[8,128,1024]{2,1,0:T(8,128)(2,1)} %slice.404), channel_id=1, source_target_pairs={{0,16},{1,17},{2,18},{3,19},{4,20},{5,21},{6,22},{7,23},{8,9},{9,8... | collective-permute-start | bytes 6291464 | tf_op jit(solution)/shard_map/ppermute | solution.py:319
  676.3 72.6 %collective-permute-start.41 = (bf16[8,32,4096]{2,1,0:T(8,128)(2,1)S(1)}, bf16[8,32,4096]{2,1,0:T(8,128)(2,1)S(1)}, u32[]{:S(2)}, u32[]{:S(2)}) collective-permute-start(bf16[8,32,4096]{2,1,0:T(8,128)(2,1)S(1)} %slice.393), channel_id=1, source_target_pairs={{0,16},{1,17},{2,18},{3,19},{4,20},{5,21},{6,22},{7,23},{8,9},{9,8... | collective-permute-start | bytes 6291464 | tf_op jit(solution)/shard_map/ppermute | solution.py:319
  678.2 5.0 collective-permute-start.38
  683.3 67.9 %collective-permute-start.39 = (bf16[1,32,1024]{2,1,0:T(8,128)(2,1)S(1)}, bf16[1,32,1024]{2,1,0:T(8,128)(2,1)S(1)}, u32[]{:S(2)}, u32[]{:S(2)}) collective-permute-start(bf16[1,32,1024]{2,1,0:T(8,128)(2,1)S(1)} %slice.386), channel_id=1, source_target_pairs={{0,4},{1,5},{2,6},{3,7},{4,0},{5,1},{6,2},{7,3},{8,12},{9,13},{10,... | collective-permute-start | bytes 196616 | tf_op jit(solution)/shard_map/ppermute | solution.py:319
  688.9 63.0 %collective-permute-start.32 = (bf16[4,32,3072]{2,1,0:T(8,128)(2,1)S(1)}, bf16[4,32,3072]{2,1,0:T(8,128)(2,1)S(1)}, u32[]{:S(2)}, u32[]{:S(2)}) collective-permute-start(bf16[4,32,3072]{2,1,0:T(8,128)(2,1)S(1)} %slice.370), channel_id=1, source_target_pairs={{0,1},{1,0},{2,3},{3,2},{4,5},{5,4},{6,7},{7,6},{8,24},{9,25},{10,... | collective-permute-start | bytes 2359304 | tf_op jit(solution)/shard_map/ppermute | solution.py:319
  718.0 36.0 %collective-permute-start.47 = (bf16[4,128,1024]{2,1,0:T(8,128)(2,1)S(1)}, bf16[4,128,1024]{2,1,0:T(8,128)(2,1)S(1)}, u32[]{:S(2)}, u32[]{:S(2)}) collective-permute-start(bf16[4,128,1024]{2,1,0:T(8,128)(2,1)S(1)} %slice.406), channel_id=1, source_target_pairs={{0,1},{1,0},{2,3},{3,2},{4,5},{5,4},{6,7},{7,6},{8,24},{9,25},{10,... | collective-permute-start | bytes 3145736 | tf_op jit(solution)/shard_map/ppermute | solution.py:319
  749.9 14.9 %collective-permute-start.42 = (bf16[4,32,4096]{2,1,0:T(8,128)(2,1)S(1)}, bf16[4,32,4096]{2,1,0:T(8,128)(2,1)S(1)}, u32[]{:S(2)}, u32[]{:S(2)}) collective-permute-start(bf16[4,32,4096]{2,1,0:T(8,128)(2,1)S(1)} %slice.395), channel_id=1, source_target_pairs={{0,1},{1,0},{2,3},{3,2},{4,5},{5,4},{6,7},{7,6},{8,24},{9,25},{10,... | collective-permute-start | bytes 3145736 | tf_op jit(solution)/shard_map/ppermute | solution.py:319
  752.1 14.8 %collective-permute-start.33 = (bf16[2,32,3072]{2,1,0:T(8,128)(2,1)S(1)}, bf16[2,32,3072]{2,1,0:T(8,128)(2,1)S(1)}, u32[]{:S(2)}, u32[]{:S(2)}) collective-permute-start(bf16[2,32,3072]{2,1,0:T(8,128)(2,1)S(1)} %slice.372), channel_id=1, source_target_pairs={{0,2},{1,3},{2,0},{3,1},{4,6},{5,7},{6,4},{7,5},{8,10},{9,11},{10,... | collective-permute-start | bytes 1179656 | tf_op jit(solution)/shard_map/ppermute | solution.py:319
  754.4 28.1 %collective-permute-start.48 = (bf16[2,128,1024]{2,1,0:T(8,128)(2,1)S(1)}, bf16[2,128,1024]{2,1,0:T(8,128)(2,1)S(1)}, u32[]{:S(2)}, u32[]{:S(2)}) collective-permute-start(bf16[2,128,1024]{2,1,0:T(8,128)(2,1)S(1)} %slice.408), channel_id=1, source_target_pairs={{0,2},{1,3},{2,0},{3,1},{4,6},{5,7},{6,4},{7,5},{8,10},{9,11},{10,... | collective-permute-start | bytes 1572872 | tf_op jit(solution)/shard_map/ppermute | solution.py:319
  765.1 27.1 %collective-permute-start.43 = (bf16[2,32,4096]{2,1,0:T(8,128)(2,1)S(1)}, bf16[2,32,4096]{2,1,0:T(8,128)(2,1)S(1)}, u32[]{:S(2)}, u32[]{:S(2)}) collective-permute-start(bf16[2,32,4096]{2,1,0:T(8,128)(2,1)S(1)} %slice.397), channel_id=1, source_target_pairs={{0,2},{1,3},{2,0},{3,1},{4,6},{5,7},{6,4},{7,5},{8,10},{9,11},{10,... | collective-permute-start | bytes 1572872 | tf_op jit(solution)/shard_map/ppermute | solution.py:319
  767.0 26.1 %collective-permute-start.34 = (bf16[1,32,3072]{2,1,0:T(8,128)(2,1)S(1)}, bf16[1,32,3072]{2,1,0:T(8,128)(2,1)S(1)}, u32[]{:S(2)}, u32[]{:S(2)}) collective-permute-start(bf16[1,32,3072]{2,1,0:T(8,128)(2,1)S(1)} %slice.374), channel_id=1, source_target_pairs={{0,4},{1,5},{2,6},{3,7},{4,0},{5,1},{6,2},{7,3},{8,12},{9,13},{10,... | collective-permute-start | bytes 589832 | tf_op jit(solution)/shard_map/ppermute | solution.py:319
  782.8 22.8 %collective-permute-start.49 = (bf16[1,128,1024]{2,1,0:T(8,128)(2,1)S(1)}, bf16[1,128,1024]{2,1,0:T(8,128)(2,1)S(1)}, u32[]{:S(2)}, u32[]{:S(2)}) collective-permute-start(bf16[1,128,1024]{2,1,0:T(8,128)(2,1)S(1)} %slice.410), channel_id=1, source_target_pairs={{0,4},{1,5},{2,6},{3,7},{4,0},{5,1},{6,2},{7,3},{8,12},{9,13},{10,... | collective-permute-start | bytes 786440 | tf_op jit(solution)/shard_map/ppermute | solution.py:319
  792.3 17.0 %collective-permute-start.44 = (bf16[1,32,4096]{2,1,0:T(8,128)(2,1)S(1)}, bf16[1,32,4096]{2,1,0:T(8,128)(2,1)S(1)}, u32[]{:S(2)}, u32[]{:S(2)}) collective-permute-start(bf16[1,32,4096]{2,1,0:T(8,128)(2,1)S(1)} %slice.399), channel_id=1, source_target_pairs={{0,4},{1,5},{2,6},{3,7},{4,0},{5,1},{6,2},{7,3},{8,12},{9,13},{10,... | collective-permute-start | bytes 786440 | tf_op jit(solution)/shard_map/ppermute | solution.py:319
  (129 other events, 1086.2 us)

commit v3 on v2

v3 whole, which is shorter than its diff:
```python
from functools import partial

import numpy as np
import jax
import jax.numpy as jnp
from jax import lax
from jax.experimental import pallas as pl
from jax.experimental.pallas import tpu as pltpu
from jax.sharding import PartitionSpec as P

EPSILON = 1e-06
HEAD_DIM = 64
LOG2E = 1.4426950408889634
RSQRT_2PI = 0.3989422804014327
TAIL_STEP = 0.305
TAIL_COEFFS = (
    0.12163971608667215,
    0.12246710281167089,
    0.10341891431417467,
    0.12102858688667265,
    -0.03799063399351653,
    0.18573260086829071,
    -0.15299777850455798,
    0.03670153882152772,
)
NT = (((1,), (1,)), ((), ()))
TN = (((0,), (0,)), ((), ()))


def dot(a, b, dims=(((1,), (0,)), ((), ()))):
    return lax.dot_general(a, b, dims, preferred_element_type=jnp.float32)


def whole(shape):
    return pl.BlockSpec(shape, lambda *_: (0,) * len(shape))


def normal_tail(u):
    size = jnp.abs(u)
    t = 1.0 / (1.0 + TAIL_STEP * size)
    bell = jnp.exp(-0.5 * (u * u))
    poly = jnp.full_like(u, TAIL_COEFFS[-1])
    for c in TAIL_COEFFS[-2::-1]:
        poly = poly * t + c
    tail = bell * (t * poly)
    return jnp.where(u < 0, tail, 1.0 - tail), bell


def row_stats(v):
    centre = v - jnp.mean(v, axis=-1, keepdims=True)
    inv = lax.rsqrt(jnp.mean(centre * centre, axis=-1, keepdims=True) + EPSILON)
    return centre * inv, inv


def norm_project(x, gain, shift, weight, bias, tn):
    rows, width = x.shape
    cols = weight.shape[1]

    def body(x_ref, g_ref, s_ref, w_ref, b_ref, a_ref, o_ref):
        @pl.when(pl.program_id(0) == 0)
        def _():
            xhat, _ = row_stats(x_ref[...].astype(jnp.float32))
            a_ref[...] = (xhat * g_ref[...] + s_ref[...]).astype(jnp.bfloat16)

        o_ref[...] = (dot(a_ref[...], w_ref[...]) + b_ref[...]).astype(jnp.bfloat16)

    return pl.pallas_call(
        body,
        grid=(cols // tn,),
        in_specs=[
            whole((rows, width)),
            whole((1, width)),
            whole((1, width)),
            pl.BlockSpec((width, tn), lambda j: (0, j)),
            pl.BlockSpec((1, tn), lambda j: (0, j)),
        ],
        out_specs=[whole((rows, width)), pl.BlockSpec((rows, tn), lambda j: (0, j))],
        out_shape=[
            jax.ShapeDtypeStruct((rows, width), jnp.bfloat16),
            jax.ShapeDtypeStruct((rows, cols), jnp.bfloat16),
        ],
        name="norm_project",
    )(x, gain, shift, weight, bias)


def attention(qkv):
    rows, width = qkv.shape[0], qkv.shape[1] // 3
    pairs = width // (2 * HEAD_DIM)
    span = 2 * HEAD_DIM

    def body(q_ref, k_ref, v_ref, o_ref, l_ref):
        q, k, v = q_ref[...], k_ref[...], v_ref[...]
        lane = lax.broadcasted_iota(jnp.int32, (rows, span), 1)
        outs, logs = [], []
        for h in range(2):
            mine = (lane < HEAD_DIM) if h == 0 else (lane >= HEAD_DIM)
            kh = jnp.where(mine, k, jnp.zeros_like(k))
            s = dot(q, kh, NT) * 0.125
            top = jnp.max(s, axis=-1, keepdims=True)
            e = jnp.exp(s - top)
            total = jnp.sum(e, axis=-1, keepdims=True)
            p = (e * (1.0 / total)).astype(jnp.bfloat16)
            outs.append(dot(p, v))
            logs.append(top + jnp.log(total))
        first = lane < HEAD_DIM
        o_ref[...] = jnp.where(first, outs[0], outs[1]).astype(jnp.bfloat16)
        both = jnp.where(first, logs[0], logs[1])
        turned = both.T
        l_ref[0, 0:1, :] = turned[0:1, :]
        l_ref[0, 1:2, :] = turned[HEAD_DIM : HEAD_DIM + 1, :]

    col = lambda base: pl.BlockSpec((rows, span), lambda j: (0, base + j))
    return pl.pallas_call(
        body,
        grid=(pairs,),
        in_specs=[col(0), col(pairs), col(2 * pairs)],
        out_specs=[col(0), pl.BlockSpec((1, 8, rows), lambda j: (j, 0, 0))],
        out_shape=[
            jax.ShapeDtypeStruct((rows, width), jnp.bfloat16),
            jax.ShapeDtypeStruct((pairs, 8, rows), jnp.float32),
        ],
        name="attention",
    )(qkv, qkv, qkv)


def attention_back(qkv, logs, d_o):
    rows, width = qkv.shape[0], qkv.shape[1] // 3
    pairs = width // (2 * HEAD_DIM)
    span = 2 * HEAD_DIM

    def body(q_ref, k_ref, v_ref, l_ref, do_ref, dq_ref, dk_ref, dv_ref, cq_ref, cv_ref):
        q, k, v, do = q_ref[...], k_ref[...], v_ref[...], do_ref[...]
        lane = lax.broadcasted_iota(jnp.int32, (rows, span), 1)
        dqs, dks, dvs = [], [], []
        for h in range(2):
            mine = (lane < HEAD_DIM) if h == 0 else (lane >= HEAD_DIM)
            kh = jnp.where(mine, k, jnp.zeros_like(k))
            vh = jnp.where(mine, v, jnp.zeros_like(v))
            st = dot(kh, q, NT) * 0.125
            pt = jnp.exp(st - l_ref[0, h : h + 1, :])
            dpt = dot(vh, do, NT)
            w = pt * dpt
            inner = jnp.sum(w, axis=0, keepdims=True)
            dst = (w - pt * inner).astype(jnp.bfloat16)
            dvs.append(dot(pt.astype(jnp.bfloat16), do))
            dks.append(dot(dst, q))
            dqs.append(dot(dst, k, TN))
        first = lane < HEAD_DIM
        dq = (jnp.where(first, dqs[0], dqs[1]) * 0.125).astype(jnp.bfloat16)
        dk = (jnp.where(first, dks[0], dks[1]) * 0.125).astype(jnp.bfloat16)
        dv = jnp.where(first, dvs[0], dvs[1]).astype(jnp.bfloat16)
        dq_ref[...] = dq
        dk_ref[...] = dk
        dv_ref[...] = dv
        cq_ref[...] = jnp.sum(dq.astype(jnp.float32), axis=0, keepdims=True)
        cv_ref[...] = jnp.sum(dv.astype(jnp.float32), axis=0, keepdims=True)

    col = lambda base: pl.BlockSpec((rows, span), lambda j: (0, base + j))
    sums = pl.BlockSpec((1, span), lambda j: (0, j))
    mat = jax.ShapeDtypeStruct((rows, width), jnp.bfloat16)
    vec = jax.ShapeDtypeStruct((1, width), jnp.float32)
    return pl.pallas_call(
        body,
        grid=(pairs,),
        in_specs=[
            col(0),
            col(pairs),
            col(2 * pairs),
            pl.BlockSpec((1, 8, rows), lambda j: (j, 0, 0)),
            col(0),
        ],
        out_specs=[col(0), col(0), col(0), sums, sums],
        out_shape=[mat, mat, mat, vec, vec],
        name="attention_back",
    )(qkv, qkv, qkv, logs, d_o)


def project_norm(o, weight, bias, x, gain, shift):
    rows, width = o.shape
    tm = rows // 2

    def body(o_ref, w_ref, b_ref, x_ref, g_ref, s_ref, x1_ref, a_ref):
        x1 = x_ref[...].astype(jnp.float32) + (dot(o_ref[...], w_ref[...]) + b_ref[...])
        x1_ref[...] = x1
        xhat, _ = row_stats(x1)
        a_ref[...] = (xhat * g_ref[...] + s_ref[...]).astype(jnp.bfloat16)

    rowblk = pl.BlockSpec((tm, width), lambda i: (i, 0))
    vec = whole((1, width))
    return pl.pallas_call(
        body,
        grid=(rows // tm,),
        in_specs=[rowblk, whole((width, width)), vec, rowblk, vec, vec],
        out_specs=[rowblk, rowblk],
        out_shape=[
            jax.ShapeDtypeStruct((rows, width), jnp.float32),
            jax.ShapeDtypeStruct((rows, width), jnp.bfloat16),
        ],
        name="project_norm",
    )(o, weight, bias, x, gain, shift)


def feed_forward(a, up, up_bias, down, down_bias, x1, tf):
    rows, width = a.shape
    hidden = up.shape[1]
    steps = hidden // tf

    def body(a_ref, u_ref, ub_ref, d_ref, db_ref, x_ref, g_ref, gp_ref, y_ref, acc):
        j = pl.program_id(0)
        u = dot(a_ref[...], u_ref[...]) + ub_ref[...]
        phi, bell = normal_tail(u)
        g = (u * phi).astype(jnp.bfloat16)
        g_ref[...] = g
        gp_ref[...] = (phi + (u * RSQRT_2PI) * bell).astype(jnp.bfloat16)

        @pl.when(j == 0)
        def _():
            acc[...] = x_ref[...] + db_ref[...]

        acc[...] += dot(g, d_ref[...])

        @pl.when(j == steps - 1)
        def _():
            y_ref[...] = acc[...].astype(jnp.bfloat16)

    return pl.pallas_call(
        body,
        grid=(steps,),
        in_specs=[
            whole((rows, width)),
            pl.BlockSpec((width, tf), lambda j: (0, j)),
            pl.BlockSpec((1, tf), lambda j: (0, j)),
            pl.BlockSpec((tf, width), lambda j: (j, 0)),
            whole((1, width)),
            whole((rows, width)),
        ],
        out_specs=[
            pl.BlockSpec((rows, tf), lambda j: (0, j)),
            pl.BlockSpec((rows, tf), lambda j: (0, j)),
            whole((rows, width)),
        ],
        out_shape=[
            jax.ShapeDtypeStruct((rows, hidden), jnp.bfloat16),
            jax.ShapeDtypeStruct((rows, hidden), jnp.bfloat16),
            jax.ShapeDtypeStruct((rows, width), jnp.bfloat16),
        ],
        scratch_shapes=[pltpu.VMEM((rows, width), jnp.float32)],
        name="feed_forward",
    )(a, up, up_bias, down, down_bias, x1)


def feed_forward_back(dy, gp, down, up, x1, gain, w_out, tf):
    rows, width = dy.shape
    hidden = gp.shape[1]
    steps = hidden // tf

    def body(
        dy_ref, gp_ref, d_ref, u_ref, x_ref, g_ref, w_ref,
        dm_ref, du_ref, dx_ref, da_ref, do_ref, cdm_ref, cdu_ref, cda_ref, cg_ref, cs_ref, acc,
    ):
        j = pl.program_id(0)

        @pl.when(j == 0)
        def _():
            low = dy_ref[...].astype(jnp.bfloat16)
            dm_ref[...] = low
            cdm_ref[...] = jnp.sum(low.astype(jnp.float32), axis=0, keepdims=True)
            acc[...] = jnp.zeros_like(acc)

        du = (dot(dm_ref[...], d_ref[...], NT) * gp_ref[...].astype(jnp.float32)).astype(jnp.bfloat16)
        du_ref[...] = du
        cdu_ref[...] = jnp.sum(du.astype(jnp.float32), axis=0, keepdims=True)
        acc[...] += dot(du, u_ref[...], NT)

        @pl.when(j == steps - 1)
        def _():
            da2 = acc[...]
            xhat, inv = row_stats(x_ref[...])
            cg_ref[...] = jnp.sum(da2 * xhat, axis=0, keepdims=True)
            cs_ref[...] = jnp.sum(da2, axis=0, keepdims=True)
            t = da2 * g_ref[...]
            m1 = jnp.mean(t, axis=-1, keepdims=True)
            m2 = jnp.mean(t * xhat, axis=-1, keepdims=True)
            dx1 = dy_ref[...] + inv * (t - m1 - xhat * m2)
            dx_ref[...] = dx1
            low = dx1.astype(jnp.bfloat16)
            da_ref[...] = low
            cda_ref[...] = jnp.sum(low.astype(jnp.float32), axis=0, keepdims=True)
            do_ref[...] = dot(low, w_ref[...], NT).astype(jnp.bfloat16)

    full = whole((rows, width))
    vec = whole((1, width))
    f = lambda s, d: jax.ShapeDtypeStruct(s, d)
    return pl.pallas_call(
        body,
        grid=(steps,),
        in_specs=[
            full,
            pl.BlockSpec((rows, tf), lambda j: (0, j)),
            pl.BlockSpec((tf, width), lambda j: (j, 0)),
            pl.BlockSpec((width, tf), lambda j: (0, j)),
            full,
            vec,
            whole((width, width)),
        ],
        out_specs=[
            full,
            pl.BlockSpec((rows, tf), lambda j: (0, j)),
            full,
            full,
            full,
            vec,
            pl.BlockSpec((1, tf), lambda j: (0, j)),
            vec,
            vec,
            vec,
        ],
        out_shape=[
            f((rows, width), jnp.bfloat16),
            f((rows, hidden), jnp.bfloat16),
            f((rows, width), jnp.float32),
            f((rows, width), jnp.bfloat16),
            f((rows, width), jnp.bfloat16),
            f((1, width), jnp.float32),
            f((1, hidden), jnp.float32),
            f((1, width), jnp.float32),
            f((1, width), jnp.float32),
            f((1, width), jnp.float32),
        ],
        scratch_shapes=[pltpu.VMEM((rows, width), jnp.float32)],
        name="feed_forward_back",
    )(dy, gp, down, up, x1, gain, w_out)


def project_back(dq, dk, dv, weight, x, gain, dx1, extra, out_dtype):
    rows, width = dq.shape
    tm = rows // 2
    have = extra is not None

    def body(*refs):
        dq_ref, dk_ref, dv_ref, w_ref, x_ref, g_ref, d_ref = refs[:7]
        out_ref, cg_ref, cs_ref = refs[-3:]
        da = dot(dq_ref[...], w_ref[:, :width], NT)
        da += dot(dk_ref[...], w_ref[:, width : 2 * width], NT)
        da += dot(dv_ref[...], w_ref[:, 2 * width :], NT)
        xhat, inv = row_stats(x_ref[...].astype(jnp.float32))
        cg = jnp.sum(da * xhat, axis=0, keepdims=True)
        cs = jnp.sum(da, axis=0, keepdims=True)

        @pl.when(pl.program_id(0) == 0)
        def _():
            cg_ref[...] = cg
            cs_ref[...] = cs

        @pl.when(pl.program_id(0) > 0)
        def _():
            cg_ref[...] += cg
            cs_ref[...] += cs

        t = da * g_ref[...]
        m1 = jnp.mean(t, axis=-1, keepdims=True)
        m2 = jnp.mean(t * xhat, axis=-1, keepdims=True)
        dx = d_ref[...] + inv * (t - m1 - xhat * m2)
        if have:
            dx = refs[7][...].astype(jnp.float32) * refs[8][...] + dx
        out_ref[...] = dx.astype(out_dtype)

    rowblk = pl.BlockSpec((tm, width), lambda i: (i, 0))
    vec = whole((1, width))
    specs = [rowblk, rowblk, rowblk, whole((width, 3 * width)), rowblk, vec, rowblk]
    args = [dq, dk, dv, weight, x, gain, dx1]
    if have:
        specs += [rowblk, pl.BlockSpec((tm, 1), lambda i: (i, 0))]
        args += list(extra)
    return pl.pallas_call(
        body,
        grid=(rows // tm,),
        in_specs=specs,
        out_specs=[rowblk, vec, vec],
        out_shape=[
            jax.ShapeDtypeStruct((rows, width), out_dtype),
            jax.ShapeDtypeStruct((1, width), jnp.float32),
            jax.ShapeDtypeStruct((1, width), jnp.float32),
        ],
        name="project_back",
    )(*args)


def weight_grad(lefts, rights, tm, tn):
    rows, m = lefts[0].shape
    cols = rights[0].shape[1]
    count = len(lefts)

    def body(*refs):
        a, b, o_ref = refs[:count], refs[count : 2 * count], refs[-1]
        total = dot(a[0][...], b[0][...], TN)
        for x, y in zip(a[1:], b[1:]):
            total += dot(x[...], y[...], TN)
        o_ref[...] = total.astype(jnp.bfloat16)

    return pl.pallas_call(
        body,
        grid=(m // tm, cols // tn),
        in_specs=[pl.BlockSpec((rows, tm), lambda i, j: (0, i))] * count
        + [pl.BlockSpec((rows, tn), lambda i, j: (0, j))] * count,
        out_specs=pl.BlockSpec((tm, tn), lambda i, j: (i, j)),
        out_shape=jax.ShapeDtypeStruct((m, cols), jnp.bfloat16),
        name="weight_grad",
    )(*lefts, *rights)


def vec(v):
    return v.astype(jnp.float32).reshape(1, -1)


def layer_forward(x, w):
    a1, qkv = norm_project(x, w["g1"], w["s1"], w["qkv"], w["bqkv"], 512)
    o, logs = attention(qkv)
    x1, a2 = project_norm(o, w["out"], w["bo"], x, w["g2"], w["s2"])
    g, gp, y = feed_forward(a2, w["up"], w["bu"], w["down"], w["bd"], x1, 512)
    return y, (x, a1, qkv, logs, o, x1, a2, g, gp)


def layer_back(dy, saved, w, extra, out_dtype):
    x, a1, qkv, logs, o, x1, a2, g, gp = saved
    dm, du, dx1, da, do, cdm, cdu, cda, cg2, cs2 = feed_forward_back(
        dy, gp, w["down"], w["up"], x1, w["g2"], w["out"], 512
    )
    dq, dk, dv, cq, cv = attention_back(qkv, logs, do)
    dx, cg1, cs1 = project_back(dq, dk, dv, w["qkv"], x, w["g1"], dx1, extra, out_dtype)
    return dx, (dm, du, da, dq, dk, dv), (cg1, cs1, cq, cv, cda, cg2, cs2, cdm, cdu)


def bits_of(ndp, nfs):
    core = nfs
    outer = [nfs << i for i in range(1, ndp.bit_length() - 1)]
    inner = [1 << i for i in range(nfs.bit_length() - 1)]
    return core, outer, inner


def stage_orders(ndp, nfs):
    core, outer, inner = bits_of(ndp, nfs)
    first, second = outer[0], inner[0]
    tail = outer[1:] + inner[1:]
    return core, ([first, second] + tail, [second, first] + tail)


def shard_table(ndp, nfs):
    n = ndp * nfs
    core, orders = stage_orders(ndp, nfs)
    table = np.zeros((n, n), np.int32)
    for me in range(n):
        for p in range(n):
            rel = core if p >= n // 2 else 0
            owner = 1 if (me ^ rel) & core else 0
            for i, mask in enumerate(orders[owner]):
                if p & (n >> (i + 2)):
                    rel ^= mask
            table[me, p] = me ^ rel
    return table


def stage_perms(ndp, nfs):
    n = ndp * nfs
    core, orders = stage_orders(ndp, nfs)
    perms = [[(i, i ^ core) for i in range(n)]]
    for a, b in zip(*orders):
        perms.append([(i, i ^ (b if i & core else a)) for i in range(n)])
    return perms


def place_blocks(pieces, table_row, scatter):
    n = pieces[0].shape[0]

    def body(t_ref, *refs):
        ins, outs, sem = refs[: len(pieces)], refs[len(pieces) : -1], refs[-1]
        copies = []
        for src, dst in zip(ins, outs):
            for i in range(n):
                j = t_ref[i]
                s, d = (i, j) if scatter else (j, i)
                copies.append(pltpu.make_async_copy(src.at[s], dst.at[d], sem))
        for c in copies:
            c.start()
        for c in copies:
            c.wait()

    return pl.pallas_call(
        body,
        out_shape=[jax.ShapeDtypeStruct(p.shape, p.dtype) for p in pieces],
        grid_spec=pltpu.PrefetchScalarGridSpec(
            num_scalar_prefetch=1,
            in_specs=[pl.BlockSpec(memory_space=pl.ANY)] * len(pieces),
            out_specs=[pl.BlockSpec(memory_space=pltpu.VMEM)] * len(pieces),
            scratch_shapes=[pltpu.SemaphoreType.DMA],
        ),
        name="place",
    )(table_row, *pieces)


AXES = ("dp", "fsdp")


def gather_relative(shard, perms):
    cur = shard[None]
    for perm in perms[:0:-1]:
        cur = jnp.concatenate([cur, lax.ppermute(cur, AXES, perm)], axis=0)
    return jnp.concatenate([cur, lax.ppermute(cur, AXES, perms[0])], axis=0)


def reduce_relative(rel, perms, wide=jnp.bfloat16):
    cur = rel
    for i, perm in enumerate(perms):
        half = cur.shape[0] // 2
        got = lax.ppermute(cur[half:], AXES, perm)
        total = cur[:half].astype(jnp.float32) + got.astype(jnp.float32)
        cur = total if i == len(perms) - 1 else total.astype(wide)
    return cur[0]


def per_device(ndp, nfs,
    tokens,
    ln1_gain,
    ln1_bias,
    w_qkv,
    bias_q,
    bias_v,
    w_out,
    bias_out,
    ln2_gain,
    ln2_bias,
    w_up,
    bias_up,
    w_down,
    bias_down,
    cot_first,
    cot_second,
    valid,
):
    n = ndp * nfs
    perms = stage_perms(ndp, nfs)
    me = lax.axis_index("dp") * nfs + lax.axis_index("fsdp")
    row = lax.dynamic_slice(jnp.asarray(shard_table(ndp, nfs)), (me, 0), (1, n))[0]
    vectors = (ln1_gain, ln1_bias, bias_q, bias_v, bias_out, ln2_gain, ln2_bias, bias_down, bias_up)
    sizes = [v.shape[0] for v in vectors]
    width = -(-sum(sizes) // 128) * 128
    packed = jnp.pad(jnp.concatenate(vectors), (0, width - sum(sizes)))[None]
    got_small = gather_relative(packed, perms)
    got_qkv = gather_relative(w_qkv, perms)
    got_out = gather_relative(w_out, perms)
    got_up = gather_relative(w_up, perms)
    got_down = gather_relative(w_down, perms)
    full_small = jnp.zeros_like(got_small).at[row].set(got_small)[:, 0]
    parts = []
    offset = 0
    for size in sizes:
        parts.append(vec(full_small[:, offset : offset + size]))
        offset += size
    g1, s1, bq, bv, bo, g2, s2, bd, bu = parts
    flat = lambda got: place_blocks([got], row, True)[0].reshape(-1, got.shape[-1])
    w = dict(g1=g1, s1=s1, bo=bo, g2=g2, s2=s2, bd=bd, bu=bu)
    w["bqkv"] = jnp.concatenate([bq, jnp.zeros_like(bq), bv], axis=1)
    w["qkv"] = flat(got_qkv)
    w["out"] = flat(got_out)
    w["up"] = flat(got_up)
    w["down"] = flat(got_down)
    first, saved_first = layer_forward(tokens[0], w)
    second, saved_second = layer_forward(first, w)
    keep_mask = valid[0].astype(jnp.float32)[:, None]
    grad_second = cot_second[0].astype(jnp.float32) * keep_mask
    grad_first, mats_second, sums_second = layer_back(
        grad_second, saved_second, w, (cot_first[0], keep_mask), jnp.float32
    )
    grad_inputs, mats_first, sums_first = layer_back(
        grad_first, saved_first, w, None, jnp.bfloat16
    )
    dm, du, da, dq, dk, dv = zip(mats_first, mats_second)
    saved = list(zip(saved_first, saved_second))

    def reduce_matrix(total):
        (rel,) = place_blocks([total.reshape(n, total.shape[0] // n, total.shape[1])], row, False)
        return reduce_relative(rel, perms)

    d_down = reduce_matrix(weight_grad(saved[7], dm, 512, 512))
    d_up = reduce_matrix(weight_grad(saved[6], du, 512, 512))
    d_out = reduce_matrix(weight_grad(saved[4], da, 512, 512))
    d_qkv = reduce_matrix(
        jnp.concatenate([weight_grad(saved[1], d, 512, 512) for d in (dq, dk, dv)], axis=1)
    )
    small = jnp.concatenate(
        [(a + b).reshape(n, -1) for a, b in zip(sums_first, sums_second)], axis=1
    )
    small = jnp.pad(small, ((0, 0), (0, width - small.shape[1])))[:, None]
    small = reduce_relative(small[row], perms, jnp.float32)[0]
    outs = []
    offset = 0
    for size in sizes:
        outs.append(small[offset : offset + size])
        offset += size
    o_g1, o_s1, o_bq, o_bv, o_bo, o_g2, o_s2, o_bd, o_bu = outs
    return (
        first[None],
        second[None],
        grad_inputs[None],
        o_g1,
        o_s1,
        d_qkv,
        o_bq,
        o_bv,
        d_out,
        o_bo,
        o_g2,
        o_s2,
        d_up,
        o_bu,
        d_down,
        o_bd,
    )


def solution(mesh):
    ndp, nfs = mesh.shape["dp"], mesh.shape["fsdp"]
    return jax.shard_map(
        partial(per_device, ndp, nfs),
        mesh=mesh,
        in_specs=(
            P(("dp", "fsdp"), None, None),
            P(("dp", "fsdp")),
            P(("dp", "fsdp")),
            P(("dp", "fsdp"), None),
            P(("dp", "fsdp")),
            P(("dp", "fsdp")),
            P(("dp", "fsdp"), None),
            P(("dp", "fsdp")),
            P(("dp", "fsdp")),
            P(("dp", "fsdp")),
            P(("dp", "fsdp"), None),
            P(("dp", "fsdp")),
            P(("dp", "fsdp"), None),
            P(("dp", "fsdp")),
            P(("dp", "fsdp"), None, None),
            P(("dp", "fsdp"), None, None),
            P(("dp", "fsdp"), None),
        ),
        out_specs=(
            P(("dp", "fsdp"), None, None),
            P(("dp", "fsdp"), None, None),
            P(("dp", "fsdp"), None, None),
            P(("dp", "fsdp")),
            P(("dp", "fsdp")),
            P(("dp", "fsdp"), None),
            P(("dp", "fsdp")),
            P(("dp", "fsdp")),
            P(("dp", "fsdp"), None),
            P(("dp", "fsdp")),
            P(("dp", "fsdp")),
            P(("dp", "fsdp")),
            P(("dp", "fsdp"), None),
            P(("dp", "fsdp")),
            P(("dp", "fsdp"), None),
            P(("dp", "fsdp")),
        ),
        check_vma=False,
    )
```

time: 817 us -> 719 us (0.88)
  matrix products: 325 us -> 0 us
  Pallas kernels: 49.2 us -> 314 us
  other arithmetic: 83.2 us -> 41.1 us
  local copies, waits for them, and re-layouts: 99.2 us -> 82.3 us
  waiting for transfers between devices: 191 us -> 207 us
    dot_general x36 -> x0, matrix products: 325 us -> none  [the longest x2 55.7 us: forward_pass(): jnp.dot(normed_two, weight_up, preferred_element_type=jnp.float32)]
    pallas_call x0 -> x20, Pallas kernels: none -> 266 us  [the longest x6 67.4 us: weight_grad(): pl.pallas_call(body, grid=(m // tm, cols // tn), in_specs=[pl.BlockSpec((...]
    reduce_sum x15 -> x0, other arithmetic: 31.4 us -> none  [the longest x2 17.3 us: attend_block(): total = jnp.sum(shifted, axis=-1, keepdims=True)]
    ppermute x20, waiting for transfers between devices: 79.4 us -> 106 us  [gather_relative(): cur = jnp.concatenate([cur, lax.ppermute(cur, AXES, perm)], axis=0)]
    convert_element_type x6 -> x0, other arithmetic: 20.2 us -> none  [the longest x2 16.4 us: attend_back(): grad_scores = (attn_probs * (grad_probs - inner_sum)).astype(jnp.bfloat16)]
    unnamed x302 -> x94, local copies, waits for them, and re-layouts: 31.4 us -> 19.7 us
    ppermute x25, waiting for transfers between devices: 111 us -> 101 us  [reduce_relative(): got = lax.ppermute(cur[half:], AXES, perm)]
    convert_element_type x14 -> x1, local copies, waits for them, and re-layouts: 9.82 us -> 1.53 us  [per_device(): keep_mask = valid[0].astype(jnp.float32)[:, None]]
  transfers between devices with their start and end apart: 50 -> 50, of which waited for: 20 -> 19; matrix products, arithmetic and copies ran while one was open for 23% -> 14% of each run, Pallas kernels for 4% -> 17%
where the time goes in v3:
time: 719 us; the launch traced here: 710 us
  Pallas kernels  314 us (44%)
  waiting for transfers between devices  207 us (29%)
  local copies, waits for them, and re-layouts  82.3 us (11%)
  starting transfers between devices  63.5 us (9%)
  other arithmetic  41.1 us (6%)
    ppermute x20, waiting for transfers between devices, gather_relative(): cur = jnp.concatenate([cur, lax.ppermute(cur, AXES, perm)], axis=0)  106 us
    ppermute x25, waiting for transfers between devices, reduce_relative(): got = lax.ppermute(cur[half:], AXES, perm)  101 us
    pallas_call x6, Pallas kernels, weight_grad(): pl.pallas_call(body, grid=(m // tm, cols // tn), in_specs=[pl.BlockSpec((...  67.4 us
    pallas_call x8, Pallas kernels, place_blocks(): pl.pallas_call(body, out_shape=[jax.ShapeDtypeStruct(p.shape, p.dtype) fo...  48.8 us
    pallas_call x2, Pallas kernels, feed_forward(): pl.pallas_call(body, grid=(steps,), in_specs=[whole((rows, width)), pl.Bl...  47.7 us
    pallas_call x2, Pallas kernels, feed_forward_back(): pl.pallas_call(body, grid=(steps,), in_specs=[full, pl.BlockSpec((rows, t...  43.9 us
    pallas_call x2, Pallas kernels, attention_back(): pl.pallas_call(body, grid=(pairs,), in_specs=[col(0), col(pairs), col(2 *...  32.1 us
    ppermute x25, starting transfers between devices, reduce_relative(): got = lax.ppermute(cur[half:], AXES, perm)  30.1 us
  transfers between devices with their start and end apart: 50, of which 19 were waited for; matrix products, arithmetic and copies ran while one was open for 14% of the time, Pallas kernels for 17%

profile of v3, /device:TPU:0, one launch (start us, length us, event | category | flops | bytes accessed | tf_op | source)
XLA Modules:
  0.0 710.5 jit_solution(1876805348423245945)
XLA Ops:
  0.7 6.1 concatenate.107
  6.8 4.1 collective-permute-start
  11.0 2.8 collective-permute-start.10
  13.9 2.8 collective-permute-start.20
  23.1 20.3 %collective-permute-done.15 = bf16[1,32,4096]{2,1,0:T(8,128)(2,1)S(1)} collective-permute-done((bf16[1,32,4096]{2,1,0:T(8,128)(2,1)}, bf16[1,32,4096]{2,1,0:T(8,128)(2,1)S(1)}, u32[]{:S(2)}, u32[]{:S(2)}) %collective-permute-start.15) | collective-permute-done | bytes 262176 | tf_op jit(solution)/shard_map/ppermute | solution.py:507
  48.4 10.9 %collective-permute-done.16 = bf16[2,32,4096]{2,1,0:T(8,128)(2,1)S(1)} collective-permute-done((bf16[2,32,4096]{2,1,0:T(8,128)(2,1)S(1)}, bf16[2,32,4096]{2,1,0:T(8,128)(2,1)S(1)}, u32[]{:S(2)}, u32[]{:S(2)}) %collective-permute-start.16) | collective-permute-done | bytes 524320 | tf_op jit(solution)/shard_map/ppermute | solution.py:507
  62.5 5.2 collective-permute-done.6
  69.4 9.4 %collective-permute-done.21 = bf16[2,128,1024]{2,1,0:T(8,128)(2,1)S(1)} collective-permute-done((bf16[2,128,1024]{2,1,0:T(8,128)(2,1)S(1)}, bf16[2,128,1024]{2,1,0:T(8,128)(2,1)S(1)}, u32[]{:S(2)}, u32[]{:S(2)}) %collective-permute-start.21) | collective-permute-done | bytes 524320 | tf_op jit(solution)/shard_map/ppermute | solution.py:507
  84.0 20.0 %collective-permute-done.22 = bf16[4,128,1024]{2,1,0:T(8,128)(2,1)S(1)} collective-permute-done((bf16[4,128,1024]{2,1,0:T(8,128)(2,1)S(1)}, bf16[4,128,1024]{2,1,0:T(8,128)(2,1)S(1)}, u32[]{:S(2)}, u32[]{:S(2)}) %collective-permute-start.22) | collective-permute-done | bytes 1048608 | tf_op jit(solution)/shard_map/ppermute | solution.py:507
  104.2 2.5 collective-permute-start.23
  111.5 3.6 collective-permute-done.18
  118.3 19.3 %collective-permute-done.23 = bf16[8,128,1024]{2,1,0:T(8,128)(2,1)S(1)} collective-permute-done((bf16[8,128,1024]{2,1,0:T(8,128)(2,1)S(1)}, bf16[8,128,1024]{2,1,0:T(8,128)(2,1)S(1)}, u32[]{:S(2)}, u32[]{:S(2)}) %collective-permute-start.23) | collective-permute-done | bytes 2097184 | tf_op jit(solution)/shard_map/ppermute | solution.py:507
  140.9 13.6 %collective-permute-done.8 = bf16[8,32,3072]{2,1,0:T(8,128)(2,1)S(1)} collective-permute-done((bf16[8,32,3072]{2,1,0:T(8,128)(2,1)S(1)}, bf16[8,32,3072]{2,1,0:T(8,128)(2,1)S(1)}, u32[]{:S(2)}, u32[]{:S(2)}) %collective-permute-start.8) | collective-permute-done | bytes 1572896 | tf_op jit(solution)/shard_map/ppermute | solution.py:507
  169.7 2.9 collective-permute-done.12
  181.7 3.9 concatenate.112
  199.8 2.3 constant_dynamic-update-slice_fusion.16.refs_0_
  202.1 3.6 place.9
  207.7 6.1 place.8
  213.8 9.6 %norm_project.2 = (bf16[512,1024]{1,0:T(8,128)(2,1)}, bf16[512,3072]{1,0:T(8,128)(2,1)}) custom-call(bf16[512,1024]{1,0:T(8,128)(2,1)} %bitcast.98, f32[1,1024]{1,0:T(1,128)} %reshape.218.g_ref.refs_5_, f32[1,1024]{1,0:T(1,128)} %reshape.220.s_ref, bf16[1024,3072]{1,0:T(8,128)(2,1)} %bitcast.83, f32[1,3072]{1,0:T(1,128)} %pad_maximum_fusion.13.b_ref), custom_call_target="tpu_custom_call" | custom-call | tf_op jit(solution)/shard_map/norm_project/pallas_call | solution.py:67
  223.4 12.8 %attention.2 = (bf16[512,1024]{1,0:T(8,128)(2,1)}, f32[8,8,512]{2,1,0:T(8,128)}) custom-call(bf16[512,3072]{1,0:T(8,128)(2,1)} %get-tuple-element.70.q_ref.k_ref.v_ref, bf16[512,3072]{1,0:T(8,128)(2,1)} %get-tuple-element.70.q_ref.k_ref.v_ref, bf16[512,3072]{1,0:T(8,128)(2,1)} %get-tuple-element.70.q_ref.k_ref.v_ref), custom_call_target="tpu_custom_call" | custom-call | tf_op jit(solution)/shard_map/attention/pallas_call | solution.py:113
  236.2 4.9 project_norm.2
  241.1 4.7 constant_dynamic-update-slice_fusion.27.refs_0_
  245.7 7.4 %place.10 = bf16[32,32,4096]{2,1,0:T(8,128)(2,1)} custom-call(s32[32]{0:T(128)} %dynamic-slice_bitcast_fusion.t_ref, bf16[32,32,4096]{2,1,0:T(8,128)(2,1)} %constant_dynamic-update-slice_fusion.27.refs_0_), custom_call_target="tpu_custom_call" | custom-call | tf_op jit(solution)/shard_map/place/pallas_call | solution.py:488
  253.1 4.8 constant_dynamic-update-slice_fusion.38.refs_0_
  257.9 7.3 %place.11 = bf16[32,128,1024]{2,1,0:T(8,128)(2,1)} custom-call(s32[32]{0:T(128)} %dynamic-slice_bitcast_fusion.t_ref, bf16[32,128,1024]{2,1,0:T(8,128)(2,1)} %constant_dynamic-update-slice_fusion.38.refs_0_), custom_call_target="tpu_custom_call" | custom-call | tf_op jit(solution)/shard_map/place/pallas_call | solution.py:488
  265.2 23.9 %feed_forward.2 = (bf16[512,4096]{1,0:T(8,128)(2,1)}, bf16[512,4096]{1,0:T(8,128)(2,1)}, bf16[512,1024]{1,0:T(8,128)(2,1)}) custom-call(bf16[512,1024]{1,0:T(8,128)(2,1)} %get-tuple-element.72.a_ref.refs_0_, bf16[1024,4096]{1,0:T(8,128)(2,1)} %bitcast.75, f32[1,4096]{1,0:T(1,128)} %bitcast.120, bf16[4096,1024]{1,0:T(8,128)(2,1)} %bitcast.79, ...), custom_call_target="tpu_custom_call" | custom-call | tf_op jit(solution)/shard_map/feed_forward/pallas_call | solution.py:226
  289.1 9.1 %norm_project.3 = (bf16[512,1024]{1,0:T(8,128)(2,1)}, bf16[512,3072]{1,0:T(8,128)(2,1)}) custom-call(bf16[512,1024]{1,0:T(8,128)(2,1)} %get-tuple-element.74.x_ref.refs_4_, f32[1,1024]{1,0:T(1,128)} %reshape.218.g_ref.refs_5_, f32[1,1024]{1,0:T(1,128)} %reshape.220.s_ref, bf16[1024,3072]{1,0:T(8,128)(2,1)} %bitcast.84, f32[1,3072]{1,0:T(1,128)} %pad_maximum_fusion.13.b_ref), custom_call_target="tpu_custom_call" | custom-call | tf_op jit(solution)/shard_map/norm_project/pallas_call | solution.py:67
  298.2 12.8 %attention.3 = (bf16[512,1024]{1,0:T(8,128)(2,1)}, f32[8,8,512]{2,1,0:T(8,128)}) custom-call(bf16[512,3072]{1,0:T(8,128)(2,1)} %get-tuple-element.75.q_ref.k_ref.v_ref, bf16[512,3072]{1,0:T(8,128)(2,1)} %get-tuple-element.75.q_ref.k_ref.v_ref, bf16[512,3072]{1,0:T(8,128)(2,1)} %get-tuple-element.75.q_ref.k_ref.v_ref), custom_call_target="tpu_custom_call" | custom-call | tf_op jit(solution)/shard_map/attention/pallas_call | solution.py:113
  310.9 4.9 project_norm.3
  315.8 23.8 %feed_forward.3 = (bf16[512,4096]{1,0:T(8,128)(2,1)}, bf16[512,4096]{1,0:T(8,128)(2,1)}, bf16[512,1024]{1,0:T(8,128)(2,1)}) custom-call(bf16[512,1024]{1,0:T(8,128)(2,1)} %get-tuple-element.77.a_ref.refs_1_, bf16[1024,4096]{1,0:T(8,128)(2,1)} %bitcast.76, f32[1,4096]{1,0:T(1,128)} %bitcast.121, bf16[4096,1024]{1,0:T(8,128)(2,1)} %bitcast.80, ...), custom_call_target="tpu_custom_call" | custom-call | tf_op jit(solution)/shard_map/feed_forward/pallas_call | solution.py:226
  339.6 22.1 %feed_forward_back.2 = (bf16[512,1024]{1,0:T(8,128)(2,1)}, bf16[512,4096]{1,0:T(8,128)(2,1)}, f32[512,1024]{1,0:T(8,128)}, bf16[512,1024]{1,0:T(8,128)(2,1)}, bf...) custom-call(f32[512,1024]{1,0:T(8,128)} %convert_multiply_fusion.dy_, ...), custom_call_target="tpu_custom_call" | custom-call | tf_op jit(solution)/shard_map/feed_forward_back/pallas_call | solution.py:294
  361.7 15.9 %attention_back.2 = (bf16[512,1024]{1,0:T(8,128)(2,1)}, bf16[512,1024]{1,0:T(8,128)(2,1)}, bf16[512,1024]{1,0:T(8,128)(2,1)}, f32[1,1024]{1,0:T(1,128)}, f32[1,1024]{1,0:T(1,128)}) custom-call(bf16[512,3072]{1,0:T(8,128)(2,1)} %get-tuple-element.75.q_ref.k_ref.v_ref, bf16[512,3072]{1,0:T(8,128)(2,1)} %get-tuple-element.75.q_ref.k_ref.v_ref, ...), custom_call_target="tpu_custom_call" | custom-call | tf_op jit(solution)/shard_map/attention_back/pallas_call | solution.py:162
  377.6 10.6 %project_back.2 = (f32[512,1024]{1,0:T(8,128)}, f32[1,1024]{1,0:T(1,128)}, f32[1,1024]{1,0:T(1,128)}) custom-call(bf16[512,1024]{1,0:T(8,128)(2,1)} %get-tuple-element.84.refs_0_.refs_3_, bf16[512,1024]{1,0:T(8,128)(2,1)} %get-tuple-element.85.refs_1_.refs_3_, bf16[512,1024]{1,0:T(8,128)(2,1)} %get-tuple-element.86.refs_2_.refs_3_, ...), custom_call_target="tpu_custom_call" | custom-call | tf_op jit(solution)/shard_map/project_back/pallas_call | solution.py:375
  388.2 21.9 %feed_forward_back.3 = (bf16[512,1024]{1,0:T(8,128)(2,1)}, bf16[512,4096]{1,0:T(8,128)(2,1)}, f32[512,1024]{1,0:T(8,128)}, bf16[512,1024]{1,0:T(8,128)(2,1)}, bf...) custom-call(f32[512,1024]{1,0:T(8,128)} %get-tuple-element.88.dy_ref, ...), custom_call_target="tpu_custom_call" | custom-call | tf_op jit(solution)/shard_map/feed_forward_back/pallas_call | solution.py:294
  410.1 16.2 %attention_back.3 = (bf16[512,1024]{1,0:T(8,128)(2,1)}, bf16[512,1024]{1,0:T(8,128)(2,1)}, bf16[512,1024]{1,0:T(8,128)(2,1)}, f32[1,1024]{1,0:T(1,128)}, f32[1,1024]{1,0:T(1,128)}) custom-call(bf16[512,3072]{1,0:T(8,128)(2,1)} %get-tuple-element.70.q_ref.k_ref.v_ref, bf16[512,3072]{1,0:T(8,128)(2,1)} %get-tuple-element.70.q_ref.k_ref.v_ref, ...), custom_call_target="tpu_custom_call" | custom-call | tf_op jit(solution)/shard_map/attention_back/pallas_call | solution.py:162
  426.3 6.4 weight_grad.8
  432.7 6.4 weight_grad.7
  439.1 6.6 weight_grad.6
  445.7 5.4 pad_maximum_fusion
  451.1 6.2 place.12
  457.2 3.8 slice.334
  461.0 6.4 weight_grad.9
  467.4 3.5 place.13
  471.0 2.3 slice.346
  473.8 19.5 %weight_grad.10 = bf16[1024,4096]{1,0:T(8,128)(2,1)} custom-call(bf16[512,1024]{1,0:T(8,128)(2,1)} %get-tuple-element.72.a_ref.refs_0_, bf16[512,1024]{1,0:T(8,128)(2,1)} %get-tuple-element.77.a_ref.refs_1_, bf16[512,4096]{1,0:T(8,128)(2,1)} %get-tuple-element.118.refs_2_, bf16[512,4096]{1,0:T(8,128)(2,1)} %get-tuple-element.119.refs_3_), custom_call_target="tpu_custom_call" | custom-call | tf_op jit(solution)/shard_map/weight_grad/pallas_call | solution.py:401
  493.3 7.4 %place.14 = bf16[32,32,4096]{2,1,0:T(8,128)(2,1)} custom-call(s32[32]{0:T(128)} %dynamic-slice_bitcast_fusion.t_ref, bf16[32,32,4096]{2,1,0:T(8,128)(2,1)} %bitcast.96), custom_call_target="tpu_custom_call" | custom-call | tf_op jit(solution)/shard_map/place/pallas_call | solution.py:488
  500.7 4.6 slice.359
  505.5 9.8 %project_back.3 = (bf16[512,1024]{1,0:T(8,128)(2,1)}, f32[1,1024]{1,0:T(1,128)}, f32[1,1024]{1,0:T(1,128)}) custom-call(bf16[512,1024]{1,0:T(8,128)(2,1)} %get-tuple-element.91.refs_0_.refs_2_, bf16[512,1024]{1,0:T(8,128)(2,1)} %get-tuple-element.92.refs_1_.refs_2_, bf16[512,1024]{1,0:T(8,128)(2,1)} %get-tuple-element.93.refs_2_, ...), custom_call_target="tpu_custom_call" | custom-call | tf_op jit(solution)/shard_map/project_back/pallas_call | solution.py:375
  520.8 7.2 %collective-permute-done.26 = f32[8,1,384]{2,0,1:T(8,128)S(1)} collective-permute-done((f32[8,1,384]{2,0,1:T(8,128)S(1)}, f32[8,1,384]{2,0,1:T(8,128)S(1)}, u32[]{:S(2)}, u32[]{:S(2)}) %collective-permute-start.26) | collective-permute-done | bytes 12320 | tf_op jit(solution)/shard_map/ppermute | solution.py:515
  537.0 22.1 %weight_grad.11 = bf16[4096,1024]{1,0:T(8,128)(2,1)} custom-call(bf16[512,4096]{1,0:T(8,128)(2,1)} %get-tuple-element.120.refs_0_, bf16[512,4096]{1,0:T(8,128)(2,1)} %get-tuple-element.121.refs_1_, bf16[512,1024]{1,0:T(8,128)(2,1)} %get-tuple-element.122.refs_2_, bf16[512,1024]{1,0:T(8,128)(2,1)} %get-tuple-element.123.refs_3_), custom_call_target="tpu_custom_call" | custom-call | tf_op jit(solution)/shard_map/weight_grad/pallas_call | solution.py:401
  559.1 7.3 %place.15 = bf16[32,128,1024]{2,1,0:T(8,128)(2,1)} custom-call(s32[32]{0:T(128)} %dynamic-slice_bitcast_fusion.t_ref, bf16[32,128,1024]{2,1,0:T(8,128)(2,1)} %bitcast.95), custom_call_target="tpu_custom_call" | custom-call | tf_op jit(solution)/shard_map/place/pallas_call | solution.py:488
  566.4 5.0 slice.370
  572.0 4.2 add_convert_fusion.2
  579.1 2.7 collective-permute-start.39
  581.8 3.7 add_convert_fusion.1
  588.3 8.6 %collective-permute-done.31 = bf16[8,32,3072]{2,1,0:T(8,128)(2,1)} collective-permute-done((bf16[8,32,3072]{2,1,0:T(8,128)(2,1)S(1)}, bf16[8,32,3072]{2,1,0:T(8,128)(2,1)}, u32[]{:S(2)}, u32[]{:S(2)}) %collective-permute-start.31) | collective-permute-done | bytes 1572896 | tf_op jit(solution)/shard_map/ppermute | solution.py:515
  602.6 4.3 add_convert_fusion
  607.8 11.8 %collective-permute-done.32 = bf16[4,32,3072]{2,1,0:T(8,128)(2,1)S(1)} collective-permute-done((bf16[4,32,3072]{2,1,0:T(8,128)(2,1)S(1)}, bf16[4,32,3072]{2,1,0:T(8,128)(2,1)S(1)}, u32[]{:S(2)}, u32[]{:S(2)}) %collective-permute-start.32) | collective-permute-done | bytes 786464 | tf_op jit(solution)/shard_map/ppermute | solution.py:515
  621.4 6.4 collective-permute-done.41
  630.5 2.7 collective-permute-start.34
  633.2 28.2 %collective-permute-done.46 = bf16[8,128,1024]{2,1,0:T(8,128)(2,1)S(1)} collective-permute-done((bf16[8,128,1024]{2,1,0:T(8,128)(2,1)S(1)}, bf16[8,128,1024]{2,1,0:T(8,128)(2,1)S(1)}, u32[]{:S(2)}, u32[]{:S(2)}) %collective-permute-start.46) | collective-permute-done | bytes 2097184 | tf_op jit(solution)/shard_map/ppermute | solution.py:515
  666.7 10.6 %collective-permute-done.47 = bf16[4,128,1024]{2,1,0:T(8,128)(2,1)S(1)} collective-permute-done((bf16[4,128,1024]{2,1,0:T(8,128)(2,1)S(1)}, bf16[4,128,1024]{2,1,0:T(8,128)(2,1)S(1)}, u32[]{:S(2)}, u32[]{:S(2)}) %collective-permute-start.47) | collective-permute-done | bytes 1048608 | tf_op jit(solution)/shard_map/ppermute | solution.py:515
  681.2 14.6 %collective-permute-done.48 = bf16[2,128,1024]{2,1,0:T(8,128)(2,1)S(1)} collective-permute-done((bf16[2,128,1024]{2,1,0:T(8,128)(2,1)S(1)}, bf16[2,128,1024]{2,1,0:T(8,128)(2,1)S(1)}, u32[]{:S(2)}, u32[]{:S(2)}) %collective-permute-start.48) | collective-permute-done | bytes 524320 | tf_op jit(solution)/shard_map/ppermute | solution.py:515
  697.6 11.6 %collective-permute-done.49 = bf16[1,128,1024]{2,1,0:T(8,128)(2,1)S(1)} collective-permute-done((bf16[1,128,1024]{2,1,0:T(8,128)(2,1)S(1)}, bf16[1,128,1024]{2,1,0:T(8,128)(2,1)S(1)}, u32[]{:S(2)}, u32[]{:S(2)}) %collective-permute-start.49) | collective-permute-done | bytes 262176 | tf_op jit(solution)/shard_map/ppermute | solution.py:515
  (275 shorter events, 117.0 us)
Async XLA Ops:
  0.6 58.6 %copy-start.7 = (bf16[32,4096]{1,0:T(8,128)(2,1)S(1)}, bf16[32,4096]{1,0:T(8,128)(2,1)}, u32[]{:S(2)}) copy-start(bf16[32,4096]{1,0:T(8,128)(2,1)} %param.28) | copy-start | bytes 786436
  0.7 47.6 %copy-start.8 = (bf16[128,1024]{1,0:T(8,128)(2,1)S(1)}, bf16[128,1024]{1,0:T(8,128)(2,1)}, u32[]{:S(2)}) copy-start(bf16[128,1024]{1,0:T(8,128)(2,1)} %param.30) | copy-start | bytes 786436
  6.8 151.9 %collective-permute-start = (bf16[1,1,384]{2,0,1:T(2,128)(2,1)S(1)}, bf16[1,1,384]{2,0,1:T(2,128)(2,1)S(1)}, u32[]{:S(2)}, u32[]{:S(2)}) collective-permute-start(bf16[1,1,384]{2,0,1:T(2,128)(2,1)S(1)} %broadcast_in_dim_broadcast_in_dim.3), channel_id=1, source_target_pairs={{0,4},{1,5},{2,6},{3,7},{4,0},{5,1},{6,2},{7,3},{8,12},{9,13},{10,... | collective-permute-start | bytes 2312 | tf_op jit(solution)/shard_map/ppermute | solution.py:507
  10.9 33.6 %collective-permute-start.5 = (bf16[1,32,3072]{2,1,0:T(8,128)(2,1)}, bf16[1,32,3072]{2,1,0:T(8,128)(2,1)S(1)}, u32[]{:S(2)}, u32[]{:S(2)}) collective-permute-start(bf16[1,32,3072]{2,1,0:T(8,128)(2,1)} %bitcast.111), channel_id=1, source_target_pairs={{0,4},{1,5},{2,6},{3,7},{4,0},{5,1},{6,2},{7,3},{8,12},{9,13},{10,... | collective-permute-start | bytes 589832 | tf_op jit(solution)/shard_map/ppermute | solution.py:507
  11.0 147.8 %collective-permute-start.10 = (bf16[1,32,1024]{2,1,0:T(8,128)(2,1)}, bf16[1,32,1024]{2,1,0:T(8,128)(2,1)S(1)}, u32[]{:S(2)}, u32[]{:S(2)}) collective-permute-start(bf16[1,32,1024]{2,1,0:T(8,128)(2,1)} %bitcast.116), channel_id=1, source_target_pairs={{0,4},{1,5},{2,6},{3,7},{4,0},{5,1},{6,2},{7,3},{8,12},{9,13},{10,... | collective-permute-start | bytes 196616 | tf_op jit(solution)/shard_map/ppermute | solution.py:507
  13.8 29.6 %collective-permute-start.15 = (bf16[1,32,4096]{2,1,0:T(8,128)(2,1)}, bf16[1,32,4096]{2,1,0:T(8,128)(2,1)S(1)}, u32[]{:S(2)}, u32[]{:S(2)}) collective-permute-start(bf16[1,32,4096]{2,1,0:T(8,128)(2,1)} %bitcast.103), channel_id=1, source_target_pairs={{0,4},{1,5},{2,6},{3,7},{4,0},{5,1},{6,2},{7,3},{8,12},{9,13},{10,... | collective-permute-start | bytes 786440 | tf_op jit(solution)/shard_map/ppermute | solution.py:507
  13.9 34.3 %collective-permute-start.20 = (bf16[1,128,1024]{2,1,0:T(8,128)(2,1)}, bf16[1,128,1024]{2,1,0:T(8,128)(2,1)S(1)}, u32[]{:S(2)}, u32[]{:S(2)}) collective-permute-start(bf16[1,128,1024]{2,1,0:T(8,128)(2,1)} %bitcast.107), channel_id=1, source_target_pairs={{0,4},{1,5},{2,6},{3,7},{4,0},{5,1},{6,2},{7,3},{8,12},{9,13},{10,... | collective-permute-start | bytes 786440 | tf_op jit(solution)/shard_map/ppermute | solution.py:507
  18.4 49.3 %copy-start.9 = (bf16[32,3072]{1,0:T(8,128)(2,1)S(1)}, bf16[32,3072]{1,0:T(8,128)(2,1)}, u32[]{:S(2)}) copy-start(bf16[32,3072]{1,0:T(8,128)(2,1)} %param.21) | copy-start | bytes 589828
  44.4 14.9 %collective-permute-start.16 = (bf16[2,32,4096]{2,1,0:T(8,128)(2,1)S(1)}, bf16[2,32,4096]{2,1,0:T(8,128)(2,1)S(1)}, u32[]{:S(2)}, u32[]{:S(2)}) collective-permute-start(bf16[2,32,4096]{2,1,0:T(8,128)(2,1)S(1)} %pad_maximum_fusion.8), channel_id=1, source_target_pairs={{0,2},{1,3},{2,0},{3,1},{4,6},{5,7},{6,4},{7,5},{8,10},{9,11},{10,... | collective-permute-start | bytes 1572872 | tf_op jit(solution)/shard_map/ppermute | solution.py:507
  45.5 22.2 %collective-permute-start.6 = (bf16[2,32,3072]{2,1,0:T(8,128)(2,1)S(1)}, bf16[2,32,3072]{2,1,0:T(8,128)(2,1)S(1)}, u32[]{:S(2)}, u32[]{:S(2)}) collective-permute-start(bf16[2,32,3072]{2,1,0:T(8,128)(2,1)S(1)} %pad_maximum_fusion.10), channel_id=1, source_target_pairs={{0,2},{1,3},{2,0},{3,1},{4,6},{5,7},{6,4},{7,5},{8,10},{9,11},{10,... | collective-permute-start | bytes 1179656 | tf_op jit(solution)/shard_map/ppermute | solution.py:507
  48.3 30.5 %collective-permute-start.21 = (bf16[2,128,1024]{2,1,0:T(8,128)(2,1)S(1)}, bf16[2,128,1024]{2,1,0:T(8,128)(2,1)S(1)}, u32[]{:S(2)}, u32[]{:S(2)}) collective-permute-start(bf16[2,128,1024]{2,1,0:T(8,128)(2,1)S(1)} %pad_maximum_fusion.9), channel_id=1, source_target_pairs={{0,2},{1,3},{2,0},{3,1},{4,6},{5,7},{6,4},{7,5},{8,10},{9,11},{10,... | collective-permute-start | bytes 1572872 | tf_op jit(solution)/shard_map/ppermute | solution.py:507
  59.4 21.9 %collective-permute-start.17 = (bf16[4,32,4096]{2,1,0:T(8,128)(2,1)S(1)}, bf16[4,32,4096]{2,1,0:T(8,128)(2,1)S(1)}, u32[]{:S(2)}, u32[]{:S(2)}) collective-permute-start(bf16[4,32,4096]{2,1,0:T(8,128)(2,1)S(1)} %pad_maximum_fusion.4), channel_id=1, source_target_pairs={{0,1},{1,0},{2,3},{3,2},{4,5},{5,4},{6,7},{7,6},{8,24},{9,25},{10,... | collective-permute-start | bytes 3145736 | tf_op jit(solution)/shard_map/ppermute | solution.py:507
  67.8 39.8 %collective-permute-start.7 = (bf16[4,32,3072]{2,1,0:T(8,128)(2,1)S(1)}, bf16[4,32,3072]{2,1,0:T(8,128)(2,1)S(1)}, u32[]{:S(2)}, u32[]{:S(2)}) collective-permute-start(bf16[4,32,3072]{2,1,0:T(8,128)(2,1)S(1)} %pad_maximum_fusion.6), channel_id=1, source_target_pairs={{0,1},{1,0},{2,3},{3,2},{4,5},{5,4},{6,7},{7,6},{8,24},{9,25},{10,... | collective-permute-start | bytes 2359304 | tf_op jit(solution)/shard_map/ppermute | solution.py:507
  78.9 25.1 %collective-permute-start.22 = (bf16[4,128,1024]{2,1,0:T(8,128)(2,1)S(1)}, bf16[4,128,1024]{2,1,0:T(8,128)(2,1)S(1)}, u32[]{:S(2)}, u32[]{:S(2)}) collective-permute-start(bf16[4,128,1024]{2,1,0:T(8,128)(2,1)S(1)} %pad_maximum_fusion.5), channel_id=1, source_target_pairs={{0,1},{1,0},{2,3},{3,2},{4,5},{5,4},{6,7},{7,6},{8,24},{9,25},{10,... | collective-permute-start | bytes 3145736 | tf_op jit(solution)/shard_map/ppermute | solution.py:507
  81.5 33.7 %collective-permute-start.18 = (bf16[8,32,4096]{2,1,0:T(8,128)(2,1)S(1)}, bf16[8,32,4096]{2,1,0:T(8,128)(2,1)S(1)}, u32[]{:S(2)}, u32[]{:S(2)}) collective-permute-start(bf16[8,32,4096]{2,1,0:T(8,128)(2,1)S(1)} %pad_maximum_fusion.1), channel_id=1, source_target_pairs={{0,16},{1,17},{2,18},{3,19},{4,20},{5,21},{6,22},{7,23},{8,9},{9,8... | collective-permute-start | bytes 6291464 | tf_op jit(solution)/shard_map/ppermute | solution.py:507
  104.2 33.5 %collective-permute-start.23 = (bf16[8,128,1024]{2,1,0:T(8,128)(2,1)S(1)}, bf16[8,128,1024]{2,1,0:T(8,128)(2,1)S(1)}, u32[]{:S(2)}, u32[]{:S(2)}) collective-permute-start(bf16[8,128,1024]{2,1,0:T(8,128)(2,1)S(1)} %pad_maximum_fusion.2), channel_id=1, source_target_pairs={{0,16},{1,17},{2,18},{3,19},{4,20},{5,21},{6,22},{7,23},{8,9},{9,8... | collective-permute-start | bytes 6291464 | tf_op jit(solution)/shard_map/ppermute | solution.py:507
  107.8 46.7 %collective-permute-start.8 = (bf16[8,32,3072]{2,1,0:T(8,128)(2,1)S(1)}, bf16[8,32,3072]{2,1,0:T(8,128)(2,1)S(1)}, u32[]{:S(2)}, u32[]{:S(2)}) collective-permute-start(bf16[8,32,3072]{2,1,0:T(8,128)(2,1)S(1)} %pad_maximum_fusion.3), channel_id=1, source_target_pairs={{0,16},{1,17},{2,18},{3,19},{4,20},{5,21},{6,22},{7,23},{8,9},{9,8... | collective-permute-start | bytes 4718600 | tf_op jit(solution)/shard_map/ppermute | solution.py:507
  117.0 39.1 %copy-start.2 = (bf16[32,32,4096]{2,1,0:T(8,128)(2,1)}, bf16[32,32,4096]{2,1,0:T(8,128)(2,1)S(1)}, u32[]{:S(2)}) copy-start(bf16[32,32,4096]{2,1,0:T(8,128)(2,1)S(1)} %get-tuple-element.127) | copy-start | bytes 25165828
  117.0 124.0 %collective-permute-start.19 = (bf16[16,32,4096]{2,1,0:T(8,128)(2,1)}, bf16[16,32,4096]{2,1,0:T(8,128)(2,1)}, u32[]{:S(2)}, u32[]{:S(2)}) collective-permute-start(bf16[16,32,4096]{2,1,0:T(8,128)(2,1)} %get-tuple-element.126), channel_id=1, source_target_pairs={{0,8},{1,9},{2,10},{3,11},{4,12},{5,13},{6,14},{7,15},{8,0},{9,1},... | collective-permute-start | bytes 12582920 | tf_op jit(solution)/shard_map/ppermute | solution.py:508
  137.7 21.1 %copy-start.10 = (bf16[32,1024]{1,0:T(8,128)(2,1)S(1)}, bf16[32,1024]{1,0:T(8,128)(2,1)}, u32[]{:S(2)}) copy-start(bf16[32,1024]{1,0:T(8,128)(2,1)} %param.24) | copy-start | bytes 196612
  137.7 23.2 %copy-start.12 = (bf16[1,512,1024]{2,1,0:T(8,128)(2,1)S(1)}, bf16[1,512,1024]{2,1,0:T(8,128)(2,1)}, u32[]{:S(2)}) copy-start(bf16[1,512,1024]{2,1,0:T(8,128)(2,1)} %param.33) | copy-start | bytes 3145732
  139.5 16.6 %copy-start.3 = (bf16[32,128,1024]{2,1,0:T(8,128)(2,1)}, bf16[32,128,1024]{2,1,0:T(8,128)(2,1)S(1)}, u32[]{:S(2)}) copy-start(bf16[32,128,1024]{2,1,0:T(8,128)(2,1)S(1)} %get-tuple-element.125) | copy-start | bytes 25165828
  139.5 113.6 %collective-permute-start.24 = (bf16[16,128,1024]{2,1,0:T(8,128)(2,1)}, bf16[16,128,1024]{2,1,0:T(8,128)(2,1)}, u32[]{:S(2)}, u32[]{:S(2)}) collective-permute-start(bf16[16,128,1024]{2,1,0:T(8,128)(2,1)} %get-tuple-element.124), channel_id=1, source_target_pairs={{0,8},{1,9},{2,10},{3,11},{4,12},{5,13},{6,14},{7,15},{8,0},{9,1},... | collective-permute-start | bytes 12582920 | tf_op jit(solution)/shard_map/ppermute | solution.py:508
  156.1 49.6 %collective-permute-start.9 = (bf16[16,32,3072]{2,1,0:T(8,128)(2,1)}, bf16[16,32,3072]{2,1,0:T(8,128)(2,1)S(1)}, u32[]{:S(2)}, u32[]{:S(2)}) collective-permute-start(bf16[16,32,3072]{2,1,0:T(8,128)(2,1)} %get-tuple-element.128), channel_id=1, source_target_pairs={{0,8},{1,9},{2,10},{3,11},{4,12},{5,13},{6,14},{7,15},{8,0},{9,1},... | collective-permute-start | bytes 9437192 | tf_op jit(solution)/shard_map/ppermute | solution.py:508
  158.7 22.9 %copy-start.15 = (bf16[1,1,384]{2,0,1:T(2,128)(2,1)}, bf16[1,1,384]{2,0,1:T(2,128)(2,1)S(1)}, u32[]{:S(2)}) copy-start(bf16[1,1,384]{2,0,1:T(2,128)(2,1)S(1)} %collective-permute-done) | copy-start | bytes 2308
  158.7 3.7 collective-permute-start.1
  158.8 6.4 collective-permute-start.11
  162.5 19.2 %copy-start.17 = (bf16[2,1,384]{2,0,1:T(2,128)(2,1)}, bf16[2,1,384]{2,0,1:T(2,128)(2,1)S(1)}, u32[]{:S(2)}) copy-start(bf16[2,1,384]{2,0,1:T(2,128)(2,1)S(1)} %collective-permute-done.1) | copy-start | bytes 4612
  163.1 5.1 collective-permute-start.2
  166.0 6.6 collective-permute-start.12
  168.1 13.5 %copy-start.16 = (bf16[4,1,384]{2,0,1:T(4,128)(2,1)}, bf16[4,1,384]{2,0,1:T(4,128)(2,1)S(1)}, u32[]{:S(2)}) copy-start(bf16[4,1,384]{2,0,1:T(4,128)(2,1)S(1)} %collective-permute-done.2) | copy-start | bytes 9220
  168.2 8.8 %collective-permute-start.3 = (bf16[8,1,384]{2,0,1:T(8,128)(2,1)S(1)}, bf16[8,1,384]{2,0,1:T(8,128)(2,1)}, u32[]{:S(2)}, u32[]{:S(2)}) collective-permute-start(bf16[8,1,384]{2,0,1:T(8,128)(2,1)S(1)} %pad_maximum_fusion.14), channel_id=1, source_target_pairs={{0,16},{1,17},{2,18},{3,19},{4,20},{5,21},{6,22},{7,23},{8,9},{9,8... | collective-permute-start | bytes 18440 | tf_op jit(solution)/shard_map/ppermute | solution.py:507
  174.3 15.8 %collective-permute-start.13 = (bf16[8,32,1024]{2,1,0:T(8,128)(2,1)}, bf16[8,32,1024]{2,1,0:T(8,128)(2,1)}, u32[]{:S(2)}, u32[]{:S(2)}) collective-permute-start(bf16[8,32,1024]{2,1,0:T(8,128)(2,1)} %pad_maximum_fusion.7), channel_id=1, source_target_pairs={{0,16},{1,17},{2,18},{3,19},{4,20},{5,21},{6,22},{7,23},{8,9},{9,8... | collective-permute-start | bytes 1572872 | tf_op jit(solution)/shard_map/ppermute | solution.py:507
  178.9 2.8 collective-permute-start.4
  192.3 7.5 %collective-permute-start.14 = (bf16[16,32,1024]{2,1,0:T(8,128)(2,1)}, bf16[16,32,1024]{2,1,0:T(8,128)(2,1)}, u32[]{:S(2)}, u32[]{:S(2)}) collective-permute-start(bf16[16,32,1024]{2,1,0:T(8,128)(2,1)} %get-tuple-element.140), channel_id=1, source_target_pairs={{0,8},{1,9},{2,10},{3,11},{4,12},{5,13},{6,14},{7,15},{8,0},{9,1},... | collective-permute-start | bytes 3145736 | tf_op jit(solution)/shard_map/ppermute | solution.py:508
  461.0 111.0 %collective-permute-start.30 = (bf16[16,32,3072]{2,1,0:T(8,128)(2,1)}, bf16[16,32,3072]{2,1,0:T(8,128)(2,1)}, u32[]{:S(2)}, u32[]{:S(2)}) collective-permute-start(bf16[16,32,3072]{2,1,0:T(8,128)(2,1)} %slice.334), channel_id=1, source_target_pairs={{0,8},{1,9},{2,10},{3,11},{4,12},{5,13},{6,14},{7,15},{8,0},{9,1},... | collective-permute-start | bytes 9437192 | tf_op jit(solution)/shard_map/ppermute | solution.py:515
  473.3 44.9 %collective-permute-start.35 = (bf16[16,32,1024]{2,1,0:T(8,128)(2,1)}, bf16[16,32,1024]{2,1,0:T(8,128)(2,1)S(1)}, u32[]{:S(2)}, u32[]{:S(2)}) collective-permute-start(bf16[16,32,1024]{2,1,0:T(8,128)(2,1)} %slice.346), channel_id=1, source_target_pairs={{0,8},{1,9},{2,10},{3,11},{4,12},{5,13},{6,14},{7,15},{8,0},{9,1},... | collective-permute-start | bytes 3145736 | tf_op jit(solution)/shard_map/ppermute | solution.py:515
  505.3 76.5 %collective-permute-start.40 = (bf16[16,32,4096]{2,1,0:T(8,128)(2,1)}, bf16[16,32,4096]{2,1,0:T(8,128)(2,1)}, u32[]{:S(2)}, u32[]{:S(2)}) collective-permute-start(bf16[16,32,4096]{2,1,0:T(8,128)(2,1)} %slice.359), channel_id=1, source_target_pairs={{0,8},{1,9},{2,10},{3,11},{4,12},{5,13},{6,14},{7,15},{8,0},{9,1},... | collective-permute-start | bytes 12582920 | tf_op jit(solution)/shard_map/ppermute | solution.py:515
  517.6 1.7 collective-permute-start.25
  518.6 15.0 %collective-permute-start.36 = (bf16[8,32,1024]{2,1,0:T(8,128)(2,1)S(1)}, bf16[8,32,1024]{2,1,0:T(8,128)(2,1)S(1)}, u32[]{:S(2)}, u32[]{:S(2)}) collective-permute-start(bf16[8,32,1024]{2,1,0:T(8,128)(2,1)S(1)} %slice.348), channel_id=1, source_target_pairs={{0,16},{1,17},{2,18},{3,19},{4,20},{5,21},{6,22},{7,23},{8,9},{9,8... | collective-permute-start | bytes 1572872 | tf_op jit(solution)/shard_map/ppermute | solution.py:515
  519.3 8.7 %collective-permute-start.26 = (f32[8,1,384]{2,0,1:T(8,128)S(1)}, f32[8,1,384]{2,0,1:T(8,128)S(1)}, u32[]{:S(2)}, u32[]{:S(2)}) collective-permute-start(f32[8,1,384]{2,0,1:T(8,128)S(1)} %slice.324), channel_id=1, source_target_pairs={{0,16},{1,17},{2,18},{3,19},{4,20},{5,21},{6,22},{7,23},{8,9},{9,8... | collective-permute-start | bytes 36872 | tf_op jit(solution)/shard_map/ppermute | solution.py:515
  528.0 3.7 collective-permute-start.27
  531.7 3.7 collective-permute-start.28
  533.8 37.7 %collective-permute-start.37 = (bf16[4,32,1024]{2,1,0:T(8,128)(2,1)S(1)}, bf16[4,32,1024]{2,1,0:T(8,128)(2,1)S(1)}, u32[]{:S(2)}, u32[]{:S(2)}) collective-permute-start(bf16[4,32,1024]{2,1,0:T(8,128)(2,1)S(1)} %slice.350), channel_id=1, source_target_pairs={{0,1},{1,0},{2,3},{3,2},{4,5},{5,4},{6,7},{7,6},{8,24},{9,25},{10,... | collective-permute-start | bytes 786440 | tf_op jit(solution)/shard_map/ppermute | solution.py:515
  535.4 36.1 %collective-permute-start.29 = (f32[1,1,384]{2,0,1:T(1,128)S(1)}, f32[1,1,384]{2,0,1:T(1,128)S(1)}, u32[]{:S(2)}, u32[]{:S(2)}) collective-permute-start(f32[1,1,384]{2,0,1:T(1,128)S(1)} %slice.330), channel_id=1, source_target_pairs={{0,4},{1,5},{2,6},{3,7},{4,0},{5,1},{6,2},{7,3},{8,12},{9,13},{10,... | collective-permute-start | bytes 4616 | tf_op jit(solution)/shard_map/ppermute | solution.py:515
  566.4 15.4 %slice-start = ((s8[8388608]{0:T(1024)(128)(4,1)}), s8[4194304]{0:T(1024)(128)(4,1)S(1)}, s32[]{:S(2)}) async-start(s8[8388608]{0:T(1024)(128)(4,1)} %bitcast.91), calls=%async_computation | async-start | bytes 8388608
  571.5 31.2 %collective-permute-start.45 = (bf16[16,128,1024]{2,1,0:T(8,128)(2,1)}, bf16[16,128,1024]{2,1,0:T(8,128)(2,1)}, u32[]{:S(2)}, u32[]{:S(2)}) collective-permute-start(bf16[16,128,1024]{2,1,0:T(8,128)(2,1)} %slice.370), channel_id=1, source_target_pairs={{0,8},{1,9},{2,10},{3,11},{4,12},{5,13},{6,14},{7,15},{8,0},{9,1},... | collective-permute-start | bytes 12582920 | tf_op jit(solution)/shard_map/ppermute | solution.py:515
  571.6 6.2 collective-permute-start.38
  576.4 20.6 %collective-permute-start.31 = (bf16[8,32,3072]{2,1,0:T(8,128)(2,1)S(1)}, bf16[8,32,3072]{2,1,0:T(8,128)(2,1)}, u32[]{:S(2)}, u32[]{:S(2)}) collective-permute-start(bf16[8,32,3072]{2,1,0:T(8,128)(2,1)S(1)} %slice.336), channel_id=1, source_target_pairs={{0,16},{1,17},{2,18},{3,19},{4,20},{5,21},{6,22},{7,23},{8,9},{9,8... | collective-permute-start | bytes 4718600 | tf_op jit(solution)/shard_map/ppermute | solution.py:515
  577.8 24.8 %slice-start.2 = ((s8[8388608]{0:T(1024)(128)(4,1)}), s8[4194304]{0:T(1024)(128)(4,1)S(1)}, s32[]{:S(2)}) async-start(s8[8388608]{0:T(1024)(128)(4,1)} %bitcast.93), calls=%async_computation.2 | async-start | bytes 8388608
  579.1 23.5 %slice-start.3 = ((s8[8388608]{0:T(1024)(128)(4,1)}), s8[4194304]{0:T(1024)(128)(4,1)S(1)}, s32[]{:S(2)}) async-start(s8[8388608]{0:T(1024)(128)(4,1)} %bitcast.93), calls=%async_computation.3 | async-start | bytes 8388608
  579.1 22.0 %collective-permute-start.39 = (bf16[1,32,1024]{2,1,0:T(8,128)(2,1)}, bf16[1,32,1024]{2,1,0:T(8,128)(2,1)}, u32[]{:S(2)}, u32[]{:S(2)}) collective-permute-start(bf16[1,32,1024]{2,1,0:T(8,128)(2,1)} %slice.354), channel_id=1, source_target_pairs={{0,4},{1,5},{2,6},{3,7},{4,0},{5,1},{6,2},{7,3},{8,12},{9,13},{10,... | collective-permute-start | bytes 196616 | tf_op jit(solution)/shard_map/ppermute | solution.py:515
  587.0 14.1 %copy-start.14 = (bf16[2,32,1024]{2,1,0:T(8,128)(2,1)S(1)}, bf16[2,32,1024]{2,1,0:T(8,128)(2,1)}, u32[]{:S(2)}) copy-start(bf16[2,32,1024]{2,1,0:T(8,128)(2,1)} %copy-done.13) | copy-start | bytes 393220
  587.0 40.7 %collective-permute-start.41 = (bf16[8,32,4096]{2,1,0:T(8,128)(2,1)}, bf16[8,32,4096]{2,1,0:T(8,128)(2,1)S(1)}, u32[]{:S(2)}, u32[]{:S(2)}) collective-permute-start(bf16[8,32,4096]{2,1,0:T(8,128)(2,1)} %slice.361), channel_id=1, source_target_pairs={{0,16},{1,17},{2,18},{3,19},{4,20},{5,21},{6,22},{7,23},{8,9},{9,8... | collective-permute-start | bytes 6291464 | tf_op jit(solution)/shard_map/ppermute | solution.py:515
  599.0 20.5 %collective-permute-start.32 = (bf16[4,32,3072]{2,1,0:T(8,128)(2,1)S(1)}, bf16[4,32,3072]{2,1,0:T(8,128)(2,1)S(1)}, u32[]{:S(2)}, u32[]{:S(2)}) collective-permute-start(bf16[4,32,3072]{2,1,0:T(8,128)(2,1)S(1)} %slice.338), channel_id=1, source_target_pairs={{0,1},{1,0},{2,3},{3,2},{4,5},{5,4},{6,7},{7,6},{8,24},{9,25},{10,... | collective-permute-start | bytes 2359304 | tf_op jit(solution)/shard_map/ppermute | solution.py:515
  607.1 54.3 %collective-permute-start.46 = (bf16[8,128,1024]{2,1,0:T(8,128)(2,1)S(1)}, bf16[8,128,1024]{2,1,0:T(8,128)(2,1)S(1)}, u32[]{:S(2)}, u32[]{:S(2)}) collective-permute-start(bf16[8,128,1024]{2,1,0:T(8,128)(2,1)S(1)} %slice.372), channel_id=1, source_target_pairs={{0,16},{1,17},{2,18},{3,19},{4,20},{5,21},{6,22},{7,23},{8,9},{9,8... | collective-permute-start | bytes 6291464 | tf_op jit(solution)/shard_map/ppermute | solution.py:515
  619.8 10.6 %collective-permute-start.33 = (bf16[2,32,3072]{2,1,0:T(8,128)(2,1)S(1)}, bf16[2,32,3072]{2,1,0:T(8,128)(2,1)S(1)}, u32[]{:S(2)}, u32[]{:S(2)}) collective-permute-start(bf16[2,32,3072]{2,1,0:T(8,128)(2,1)S(1)} %slice.340), channel_id=1, source_target_pairs={{0,2},{1,3},{2,0},{3,1},{4,6},{5,7},{6,4},{7,5},{8,10},{9,11},{10,... | collective-permute-start | bytes 1179656 | tf_op jit(solution)/shard_map/ppermute | solution.py:515
  628.8 35.3 %collective-permute-start.42 = (bf16[4,32,4096]{2,1,0:T(8,128)(2,1)S(1)}, bf16[4,32,4096]{2,1,0:T(8,128)(2,1)S(1)}, u32[]{:S(2)}, u32[]{:S(2)}) collective-permute-start(bf16[4,32,4096]{2,1,0:T(8,128)(2,1)S(1)} %slice.363), channel_id=1, source_target_pairs={{0,1},{1,0},{2,3},{3,2},{4,5},{5,4},{6,7},{7,6},{8,24},{9,25},{10,... | collective-permute-start | bytes 3145736 | tf_op jit(solution)/shard_map/ppermute | solution.py:515
  630.5 35.5 %collective-permute-start.34 = (bf16[1,32,3072]{2,1,0:T(8,128)(2,1)S(1)}, bf16[1,32,3072]{2,1,0:T(8,128)(2,1)S(1)}, u32[]{:S(2)}, u32[]{:S(2)}) collective-permute-start(bf16[1,32,3072]{2,1,0:T(8,128)(2,1)S(1)} %slice.342), channel_id=1, source_target_pairs={{0,4},{1,5},{2,6},{3,7},{4,0},{5,1},{6,2},{7,3},{8,12},{9,13},{10,... | collective-permute-start | bytes 589832 | tf_op jit(solution)/shard_map/ppermute | solution.py:515
  662.5 14.9 %collective-permute-start.47 = (bf16[4,128,1024]{2,1,0:T(8,128)(2,1)S(1)}, bf16[4,128,1024]{2,1,0:T(8,128)(2,1)S(1)}, u32[]{:S(2)}, u32[]{:S(2)}) collective-permute-start(bf16[4,128,1024]{2,1,0:T(8,128)(2,1)S(1)} %slice.374), channel_id=1, source_target_pairs={{0,1},{1,0},{2,3},{3,2},{4,5},{5,4},{6,7},{7,6},{8,24},{9,25},{10,... | collective-permute-start | bytes 3145736 | tf_op jit(solution)/shard_map/ppermute | solution.py:515
  664.4 15.0 %collective-permute-start.43 = (bf16[2,32,4096]{2,1,0:T(8,128)(2,1)S(1)}, bf16[2,32,4096]{2,1,0:T(8,128)(2,1)S(1)}, u32[]{:S(2)}, u32[]{:S(2)}) collective-permute-start(bf16[2,32,4096]{2,1,0:T(8,128)(2,1)S(1)} %slice.365), channel_id=1, source_target_pairs={{0,2},{1,3},{2,0},{3,1},{4,6},{5,7},{6,4},{7,5},{8,10},{9,11},{10,... | collective-permute-start | bytes 1572872 | tf_op jit(solution)/shard_map/ppermute | solution.py:515
  677.8 18.0 %collective-permute-start.48 = (bf16[2,128,1024]{2,1,0:T(8,128)(2,1)S(1)}, bf16[2,128,1024]{2,1,0:T(8,128)(2,1)S(1)}, u32[]{:S(2)}, u32[]{:S(2)}) collective-permute-start(bf16[2,128,1024]{2,1,0:T(8,128)(2,1)S(1)} %slice.376), channel_id=1, source_target_pairs={{0,2},{1,3},{2,0},{3,1},{4,6},{5,7},{6,4},{7,5},{8,10},{9,11},{10,... | collective-permute-start | bytes 1572872 | tf_op jit(solution)/shard_map/ppermute | solution.py:515
  679.6 17.2 %collective-permute-start.44 = (bf16[1,32,4096]{2,1,0:T(8,128)(2,1)S(1)}, bf16[1,32,4096]{2,1,0:T(8,128)(2,1)S(1)}, u32[]{:S(2)}, u32[]{:S(2)}) collective-permute-start(bf16[1,32,4096]{2,1,0:T(8,128)(2,1)S(1)} %slice.367), channel_id=1, source_target_pairs={{0,4},{1,5},{2,6},{3,7},{4,0},{5,1},{6,2},{7,3},{8,12},{9,13},{10,... | collective-permute-start | bytes 786440 | tf_op jit(solution)/shard_map/ppermute | solution.py:515
  696.0 13.2 %collective-permute-start.49 = (bf16[1,128,1024]{2,1,0:T(8,128)(2,1)S(1)}, bf16[1,128,1024]{2,1,0:T(8,128)(2,1)S(1)}, u32[]{:S(2)}, u32[]{:S(2)}) collective-permute-start(bf16[1,128,1024]{2,1,0:T(8,128)(2,1)S(1)} %slice.378), channel_id=1, source_target_pairs={{0,4},{1,5},{2,6},{3,7},{4,0},{5,1},{6,2},{7,3},{8,12},{9,13},{10,... | collective-permute-start | bytes 786440 | tf_op jit(solution)/shard_map/ppermute | solution.py:515
  (25 other events, 235.6 us)

commit v4 on v3

--- a/solution.py
+++ b/solution.py
@@ -52,9 +52,8 @@
     return centre * inv, inv
 
 
-def norm_project(x, gain, shift, weight, bias, tn):
+def norm_project(x, gain, shift, weight, bias, tn, cols):
     rows, width = x.shape
-    cols = weight.shape[1]
 
     def body(x_ref, g_ref, s_ref, w_ref, b_ref, a_ref, o_ref):
         @pl.when(pl.program_id(0) == 0)
@@ -123,12 +122,12 @@
     )(qkv, qkv, qkv)
 
 
-def attention_back(qkv, logs, d_o):
+def attention_back(qkv, logs, d_o, first_pair, pairs):
     rows, width = qkv.shape[0], qkv.shape[1] // 3
-    pairs = width // (2 * HEAD_DIM)
+    every = width // (2 * HEAD_DIM)
     span = 2 * HEAD_DIM
 
-    def body(q_ref, k_ref, v_ref, l_ref, do_ref, dq_ref, dk_ref, dv_ref, cq_ref, cv_ref):
+    def body(q_ref, k_ref, v_ref, l_ref, do_ref, d_ref, cq_ref, cv_ref):
         q, k, v, do = q_ref[...], k_ref[...], v_ref[...], do_ref[...]
         lane = lax.broadcasted_iota(jnp.int32, (rows, span), 1)
         dqs, dks, dvs = [], [], []
@@ -149,33 +148,36 @@
         dq = (jnp.where(first, dqs[0], dqs[1]) * 0.125).astype(jnp.bfloat16)
         dk = (jnp.where(first, dks[0], dks[1]) * 0.125).astype(jnp.bfloat16)
         dv = jnp.where(first, dvs[0], dvs[1]).astype(jnp.bfloat16)
-        dq_ref[...] = dq
-        dk_ref[...] = dk
-        dv_ref[...] = dv
+        d_ref[0] = dq
+        d_ref[1] = dk
+        d_ref[2] = dv
         cq_ref[...] = jnp.sum(dq.astype(jnp.float32), axis=0, keepdims=True)
         cv_ref[...] = jnp.sum(dv.astype(jnp.float32), axis=0, keepdims=True)
 
     col = lambda base: pl.BlockSpec((rows, span), lambda j: (0, base + j))
     sums = pl.BlockSpec((1, span), lambda j: (0, j))
-    mat = jax.ShapeDtypeStruct((rows, width), jnp.bfloat16)
-    vec = jax.ShapeDtypeStruct((1, width), jnp.float32)
+    vec_shape = jax.ShapeDtypeStruct((1, pairs * span), jnp.float32)
     return pl.pallas_call(
         body,
         grid=(pairs,),
         in_specs=[
-            col(0),
-            col(pairs),
-            col(2 * pairs),
-            pl.BlockSpec((1, 8, rows), lambda j: (j, 0, 0)),
-            col(0),
-        ],
-        out_specs=[col(0), col(0), col(0), sums, sums],
-        out_shape=[mat, mat, mat, vec, vec],
+            col(first_pair),
+            col(every + first_pair),
+            col(2 * every + first_pair),
+            pl.BlockSpec((1, 8, rows), lambda j: (first_pair + j, 0, 0)),
+            col(first_pair),
+        ],
+        out_specs=[pl.BlockSpec((3, rows, span), lambda j: (0, 0, j)), sums, sums],
+        out_shape=[
+            jax.ShapeDtypeStruct((3, rows, pairs * span), jnp.bfloat16),
+            vec_shape,
+            vec_shape,
+        ],
         name="attention_back",
     )(qkv, qkv, qkv, logs, d_o)
 
 
-def project_norm(o, weight, bias, x, gain, shift):
+def project_norm(o, weight, bias, x, gain, shift, at):
     rows, width = o.shape
     tm = rows // 2
 
@@ -190,7 +192,7 @@
     return pl.pallas_call(
         body,
         grid=(rows // tm,),
-        in_specs=[rowblk, whole((width, width)), vec, rowblk, vec, vec],
+        in_specs=[rowblk, pl.BlockSpec((width, width), lambda i: (0, at // width)), vec, rowblk, vec, vec],
         out_specs=[rowblk, rowblk],
         out_shape=[
             jax.ShapeDtypeStruct((rows, width), jnp.float32),
@@ -249,7 +251,7 @@
     )(a, up, up_bias, down, down_bias, x1)
 
 
-def feed_forward_back(dy, gp, down, up, x1, gain, w_out, tf):
+def feed_forward_back(dy, gp, down, up, x1, gain, w_out, at, tf):
     rows, width = dy.shape
     hidden = gp.shape[1]
     steps = hidden // tf
@@ -301,7 +303,7 @@
             pl.BlockSpec((width, tf), lambda j: (0, j)),
             full,
             vec,
-            whole((width, width)),
+            pl.BlockSpec((width, width), lambda j: (0, at // width)),
         ],
         out_specs=[
             full,
@@ -332,17 +334,24 @@
     )(dy, gp, down, up, x1, gain, w_out)
 
 
-def project_back(dq, dk, dv, weight, x, gain, dx1, extra, out_dtype):
-    rows, width = dq.shape
+def project_back(grads, weight, x, gain, dx1, extra, out_dtype):
+    rows, width = x.shape
     tm = rows // 2
     have = extra is not None
+    count = len(grads)
+    part = width // count
 
     def body(*refs):
-        dq_ref, dk_ref, dv_ref, w_ref, x_ref, g_ref, d_ref = refs[:7]
+        d_refs = refs[:count]
+        w_ref, x_ref, g_ref, dx_ref = refs[count : count + 4]
+        more = refs[count + 4 : -3]
         out_ref, cg_ref, cs_ref = refs[-3:]
-        da = dot(dq_ref[...], w_ref[:, :width], NT)
-        da += dot(dk_ref[...], w_ref[:, width : 2 * width], NT)
-        da += dot(dv_ref[...], w_ref[:, 2 * width :], NT)
+        da = None
+        for kind in range(3):
+            for i in range(count):
+                at = kind * width + i * part
+                term = dot(d_refs[i][kind], w_ref[:, at : at + part], NT)
+                da = term if da is None else da + term
         xhat, inv = row_stats(x_ref[...].astype(jnp.float32))
         cg = jnp.sum(da * xhat, axis=0, keepdims=True)
         cs = jnp.sum(da, axis=0, keepdims=True)
@@ -360,15 +369,16 @@
         t = da * g_ref[...]
         m1 = jnp.mean(t, axis=-1, keepdims=True)
         m2 = jnp.mean(t * xhat, axis=-1, keepdims=True)
-        dx = d_ref[...] + inv * (t - m1 - xhat * m2)
+        dx = dx_ref[...] + inv * (t - m1 - xhat * m2)
         if have:
-            dx = refs[7][...].astype(jnp.float32) * refs[8][...] + dx
+            dx = more[0][...].astype(jnp.float32) * more[1][...] + dx
         out_ref[...] = dx.astype(out_dtype)
 
     rowblk = pl.BlockSpec((tm, width), lambda i: (i, 0))
-    vec = whole((1, width))
-    specs = [rowblk, rowblk, rowblk, whole((width, 3 * width)), rowblk, vec, rowblk]
-    args = [dq, dk, dv, weight, x, gain, dx1]
+    vec_spec = whole((1, width))
+    specs = [pl.BlockSpec((3, tm, part), lambda i: (0, i, 0))] * count
+    specs += [whole((width, 3 * width)), rowblk, vec_spec, rowblk]
+    args = list(grads) + [weight, x, gain, dx1]
     if have:
         specs += [rowblk, pl.BlockSpec((tm, 1), lambda i: (i, 0))]
         args += list(extra)
@@ -376,7 +386,7 @@
         body,
         grid=(rows // tm,),
         in_specs=specs,
-        out_specs=[rowblk, vec, vec],
+        out_specs=[rowblk, vec_spec, vec_spec],
         out_shape=[
             jax.ShapeDtypeStruct((rows, width), out_dtype),
             jax.ShapeDtypeStruct((1, width), jnp.float32),
@@ -386,49 +396,62 @@
     )(*args)
 
 
-def weight_grad(lefts, rights, tm, tn):
+def weight_grad_half(lefts, rights, index, blocks, tn, arrived=None):
     rows, m = lefts[0].shape
-    cols = rights[0].shape[1]
+    stacked = rights[0].ndim == 3
+    part = rights[0].shape[-1]
+    cols = part * 3 if stacked else part
+    ndp, nfs, r = blocks
+    tiles = ndp // 2
+    wide = nfs * r
     count = len(lefts)
-
-    def body(*refs):
-        a, b, o_ref = refs[:count], refs[count : 2 * count], refs[-1]
-        total = dot(a[0][...], b[0][...], TN)
-        for x, y in zip(a[1:], b[1:]):
-            total += dot(x[...], y[...], TN)
-        o_ref[...] = total.astype(jnp.bfloat16)
-
-    return pl.pallas_call(
-        body,
-        grid=(m // tm, cols // tn),
-        in_specs=[pl.BlockSpec((rows, tm), lambda i, j: (0, i))] * count
-        + [pl.BlockSpec((rows, tn), lambda i, j: (0, j))] * count,
-        out_specs=pl.BlockSpec((tm, tn), lambda i, j: (i, j)),
-        out_shape=jax.ShapeDtypeStruct((m, cols), jnp.bfloat16),
+    npos = tiles * nfs
+    final = arrived is not None
+    take = (lambda ref: ref[0]) if stacked else (lambda ref: ref[...])
+    if stacked:
+        right = pl.BlockSpec((1, rows, tn), lambda j, i_ref: (j * tn // part, 0, j % (part // tn)))
+    else:
+        right = pl.BlockSpec((rows, tn), lambda j, i_ref: (0, j))
+
+    def body(i_ref, *refs):
+        a = refs[: count * tiles]
+        b = refs[count * tiles : count * tiles + count]
+        rest = refs[count * tiles + count :]
+        scr = rest[-1]
+        outs = rest[1:-1] if final else rest[:-1]
+        for t in range(tiles):
+            total = dot(a[t][...], take(b[0]), TN)
+            for s in range(1, count):
+                total += dot(a[s * tiles + t][...], take(b[s]), TN)
+            for f in range(nfs):
+                scr[t * nfs + f] = total[f * r : (f + 1) * r]
+        for p in range(npos):
+            value = scr[i_ref[tiles + p]]
+            if final:
+                value += rest[0][p].astype(jnp.float32)
+            share = npos // len(outs)
+            outs[p // share][p % share] = value.astype(jnp.bfloat16)
+
+    left_spec = lambda t: pl.BlockSpec((rows, wide), lambda j, i_ref: (0, i_ref[t]))
+    share = npos // 2 if final else npos
+    specs = [left_spec(t) for _ in range(count) for t in range(tiles)]
+    specs += [right] * count
+    args = [left for left in lefts for _ in range(tiles)] + list(rights)
+    if final:
+        specs.append(pl.BlockSpec((npos, r, tn), lambda j, i_ref: (0, 0, j)))
+        args.append(arrived)
+    return pl.pallas_call(
+        body,
+        grid_spec=pltpu.PrefetchScalarGridSpec(
+            num_scalar_prefetch=1,
+            grid=(cols // tn,),
+            in_specs=specs,
+            out_specs=[pl.BlockSpec((share, r, tn), lambda j, i_ref: (0, 0, j))] * (npos // share),
+            scratch_shapes=[pltpu.VMEM((npos, r, tn), jnp.float32)],
+        ),
+        out_shape=[jax.ShapeDtypeStruct((share, r, cols), jnp.bfloat16)] * (npos // share),
         name="weight_grad",
-    )(*lefts, *rights)
-
-
-def vec(v):
-    return v.astype(jnp.float32).reshape(1, -1)
-
-
-def layer_forward(x, w):
-    a1, qkv = norm_project(x, w["g1"], w["s1"], w["qkv"], w["bqkv"], 512)
-    o, logs = attention(qkv)
-    x1, a2 = project_norm(o, w["out"], w["bo"], x, w["g2"], w["s2"])
-    g, gp, y = feed_forward(a2, w["up"], w["bu"], w["down"], w["bd"], x1, 512)
-    return y, (x, a1, qkv, logs, o, x1, a2, g, gp)
-
-
-def layer_back(dy, saved, w, extra, out_dtype):
-    x, a1, qkv, logs, o, x1, a2, g, gp = saved
-    dm, du, dx1, da, do, cdm, cdu, cda, cg2, cs2 = feed_forward_back(
-        dy, gp, w["down"], w["up"], x1, w["g2"], w["out"], 512
-    )
-    dq, dk, dv, cq, cv = attention_back(qkv, logs, do)
-    dx, cg1, cs1 = project_back(dq, dk, dv, w["qkv"], x, w["g1"], dx1, extra, out_dtype)
-    return dx, (dm, du, da, dq, dk, dv), (cg1, cs1, cq, cv, cda, cg2, cs2, cdm, cdu)
+    )(index, *args)
 
 
 def bits_of(ndp, nfs):
@@ -469,53 +492,158 @@
     return perms
 
 
-def place_blocks(pieces, table_row, scatter):
-    n = pieces[0].shape[0]
+AXES = ("dp", "fsdp")
+
+
+def send(x, perm):
+    return lax.ppermute(x, AXES, perm)
+
+
+class Line:
+    def __init__(self):
+        self.last = None
+
+    def after(self, *arrays):
+        if self.last is not None:
+            arrays = lax.optimization_barrier((self.last,) + arrays)[1:]
+        return arrays
+
+    def mark(self, array):
+        self.last = array
+
+
+def place_shards(groups, table_row, shapes, slots):
+    n = sum(p.shape[0] for p in groups[0])
+    count = len(groups)
 
     def body(t_ref, *refs):
-        ins, outs, sem = refs[: len(pieces)], refs[len(pieces) : -1], refs[-1]
-        copies = []
-        for src, dst in zip(ins, outs):
-            for i in range(n):
-                j = t_ref[i]
-                s, d = (i, j) if scatter else (j, i)
-                copies.append(pltpu.make_async_copy(src.at[s], dst.at[d], sem))
-        for c in copies:
+        ins = refs[: 4 * count]
+        outs = refs[4 * count : 4 * count + len(shapes)]
+        bufs = refs[4 * count + len(shapes) : -2]
+        in_sem, out_sem = refs[-2:]
+        loads, stores = [], []
+        for i in range(count):
+            which, middle, col = slots[i]
+            width = bufs[i].shape[-1]
+            for p in range(n):
+                piece = ins[4 * i + p // (n // 4)]
+                loads.append(
+                    pltpu.make_async_copy(piece.at[p % (n // 4)], bufs[i].at[p], in_sem.at[i, p])
+                )
+                target = outs[which].at[t_ref[p]]
+                if middle is not None:
+                    target = target.at[middle]
+                stores.append(
+                    pltpu.make_async_copy(
+                        bufs[i].at[p], target.at[:, col : col + width], out_sem.at[i, p]
+                    )
+                )
+        for c in loads:
             c.start()
-        for c in copies:
-            c.wait()
-
-    return pl.pallas_call(
-        body,
-        out_shape=[jax.ShapeDtypeStruct(p.shape, p.dtype) for p in pieces],
+        for a, b in zip(loads, stores):
+            a.wait()
+            b.start()
+        for b in stores:
+            b.wait()
+
+    flat = [p for g in groups for p in g]
+    anywhere = pl.BlockSpec(memory_space=pl.ANY)
+    return pl.pallas_call(
+        body,
+        out_shape=[jax.ShapeDtypeStruct(s, jnp.bfloat16) for s in shapes],
         grid_spec=pltpu.PrefetchScalarGridSpec(
             num_scalar_prefetch=1,
-            in_specs=[pl.BlockSpec(memory_space=pl.ANY)] * len(pieces),
-            out_specs=[pl.BlockSpec(memory_space=pltpu.VMEM)] * len(pieces),
-            scratch_shapes=[pltpu.SemaphoreType.DMA],
+            in_specs=[anywhere] * len(flat),
+            out_specs=[anywhere] * len(shapes),
+            scratch_shapes=[pltpu.VMEM((n,) + g[0].shape[1:], jnp.bfloat16) for g in groups]
+            + [pltpu.SemaphoreType.DMA((count, n))] * 2,
         ),
-        name="place",
-    )(table_row, *pieces)
-
-
-AXES = ("dp", "fsdp")
-
-
-def gather_relative(shard, perms):
-    cur = shard[None]
-    for perm in perms[:0:-1]:
-        cur = jnp.concatenate([cur, lax.ppermute(cur, AXES, perm)], axis=0)
-    return jnp.concatenate([cur, lax.ppermute(cur, AXES, perms[0])], axis=0)
-
-
-def reduce_relative(rel, perms, wide=jnp.bfloat16):
-    cur = rel
-    for i, perm in enumerate(perms):
-        half = cur.shape[0] // 2
-        got = lax.ppermute(cur[half:], AXES, perm)
-        total = cur[:half].astype(jnp.float32) + got.astype(jnp.float32)
-        cur = total if i == len(perms) - 1 else total.astype(wide)
-    return cur[0]
+        name="place_shards",
+    )(table_row, *flat)
+
+
+def unpack_vectors(got, inverse_row, sizes, layout):
+    n = got.shape[0]
+
+    def body(i_ref, got_ref, *outs):
+        for rows, out in zip(layout, outs):
+            col = 0
+            for r in rows:
+                k = sizes[0] if r is None else sizes[r]
+                per = 128 // k if k < 128 else 1
+                for d in range(0, n, per):
+                    if r is None:
+                        value = jnp.zeros((1, per * k), jnp.float32)
+                    else:
+                        value = jnp.concatenate(
+                            [got_ref[i_ref[d + e], r : r + 1, 0:k] for e in range(per)], axis=1
+                        )
+                    out[0:1, col + d * k : col + (d + per) * k] = value
+                col += n * k
+
+    widths = [sum(n * (sizes[0] if r is None else sizes[r]) for r in rows) for rows in layout]
+    return pl.pallas_call(
+        body,
+        grid_spec=pltpu.PrefetchScalarGridSpec(
+            num_scalar_prefetch=1,
+            grid=(1,),
+            in_specs=[whole(got.shape)],
+            out_specs=[whole((1, w)) for w in widths],
+        ),
+        out_shape=[jax.ShapeDtypeStruct((1, w), jnp.float32) for w in widths],
+        name="unpack_vectors",
+    )(inverse_row, got)
+
+
+def pack_sums(parts, inverse_row, n, rows):
+    flat = [a for group in parts for a in group]
+
+    def body(i_ref, *refs):
+        out = refs[-1]
+        out[...] = jnp.zeros_like(out)
+        at = 0
+        for r, group in enumerate(parts):
+            total = refs[at][...]
+            for k in range(1, len(group)):
+                total += refs[at + k][...]
+            at += len(group)
+            k = total.shape[1] // n
+            for d in range(n):
+                out[i_ref[d], r : r + 1, 0:k] = total[:, d * k : (d + 1) * k]
+
+    return pl.pallas_call(
+        body,
+        grid_spec=pltpu.PrefetchScalarGridSpec(
+            num_scalar_prefetch=1,
+            grid=(1,),
+            in_specs=[whole(a.shape) for a in flat],
+            out_specs=whole((n, rows, 128)),
+        ),
+        out_shape=jax.ShapeDtypeStruct((n, rows, 128), jnp.float32),
+        name="pack_sums",
+    )(inverse_row, *flat)
+
+
+class Reduction:
+    def __init__(self, perms, kept, sent, stage):
+        self.perms, self.stage = perms, stage
+        self.kept, self.got = kept, send(sent, perms[stage])
+        self.done = None
+
+    def step(self, line, wide=jnp.bfloat16):
+        kept, got = line.after(self.kept, self.got)
+        total = kept.astype(jnp.float32) + got.astype(jnp.float32)
+        self.stage += 1
+        if self.stage == len(self.perms):
+            self.done = total[0]
+            line.mark(self.done)
+            return
+        total = total.astype(wide)
+        half = total.shape[0] // 2
+        sent = total[half:]
+        self.kept = total[:half]
+        line.mark(sent)
+        self.got = send(sent, self.perms[self.stage])
 
 
 def per_device(ndp, nfs,
@@ -539,65 +667,243 @@
 ):
     n = ndp * nfs
     perms = stage_perms(ndp, nfs)
+    gather_perms = perms[:0:-1]
+    core_perm = perms[0]
+    stages = len(gather_perms)
+    table = shard_table(ndp, nfs)
     me = lax.axis_index("dp") * nfs + lax.axis_index("fsdp")
-    row = lax.dynamic_slice(jnp.asarray(shard_table(ndp, nfs)), (me, 0), (1, n))[0]
+    both = np.concatenate([table, np.argsort(table, axis=1).astype(np.int32)], axis=1)
+    both = lax.dynamic_slice(jnp.asarray(both), (me, 0), (1, 2 * n))[0]
+    row, inverse_row = both[:n], both[n:]
+    rows_in, width = tokens.shape[1:]
+    r_in, r_ff = w_up.shape[0], w_down.shape[0]
+    hidden = w_up.shape[1]
+    half_ff = r_ff // 2
+
     vectors = (ln1_gain, ln1_bias, bias_q, bias_v, bias_out, ln2_gain, ln2_bias, bias_down, bias_up)
     sizes = [v.shape[0] for v in vectors]
-    width = -(-sum(sizes) // 128) * 128
-    packed = jnp.pad(jnp.concatenate(vectors), (0, width - sum(sizes)))[None]
-    got_small = gather_relative(packed, perms)
-    got_qkv = gather_relative(w_qkv, perms)
-    got_out = gather_relative(w_out, perms)
-    got_up = gather_relative(w_up, perms)
-    got_down = gather_relative(w_down, perms)
-    full_small = jnp.zeros_like(got_small).at[row].set(got_small)[:, 0]
-    parts = []
-    offset = 0
-    for size in sizes:
-        parts.append(vec(full_small[:, offset : offset + size]))
-        offset += size
-    g1, s1, bq, bv, bo, g2, s2, bd, bu = parts
-    flat = lambda got: place_blocks([got], row, True)[0].reshape(-1, got.shape[-1])
-    w = dict(g1=g1, s1=s1, bo=bo, g2=g2, s2=s2, bd=bd, bu=bu)
-    w["bqkv"] = jnp.concatenate([bq, jnp.zeros_like(bq), bv], axis=1)
-    w["qkv"] = flat(got_qkv)
-    w["out"] = flat(got_out)
-    w["up"] = flat(got_up)
-    w["down"] = flat(got_down)
-    first, saved_first = layer_forward(tokens[0], w)
-    second, saved_second = layer_forward(first, w)
+    packed = jnp.stack([jnp.pad(v.astype(jnp.float32), (0, 128 - v.shape[0])) for v in vectors])
+
+    line = Line()
+    first_cols = jnp.concatenate([w_qkv, w_out], axis=1)
+    mid = first_cols.shape[1] // 2
+    shards = [
+        first_cols[:, :mid],
+        first_cols[:, mid:],
+        w_up[:, : hidden // 2],
+        w_up[:, hidden // 2 :],
+        w_down[:half_ff],
+        w_down[half_ff:],
+    ]
+    small = packed[None]
+    held = [s[None] for s in shards]
+    got = [None] * len(shards)
+    pieces = [None] * len(shards)
+
+    def gather_round(index):
+        nonlocal small
+        for i in range(len(shards)):
+            k = index - i
+            if k < 0 or k > stages:
+                continue
+            if 0 < k < stages:
+                mine, theirs = line.after(held[i], got[i])
+                held[i] = jnp.concatenate([mine, theirs], axis=0)
+                line.mark(held[i])
+            if k < stages:
+                got[i] = send(held[i], gather_perms[k])
+            if k == stages - 1:
+                pieces[i] = [held[i], None, send(held[i], core_perm), None]
+            if k == stages:
+                pieces[i][1] = got[i]
+                pieces[i][3] = send(got[i], core_perm)
+        if index < stages:
+            theirs = send(small, gather_perms[index])
+            small = jnp.concatenate([small, theirs], axis=0)
+        elif index == stages:
+            small = jnp.concatenate([small, send(small, core_perm)], axis=0)
+
+    def place(which, shapes, slots):
+        flat = [p for i in which for p in pieces[i]]
+        flat = line.after(*flat)
+        groups = [flat[4 * i : 4 * i + 4] for i in range(len(which))]
+        outs = place_shards(groups, row, shapes, slots)
+        line.mark(outs[0])
+        return outs
+
+    w = {}
+    for index in range(stages + 2):
+        gather_round(index)
+    g1, s1, bqkv, bo, g2, s2, bd, bu = unpack_vectors(
+        small, inverse_row, sizes, [[0], [1], [2, None, 3], [4], [5], [6], [7], [8]]
+    )
+    qkv_cols = w_qkv.shape[1]
+    (first_full,) = place([0, 1], [(n, r_in, 2 * mid)], [(0, None, 0), (0, None, mid)])
+    first_full = first_full.reshape(n * r_in, 2 * mid)
+    w["first"] = first_full
+
+    def forward(x, before=None):
+        a1, qkv = norm_project(*line.after(x), g1, s1, w["first"], bqkv, 512, qkv_cols)
+        line.mark(a1)
+        if before:
+            before()
+        o, logs = attention(*line.after(qkv))
+        line.mark(o)
+        if before:
+            before()
+        x1, a2 = project_norm(*line.after(o), w["first"], bo, x, g2, s2, qkv_cols)
+        line.mark(a2)
+        if before:
+            before()
+        a2 = line.after(a2)[0]
+        g, gp, y = feed_forward(a2, w["up"], bu, w["down"], bd, x1, 512)
+        line.mark(y)
+        return y, (x, a1, qkv, logs, o, x1, a2, g, gp)
+
+    calls = [0]
+
+    def more():
+        calls[0] += 1
+        gather_round(stages + 1 + calls[0])
+        if calls[0] == 2:
+            (up,) = place([2, 3], [(n, r_in, hidden)], [(0, None, 0), (0, None, hidden // 2)])
+            w["up"] = up.reshape(n * r_in, hidden)
+        if calls[0] == 3:
+            gather_round(stages + 5)
+            (down,) = place([4, 5], [(n, 2, half_ff, width)], [(0, 0, 0), (0, 1, 0)])
+            w["down"] = down.reshape(n * r_ff, width)
+
+    first, saved_first = forward(tokens[0], more)
+    second, saved_second = forward(first)
+
     keep_mask = valid[0].astype(jnp.float32)[:, None]
     grad_second = cot_second[0].astype(jnp.float32) * keep_mask
-    grad_first, mats_second, sums_second = layer_back(
-        grad_second, saved_second, w, (cot_first[0], keep_mask), jnp.float32
+    pairs = width // (2 * HEAD_DIM)
+    parts = 2
+
+    def ff_back(dy, saved):
+        x, a1, qkv, logs, o, x1, a2, g, gp = saved
+        outs = feed_forward_back(
+            *line.after(dy), gp, w["down"], w["up"], x1, g2, w["first"], qkv_cols, 512
+        )
+        line.mark(outs[0])
+        return outs
+
+    def heads_back(saved, d_o, i):
+        outs = attention_back(
+            saved[2], saved[3], *line.after(d_o), i * pairs // parts, pairs // parts
+        )
+        line.mark(outs[0])
+        return outs
+
+    def qkv_back(heads, saved, dx1, extra, dtype):
+        dx, cg, cs = project_back(
+            [line.after(h[0])[0] for h in heads], w["first"], saved[0], g1, dx1, extra, dtype
+        )
+        line.mark(dx)
+        return dx, cg, cs
+
+    dm2, du2, dx2, da2, do2, cdm2, cdu2, cda2, cg22, cs22 = ff_back(grad_second, saved_second)
+    heads2 = [heads_back(saved_second, do2, i) for i in range(parts)]
+    grad_first, cg12, cs12 = qkv_back(
+        heads2, saved_second, dx2, (cot_first[0], keep_mask), jnp.float32
     )
-    grad_inputs, mats_first, sums_first = layer_back(
-        grad_first, saved_first, w, None, jnp.bfloat16
+
+    local = (row // nfs) // 2 * nfs + row % nfs
+    half = n // 2
+    tiles = ndp // 2
+    core = (me // nfs) % 2
+    lanes = 2 * jnp.arange(tiles, dtype=jnp.int32)
+    index_keep = jnp.concatenate([lanes + core, local[:half]]).astype(jnp.int32)
+    index_send = jnp.concatenate([lanes + (1 - core), local[half:]]).astype(jnp.int32)
+
+    def grad_send(lefts, rights, r, tn):
+        lefts = line.after(*lefts)
+        (out,) = weight_grad_half(lefts, rights, index_send, (ndp, nfs, r), tn)
+        line.mark(out)
+        return send(out, core_perm)
+
+    def grad_keep(lefts, rights, r, tn, arrived):
+        arrived = line.after(arrived)[0]
+        kept, sent = weight_grad_half(lefts, rights, index_keep, (ndp, nfs, r), tn, arrived)
+        line.mark(sent)
+        return kept, sent
+
+    dm1 = grad_first.astype(jnp.bfloat16)
+    sg = list(zip(saved_first, saved_second))
+    arrived = grad_send(sg[7], (dm1, dm2), r_ff, 256)
+    red_down = Reduction(perms, *grad_keep(sg[7], (dm1, dm2), r_ff, 256, arrived), 1)
+    _, du1, dx1, da1, do1, cdm1, cdu1, cda1, cg21, cs21 = ff_back(grad_first, saved_first)
+    red_down.step(line)
+    arrived = grad_send(sg[6], (du1, du2), r_in, 1024)
+    red_down.step(line)
+    red_up = Reduction(perms, *grad_keep(sg[6], (du1, du2), r_in, 1024, arrived), 1)
+    red_down.step(line)
+    arrived_out = grad_send(sg[4], (da1, da2), r_in, 1024)
+    heads1 = [heads_back(saved_first, do1, 0)]
+    kept_out, sent_out = grad_keep(sg[4], (da1, da2), r_in, 1024, arrived_out)
+    red_down.step(line)
+    rights = lambda i: (heads1[i][0], heads2[i][0])
+    arrived = grad_send(sg[1], rights(0), r_in, 512)
+    red_up.step(line)
+    kept_q, sent_q = grad_keep(sg[1], rights(0), r_in, 512, arrived)
+    red_one = Reduction(
+        perms,
+        jnp.concatenate([kept_out, kept_q], axis=2),
+        jnp.concatenate([sent_out, sent_q], axis=2),
+        1,
     )
-    dm, du, da, dq, dk, dv = zip(mats_first, mats_second)
-    saved = list(zip(saved_first, saved_second))
-
-    def reduce_matrix(total):
-        (rel,) = place_blocks([total.reshape(n, total.shape[0] // n, total.shape[1])], row, False)
-        return reduce_relative(rel, perms)
-
-    d_down = reduce_matrix(weight_grad(saved[7], dm, 512, 512))
-    d_up = reduce_matrix(weight_grad(saved[6], du, 512, 512))
-    d_out = reduce_matrix(weight_grad(saved[4], da, 512, 512))
-    d_qkv = reduce_matrix(
-        jnp.concatenate([weight_grad(saved[1], d, 512, 512) for d in (dq, dk, dv)], axis=1)
+    heads1.append(heads_back(saved_first, do1, 1))
+    red_up.step(line)
+    arrived = grad_send(sg[1], rights(1), r_in, 512)
+    red_two = Reduction(perms, *grad_keep(sg[1], rights(1), r_in, 512, arrived), 1)
+    red_one.step(line)
+    red_up.step(line)
+    grad_inputs, cg11, cs11 = qkv_back(heads1, saved_first, dx1, None, jnp.bfloat16)
+    red_one.step(line)
+    red_two.step(line)
+    cq = [[h[i][1] for h in (heads1, heads2)] for i in range(parts)]
+    cv = [[h[i][2] for h in (heads1, heads2)] for i in range(parts)]
+    joined = lambda c: [jnp.concatenate([c[i][s] for i in range(parts)], axis=1) for s in range(2)]
+    sums = pack_sums(
+        [
+            [cg11, cg12],
+            [cs11, cs12],
+            joined(cq),
+            joined(cv),
+            [cda1, cda2],
+            [cg21, cg22],
+            [cs21, cs22],
+            [cdm1, cdm2],
+            [cdu1, cdu2],
+        ],
+        inverse_row,
+        n,
+        len(vectors),
     )
-    small = jnp.concatenate(
-        [(a + b).reshape(n, -1) for a, b in zip(sums_first, sums_second)], axis=1
-    )
-    small = jnp.pad(small, ((0, 0), (0, width - small.shape[1])))[:, None]
-    small = reduce_relative(small[row], perms, jnp.float32)[0]
-    outs = []
-    offset = 0
-    for size in sizes:
-        outs.append(small[offset : offset + size])
-        offset += size
+    red_small = Reduction(perms, sums[:half], sums[half:], 0)
+    red_up.step(line)
+    for _ in range(stages):
+        for red in (red_one, red_two):
+            if red.done is None:
+                red.step(line)
+        if red_small.done is None:
+            red_small.step(line, jnp.float32)
+    for red in (red_down, red_up, red_one, red_two):
+        while red.done is None:
+            red.step(line)
+    while red_small.done is None:
+        red_small.step(line, jnp.float32)
+    outs = [red_small.done[i, : sizes[i]] for i in range(len(vectors))]
     o_g1, o_s1, o_bq, o_bv, o_bo, o_g2, o_s2, o_bd, o_bu = outs
+    one = red_one.done
+    d_out = one[:, :width]
+    third = width // parts
+    blocks = []
+    for kind in range(3):
+        blocks.append(one[:, width + kind * third : width + (kind + 1) * third])
+        blocks.append(red_two.done[:, kind * third : (kind + 1) * third])
+    d_qkv = jnp.concatenate(blocks, axis=1)
     return (
         first[None],
         second[None],
@@ -611,9 +917,9 @@
         o_bo,
         o_g2,
         o_s2,
-        d_up,
+        red_up.done,
         o_bu,
-        d_down,
+        red_down.done,
         o_bd,
     )
 

time: 719 us -> 572 us (0.80)
  waiting for transfers between devices: 207 us -> 135 us
  local copies, waits for them, and re-layouts: 82.3 us -> 31.2 us
  other arithmetic: 41.1 us -> 25 us
    ppermute x50 -> x67, waiting for transfers between devices: 207 us -> 135 us  [send(): return lax.ppermute(x, AXES, perm)]
    concatenate x13 -> x20, local copies, waits for them, and re-layouts: 33.2 us -> 9.01 us  [the longest x17 7.7 us: gather_round(): held[i] = jnp.concatenate([mine, theirs], axis=0)]
    slice x27 -> x20, local copies, waits for them, and re-layouts: 19.9 us -> 4.04 us  [the longest x16 1.73 us: step(): self.kept = total[:half]]
    unnamed x94 -> x89, local copies, waits for them, and re-layouts: 19.7 us -> 10 us
    convert_element_type x16 -> x13, other arithmetic: 18.1 us -> 13 us  [the longest x12 10.2 us: step(): total = total.astype(wide)]
    pallas_call x18 -> x21, Pallas kernels: 158 us -> 153 us  [the longest x10 77.5 us: weight_grad_half(): pl.pallas_call(body, grid_spec=pltpu.PrefetchScalarGridSpec(num_scalar_pr...]
    ppermute x50 -> x67, starting transfers between devices: 63.5 us -> 64.7 us  [send(): return lax.ppermute(x, AXES, perm)]
  transfers between devices with their start and end apart: 50 -> 67, of which waited for: 19 -> 28; matrix products, arithmetic and copies ran while one was open for 14% -> 8% of each run, Pallas kernels for 17% -> 24%
where the time goes in v4:
time: 572 us; the launch traced here: 567 us
  Pallas kernels  309 us (54%)
  waiting for transfers between devices  135 us (24%)
  starting transfers between devices  64.7 us (11%)
  local copies, waits for them, and re-layouts  31.2 us (5%)
  other arithmetic  25 us (4%)
    ppermute x67, waiting for transfers between devices, send(): return lax.ppermute(x, AXES, perm)  135 us
    pallas_call x10, Pallas kernels, weight_grad_half(): pl.pallas_call(body, grid_spec=pltpu.PrefetchScalarGridSpec(num_scalar_pr...  77.5 us
    ppermute x67, starting transfers between devices, send(): return lax.ppermute(x, AXES, perm)  64.7 us
    pallas_call x2, Pallas kernels, feed_forward(): pl.pallas_call(body, grid=(steps,), in_specs=[whole((rows, width)), pl.Bl...  47.7 us
    pallas_call x2, Pallas kernels, feed_forward_back(): pl.pallas_call(body, grid=(steps,), in_specs=[full, pl.BlockSpec((rows, t...  44 us
    pallas_call x4, Pallas kernels, attention_back(): pl.pallas_call(body, grid=(pairs,), in_specs=[col(first_pair), col(every...  35.7 us
    pallas_call x2, Pallas kernels, attention(): pl.pallas_call(body, grid=(pairs,), in_specs=[col(0), col(pairs), col(2 *...  25.6 us
    pallas_call x3, Pallas kernels, place_shards(): pl.pallas_call(body, out_shape=[jax.ShapeDtypeStruct(s, jnp.bfloat16) for...  25 us
  transfers between devices with their start and end apart: 67, of which 28 were waited for; matrix products, arithmetic and copies ran while one was open for 8% of the time, Pallas kernels for 24%

profile of v4, /device:TPU:0, one launch (start us, length us, event | category | flops | bytes accessed | tf_op | source)
XLA Modules:
  0.0 566.6 jit_solution(17044322726907574027)
XLA Ops:
  1.6 4.1 collective-permute-start
  6.8 2.9 collective-permute-start.5
  13.2 2.8 collective-permute-start.18
  18.4 10.9 %collective-permute-done.18 = f32[1,9,128]{2,1,0:T(8,128)S(1)} collective-permute-done((f32[1,9,128]{2,1,0:T(8,128)S(1)}, f32[1,9,128]{2,1,0:T(8,128)S(1)}, u32[]{:S(2)}, u32[]{:S(2)}) %collective-permute-start.18) | collective-permute-done | bytes 4640 | tf_op jit(solution)/shard_map/ppermute | solution.py:499
  35.3 2.9 collective-permute-done.1
  41.9 5.6 collective-permute-done.3
  51.9 11.2 %collective-permute-done.6 = bf16[4,32,2048]{2,1,0:T(8,128)(2,1)S(1)} collective-permute-done((bf16[4,32,2048]{2,1,0:T(8,128)(2,1)S(1)}, bf16[4,32,2048]{2,1,0:T(8,128)(2,1)S(1)}, u32[]{:S(2)}, u32[]{:S(2)}) %collective-permute-start.6) | collective-permute-done | bytes 524320 | tf_op jit(solution)/shard_map/ppermute | solution.py:499
  68.0 11.2 %collective-permute-done.9 = bf16[4,32,2048]{2,1,0:T(8,128)(2,1)S(1)} collective-permute-done((bf16[4,32,2048]{2,1,0:T(8,128)(2,1)S(1)}, bf16[4,32,2048]{2,1,0:T(8,128)(2,1)S(1)}, u32[]{:S(2)}, u32[]{:S(2)}) %collective-permute-start.9) | collective-permute-done | bytes 524320 | tf_op jit(solution)/shard_map/ppermute | solution.py:499
  79.8 3.2 collective-permute-done.15.refs_5_
  83.0 1.8 collective-permute-start.17
  85.6 3.3 collective-permute-start.11
  89.6 5.1 collective-permute-done.11
  98.8 2.5 unpack_vectors.1
  103.8 8.3 %place_shards.3 = bf16[32,32,4096]{2,1,0:T(8,128)(2,1)} custom-call(s32[32]{0:T(128)} %get-tuple-element.488.t_ref, bf16[8,32,2048]{2,1,0:T(8,128)(2,1)} %copy-done.1, bf16[8,32,2048]{2,1,0:T(8,128)(2,1)} %collective-permute-done.12.refs_1_, bf16[8,32,2048]{2,1,0:T(8,128)(2,1)} %collective-permute-done.13.refs_2_, ...), custom_call_target="tpu_custom_call" | custom-call | tf_op jit(solution)/shard_map/place_shards/pallas_call | solution.py:551
  112.1 9.6 %norm_project.2 = (bf16[512,1024]{1,0:T(8,128)(2,1)}, bf16[512,3072]{1,0:T(8,128)(2,1)}) custom-call(bf16[512,1024]{1,0:T(8,128)(2,1)} %bitcast.98, f32[1,1024]{1,0:T(1,128)} %get-tuple-element.252.g_ref.refs_4_, f32[1,1024]{1,0:T(1,128)} %get-tuple-element.253.s_ref, bf16[1024,4096]{1,0:T(8,128)(2,1)} %bitcast.81, f32[1,3072]{1,0:T(1,128)} %get-tuple-element.254.b_ref), custom_call_target="tpu_custom_call" | custom-call | tf_op jit(solution)/shard_map/norm_project/pallas_call | solution.py:66
  125.5 6.5 %collective-permute-done.24 = bf16[2,64,1024]{2,1,0:T(8,128)(2,1)S(1)} collective-permute-done((bf16[2,64,1024]{2,1,0:T(8,128)(2,1)S(1)}, bf16[2,64,1024]{2,1,0:T(8,128)(2,1)S(1)}, u32[]{:S(2)}, u32[]{:S(2)}) %collective-permute-start.24) | collective-permute-done | bytes 262176 | tf_op jit(solution)/shard_map/ppermute | solution.py:499
  135.9 5.0 collective-permute-done.25
  140.9 3.5 collective-permute-done.31.refs_5_
  144.6 12.9 %attention.2 = (bf16[512,1024]{1,0:T(8,128)(2,1)}, f32[8,8,512]{2,1,0:T(8,128)}) custom-call(bf16[512,3072]{1,0:T(8,128)(2,1)} %get-tuple-element.263.q_ref.k_ref.v_ref, bf16[512,3072]{1,0:T(8,128)(2,1)} %get-tuple-element.263.q_ref.k_ref.v_ref, bf16[512,3072]{1,0:T(8,128)(2,1)} %get-tuple-element.263.q_ref.k_ref.v_ref), custom_call_target="tpu_custom_call" | custom-call | tf_op jit(solution)/shard_map/attention/pallas_call | solution.py:112
  163.5 8.3 %place_shards.4 = bf16[32,32,4096]{2,1,0:T(8,128)(2,1)} custom-call(s32[32]{0:T(128)} %get-tuple-element.488.t_ref, bf16[8,32,2048]{2,1,0:T(8,128)(2,1)} %copy-done, bf16[8,32,2048]{2,1,0:T(8,128)(2,1)} %collective-permute-done.28.refs_1_, bf16[8,32,2048]{2,1,0:T(8,128)(2,1)} %collective-permute-done.29.refs_2_, ...), custom_call_target="tpu_custom_call" | custom-call | tf_op jit(solution)/shard_map/place_shards/pallas_call | solution.py:551
  171.8 4.9 project_norm.2
  182.9 11.0 %collective-permute-done.38.refs_5_ = bf16[8,64,1024]{2,1,0:T(8,128)(2,1)S(1)} collective-permute-done((bf16[8,64,1024]{2,1,0:T(8,128)(2,1)S(1)}, bf16[8,64,1024]{2,1,0:T(8,128)(2,1)S(1)}, u32[]{:S(2)}, u32[]{:S(2)}) %collective-permute-start.38) | collective-permute-done | bytes 1048608 | tf_op jit(solution)/shard_map/ppermute | solution.py:499
  195.6 2.8 convert_multiply_fusion.dy_ref
  198.4 8.3 %place_shards.5 = bf16[32,2,64,1024]{3,2,1,0:T(8,128)(2,1)} custom-call(s32[32]{0:T(128)} %get-tuple-element.488.t_ref, bf16[8,64,1024]{2,1,0:T(8,128)(2,1)} %copy-done.4, bf16[8,64,1024]{2,1,0:T(8,128)(2,1)} %collective-permute-done.35.refs_1_, bf16[8,64,1024]{2,1,0:T(8,128)(2,1)} %collective-permute-done.36.refs_2_, ...), custom_call_target="tpu_custom_call" | custom-call | tf_op jit(solution)/shard_map/place_shards/pallas_call | solution.py:551
  206.7 23.8 %feed_forward.2 = (bf16[512,4096]{1,0:T(8,128)(2,1)}, bf16[512,4096]{1,0:T(8,128)(2,1)}, bf16[512,1024]{1,0:T(8,128)(2,1)}) custom-call(bf16[512,1024]{1,0:T(8,128)(2,1)} %get-tuple-element.332.a_ref.refs_0_.refs_1_, bf16[1024,4096]{1,0:T(8,128)(2,1)} %bitcast.89, f32[1,4096]{1,0:T(1,128)} %get-tuple-element.293.ub_ref, bf16[4096,1024]{1,0:T(8,128)(2,1)} %bitcast.93, ...), custom_call_target="tpu_custom_call" | custom-call | tf_op jit(solution)/shard_map/feed_forward/pallas_call | solution.py:228
  230.6 9.1 %norm_project.3 = (bf16[512,1024]{1,0:T(8,128)(2,1)}, bf16[512,3072]{1,0:T(8,128)(2,1)}) custom-call(bf16[512,1024]{1,0:T(8,128)(2,1)} %get-tuple-element.297.x_ref.refs_3_, f32[1,1024]{1,0:T(1,128)} %get-tuple-element.252.g_ref.refs_4_, f32[1,1024]{1,0:T(1,128)} %get-tuple-element.253.s_ref, bf16[1024,4096]{1,0:T(8,128)(2,1)} %bitcast.83, ...), custom_call_target="tpu_custom_call" | custom-call | tf_op jit(solution)/shard_map/norm_project/pallas_call | solution.py:66
  239.6 12.8 %attention.3 = (bf16[512,1024]{1,0:T(8,128)(2,1)}, f32[8,8,512]{2,1,0:T(8,128)}) custom-call(bf16[512,3072]{1,0:T(8,128)(2,1)} %get-tuple-element.298.q_ref.k_ref.v_ref, bf16[512,3072]{1,0:T(8,128)(2,1)} %get-tuple-element.298.q_ref.k_ref.v_ref, bf16[512,3072]{1,0:T(8,128)(2,1)} %get-tuple-element.298.q_ref.k_ref.v_ref), custom_call_target="tpu_custom_call" | custom-call | tf_op jit(solution)/shard_map/attention/pallas_call | solution.py:112
  252.4 5.0 project_norm.3
  257.4 23.8 %feed_forward.3 = (bf16[512,4096]{1,0:T(8,128)(2,1)}, bf16[512,4096]{1,0:T(8,128)(2,1)}, bf16[512,1024]{1,0:T(8,128)(2,1)}) custom-call(bf16[512,1024]{1,0:T(8,128)(2,1)} %get-tuple-element.333.a_ref.refs_2_.refs_3_, bf16[1024,4096]{1,0:T(8,128)(2,1)} %bitcast.90, f32[1,4096]{1,0:T(1,128)} %get-tuple-element.293.ub_ref, bf16[4096,1024]{1,0:T(8,128)(2,1)} %bitcast.94, ...), custom_call_target="tpu_custom_call" | custom-call | tf_op jit(solution)/shard_map/feed_forward/pallas_call | solution.py:228
  281.3 22.0 %feed_forward_back.2 = (bf16[512,1024]{1,0:T(8,128)(2,1)}, bf16[512,4096]{1,0:T(8,128)(2,1)}, f32[512,1024]{1,0:T(8,128)}, bf16[512,1024]{1,0:T(8,128)(2,1)}, bf...) custom-call(f32[512,1024]{1,0:T(8,128)} %convert_multiply_fusion.dy_, ...), custom_call_target="tpu_custom_call" | custom-call | tf_op jit(solution)/shard_map/feed_forward_back/pallas_call | solution.py:296
  303.3 8.9 %attention_back.4 = (bf16[3,512,512]{2,1,0:T(8,128)(2,1)}, f32[1,512]{1,0:T(1,128)}, f32[1,512]{1,0:T(1,128)}) custom-call(bf16[512,3072]{1,0:T(8,128)(2,1)} %get-tuple-element.298.q_ref.k_ref.v_ref, bf16[512,3072]{1,0:T(8,128)(2,1)} %get-tuple-element.298.q_ref.k_ref.v_ref, bf16[512,3072]{1,0:T(8,128)(2,1)} %get-tuple-element.298.q_ref.k_ref.v_ref, ...), custom_call_target="tpu_custom_call" | custom-call | tf_op jit(solution)/shard_map/attention_back/pallas_call | solution.py:160
  312.2 9.0 %attention_back.5 = (bf16[3,512,512]{2,1,0:T(8,128)(2,1)}, f32[1,512]{1,0:T(1,128)}, f32[1,512]{1,0:T(1,128)}) custom-call(bf16[512,3072]{1,0:T(8,128)(2,1)} %get-tuple-element.298.q_ref.k_ref.v_ref, bf16[512,3072]{1,0:T(8,128)(2,1)} %get-tuple-element.298.q_ref.k_ref.v_ref, bf16[512,3072]{1,0:T(8,128)(2,1)} %get-tuple-element.298.q_ref.k_ref.v_ref, ...), custom_call_target="tpu_custom_call" | custom-call | tf_op jit(solution)/shard_map/attention_back/pallas_call | solution.py:160
  321.2 10.2 %project_back.2 = (f32[512,1024]{1,0:T(8,128)}, f32[1,1024]{1,0:T(1,128)}, f32[1,1024]{1,0:T(1,128)}) custom-call(bf16[3,512,512]{2,1,0:T(8,128)(2,1)} %get-tuple-element.317.refs_0_.refs_5_, bf16[3,512,512]{2,1,0:T(8,128)(2,1)} %get-tuple-element.318.refs_1_.refs_5_, bf16[1024,4096]{1,0:T(8,128)(2,1)} %bitcast.86, ...), custom_call_target="tpu_custom_call" | custom-call | tf_op jit(solution)/shard_map/project_back/pallas_call | solution.py:385
  331.4 2.8 convert_element_type.181.refs_4_
  334.2 10.0 %weight_grad.10 = bf16[16,128,1024]{2,1,0:T(8,128)(2,1)} custom-call(s32[18]{0:T(128)} %pad_add_fusion.1.i_ref, bf16[512,4096]{1,0:T(8,128)(2,1)} %get-tuple-element.321.refs_0_.refs_1_, bf16[512,4096]{1,0:T(8,128)(2,1)} %get-tuple-element.321.refs_0_.refs_1_, bf16[512,4096]{1,0:T(8,128)(2,1)} %get-tuple-element.322.refs_2_.refs_3_, ...), custom_call_target="tpu_custom_call" | custom-call | tf_op jit(solution)/shard_map/weight_grad/pallas_call | solution.py:443
  345.1 6.6 %collective-permute-done.41.refs_6_ = bf16[16,128,1024]{2,1,0:T(8,128)(2,1)} collective-permute-done((bf16[16,128,1024]{2,1,0:T(8,128)(2,1)}, bf16[16,128,1024]{2,1,0:T(8,128)(2,1)}, u32[]{:S(2)}, u32[]{:S(2)}) %collective-permute-start.41) | collective-permute-done | bytes 4194336 | tf_op jit(solution)/shard_map/ppermute | solution.py:499
  351.7 10.8 %weight_grad.11 = (bf16[8,128,1024]{2,1,0:T(8,128)(2,1)}, bf16[8,128,1024]{2,1,0:T(8,128)(2,1)}) custom-call(s32[18]{0:T(128)} %pad_add_fusion.i_ref, bf16[512,4096]{1,0:T(8,128)(2,1)} %get-tuple-element.321.refs_0_.refs_1_, bf16[512,4096]{1,0:T(8,128)(2,1)} %get-tuple-element.321.refs_0_.refs_1_, bf16[512,4096]{1,0:T(8,128)(2,1)} %get-tuple-element.322.refs_2_.refs_3_, ...), custom_call_target="tpu_custom_call" | custom-call | tf_op jit(solution)/shard_map/weight_grad/pallas_call | solution.py:443
  364.3 22.0 %feed_forward_back.3 = (bf16[512,1024]{1,0:T(8,128)(2,1)}, bf16[512,4096]{1,0:T(8,128)(2,1)}, f32[512,1024]{1,0:T(8,128)}, bf16[512,1024]{1,0:T(8,128)(2,1)}, bf...) custom-call(f32[512,1024]{1,0:T(8,128)} %get-tuple-element.325.dy_re, ...), custom_call_target="tpu_custom_call" | custom-call | tf_op jit(solution)/shard_map/feed_forward_back/pallas_call | solution.py:296
  386.3 2.6 collective-permute-done.42
  388.8 2.6 add_convert_fusion.1
  391.6 10.1 %weight_grad.12 = bf16[16,32,4096]{2,1,0:T(8,128)(2,1)} custom-call(s32[18]{0:T(128)} %pad_add_fusion.1.i_ref, bf16[512,1024]{1,0:T(8,128)(2,1)} %get-tuple-element.332.a_ref.refs_0_.refs_1_, bf16[512,1024]{1,0:T(8,128)(2,1)} %get-tuple-element.332.a_ref.refs_0_.refs_1_, bf16[512,1024]{1,0:T(8,128)(2,1)} %get-tuple-element.333.a_ref.refs_2_.refs_3_, ...), custom_call_target="tpu_custom_call" | custom-call | tf_op jit(solution)/shard_map/weight_grad/pallas_call | solution.py:443
  401.8 2.0 collective-permute-start.43
  403.8 12.9 %collective-permute-done.43 = bf16[4,128,1024]{2,1,0:T(8,128)(2,1)S(1)} collective-permute-done((bf16[4,128,1024]{2,1,0:T(8,128)(2,1)S(1)}, bf16[4,128,1024]{2,1,0:T(8,128)(2,1)S(1)}, u32[]{:S(2)}, u32[]{:S(2)}) %collective-permute-start.43) | collective-permute-done | bytes 1048608 | tf_op jit(solution)/shard_map/ppermute | solution.py:499
  417.1 2.2 collective-permute-start.45
  419.3 10.9 %weight_grad.13 = (bf16[8,32,4096]{2,1,0:T(8,128)(2,1)}, bf16[8,32,4096]{2,1,0:T(8,128)(2,1)}) custom-call(s32[18]{0:T(128)} %pad_add_fusion.i_ref, bf16[512,1024]{1,0:T(8,128)(2,1)} %get-tuple-element.332.a_ref.refs_0_.refs_1_, bf16[512,1024]{1,0:T(8,128)(2,1)} %get-tuple-element.332.a_ref.refs_0_.refs_1_, ...), custom_call_target="tpu_custom_call" | custom-call | tf_op jit(solution)/shard_map/weight_grad/pallas_call | solution.py:443
  432.0 4.9 weight_grad.14
  437.0 2.4 collective-permute-start.47
  439.4 8.9 %attention_back.6 = (bf16[3,512,512]{2,1,0:T(8,128)(2,1)}, f32[1,512]{1,0:T(1,128)}, f32[1,512]{1,0:T(1,128)}) custom-call(bf16[512,3072]{1,0:T(8,128)(2,1)} %get-tuple-element.263.q_ref.k_ref.v_ref, bf16[512,3072]{1,0:T(8,128)(2,1)} %get-tuple-element.263.q_ref.k_ref.v_ref, bf16[512,3072]{1,0:T(8,128)(2,1)} %get-tuple-element.263.q_ref.k_ref.v_ref, ...), custom_call_target="tpu_custom_call" | custom-call | tf_op jit(solution)/shard_map/attention_back/pallas_call | solution.py:160
  449.3 5.2 weight_grad.15
  455.4 6.2 %weight_grad.16 = bf16[16,32,1536]{2,1,0:T(8,128)(2,1)} custom-call(s32[18]{0:T(128)} %pad_add_fusion.1.i_ref, bf16[512,1024]{1,0:T(8,128)(2,1)} %get-tuple-element.362.refs_0_.refs_1_, bf16[512,1024]{1,0:T(8,128)(2,1)} %get-tuple-element.362.refs_0_.refs_1_, bf16[512,1024]{1,0:T(8,128)(2,1)} %get-tuple-element.363.refs_2_.refs_3_, ...), custom_call_target="tpu_custom_call" | custom-call | tf_op jit(solution)/shard_map/weight_grad/pallas_call | solution.py:443
  461.8 2.4 add_convert_fusion
  466.2 6.5 %weight_grad.17 = (bf16[8,32,1536]{2,1,0:T(8,128)(2,1)}, bf16[8,32,1536]{2,1,0:T(8,128)(2,1)}) custom-call(s32[18]{0:T(128)} %pad_add_fusion.i_ref, bf16[512,1024]{1,0:T(8,128)(2,1)} %get-tuple-element.362.refs_0_.refs_1_, bf16[512,1024]{1,0:T(8,128)(2,1)} %get-tuple-element.362.refs_0_.refs_1_, bf16[512,1024]{1,0:T(8,128)(2,1)} %get-tuple-element.363.refs_2_.refs_3_, ...), custom_call_target="tpu_custom_call" | custom-call | tf_op jit(solution)/shard_map/weight_grad/pallas_call | solution.py:443
  472.7 8.9 %attention_back.7 = (bf16[3,512,512]{2,1,0:T(8,128)(2,1)}, f32[1,512]{1,0:T(1,128)}, f32[1,512]{1,0:T(1,128)}) custom-call(bf16[512,3072]{1,0:T(8,128)(2,1)} %get-tuple-element.263.q_ref.k_ref.v_ref, bf16[512,3072]{1,0:T(8,128)(2,1)} %get-tuple-element.263.q_ref.k_ref.v_ref, bf16[512,3072]{1,0:T(8,128)(2,1)} %get-tuple-element.263.q_ref.k_ref.v_ref, ...), custom_call_target="tpu_custom_call" | custom-call | tf_op jit(solution)/shard_map/attention_back/pallas_call | solution.py:160
  482.8 6.2 %weight_grad.18 = bf16[16,32,1536]{2,1,0:T(8,128)(2,1)} custom-call(s32[18]{0:T(128)} %pad_add_fusion.1.i_ref, bf16[512,1024]{1,0:T(8,128)(2,1)} %get-tuple-element.362.refs_0_.refs_1_, bf16[512,1024]{1,0:T(8,128)(2,1)} %get-tuple-element.362.refs_0_.refs_1_, bf16[512,1024]{1,0:T(8,128)(2,1)} %get-tuple-element.363.refs_2_.refs_3_, ...), custom_call_target="tpu_custom_call" | custom-call | tf_op jit(solution)/shard_map/weight_grad/pallas_call | solution.py:443
  495.6 6.7 %weight_grad.19 = (bf16[8,32,1536]{2,1,0:T(8,128)(2,1)}, bf16[8,32,1536]{2,1,0:T(8,128)(2,1)}) custom-call(s32[18]{0:T(128)} %pad_add_fusion.i_ref, bf16[512,1024]{1,0:T(8,128)(2,1)} %get-tuple-element.362.refs_0_.refs_1_, bf16[512,1024]{1,0:T(8,128)(2,1)} %get-tuple-element.362.refs_0_.refs_1_, bf16[512,1024]{1,0:T(8,128)(2,1)} %get-tuple-element.363.refs_2_.refs_3_, ...), custom_call_target="tpu_custom_call" | custom-call | tf_op jit(solution)/shard_map/weight_grad/pallas_call | solution.py:443
  502.3 5.9 %collective-permute-done.52 = bf16[8,32,2560]{2,1,0:T(8,128)(2,1)} collective-permute-done((bf16[8,32,2560]{2,1,0:T(8,128)(2,1)}, bf16[8,32,2560]{2,1,0:T(8,128)(2,1)}, u32[]{:S(2)}, u32[]{:S(2)}) %collective-permute-start.52) | collective-permute-done | bytes 1310752 | tf_op jit(solution)/shard_map/ppermute | solution.py:499
  513.5 9.3 %project_back.3 = (bf16[512,1024]{1,0:T(8,128)(2,1)}, f32[1,1024]{1,0:T(1,128)}, f32[1,1024]{1,0:T(1,128)}) custom-call(bf16[3,512,512]{2,1,0:T(8,128)(2,1)} %get-tuple-element.372.refs_4_.refs_0_, bf16[3,512,512]{2,1,0:T(8,128)(2,1)} %get-tuple-element.373.refs_4_.refs_1_, bf16[1024,4096]{1,0:T(8,128)(2,1)} %bitcast.88, bf16[512,1024]{1,0:T(8,128)(2,1)} %bitcast.100, ...), custom_call_target="tpu_custom_call" | custom-call | tf_op jit(solution)/shard_map/project_back/pallas_call | solution.py:385
  522.7 2.5 pack_sums.1
  532.2 5.6 collective-permute-done.57
  537.9 2.9 collective-permute-start.60
  542.7 5.8 %collective-permute-done.60 = bf16[1,32,2560]{2,1,0:T(8,128)(2,1)S(1)} collective-permute-done((bf16[1,32,2560]{2,1,0:T(8,128)(2,1)S(1)}, bf16[1,32,2560]{2,1,0:T(8,128)(2,1)S(1)}, u32[]{:S(2)}, u32[]{:S(2)}) %collective-permute-start.60) | collective-permute-done | bytes 163872 | tf_op jit(solution)/shard_map/ppermute | solution.py:499
  551.3 5.5 collective-permute-done.63
  557.0 3.8 collective-permute-done.65
  561.1 4.2 collective-permute-done.66
  (283 shorter events, 92.5 us)
Async XLA Ops:
  1.6 28.3 %collective-permute-start = (bf16[1,32,2048]{2,1,0:T(8,128)(2,1)S(1)}, bf16[1,32,2048]{2,1,0:T(8,128)(2,1)S(1)}, u32[]{:S(2)}, u32[]{:S(2)}) collective-permute-start(bf16[1,32,2048]{2,1,0:T(8,128)(2,1)S(1)} %get-tuple-element.456), channel_id=1, source_target_pairs={{0,4},{1,5},{2,6},{3,7},{4,0},{5,1},{6,2},{7,3},{8,12},{9,13},{10,... | collective-permute-start | bytes 393224 | tf_op jit(solution)/shard_map/ppermute | solution.py:499
  5.7 35.7 %collective-permute-start.2 = (bf16[1,32,2048]{2,1,0:T(8,128)(2,1)S(1)}, bf16[1,32,2048]{2,1,0:T(8,128)(2,1)S(1)}, u32[]{:S(2)}, u32[]{:S(2)}) collective-permute-start(bf16[1,32,2048]{2,1,0:T(8,128)(2,1)S(1)} %get-tuple-element.223), channel_id=1, source_target_pairs={{0,4},{1,5},{2,6},{3,7},{4,0},{5,1},{6,2},{7,3},{8,12},{9,13},{10,... | collective-permute-start | bytes 393224 | tf_op jit(solution)/shard_map/ppermute | solution.py:499
  6.8 44.6 %collective-permute-start.5 = (bf16[1,32,2048]{2,1,0:T(8,128)(2,1)S(1)}, bf16[1,32,2048]{2,1,0:T(8,128)(2,1)S(1)}, u32[]{:S(2)}, u32[]{:S(2)}) collective-permute-start(bf16[1,32,2048]{2,1,0:T(8,128)(2,1)S(1)} %get-tuple-element.229), channel_id=1, source_target_pairs={{0,4},{1,5},{2,6},{3,7},{4,0},{5,1},{6,2},{7,3},{8,12},{9,13},{10,... | collective-permute-start | bytes 393224 | tf_op jit(solution)/shard_map/ppermute | solution.py:499
  9.7 56.8 %collective-permute-start.8 = (bf16[1,32,2048]{2,1,0:T(8,128)(2,1)S(1)}, bf16[1,32,2048]{2,1,0:T(8,128)(2,1)}, u32[]{:S(2)}, u32[]{:S(2)}) collective-permute-start(bf16[1,32,2048]{2,1,0:T(8,128)(2,1)S(1)} %get-tuple-element.235), channel_id=1, source_target_pairs={{0,4},{1,5},{2,6},{3,7},{4,0},{5,1},{6,2},{7,3},{8,12},{9,13},{10,... | collective-permute-start | bytes 393224 | tf_op jit(solution)/shard_map/ppermute | solution.py:499
  13.2 16.1 %collective-permute-start.18 = (f32[1,9,128]{2,1,0:T(8,128)S(1)}, f32[1,9,128]{2,1,0:T(8,128)S(1)}, u32[]{:S(2)}, u32[]{:S(2)}) collective-permute-start(f32[1,9,128]{2,1,0:T(8,128)S(1)} %bitcast_convert_fusion), channel_id=1, source_target_pairs={{0,4},{1,5},{2,6},{3,7},{4,0},{5,1},{6,2},{7,3},{8,12},{9,13},{10,... | collective-permute-start | bytes 13832 | tf_op jit(solution)/shard_map/ppermute | solution.py:499
  30.0 8.2 %collective-permute-start.1 = (bf16[2,32,2048]{2,1,0:T(8,128)(2,1)S(1)}, bf16[2,32,2048]{2,1,0:T(8,128)(2,1)S(1)}, u32[]{:S(2)}, u32[]{:S(2)}) collective-permute-start(bf16[2,32,2048]{2,1,0:T(8,128)(2,1)S(1)} %pad_maximum_fusion.2), channel_id=1, source_target_pairs={{0,2},{1,3},{2,0},{3,1},{4,6},{5,7},{6,4},{7,5},{8,10},{9,11},{10,... | collective-permute-start | bytes 786440 | tf_op jit(solution)/shard_map/ppermute | solution.py:499
  33.1 6.7 %collective-permute-start.20 = (f32[4,9,128]{2,1,0:T(8,128)S(1)}, f32[4,9,128]{2,1,0:T(8,128)S(1)}, u32[]{:S(2)}, u32[]{:S(2)}) collective-permute-start(f32[4,9,128]{2,1,0:T(8,128)S(1)} %pad_maximum_fusion.5), channel_id=1, source_target_pairs={{0,1},{1,0},{2,3},{3,2},{4,5},{5,4},{6,7},{7,6},{8,24},{9,25},{10,... | collective-permute-start | bytes 55304 | tf_op jit(solution)/shard_map/ppermute | solution.py:499
  38.3 9.3 %collective-permute-start.3 = (bf16[4,32,2048]{2,1,0:T(8,128)(2,1)S(1)}, bf16[4,32,2048]{2,1,0:T(8,128)(2,1)S(1)}, u32[]{:S(2)}, u32[]{:S(2)}) collective-permute-start(bf16[4,32,2048]{2,1,0:T(8,128)(2,1)S(1)} %constant_dynamic-update-slice_fusion), channel_id=1, source_target_pairs={{0,1},{1,0},{2,3},{3,2},{4,5},{5,4},{6,7},{7,6},{8,24},{9,25},{10,... | collective-permute-start | bytes 1572872 | tf_op jit(solution)/shard_map/ppermute | solution.py:499
  39.9 26.0 %collective-permute-start.21 = (f32[8,9,128]{2,1,0:T(8,128)S(1)}, f32[8,9,128]{2,1,0:T(8,128)S(1)}, u32[]{:S(2)}, u32[]{:S(2)}) collective-permute-start(f32[8,9,128]{2,1,0:T(8,128)S(1)} %pad_maximum_fusion.4), channel_id=1, source_target_pairs={{0,16},{1,17},{2,18},{3,19},{4,20},{5,21},{6,22},{7,23},{8,9},{9,8... | collective-permute-start | bytes 110600 | tf_op jit(solution)/shard_map/ppermute | solution.py:499
  41.4 6.7 %collective-permute-start.4 = (bf16[2,32,2048]{2,1,0:T(8,128)(2,1)S(1)}, bf16[2,32,2048]{2,1,0:T(8,128)(2,1)S(1)}, u32[]{:S(2)}, u32[]{:S(2)}) collective-permute-start(bf16[2,32,2048]{2,1,0:T(8,128)(2,1)S(1)} %constant_dynamic-update-slice_fusion.2), channel_id=1, source_target_pairs={{0,2},{1,3},{2,0},{3,1},{4,6},{5,7},{6,4},{7,5},{8,10},{9,11},{10,... | collective-permute-start | bytes 786440 | tf_op jit(solution)/shard_map/ppermute | solution.py:499
  48.2 14.8 %collective-permute-start.6 = (bf16[4,32,2048]{2,1,0:T(8,128)(2,1)S(1)}, bf16[4,32,2048]{2,1,0:T(8,128)(2,1)S(1)}, u32[]{:S(2)}, u32[]{:S(2)}) collective-permute-start(bf16[4,32,2048]{2,1,0:T(8,128)(2,1)S(1)} %constant_dynamic-update-slice_fusion.6), channel_id=1, source_target_pairs={{0,1},{1,0},{2,3},{3,2},{4,5},{5,4},{6,7},{7,6},{8,24},{9,25},{10,... | collective-permute-start | bytes 1572872 | tf_op jit(solution)/shard_map/ppermute | solution.py:499
  49.9 29.8 %collective-permute-start.12 = (bf16[8,32,2048]{2,1,0:T(8,128)(2,1)S(1)}, bf16[8,32,2048]{2,1,0:T(8,128)(2,1)}, u32[]{:S(2)}, u32[]{:S(2)}) collective-permute-start(bf16[8,32,2048]{2,1,0:T(8,128)(2,1)S(1)} %constant_dynamic-update-slice_fusion.4.refs_0_), channel_id=1, source_target_pairs={{0,16},{1,17},{2,18},{3,19},{4,20},{5,21},{6,22},{7,23},{8,9},{9,8... | collective-permute-start | bytes 3145736 | tf_op jit(solution)/shard_map/ppermute | solution.py:499
  51.4 12.8 %collective-permute-start.7 = (bf16[2,32,2048]{2,1,0:T(8,128)(2,1)S(1)}, bf16[2,32,2048]{2,1,0:T(8,128)(2,1)S(1)}, u32[]{:S(2)}, u32[]{:S(2)}) collective-permute-start(bf16[2,32,2048]{2,1,0:T(8,128)(2,1)S(1)} %constant_dynamic-update-slice_fusion.8), channel_id=1, source_target_pairs={{0,2},{1,3},{2,0},{3,1},{4,6},{5,7},{6,4},{7,5},{8,10},{9,11},{10,... | collective-permute-start | bytes 786440 | tf_op jit(solution)/shard_map/ppermute | solution.py:499
  63.2 19.8 %collective-permute-start.15 = (bf16[8,32,2048]{2,1,0:T(8,128)(2,1)S(1)}, bf16[8,32,2048]{2,1,0:T(8,128)(2,1)}, u32[]{:S(2)}, u32[]{:S(2)}) collective-permute-start(bf16[8,32,2048]{2,1,0:T(8,128)(2,1)S(1)} %constant_dynamic-update-slice_fusion.10.refs_4_), channel_id=1, source_target_pairs={{0,16},{1,17},{2,18},{3,19},{4,20},{5,21},{6,22},{7,23},{8,9},{9,8... | collective-permute-start | bytes 3145736 | tf_op jit(solution)/shard_map/ppermute | solution.py:499
  64.3 14.9 %collective-permute-start.9 = (bf16[4,32,2048]{2,1,0:T(8,128)(2,1)S(1)}, bf16[4,32,2048]{2,1,0:T(8,128)(2,1)S(1)}, u32[]{:S(2)}, u32[]{:S(2)}) collective-permute-start(bf16[4,32,2048]{2,1,0:T(8,128)(2,1)S(1)} %constant_dynamic-update-slice_fusion.12), channel_id=1, source_target_pairs={{0,1},{1,0},{2,3},{3,2},{4,5},{5,4},{6,7},{7,6},{8,24},{9,25},{10,... | collective-permute-start | bytes 1572872 | tf_op jit(solution)/shard_map/ppermute | solution.py:499
  66.5 36.6 %collective-permute-start.13 = (bf16[8,32,2048]{2,1,0:T(8,128)(2,1)S(1)}, bf16[8,32,2048]{2,1,0:T(8,128)(2,1)}, u32[]{:S(2)}, u32[]{:S(2)}) collective-permute-start(bf16[8,32,2048]{2,1,0:T(8,128)(2,1)S(1)} %constant_dynamic-update-slice_fusion.4.refs_0_), channel_id=1, source_target_pairs={{0,8},{1,9},{2,10},{3,11},{4,12},{5,13},{6,14},{7,15},{8,0},{9,1},... | collective-permute-start | bytes 3145736 | tf_op jit(solution)/shard_map/ppermute | solution.py:499
  66.5 37.2 %collective-permute-start.16 = (bf16[8,32,2048]{2,1,0:T(8,128)(2,1)S(1)}, bf16[8,32,2048]{2,1,0:T(8,128)(2,1)}, u32[]{:S(2)}, u32[]{:S(2)}) collective-permute-start(bf16[8,32,2048]{2,1,0:T(8,128)(2,1)S(1)} %constant_dynamic-update-slice_fusion.10.refs_4_), channel_id=1, source_target_pairs={{0,8},{1,9},{2,10},{3,11},{4,12},{5,13},{6,14},{7,15},{8,0},{9,1},... | collective-permute-start | bytes 3145736 | tf_op jit(solution)/shard_map/ppermute | solution.py:499
  79.2 6.4 %collective-permute-start.10 = (bf16[2,32,2048]{2,1,0:T(8,128)(2,1)S(1)}, bf16[2,32,2048]{2,1,0:T(8,128)(2,1)S(1)}, u32[]{:S(2)}, u32[]{:S(2)}) collective-permute-start(bf16[2,32,2048]{2,1,0:T(8,128)(2,1)S(1)} %constant_dynamic-update-slice_fusion.14), channel_id=1, source_target_pairs={{0,2},{1,3},{2,0},{3,1},{4,6},{5,7},{6,4},{7,5},{8,10},{9,11},{10,... | collective-permute-start | bytes 786440 | tf_op jit(solution)/shard_map/ppermute | solution.py:499
  79.7 24.0 %collective-permute-start.14 = (bf16[8,32,2048]{2,1,0:T(8,128)(2,1)}, bf16[8,32,2048]{2,1,0:T(8,128)(2,1)}, u32[]{:S(2)}, u32[]{:S(2)}) collective-permute-start(bf16[8,32,2048]{2,1,0:T(8,128)(2,1)} %collective-permute-done.12.refs_1_), channel_id=1, source_target_pairs={{0,8},{1,9},{2,10},{3,11},{4,12},{5,13},{6,14},{7,15},{8,0},{9,1},... | collective-permute-start | bytes 3145736 | tf_op jit(solution)/shard_map/ppermute | solution.py:499
  83.0 20.8 %collective-permute-start.17 = (bf16[8,32,2048]{2,1,0:T(8,128)(2,1)}, bf16[8,32,2048]{2,1,0:T(8,128)(2,1)}, u32[]{:S(2)}, u32[]{:S(2)}) collective-permute-start(bf16[8,32,2048]{2,1,0:T(8,128)(2,1)} %collective-permute-done.15.refs_5_), channel_id=1, source_target_pairs={{0,8},{1,9},{2,10},{3,11},{4,12},{5,13},{6,14},{7,15},{8,0},{9,1},... | collective-permute-start | bytes 3145736 | tf_op jit(solution)/shard_map/ppermute | solution.py:499
  85.6 9.1 %collective-permute-start.11 = (bf16[1,64,1024]{2,1,0:T(8,128)(2,1)S(1)}, bf16[1,64,1024]{2,1,0:T(8,128)(2,1)S(1)}, u32[]{:S(2)}, u32[]{:S(2)}) collective-permute-start(bf16[1,64,1024]{2,1,0:T(8,128)(2,1)S(1)} %get-tuple-element.241), channel_id=1, source_target_pairs={{0,4},{1,5},{2,6},{3,7},{4,0},{5,1},{6,2},{7,3},{8,12},{9,13},{10,... | collective-permute-start | bytes 393224 | tf_op jit(solution)/shard_map/ppermute | solution.py:499
  96.1 25.6 %collective-permute-start.23 = (bf16[4,32,2048]{2,1,0:T(8,128)(2,1)}, bf16[4,32,2048]{2,1,0:T(8,128)(2,1)}, u32[]{:S(2)}, u32[]{:S(2)}) collective-permute-start(bf16[4,32,2048]{2,1,0:T(8,128)(2,1)} %constant_dynamic-update-slice_fusion.18), channel_id=1, source_target_pairs={{0,1},{1,0},{2,3},{3,2},{4,5},{5,4},{6,7},{7,6},{8,24},{9,25},{10,... | collective-permute-start | bytes 1572872 | tf_op jit(solution)/shard_map/ppermute | solution.py:499
  103.2 32.2 %collective-permute-start.28 = (bf16[8,32,2048]{2,1,0:T(8,128)(2,1)S(1)}, bf16[8,32,2048]{2,1,0:T(8,128)(2,1)}, u32[]{:S(2)}, u32[]{:S(2)}) collective-permute-start(bf16[8,32,2048]{2,1,0:T(8,128)(2,1)S(1)} %constant_dynamic-update-slice_fusion.16.refs_0_), channel_id=1, source_target_pairs={{0,16},{1,17},{2,18},{3,19},{4,20},{5,21},{6,22},{7,23},{8,9},{9,8... | collective-permute-start | bytes 3145736 | tf_op jit(solution)/shard_map/ppermute | solution.py:499
  123.9 20.6 %collective-permute-start.31 = (bf16[8,32,2048]{2,1,0:T(8,128)(2,1)S(1)}, bf16[8,32,2048]{2,1,0:T(8,128)(2,1)}, u32[]{:S(2)}, u32[]{:S(2)}) collective-permute-start(bf16[8,32,2048]{2,1,0:T(8,128)(2,1)S(1)} %constant_dynamic-update-slice_fusion.33.refs_4_), channel_id=1, source_target_pairs={{0,16},{1,17},{2,18},{3,19},{4,20},{5,21},{6,22},{7,23},{8,9},{9,8... | collective-permute-start | bytes 3145736 | tf_op jit(solution)/shard_map/ppermute | solution.py:499
  125.4 6.6 %collective-permute-start.24 = (bf16[2,64,1024]{2,1,0:T(8,128)(2,1)S(1)}, bf16[2,64,1024]{2,1,0:T(8,128)(2,1)S(1)}, u32[]{:S(2)}, u32[]{:S(2)}) collective-permute-start(bf16[2,64,1024]{2,1,0:T(8,128)(2,1)S(1)} %constant_dynamic-update-slice_fusion.20), channel_id=1, source_target_pairs={{0,2},{1,3},{2,0},{3,1},{4,6},{5,7},{6,4},{7,5},{8,10},{9,11},{10,... | collective-permute-start | bytes 786440 | tf_op jit(solution)/shard_map/ppermute | solution.py:499
  132.0 12.4 %collective-permute-start.26 = (bf16[4,64,1024]{2,1,0:T(8,128)(2,1)S(1)}, bf16[4,64,1024]{2,1,0:T(8,128)(2,1)S(1)}, u32[]{:S(2)}, u32[]{:S(2)}) collective-permute-start(bf16[4,64,1024]{2,1,0:T(8,128)(2,1)S(1)} %constant_dynamic-update-slice_fusion.35), channel_id=1, source_target_pairs={{0,1},{1,0},{2,3},{3,2},{4,5},{5,4},{6,7},{7,6},{8,24},{9,25},{10,... | collective-permute-start | bytes 1572872 | tf_op jit(solution)/shard_map/ppermute | solution.py:499
  133.6 7.3 %collective-permute-start.25 = (bf16[1,64,1024]{2,1,0:T(8,128)(2,1)S(1)}, bf16[1,64,1024]{2,1,0:T(8,128)(2,1)S(1)}, u32[]{:S(2)}, u32[]{:S(2)}) collective-permute-start(bf16[1,64,1024]{2,1,0:T(8,128)(2,1)S(1)} %get-tuple-element.260), channel_id=1, source_target_pairs={{0,4},{1,5},{2,6},{3,7},{4,0},{5,1},{6,2},{7,3},{8,12},{9,13},{10,... | collective-permute-start | bytes 393224 | tf_op jit(solution)/shard_map/ppermute | solution.py:499
  135.4 26.7 %collective-permute-start.29 = (bf16[8,32,2048]{2,1,0:T(8,128)(2,1)S(1)}, bf16[8,32,2048]{2,1,0:T(8,128)(2,1)}, u32[]{:S(2)}, u32[]{:S(2)}) collective-permute-start(bf16[8,32,2048]{2,1,0:T(8,128)(2,1)S(1)} %constant_dynamic-update-slice_fusion.16.refs_0_), channel_id=1, source_target_pairs={{0,8},{1,9},{2,10},{3,11},{4,12},{5,13},{6,14},{7,15},{8,0},{9,1},... | collective-permute-start | bytes 3145736 | tf_op jit(solution)/shard_map/ppermute | solution.py:499
  135.4 28.1 %collective-permute-start.30 = (bf16[8,32,2048]{2,1,0:T(8,128)(2,1)}, bf16[8,32,2048]{2,1,0:T(8,128)(2,1)}, u32[]{:S(2)}, u32[]{:S(2)}) collective-permute-start(bf16[8,32,2048]{2,1,0:T(8,128)(2,1)} %collective-permute-done.28.refs_1_), channel_id=1, source_target_pairs={{0,8},{1,9},{2,10},{3,11},{4,12},{5,13},{6,14},{7,15},{8,0},{9,1},... | collective-permute-start | bytes 3145736 | tf_op jit(solution)/shard_map/ppermute | solution.py:499
  140.9 22.6 %collective-permute-start.32 = (bf16[8,32,2048]{2,1,0:T(8,128)(2,1)S(1)}, bf16[8,32,2048]{2,1,0:T(8,128)(2,1)}, u32[]{:S(2)}, u32[]{:S(2)}) collective-permute-start(bf16[8,32,2048]{2,1,0:T(8,128)(2,1)S(1)} %constant_dynamic-update-slice_fusion.33.refs_4_), channel_id=1, source_target_pairs={{0,8},{1,9},{2,10},{3,11},{4,12},{5,13},{6,14},{7,15},{8,0},{9,1},... | collective-permute-start | bytes 3145736 | tf_op jit(solution)/shard_map/ppermute | solution.py:499
  144.5 19.0 %collective-permute-start.33 = (bf16[8,32,2048]{2,1,0:T(8,128)(2,1)}, bf16[8,32,2048]{2,1,0:T(8,128)(2,1)}, u32[]{:S(2)}, u32[]{:S(2)}) collective-permute-start(bf16[8,32,2048]{2,1,0:T(8,128)(2,1)} %collective-permute-done.31.refs_5_), channel_id=1, source_target_pairs={{0,8},{1,9},{2,10},{3,11},{4,12},{5,13},{6,14},{7,15},{8,0},{9,1},... | collective-permute-start | bytes 3145736 | tf_op jit(solution)/shard_map/ppermute | solution.py:499
  144.5 15.1 %collective-permute-start.27 = (bf16[2,64,1024]{2,1,0:T(8,128)(2,1)S(1)}, bf16[2,64,1024]{2,1,0:T(8,128)(2,1)}, u32[]{:S(2)}, u32[]{:S(2)}) collective-permute-start(bf16[2,64,1024]{2,1,0:T(8,128)(2,1)S(1)} %constant_dynamic-update-slice_fusion.37), channel_id=1, source_target_pairs={{0,2},{1,3},{2,0},{3,1},{4,6},{5,7},{6,4},{7,5},{8,10},{9,11},{10,... | collective-permute-start | bytes 786440 | tf_op jit(solution)/shard_map/ppermute | solution.py:499
  162.1 14.7 %collective-permute-start.34 = (bf16[4,64,1024]{2,1,0:T(8,128)(2,1)}, bf16[4,64,1024]{2,1,0:T(8,128)(2,1)}, u32[]{:S(2)}, u32[]{:S(2)}) collective-permute-start(bf16[4,64,1024]{2,1,0:T(8,128)(2,1)} %constant_dynamic-update-slice_fusion.41), channel_id=1, source_target_pairs={{0,1},{1,0},{2,3},{3,2},{4,5},{5,4},{6,7},{7,6},{8,24},{9,25},{10,... | collective-permute-start | bytes 1572872 | tf_op jit(solution)/shard_map/ppermute | solution.py:499
  162.1 20.3 %collective-permute-start.35 = (bf16[8,64,1024]{2,1,0:T(8,128)(2,1)S(1)}, bf16[8,64,1024]{2,1,0:T(8,128)(2,1)}, u32[]{:S(2)}, u32[]{:S(2)}) collective-permute-start(bf16[8,64,1024]{2,1,0:T(8,128)(2,1)S(1)} %constant_dynamic-update-slice_fusion.39.refs_0_), channel_id=1, source_target_pairs={{0,16},{1,17},{2,18},{3,19},{4,20},{5,21},{6,22},{7,23},{8,9},{9,8... | collective-permute-start | bytes 3145736 | tf_op jit(solution)/shard_map/ppermute | solution.py:499
  179.0 14.9 %collective-permute-start.38 = (bf16[8,64,1024]{2,1,0:T(8,128)(2,1)S(1)}, bf16[8,64,1024]{2,1,0:T(8,128)(2,1)S(1)}, u32[]{:S(2)}, u32[]{:S(2)}) collective-permute-start(bf16[8,64,1024]{2,1,0:T(8,128)(2,1)S(1)} %constant_dynamic-update-slice_fusion.43.refs_4_), channel_id=1, source_target_pairs={{0,16},{1,17},{2,18},{3,19},{4,20},{5,21},{6,22},{7,23},{8,9},{9,8... | collective-permute-start | bytes 3145736 | tf_op jit(solution)/shard_map/ppermute | solution.py:499
  180.8 17.5 %collective-permute-start.36 = (bf16[8,64,1024]{2,1,0:T(8,128)(2,1)S(1)}, bf16[8,64,1024]{2,1,0:T(8,128)(2,1)}, u32[]{:S(2)}, u32[]{:S(2)}) collective-permute-start(bf16[8,64,1024]{2,1,0:T(8,128)(2,1)S(1)} %constant_dynamic-update-slice_fusion.39.refs_0_), channel_id=1, source_target_pairs={{0,8},{1,9},{2,10},{3,11},{4,12},{5,13},{6,14},{7,15},{8,0},{9,1},... | collective-permute-start | bytes 3145736 | tf_op jit(solution)/shard_map/ppermute | solution.py:499
  182.3 16.0 %collective-permute-start.37 = (bf16[8,64,1024]{2,1,0:T(8,128)(2,1)}, bf16[8,64,1024]{2,1,0:T(8,128)(2,1)}, u32[]{:S(2)}, u32[]{:S(2)}) collective-permute-start(bf16[8,64,1024]{2,1,0:T(8,128)(2,1)} %collective-permute-done.35.refs_1_), channel_id=1, source_target_pairs={{0,8},{1,9},{2,10},{3,11},{4,12},{5,13},{6,14},{7,15},{8,0},{9,1},... | collective-permute-start | bytes 3145736 | tf_op jit(solution)/shard_map/ppermute | solution.py:499
  182.8 15.5 %collective-permute-start.39 = (bf16[8,64,1024]{2,1,0:T(8,128)(2,1)S(1)}, bf16[8,64,1024]{2,1,0:T(8,128)(2,1)}, u32[]{:S(2)}, u32[]{:S(2)}) collective-permute-start(bf16[8,64,1024]{2,1,0:T(8,128)(2,1)S(1)} %constant_dynamic-update-slice_fusion.43.refs_4_), channel_id=1, source_target_pairs={{0,8},{1,9},{2,10},{3,11},{4,12},{5,13},{6,14},{7,15},{8,0},{9,1},... | collective-permute-start | bytes 3145736 | tf_op jit(solution)/shard_map/ppermute | solution.py:499
  193.9 4.5 collective-permute-start.40
  344.2 7.5 %collective-permute-start.41 = (bf16[16,128,1024]{2,1,0:T(8,128)(2,1)}, bf16[16,128,1024]{2,1,0:T(8,128)(2,1)}, u32[]{:S(2)}, u32[]{:S(2)}) collective-permute-start(bf16[16,128,1024]{2,1,0:T(8,128)(2,1)} %weight_grad.10), channel_id=1, source_target_pairs={{0,8},{1,9},{2,10},{3,11},{4,12},{5,13},{6,14},{7,15},{8,0},{9,1},... | collective-permute-start | bytes 12582920 | tf_op jit(solution)/shard_map/ppermute | solution.py:499
  362.5 26.4 %collective-permute-start.42 = (bf16[8,128,1024]{2,1,0:T(8,128)(2,1)}, bf16[8,128,1024]{2,1,0:T(8,128)(2,1)}, u32[]{:S(2)}, u32[]{:S(2)}) collective-permute-start(bf16[8,128,1024]{2,1,0:T(8,128)(2,1)} %get-tuple-element.324), channel_id=1, source_target_pairs={{0,16},{1,17},{2,18},{3,19},{4,20},{5,21},{6,22},{7,23},{8,9},{9,8... | collective-permute-start | bytes 6291464 | tf_op jit(solution)/shard_map/ppermute | solution.py:499
  401.7 17.6 %collective-permute-start.44 = (bf16[16,32,4096]{2,1,0:T(8,128)(2,1)}, bf16[16,32,4096]{2,1,0:T(8,128)(2,1)}, u32[]{:S(2)}, u32[]{:S(2)}) collective-permute-start(bf16[16,32,4096]{2,1,0:T(8,128)(2,1)} %weight_grad.12), channel_id=1, source_target_pairs={{0,8},{1,9},{2,10},{3,11},{4,12},{5,13},{6,14},{7,15},{8,0},{9,1},... | collective-permute-start | bytes 12582920 | tf_op jit(solution)/shard_map/ppermute | solution.py:499
  401.8 14.9 %collective-permute-start.43 = (bf16[4,128,1024]{2,1,0:T(8,128)(2,1)S(1)}, bf16[4,128,1024]{2,1,0:T(8,128)(2,1)S(1)}, u32[]{:S(2)}, u32[]{:S(2)}) collective-permute-start(bf16[4,128,1024]{2,1,0:T(8,128)(2,1)S(1)} %get-tuple-element.428), channel_id=1, source_target_pairs={{0,1},{1,0},{2,3},{3,2},{4,5},{5,4},{6,7},{7,6},{8,24},{9,25},{10,... | collective-permute-start | bytes 3145736 | tf_op jit(solution)/shard_map/ppermute | solution.py:499
  417.1 14.6 %collective-permute-start.45 = (bf16[2,128,1024]{2,1,0:T(8,128)(2,1)S(1)}, bf16[2,128,1024]{2,1,0:T(8,128)(2,1)S(1)}, u32[]{:S(2)}, u32[]{:S(2)}) collective-permute-start(bf16[2,128,1024]{2,1,0:T(8,128)(2,1)S(1)} %get-tuple-element.434), channel_id=1, source_target_pairs={{0,2},{1,3},{2,0},{3,1},{4,6},{5,7},{6,4},{7,5},{8,10},{9,11},{10,... | collective-permute-start | bytes 1572872 | tf_op jit(solution)/shard_map/ppermute | solution.py:499
  430.3 31.5 %collective-permute-start.48 = (bf16[8,32,4096]{2,1,0:T(8,128)(2,1)}, bf16[8,32,4096]{2,1,0:T(8,128)(2,1)}, u32[]{:S(2)}, u32[]{:S(2)}) collective-permute-start(bf16[8,32,4096]{2,1,0:T(8,128)(2,1)} %get-tuple-element.337), channel_id=1, source_target_pairs={{0,16},{1,17},{2,18},{3,19},{4,20},{5,21},{6,22},{7,23},{8,9},{9,8... | collective-permute-start | bytes 6291464 | tf_op jit(solution)/shard_map/ppermute | solution.py:499
  436.9 11.3 %collective-permute-start.46 = (bf16[16,32,1024]{2,1,0:T(8,128)(2,1)}, bf16[16,32,1024]{2,1,0:T(8,128)(2,1)S(1)}, u32[]{:S(2)}, u32[]{:S(2)}) collective-permute-start(bf16[16,32,1024]{2,1,0:T(8,128)(2,1)} %weight_grad.14), channel_id=1, source_target_pairs={{0,8},{1,9},{2,10},{3,11},{4,12},{5,13},{6,14},{7,15},{8,0},{9,1},... | collective-permute-start | bytes 3145736 | tf_op jit(solution)/shard_map/ppermute | solution.py:499
  437.0 17.6 %collective-permute-start.47 = (bf16[1,128,1024]{2,1,0:T(8,128)(2,1)S(1)}, bf16[1,128,1024]{2,1,0:T(8,128)(2,1)S(1)}, u32[]{:S(2)}, u32[]{:S(2)}) collective-permute-start(bf16[1,128,1024]{2,1,0:T(8,128)(2,1)S(1)} %get-tuple-element.442), channel_id=1, source_target_pairs={{0,4},{1,5},{2,6},{3,7},{4,0},{5,1},{6,2},{7,3},{8,12},{9,13},{10,... | collective-permute-start | bytes 786440 | tf_op jit(solution)/shard_map/ppermute | solution.py:499
  461.5 4.6 collective-permute-start.49
  464.4 17.3 %collective-permute-start.50 = (bf16[4,32,4096]{2,1,0:T(8,128)(2,1)S(1)}, bf16[4,32,4096]{2,1,0:T(8,128)(2,1)S(1)}, u32[]{:S(2)}, u32[]{:S(2)}) collective-permute-start(bf16[4,32,4096]{2,1,0:T(8,128)(2,1)S(1)} %get-tuple-element.426), channel_id=1, source_target_pairs={{0,1},{1,0},{2,3},{3,2},{4,5},{5,4},{6,7},{7,6},{8,24},{9,25},{10,... | collective-permute-start | bytes 3145736 | tf_op jit(solution)/shard_map/ppermute | solution.py:499
  489.1 5.4 collective-permute-start.51
  490.3 17.9 %collective-permute-start.52 = (bf16[8,32,2560]{2,1,0:T(8,128)(2,1)}, bf16[8,32,2560]{2,1,0:T(8,128)(2,1)}, u32[]{:S(2)}, u32[]{:S(2)}) collective-permute-start(bf16[8,32,2560]{2,1,0:T(8,128)(2,1)} %pad_maximum_fusion.1), channel_id=1, source_target_pairs={{0,16},{1,17},{2,18},{3,19},{4,20},{5,21},{6,22},{7,23},{8,9},{9,8... | collective-permute-start | bytes 3932168 | tf_op jit(solution)/shard_map/ppermute | solution.py:499
  493.7 17.5 %collective-permute-start.53 = (bf16[2,32,4096]{2,1,0:T(8,128)(2,1)}, bf16[2,32,4096]{2,1,0:T(8,128)(2,1)}, u32[]{:S(2)}, u32[]{:S(2)}) collective-permute-start(bf16[2,32,4096]{2,1,0:T(8,128)(2,1)} %get-tuple-element.432), channel_id=1, source_target_pairs={{0,2},{1,3},{2,0},{3,1},{4,6},{5,7},{6,4},{7,5},{8,10},{9,11},{10,... | collective-permute-start | bytes 1572872 | tf_op jit(solution)/shard_map/ppermute | solution.py:499
  510.0 17.3 %collective-permute-start.54 = (bf16[4,32,2560]{2,1,0:T(8,128)(2,1)S(1)}, bf16[4,32,2560]{2,1,0:T(8,128)(2,1)}, u32[]{:S(2)}, u32[]{:S(2)}) collective-permute-start(bf16[4,32,2560]{2,1,0:T(8,128)(2,1)S(1)} %get-tuple-element.430), channel_id=1, source_target_pairs={{0,1},{1,0},{2,3},{3,2},{4,5},{5,4},{6,7},{7,6},{8,24},{9,25},{10,... | collective-permute-start | bytes 1966088 | tf_op jit(solution)/shard_map/ppermute | solution.py:499
  512.4 16.7 %collective-permute-start.55 = (bf16[8,32,1536]{2,1,0:T(8,128)(2,1)}, bf16[8,32,1536]{2,1,0:T(8,128)(2,1)S(1)}, u32[]{:S(2)}, u32[]{:S(2)}) collective-permute-start(bf16[8,32,1536]{2,1,0:T(8,128)(2,1)} %get-tuple-element.365), channel_id=1, source_target_pairs={{0,16},{1,17},{2,18},{3,19},{4,20},{5,21},{6,22},{7,23},{8,9},{9,8... | collective-permute-start | bytes 2359304 | tf_op jit(solution)/shard_map/ppermute | solution.py:499
  513.4 17.0 %collective-permute-start.56 = (bf16[1,32,4096]{2,1,0:T(8,128)(2,1)S(1)}, bf16[1,32,4096]{2,1,0:T(8,128)(2,1)}, u32[]{:S(2)}, u32[]{:S(2)}) collective-permute-start(bf16[1,32,4096]{2,1,0:T(8,128)(2,1)S(1)} %get-tuple-element.440), channel_id=1, source_target_pairs={{0,4},{1,5},{2,6},{3,7},{4,0},{5,1},{6,2},{7,3},{8,12},{9,13},{10,... | collective-permute-start | bytes 786440 | tf_op jit(solution)/shard_map/ppermute | solution.py:499
  526.2 15.4 %collective-permute-start.59 = (f32[16,9,128]{2,1,0:T(8,128)S(1)}, f32[16,9,128]{2,1,0:T(8,128)S(1)}, u32[]{:S(2)}, u32[]{:S(2)}) collective-permute-start(f32[16,9,128]{2,1,0:T(8,128)S(1)} %get-tuple-element.447), channel_id=1, source_target_pairs={{0,8},{1,9},{2,10},{3,11},{4,12},{5,13},{6,14},{7,15},{8,0},{9,1},... | collective-permute-start | bytes 221192 | tf_op jit(solution)/shard_map/ppermute | solution.py:499
  528.6 9.2 %collective-permute-start.57 = (bf16[2,32,2560]{2,1,0:T(8,128)(2,1)S(1)}, bf16[2,32,2560]{2,1,0:T(8,128)(2,1)S(1)}, u32[]{:S(2)}, u32[]{:S(2)}) collective-permute-start(bf16[2,32,2560]{2,1,0:T(8,128)(2,1)S(1)} %get-tuple-element.438), channel_id=1, source_target_pairs={{0,2},{1,3},{2,0},{3,1},{4,6},{5,7},{6,4},{7,5},{8,10},{9,11},{10,... | collective-permute-start | bytes 983048 | tf_op jit(solution)/shard_map/ppermute | solution.py:499
  529.3 11.5 %collective-permute-start.58 = (bf16[4,32,1536]{2,1,0:T(8,128)(2,1)S(1)}, bf16[4,32,1536]{2,1,0:T(8,128)(2,1)S(1)}, u32[]{:S(2)}, u32[]{:S(2)}) collective-permute-start(bf16[4,32,1536]{2,1,0:T(8,128)(2,1)S(1)} %get-tuple-element.436), channel_id=1, source_target_pairs={{0,1},{1,0},{2,3},{3,2},{4,5},{5,4},{6,7},{7,6},{8,24},{9,25},{10,... | collective-permute-start | bytes 1179656 | tf_op jit(solution)/shard_map/ppermute | solution.py:499
  537.9 10.6 %collective-permute-start.60 = (bf16[1,32,2560]{2,1,0:T(8,128)(2,1)S(1)}, bf16[1,32,2560]{2,1,0:T(8,128)(2,1)S(1)}, u32[]{:S(2)}, u32[]{:S(2)}) collective-permute-start(bf16[1,32,2560]{2,1,0:T(8,128)(2,1)S(1)} %get-tuple-element.446), channel_id=1, source_target_pairs={{0,4},{1,5},{2,6},{3,7},{4,0},{5,1},{6,2},{7,3},{8,12},{9,13},{10,... | collective-permute-start | bytes 491528 | tf_op jit(solution)/shard_map/ppermute | solution.py:499
  540.9 9.1 %collective-permute-start.61 = (bf16[2,32,1536]{2,1,0:T(8,128)(2,1)S(1)}, bf16[2,32,1536]{2,1,0:T(8,128)(2,1)S(1)}, u32[]{:S(2)}, u32[]{:S(2)}) collective-permute-start(bf16[2,32,1536]{2,1,0:T(8,128)(2,1)S(1)} %get-tuple-element.444), channel_id=1, source_target_pairs={{0,2},{1,3},{2,0},{3,1},{4,6},{5,7},{6,4},{7,5},{8,10},{9,11},{10,... | collective-permute-start | bytes 589832 | tf_op jit(solution)/shard_map/ppermute | solution.py:499
  541.7 8.7 %collective-permute-start.62 = (f32[8,9,128]{2,1,0:T(8,128)S(1)}, f32[8,9,128]{2,1,0:T(8,128)S(1)}, u32[]{:S(2)}, u32[]{:S(2)}) collective-permute-start(f32[8,9,128]{2,1,0:T(8,128)S(1)} %get-tuple-element.458), channel_id=1, source_target_pairs={{0,16},{1,17},{2,18},{3,19},{4,20},{5,21},{6,22},{7,23},{8,9},{9,8... | collective-permute-start | bytes 110600 | tf_op jit(solution)/shard_map/ppermute | solution.py:499
  550.2 6.6 %collective-permute-start.63 = (bf16[1,32,1536]{2,1,0:T(8,128)(2,1)S(1)}, bf16[1,32,1536]{2,1,0:T(8,128)(2,1)S(1)}, u32[]{:S(2)}, u32[]{:S(2)}) collective-permute-start(bf16[1,32,1536]{2,1,0:T(8,128)(2,1)S(1)} %get-tuple-element.454), channel_id=1, source_target_pairs={{0,4},{1,5},{2,6},{3,7},{4,0},{5,1},{6,2},{7,3},{8,12},{9,13},{10,... | collective-permute-start | bytes 294920 | tf_op jit(solution)/shard_map/ppermute | solution.py:499
  550.4 6.4 %collective-permute-start.64 = (f32[4,9,128]{2,1,0:T(8,128)S(1)}, f32[4,9,128]{2,1,0:T(8,128)S(1)}, u32[]{:S(2)}, u32[]{:S(2)}) collective-permute-start(f32[4,9,128]{2,1,0:T(8,128)S(1)} %get-tuple-element.460), channel_id=1, source_target_pairs={{0,1},{1,0},{2,3},{3,2},{4,5},{5,4},{6,7},{7,6},{8,24},{9,25},{10,... | collective-permute-start | bytes 55304 | tf_op jit(solution)/shard_map/ppermute | solution.py:499
  560.8 4.6 collective-permute-start.66
  (35 other events, 394.1 us)

commit v5 on v4

--- a/solution.py
+++ b/solution.py
@@ -8,21 +8,16 @@
 from jax.experimental.pallas import tpu as pltpu
 from jax.sharding import PartitionSpec as P
 
+CHEAP = pl.CostEstimate(flops=1, transcendentals=0, bytes_accessed=1)
+call = partial(pl.pallas_call, cost_estimate=CHEAP)
+
+
 EPSILON = 1e-06
 HEAD_DIM = 64
 LOG2E = 1.4426950408889634
 RSQRT_2PI = 0.3989422804014327
-TAIL_STEP = 0.305
-TAIL_COEFFS = (
-    0.12163971608667215,
-    0.12246710281167089,
-    0.10341891431417467,
-    0.12102858688667265,
-    -0.03799063399351653,
-    0.18573260086829071,
-    -0.15299777850455798,
-    0.03670153882152772,
-)
+SQRT_HALF = 0.7071067811865476
+SCORE_SCALE = HEAD_DIM**-0.5 * LOG2E
 NT = (((1,), (1,)), ((), ()))
 TN = (((0,), (0,)), ((), ()))
 
@@ -35,15 +30,8 @@
     return pl.BlockSpec(shape, lambda *_: (0,) * len(shape))
 
 
-def normal_tail(u):
-    size = jnp.abs(u)
-    t = 1.0 / (1.0 + TAIL_STEP * size)
-    bell = jnp.exp(-0.5 * (u * u))
-    poly = jnp.full_like(u, TAIL_COEFFS[-1])
-    for c in TAIL_COEFFS[-2::-1]:
-        poly = poly * t + c
-    tail = bell * (t * poly)
-    return jnp.where(u < 0, tail, 1.0 - tail), bell
+def normal_cdf(u):
+    return 0.5 + 0.5 * lax.erf(u * SQRT_HALF), jnp.exp2((-0.5 * LOG2E) * (u * u))
 
 
 def row_stats(v):
@@ -63,7 +51,7 @@
 
         o_ref[...] = (dot(a_ref[...], w_ref[...]) + b_ref[...]).astype(jnp.bfloat16)
 
-    return pl.pallas_call(
+    return call(
         body,
         grid=(cols // tn,),
         in_specs=[
@@ -94,13 +82,12 @@
         for h in range(2):
             mine = (lane < HEAD_DIM) if h == 0 else (lane >= HEAD_DIM)
             kh = jnp.where(mine, k, jnp.zeros_like(k))
-            s = dot(q, kh, NT) * 0.125
-            top = jnp.max(s, axis=-1, keepdims=True)
-            e = jnp.exp(s - top)
+            s = dot(q, kh, NT)
+            top = jnp.max(s, axis=-1, keepdims=True) * SCORE_SCALE
+            e = jnp.exp2(s * SCORE_SCALE - top)
             total = jnp.sum(e, axis=-1, keepdims=True)
-            p = (e * (1.0 / total)).astype(jnp.bfloat16)
-            outs.append(dot(p, v))
-            logs.append(top + jnp.log(total))
+            outs.append(dot(e.astype(jnp.bfloat16), v) * (1.0 / total))
+            logs.append(top + jnp.log2(total))
         first = lane < HEAD_DIM
         o_ref[...] = jnp.where(first, outs[0], outs[1]).astype(jnp.bfloat16)
         both = jnp.where(first, logs[0], logs[1])
@@ -109,7 +96,7 @@
         l_ref[0, 1:2, :] = turned[HEAD_DIM : HEAD_DIM + 1, :]
 
     col = lambda base: pl.BlockSpec((rows, span), lambda j: (0, base + j))
-    return pl.pallas_call(
+    return call(
         body,
         grid=(pairs,),
         in_specs=[col(0), col(pairs), col(2 * pairs)],
@@ -122,25 +109,23 @@
     )(qkv, qkv, qkv)
 
 
-def attention_back(qkv, logs, d_o, first_pair, pairs):
+def attention_back(qkv, logs, o, d_o, first_pair, pairs):
     rows, width = qkv.shape[0], qkv.shape[1] // 3
     every = width // (2 * HEAD_DIM)
     span = 2 * HEAD_DIM
 
-    def body(q_ref, k_ref, v_ref, l_ref, do_ref, d_ref, cq_ref, cv_ref):
+    def body(q_ref, k_ref, v_ref, l_ref, o_ref, do_ref, d_ref, cq_ref, cv_ref):
         q, k, v, do = q_ref[...], k_ref[...], v_ref[...], do_ref[...]
         lane = lax.broadcasted_iota(jnp.int32, (rows, span), 1)
+        turned = (do.astype(jnp.float32) * o_ref[...].astype(jnp.float32)).T
         dqs, dks, dvs = [], [], []
         for h in range(2):
             mine = (lane < HEAD_DIM) if h == 0 else (lane >= HEAD_DIM)
             kh = jnp.where(mine, k, jnp.zeros_like(k))
             vh = jnp.where(mine, v, jnp.zeros_like(v))
-            st = dot(kh, q, NT) * 0.125
-            pt = jnp.exp(st - l_ref[0, h : h + 1, :])
-            dpt = dot(vh, do, NT)
-            w = pt * dpt
-            inner = jnp.sum(w, axis=0, keepdims=True)
-            dst = (w - pt * inner).astype(jnp.bfloat16)
+            pt = jnp.exp2(dot(kh, q, NT) * SCORE_SCALE - l_ref[0, h : h + 1, :])
+            inner = jnp.sum(turned[h * HEAD_DIM : (h + 1) * HEAD_DIM], axis=0, keepdims=True)
+            dst = (pt * (dot(vh, do, NT) - inner)).astype(jnp.bfloat16)
             dvs.append(dot(pt.astype(jnp.bfloat16), do))
             dks.append(dot(dst, q))
             dqs.append(dot(dst, k, TN))
@@ -157,7 +142,7 @@
     col = lambda base: pl.BlockSpec((rows, span), lambda j: (0, base + j))
     sums = pl.BlockSpec((1, span), lambda j: (0, j))
     vec_shape = jax.ShapeDtypeStruct((1, pairs * span), jnp.float32)
-    return pl.pallas_call(
+    return call(
         body,
         grid=(pairs,),
         in_specs=[
@@ -166,6 +151,7 @@
             col(2 * every + first_pair),
             pl.BlockSpec((1, 8, rows), lambda j: (first_pair + j, 0, 0)),
             col(first_pair),
+            col(first_pair),
         ],
         out_specs=[pl.BlockSpec((3, rows, span), lambda j: (0, 0, j)), sums, sums],
         out_shape=[
@@ -174,7 +160,7 @@
             vec_shape,
         ],
         name="attention_back",
-    )(qkv, qkv, qkv, logs, d_o)
+    )(qkv, qkv, qkv, logs, o, d_o)
 
 
 def project_norm(o, weight, bias, x, gain, shift, at):
@@ -189,7 +175,7 @@
 
     rowblk = pl.BlockSpec((tm, width), lambda i: (i, 0))
     vec = whole((1, width))
-    return pl.pallas_call(
+    return call(
         body,
         grid=(rows // tm,),
         in_specs=[rowblk, pl.BlockSpec((width, width), lambda i: (0, at // width)), vec, rowblk, vec, vec],
@@ -202,15 +188,30 @@
     )(o, weight, bias, x, gain, shift)
 
 
-def feed_forward(a, up, up_bias, down, down_bias, x1, tf):
+def flat(ref):
+    return ref[...].reshape(-1, ref.shape[-1])
+
+
+def up_spec(packed, r_in):
+    n, _, width = packed.shape
+    return pl.BlockSpec((n, r_in, width), lambda j: (0, j, 0))
+
+
+def down_spec(packed, r_ff):
+    width = packed.shape[2]
+    return pl.BlockSpec((width // r_ff, r_ff, width), lambda j: (j, 1, 0))
+
+
+def feed_forward(a, packed, r_in, r_ff, up_bias, down_bias, x1):
     rows, width = a.shape
-    hidden = up.shape[1]
+    hidden = up_bias.shape[1]
+    tf = width
     steps = hidden // tf
 
     def body(a_ref, u_ref, ub_ref, d_ref, db_ref, x_ref, g_ref, gp_ref, y_ref, acc):
         j = pl.program_id(0)
-        u = dot(a_ref[...], u_ref[...]) + ub_ref[...]
-        phi, bell = normal_tail(u)
+        u = dot(a_ref[...], flat(u_ref)) + ub_ref[...]
+        phi, bell = normal_cdf(u)
         g = (u * phi).astype(jnp.bfloat16)
         g_ref[...] = g
         gp_ref[...] = (phi + (u * RSQRT_2PI) * bell).astype(jnp.bfloat16)
@@ -219,20 +220,20 @@
         def _():
             acc[...] = x_ref[...] + db_ref[...]
 
-        acc[...] += dot(g, d_ref[...])
+        acc[...] += dot(g, flat(d_ref))
 
         @pl.when(j == steps - 1)
         def _():
             y_ref[...] = acc[...].astype(jnp.bfloat16)
 
-    return pl.pallas_call(
+    return call(
         body,
         grid=(steps,),
         in_specs=[
             whole((rows, width)),
-            pl.BlockSpec((width, tf), lambda j: (0, j)),
+            up_spec(packed, r_in),
             pl.BlockSpec((1, tf), lambda j: (0, j)),
-            pl.BlockSpec((tf, width), lambda j: (j, 0)),
+            down_spec(packed, r_ff),
             whole((1, width)),
             whole((rows, width)),
         ],
@@ -248,12 +249,13 @@
         ],
         scratch_shapes=[pltpu.VMEM((rows, width), jnp.float32)],
         name="feed_forward",
-    )(a, up, up_bias, down, down_bias, x1)
-
-
-def feed_forward_back(dy, gp, down, up, x1, gain, w_out, at, tf):
+    )(a, packed, up_bias, packed, down_bias, x1)
+
+
+def feed_forward_back(dy, gp, packed, r_in, r_ff, x1, gain, w_out, at):
     rows, width = dy.shape
     hidden = gp.shape[1]
+    tf = width
     steps = hidden // tf
 
     def body(
@@ -269,10 +271,10 @@
             cdm_ref[...] = jnp.sum(low.astype(jnp.float32), axis=0, keepdims=True)
             acc[...] = jnp.zeros_like(acc)
 
-        du = (dot(dm_ref[...], d_ref[...], NT) * gp_ref[...].astype(jnp.float32)).astype(jnp.bfloat16)
+        du = (dot(dm_ref[...], flat(d_ref), NT) * gp_ref[...].astype(jnp.float32)).astype(jnp.bfloat16)
         du_ref[...] = du
         cdu_ref[...] = jnp.sum(du.astype(jnp.float32), axis=0, keepdims=True)
-        acc[...] += dot(du, u_ref[...], NT)
+        acc[...] += dot(du, flat(u_ref), NT)
 
         @pl.when(j == steps - 1)
         def _():
@@ -293,14 +295,14 @@
     full = whole((rows, width))
     vec = whole((1, width))
     f = lambda s, d: jax.ShapeDtypeStruct(s, d)
-    return pl.pallas_call(
+    return call(
         body,
         grid=(steps,),
         in_specs=[
             full,
             pl.BlockSpec((rows, tf), lambda j: (0, j)),
-            pl.BlockSpec((tf, width), lambda j: (j, 0)),
-            pl.BlockSpec((width, tf), lambda j: (0, j)),
+            down_spec(packed, r_ff),
+            up_spec(packed, r_in),
             full,
             vec,
             pl.BlockSpec((width, width), lambda j: (0, at // width)),
@@ -331,7 +333,7 @@
         ],
         scratch_shapes=[pltpu.VMEM((rows, width), jnp.float32)],
         name="feed_forward_back",
-    )(dy, gp, down, up, x1, gain, w_out)
+    )(dy, gp, packed, packed, x1, gain, w_out)
 
 
 def project_back(grads, weight, x, gain, dx1, extra, out_dtype):
@@ -382,7 +384,7 @@
     if have:
         specs += [rowblk, pl.BlockSpec((tm, 1), lambda i: (i, 0))]
         args += list(extra)
-    return pl.pallas_call(
+    return call(
         body,
         grid=(rows // tm,),
         in_specs=specs,
@@ -440,7 +442,7 @@
     if final:
         specs.append(pl.BlockSpec((npos, r, tn), lambda j, i_ref: (0, 0, j)))
         args.append(arrived)
-    return pl.pallas_call(
+    return call(
         body,
         grid_spec=pltpu.PrefetchScalarGridSpec(
             num_scalar_prefetch=1,
@@ -526,10 +528,8 @@
             which, middle, col = slots[i]
             width = bufs[i].shape[-1]
             for p in range(n):
-                piece = ins[4 * i + p // (n // 4)]
-                loads.append(
-                    pltpu.make_async_copy(piece.at[p % (n // 4)], bufs[i].at[p], in_sem.at[i, p])
-                )
+                piece = ins[4 * i + p // (n // 4)].at[p % (n // 4), 0 : bufs[i].shape[1]]
+                loads.append(pltpu.make_async_copy(piece, bufs[i].at[p], in_sem.at[i, p]))
                 target = outs[which].at[t_ref[p]]
                 if middle is not None:
                     target = target.at[middle]
@@ -548,24 +548,31 @@
 
     flat = [p for g in groups for p in g]
     anywhere = pl.BlockSpec(memory_space=pl.ANY)
-    return pl.pallas_call(
+    return call(
         body,
         out_shape=[jax.ShapeDtypeStruct(s, jnp.bfloat16) for s in shapes],
         grid_spec=pltpu.PrefetchScalarGridSpec(
             num_scalar_prefetch=1,
             in_specs=[anywhere] * len(flat),
             out_specs=[anywhere] * len(shapes),
-            scratch_shapes=[pltpu.VMEM((n,) + g[0].shape[1:], jnp.bfloat16) for g in groups]
+            scratch_shapes=[
+                pltpu.VMEM((n, shapes[s[0]][-2], g[0].shape[-1]), jnp.bfloat16)
+                for g, s in zip(groups, slots)
+            ]
             + [pltpu.SemaphoreType.DMA((count, n))] * 2,
         ),
         name="place_shards",
     )(table_row, *flat)
 
 
-def unpack_vectors(got, inverse_row, sizes, layout):
-    n = got.shape[0]
-
-    def body(i_ref, got_ref, *outs):
+def unpack_vectors(pieces, at, inverse_row, sizes, layout):
+    per_piece = pieces[0].shape[0]
+    n = per_piece * len(pieces)
+
+    def body(i_ref, *refs):
+        ins, outs, scr = refs[: len(pieces)], refs[len(pieces) : -1], refs[-1]
+        for i, ref in enumerate(ins):
+            scr[i * per_piece : (i + 1) * per_piece] = ref[...].astype(jnp.float32)
         for rows, out in zip(layout, outs):
             col = 0
             for r in rows:
@@ -576,23 +583,27 @@
                         value = jnp.zeros((1, per * k), jnp.float32)
                     else:
                         value = jnp.concatenate(
-                            [got_ref[i_ref[d + e], r : r + 1, 0:k] for e in range(per)], axis=1
+                            [scr[i_ref[d + e], 0:1, r * 128 : r * 128 + k] for e in range(per)],
+                            axis=1,
                         )
                     out[0:1, col + d * k : col + (d + per) * k] = value
                 col += n * k
 
     widths = [sum(n * (sizes[0] if r is None else sizes[r]) for r in rows) for rows in layout]
-    return pl.pallas_call(
+    lanes = 128 * len(sizes)
+    return call(
         body,
         grid_spec=pltpu.PrefetchScalarGridSpec(
             num_scalar_prefetch=1,
             grid=(1,),
-            in_specs=[whole(got.shape)],
-            out_specs=[whole((1, w)) for w in widths],
+            in_specs=[pl.BlockSpec((per_piece, 8, lanes), lambda i, i_ref: (0, at // 8, 0))]
+            * len(pieces),
+            out_specs=[pl.BlockSpec((1, w), lambda i, i_ref: (0, 0)) for w in widths],
+            scratch_shapes=[pltpu.VMEM((n, 8, lanes), jnp.float32)],
         ),
         out_shape=[jax.ShapeDtypeStruct((1, w), jnp.float32) for w in widths],
         name="unpack_vectors",
-    )(inverse_row, got)
+    )(inverse_row, *pieces)
 
 
 def pack_sums(parts, inverse_row, n, rows):
@@ -611,7 +622,7 @@
             for d in range(n):
                 out[i_ref[d], r : r + 1, 0:k] = total[:, d * k : (d + 1) * k]
 
-    return pl.pallas_call(
+    return call(
         body,
         grid_spec=pltpu.PrefetchScalarGridSpec(
             num_scalar_prefetch=1,
@@ -678,34 +689,32 @@
     rows_in, width = tokens.shape[1:]
     r_in, r_ff = w_up.shape[0], w_down.shape[0]
     hidden = w_up.shape[1]
-    half_ff = r_ff // 2
 
     vectors = (ln1_gain, ln1_bias, bias_q, bias_v, bias_out, ln2_gain, ln2_bias, bias_down, bias_up)
     sizes = [v.shape[0] for v in vectors]
-    packed = jnp.stack([jnp.pad(v.astype(jnp.float32), (0, 128 - v.shape[0])) for v in vectors])
+    lanes_of = lambda v: jnp.pad(v, (0, 128 - v.shape[0]))
+    packed = jnp.concatenate([lanes_of(v) for v in vectors])
 
     line = Line()
-    first_cols = jnp.concatenate([w_qkv, w_out], axis=1)
-    mid = first_cols.shape[1] // 2
+    mid = 2 * width
+    packed = jnp.pad(packed[None], ((0, 7), (0, mid - packed.shape[0])))
     shards = [
-        first_cols[:, :mid],
-        first_cols[:, mid:],
-        w_up[:, : hidden // 2],
-        w_up[:, hidden // 2 :],
-        w_down[:half_ff],
-        w_down[half_ff:],
+        jnp.concatenate([w_qkv[:, :mid], packed], axis=0),
+        jnp.concatenate([w_qkv[:, mid:], w_out], axis=1),
     ]
-    small = packed[None]
+    split = w_up.reshape(r_in, hidden // width, width).swapaxes(0, 1).reshape(r_ff, width)
+    w = {"ff": lax.all_gather(jnp.concatenate([split, w_down], axis=0), AXES)}
     held = [s[None] for s in shards]
     got = [None] * len(shards)
     pieces = [None] * len(shards)
 
     def gather_round(index):
-        nonlocal small
         for i in range(len(shards)):
             k = index - i
             if k < 0 or k > stages:
                 continue
+            if k == 0 and i:
+                (held[i],) = line.after(held[i])
             if 0 < k < stages:
                 mine, theirs = line.after(held[i], got[i])
                 held[i] = jnp.concatenate([mine, theirs], axis=0)
@@ -717,11 +726,6 @@
             if k == stages:
                 pieces[i][1] = got[i]
                 pieces[i][3] = send(got[i], core_perm)
-        if index < stages:
-            theirs = send(small, gather_perms[index])
-            small = jnp.concatenate([small, theirs], axis=0)
-        elif index == stages:
-            small = jnp.concatenate([small, send(small, core_perm)], axis=0)
 
     def place(which, shapes, slots):
         flat = [p for i in which for p in pieces[i]]
@@ -731,49 +735,29 @@
         line.mark(outs[0])
         return outs
 
-    w = {}
     for index in range(stages + 2):
         gather_round(index)
     g1, s1, bqkv, bo, g2, s2, bd, bu = unpack_vectors(
-        small, inverse_row, sizes, [[0], [1], [2, None, 3], [4], [5], [6], [7], [8]]
+        pieces[0], r_in, inverse_row, sizes, [[0], [1], [2, None, 3], [4], [5], [6], [7], [8]]
     )
     qkv_cols = w_qkv.shape[1]
     (first_full,) = place([0, 1], [(n, r_in, 2 * mid)], [(0, None, 0), (0, None, mid)])
     first_full = first_full.reshape(n * r_in, 2 * mid)
     w["first"] = first_full
 
-    def forward(x, before=None):
-        a1, qkv = norm_project(*line.after(x), g1, s1, w["first"], bqkv, 512, qkv_cols)
+    def forward(x):
+        a1, qkv = norm_project(*line.after(x), g1, s1, w["first"], bqkv, qkv_cols // 2, qkv_cols)
         line.mark(a1)
-        if before:
-            before()
         o, logs = attention(*line.after(qkv))
         line.mark(o)
-        if before:
-            before()
         x1, a2 = project_norm(*line.after(o), w["first"], bo, x, g2, s2, qkv_cols)
         line.mark(a2)
-        if before:
-            before()
         a2 = line.after(a2)[0]
-        g, gp, y = feed_forward(a2, w["up"], bu, w["down"], bd, x1, 512)
+        g, gp, y = feed_forward(a2, w["ff"], r_in, r_ff, bu, bd, x1)
         line.mark(y)
         return y, (x, a1, qkv, logs, o, x1, a2, g, gp)
 
-    calls = [0]
-
-    def more():
-        calls[0] += 1
-        gather_round(stages + 1 + calls[0])
-        if calls[0] == 2:
-            (up,) = place([2, 3], [(n, r_in, hidden)], [(0, None, 0), (0, None, hidden // 2)])
-            w["up"] = up.reshape(n * r_in, hidden)
-        if calls[0] == 3:
-            gather_round(stages + 5)
-            (down,) = place([4, 5], [(n, 2, half_ff, width)], [(0, 0, 0), (0, 1, 0)])
-            w["down"] = down.reshape(n * r_ff, width)
-
-    first, saved_first = forward(tokens[0], more)
+    first, saved_first = forward(tokens[0])
     second, saved_second = forward(first)
 
     keep_mask = valid[0].astype(jnp.float32)[:, None]
@@ -784,14 +768,14 @@
     def ff_back(dy, saved):
         x, a1, qkv, logs, o, x1, a2, g, gp = saved
         outs = feed_forward_back(
-            *line.after(dy), gp, w["down"], w["up"], x1, g2, w["first"], qkv_cols, 512
+            *line.after(dy), gp, w["ff"], r_in, r_ff, x1, g2, w["first"], qkv_cols
         )
         line.mark(outs[0])
         return outs
 
     def heads_back(saved, d_o, i):
         outs = attention_back(
-            saved[2], saved[3], *line.after(d_o), i * pairs // parts, pairs // parts
+            saved[2], saved[3], saved[4], *line.after(d_o), i * pairs // parts, pairs // parts
         )
         line.mark(outs[0])
         return outs

time: 572 us -> 540 us (0.944)
  Pallas kernels: 309 us -> 269 us
  waiting for transfers between devices: 135 us -> 164 us
  starting transfers between devices: 64.7 us -> 42.4 us
  local copies, waits for them, and re-layouts: 31.2 us -> 15.7 us
  between operations: 1.74 us -> 15.3 us
    pallas_call x31 -> x29, Pallas kernels: 309 us -> 269 us  [the longest x10 77 us: weight_grad_half(): call(body, grid_spec=pltpu.PrefetchScalarGridSpec(num_scalar_prefetch=1,...]
    ppermute x67 -> x38, waiting for transfers between devices: 135 us -> 164 us  [send(): return lax.ppermute(x, AXES, perm)]
    ppermute x67 -> x38, starting transfers between devices: 64.7 us -> 42.4 us  [send(): return lax.ppermute(x, AXES, perm)]
    concatenate x17 -> x5, local copies, waits for them, and re-layouts: 7.7 us -> 0.93 us  [gather_round(): held[i] = jnp.concatenate([mine, theirs], axis=0)]
  transfers between devices with their start and end apart: 67 -> 39, of which waited for: 28 -> 19; matrix products, arithmetic and copies ran while one was open for 8% -> 5% of each run, Pallas kernels for 24% -> 24%
where the time goes in v5:
time: 540 us; the launch traced here: 531 us
  Pallas kernels  269 us (50%)
  waiting for transfers between devices  164 us (30%)
  starting transfers between devices  42.4 us (8%)
  other arithmetic  24.1 us (4%)
  local copies, waits for them, and re-layouts  15.7 us (3%)
  between operations  15.3 us (3%)
    ppermute x38, waiting for transfers between devices, send(): return lax.ppermute(x, AXES, perm)  164 us
    pallas_call x10, Pallas kernels, weight_grad_half(): call(body, grid_spec=pltpu.PrefetchScalarGridSpec(num_scalar_prefetch=1,...  77 us
    ppermute x38, starting transfers between devices, send(): return lax.ppermute(x, AXES, perm)  42.4 us
    pallas_call x2, Pallas kernels, feed_forward_back(): call(body, grid=(steps,), in_specs=[full, pl.BlockSpec((rows, tf), lambda...  40.7 us
    pallas_call x2, Pallas kernels, feed_forward(): call(body, grid=(steps,), in_specs=[whole((rows, width)), up_spec(packed,...  35.7 us
    pallas_call x4, Pallas kernels, attention_back(): call(body, grid=(pairs,), in_specs=[col(first_pair), col(every + first_pa...  34.6 us
    pallas_call x2, Pallas kernels, attention(): call(body, grid=(pairs,), in_specs=[col(0), col(pairs), col(2 * pairs)],...  21.7 us
    pallas_call x2, Pallas kernels, project_back(): call(body, grid=(rows // tm,), in_specs=specs, out_specs=[rowblk, vec_spe...  19.3 us
  transfers between devices with their start and end apart: 39, of which 19 were waited for; matrix products, arithmetic and copies ran while one was open for 5% of the time, Pallas kernels for 24%

profile of v5, /device:TPU:0, one launch (start us, length us, event | category | flops | bytes accessed | tf_op | source)
XLA Modules:
  0.0 530.7 jit_solution(14348916988304875682)
XLA Ops:
  8.4 1.8 pad_maximum_fusion.2
  12.2 4.1 collective-permute-start
  16.3 7.7 %collective-permute-done = bf16[1,40,2048]{2,1,0:T(8,128)(2,1)S(1)} collective-permute-done((bf16[1,40,2048]{2,1,0:T(8,128)(2,1)S(1)}, bf16[1,40,2048]{2,1,0:T(8,128)(2,1)S(1)}, u32[]{:S(2)}, u32[]{:S(2)}) %collective-permute-start) | collective-permute-done | bytes 163872 | tf_op jit(solution)/shard_map/ppermute | solution.py:501
  24.8 18.0 %collective-permute-done.1 = bf16[2,40,2048]{2,1,0:T(8,128)(2,1)S(1)} collective-permute-done((bf16[2,40,2048]{2,1,0:T(8,128)(2,1)S(1)}, bf16[2,40,2048]{2,1,0:T(8,128)(2,1)S(1)}, u32[]{:S(2)}, u32[]{:S(2)}) %collective-permute-start.1) | collective-permute-done | bytes 327712 | tf_op jit(solution)/shard_map/ppermute | solution.py:501
  42.8 1.3 collective-permute-start.3
  44.2 2.2 collective-permute-start.2
  46.4 6.6 %collective-permute-done.2 = bf16[1,32,2048]{2,1,0:T(8,128)(2,1)S(1)} collective-permute-done((bf16[1,32,2048]{2,1,0:T(8,128)(2,1)S(1)}, bf16[1,32,2048]{2,1,0:T(8,128)(2,1)S(1)}, u32[]{:S(2)}, u32[]{:S(2)}) %collective-permute-start.2) | collective-permute-done | bytes 131104 | tf_op jit(solution)/shard_map/ppermute | solution.py:501
  53.0 3.0 collective-permute-start.4
  56.1 19.8 %collective-permute-done.4 = bf16[2,32,2048]{2,1,0:T(8,128)(2,1)S(1)} collective-permute-done((bf16[2,32,2048]{2,1,0:T(8,128)(2,1)S(1)}, bf16[2,32,2048]{2,1,0:T(8,128)(2,1)S(1)}, u32[]{:S(2)}, u32[]{:S(2)}) %collective-permute-start.4) | collective-permute-done | bytes 262176 | tf_op jit(solution)/shard_map/ppermute | solution.py:501
  77.1 15.7 %collective-permute-done.5 = bf16[4,32,2048]{2,1,0:T(8,128)(2,1)S(1)} collective-permute-done((bf16[4,32,2048]{2,1,0:T(8,128)(2,1)S(1)}, bf16[4,32,2048]{2,1,0:T(8,128)(2,1)S(1)}, u32[]{:S(2)}, u32[]{:S(2)}) %collective-permute-start.5) | collective-permute-done | bytes 524320 | tf_op jit(solution)/shard_map/ppermute | solution.py:501
  95.1 15.1 %collective-permute-done.6.refs_1_ = bf16[8,40,2048]{2,1,0:T(8,128)(2,1)S(1)} collective-permute-done((bf16[8,40,2048]{2,1,0:T(8,128)(2,1)S(1)}, bf16[8,40,2048]{2,1,0:T(8,128)(2,1)S(1)}, u32[]{:S(2)}, u32[]{:S(2)}) %collective-permute-start.6) | collective-permute-done | bytes 1310752 | tf_op jit(solution)/shard_map/ppermute | solution.py:501
  110.8 26.5 %collective-permute-done.9.refs_5_ = bf16[8,32,2048]{2,1,0:T(8,128)(2,1)} collective-permute-done((bf16[8,32,2048]{2,1,0:T(8,128)(2,1)}, bf16[8,32,2048]{2,1,0:T(8,128)(2,1)}, u32[]{:S(2)}, u32[]{:S(2)}) %collective-permute-start.9) | collective-permute-done | bytes 1048608 | tf_op jit(solution)/shard_map/ppermute | solution.py:501
  138.1 2.8 convert_multiply_fusion.dy_ref
  143.1 3.0 unpack_vectors.1
  146.1 8.6 %place_shards.1 = bf16[32,32,4096]{2,1,0:T(8,128)(2,1)} custom-call(s32[32]{0:T(128)} %get-tuple-element.391.t_ref, bf16[8,40,2048]{2,1,0:T(8,128)(2,1)} %copy-done, bf16[8,40,2048]{2,1,0:T(8,128)(2,1)} %copy-done.1, bf16[8,40,2048]{2,1,0:T(8,128)(2,1)} %copy-done.2, bf16[8,40,2048]{2,1,0:T(8,128)(2,1)} %copy-done.3, ...), custom_call_target="tpu_custom_call" | custom-call | flops 1 | bytes 1 | tf_op jit(solution)/shard_map/place_shards/pallas_call | solution.py:551
  154.7 7.9 %norm_project.2 = (bf16[512,1024]{1,0:T(8,128)(2,1)}, bf16[512,3072]{1,0:T(8,128)(2,1)}) custom-call(bf16[512,1024]{1,0:T(8,128)(2,1)} %bitcast.74, f32[1,1024]{1,0:T(1,128)} %get-tuple-element.201.g_ref.refs_4_, f32[1,1024]{1,0:T(1,128)} %get-tuple-element.202.s_ref, bf16[1024,4096]{1,0:T(8,128)(2,1)} %bitcast.65, f32[1,3072]{1,0:T(1,128)} %get-tuple-element.203.b_ref), custom_call_target="tpu_custom_call" | custom-call | flops 1 | bytes 1 | tf_op jit(solution)/shard_map/norm_project/pallas_call | solution.py:54
  163.2 10.8 %attention.2 = (bf16[512,1024]{1,0:T(8,128)(2,1)}, f32[8,8,512]{2,1,0:T(8,128)}) custom-call(bf16[512,3072]{1,0:T(8,128)(2,1)} %get-tuple-element.204.q_ref.k_ref.v_ref, bf16[512,3072]{1,0:T(8,128)(2,1)} %get-tuple-element.204.q_ref.k_ref.v_ref, bf16[512,3072]{1,0:T(8,128)(2,1)} %get-tuple-element.204.q_ref.k_ref.v_ref), custom_call_target="tpu_custom_call" | custom-call | flops 1 | bytes 1 | tf_op jit(solution)/shard_map/attention/pallas_call | solution.py:99
  174.0 4.9 project_norm.2
  179.0 17.9 %feed_forward.2 = (bf16[512,4096]{1,0:T(8,128)(2,1)}, bf16[512,4096]{1,0:T(8,128)(2,1)}, bf16[512,1024]{1,0:T(8,128)(2,1)}) custom-call(bf16[512,1024]{1,0:T(8,128)(2,1)} %get-tuple-element.251.a_ref.refs_0_.refs_1_, bf16[32,256,1024]{2,1,0:T(8,128)(2,1)} %bitcast.57, f32[1,4096]{1,0:T(1,128)} %get-tuple-element.211.ub_ref, bf16[32,256,1024]{2,1,0:T(8,128)(2,1)} %bitcast.58, ...), custom_call_target="tpu_custom_call" | custom-call | flops 1 | bytes 1 | tf_op jit(solution)/shard_map/feed_forward/pallas_call | solution.py:229
  196.8 8.0 %norm_project.3 = (bf16[512,1024]{1,0:T(8,128)(2,1)}, bf16[512,3072]{1,0:T(8,128)(2,1)}) custom-call(bf16[512,1024]{1,0:T(8,128)(2,1)} %get-tuple-element.215.x_ref.refs_3_, f32[1,1024]{1,0:T(1,128)} %get-tuple-element.201.g_ref.refs_4_, f32[1,1024]{1,0:T(1,128)} %get-tuple-element.202.s_ref, bf16[1024,4096]{1,0:T(8,128)(2,1)} %bitcast.67, ...), custom_call_target="tpu_custom_call" | custom-call | flops 1 | bytes 1 | tf_op jit(solution)/shard_map/norm_project/pallas_call | solution.py:54
  205.7 10.8 %attention.3 = (bf16[512,1024]{1,0:T(8,128)(2,1)}, f32[8,8,512]{2,1,0:T(8,128)}) custom-call(bf16[512,3072]{1,0:T(8,128)(2,1)} %get-tuple-element.216.q_ref.k_ref.v_ref, bf16[512,3072]{1,0:T(8,128)(2,1)} %get-tuple-element.216.q_ref.k_ref.v_ref, bf16[512,3072]{1,0:T(8,128)(2,1)} %get-tuple-element.216.q_ref.k_ref.v_ref), custom_call_target="tpu_custom_call" | custom-call | flops 1 | bytes 1 | tf_op jit(solution)/shard_map/attention/pallas_call | solution.py:99
  216.5 4.9 project_norm.3
  221.4 17.9 %feed_forward.3 = (bf16[512,4096]{1,0:T(8,128)(2,1)}, bf16[512,4096]{1,0:T(8,128)(2,1)}, bf16[512,1024]{1,0:T(8,128)(2,1)}) custom-call(bf16[512,1024]{1,0:T(8,128)(2,1)} %get-tuple-element.252.a_ref.refs_2_.refs_3_, bf16[32,256,1024]{2,1,0:T(8,128)(2,1)} %bitcast.59, f32[1,4096]{1,0:T(1,128)} %get-tuple-element.211.ub_ref, bf16[32,256,1024]{2,1,0:T(8,128)(2,1)} %bitcast.60, ...), custom_call_target="tpu_custom_call" | custom-call | flops 1 | bytes 1 | tf_op jit(solution)/shard_map/feed_forward/pallas_call | solution.py:229
  239.3 20.2 %feed_forward_back.2 = (bf16[512,1024]{1,0:T(8,128)(2,1)}, bf16[512,4096]{1,0:T(8,128)(2,1)}, f32[512,1024]{1,0:T(8,128)}, bf16[512,1024]{1,0:T(8,128)(2,1)}, bf...) custom-call(f32[512,1024]{1,0:T(8,128)} %convert_multiply_fusion.dy_, ...), custom_call_target="tpu_custom_call" | custom-call | flops 1 | bytes 1 | tf_op jit(solution)/shard_map/feed_forward_back/pallas_call | solution.py:298
  259.5 8.9 %attention_back.4 = (bf16[3,512,512]{2,1,0:T(8,128)(2,1)}, f32[1,512]{1,0:T(1,128)}, f32[1,512]{1,0:T(1,128)}) custom-call(bf16[512,3072]{1,0:T(8,128)(2,1)} %get-tuple-element.216.q_ref.k_ref.v_ref, bf16[512,3072]{1,0:T(8,128)(2,1)} %get-tuple-element.216.q_ref.k_ref.v_ref, bf16[512,3072]{1,0:T(8,128)(2,1)} %get-tuple-element.216.q_ref.k_ref.v_ref, ...), custom_call_target="tpu_custom_call" | custom-call | flops 1 | bytes 1 | tf_op jit(solution)/shard_map/attention_back/pallas_call | solution.py:145
  268.5 8.5 %attention_back.5 = (bf16[3,512,512]{2,1,0:T(8,128)(2,1)}, f32[1,512]{1,0:T(1,128)}, f32[1,512]{1,0:T(1,128)}) custom-call(bf16[512,3072]{1,0:T(8,128)(2,1)} %get-tuple-element.216.q_ref.k_ref.v_ref, bf16[512,3072]{1,0:T(8,128)(2,1)} %get-tuple-element.216.q_ref.k_ref.v_ref, bf16[512,3072]{1,0:T(8,128)(2,1)} %get-tuple-element.216.q_ref.k_ref.v_ref, ...), custom_call_target="tpu_custom_call" | custom-call | flops 1 | bytes 1 | tf_op jit(solution)/shard_map/attention_back/pallas_call | solution.py:145
  277.0 10.0 %project_back.2 = (f32[512,1024]{1,0:T(8,128)}, f32[1,1024]{1,0:T(1,128)}, f32[1,1024]{1,0:T(1,128)}) custom-call(bf16[3,512,512]{2,1,0:T(8,128)(2,1)} %get-tuple-element.236.refs_0_.refs_5_, bf16[3,512,512]{2,1,0:T(8,128)(2,1)} %get-tuple-element.237.refs_1_.refs_5_, bf16[1024,4096]{1,0:T(8,128)(2,1)} %bitcast.70, ...), custom_call_target="tpu_custom_call" | custom-call | flops 1 | bytes 1 | tf_op jit(solution)/shard_map/project_back/pallas_call | solution.py:387
  287.0 2.8 convert_element_type.174.refs_4_
  289.8 10.0 %weight_grad.10 = bf16[16,128,1024]{2,1,0:T(8,128)(2,1)} custom-call(s32[18]{0:T(128)} %pad_add_fusion.1.i_ref, bf16[512,4096]{1,0:T(8,128)(2,1)} %get-tuple-element.240.refs_0_.refs_1_, bf16[512,4096]{1,0:T(8,128)(2,1)} %get-tuple-element.240.refs_0_.refs_1_, bf16[512,4096]{1,0:T(8,128)(2,1)} %get-tuple-element.241.refs_2_.refs_3_, ...), custom_call_target="tpu_custom_call" | custom-call | flops 1 | bytes 1 | tf_op jit(solution)/shard_map/weight_grad/pallas_call | solution.py:445
  300.4 6.9 %collective-permute-done.12.refs_6_ = bf16[16,128,1024]{2,1,0:T(8,128)(2,1)} collective-permute-done((bf16[16,128,1024]{2,1,0:T(8,128)(2,1)}, bf16[16,128,1024]{2,1,0:T(8,128)(2,1)}, u32[]{:S(2)}, u32[]{:S(2)}) %collective-permute-start.12) | collective-permute-done | bytes 4194336 | tf_op jit(solution)/shard_map/ppermute | solution.py:501
  307.3 10.8 %weight_grad.11 = (bf16[8,128,1024]{2,1,0:T(8,128)(2,1)}, bf16[8,128,1024]{2,1,0:T(8,128)(2,1)}) custom-call(s32[18]{0:T(128)} %pad_add_fusion.i_ref, bf16[512,4096]{1,0:T(8,128)(2,1)} %get-tuple-element.240.refs_0_.refs_1_, bf16[512,4096]{1,0:T(8,128)(2,1)} %get-tuple-element.240.refs_0_.refs_1_, bf16[512,4096]{1,0:T(8,128)(2,1)} %get-tuple-element.241.refs_2_.refs_3_, ...), custom_call_target="tpu_custom_call" | custom-call | flops 1 | bytes 1 | tf_op jit(solution)/shard_map/weight_grad/pallas_call | solution.py:445
  319.1 20.5 %feed_forward_back.3 = (bf16[512,1024]{1,0:T(8,128)(2,1)}, bf16[512,4096]{1,0:T(8,128)(2,1)}, f32[512,1024]{1,0:T(8,128)}, bf16[512,1024]{1,0:T(8,128)(2,1)}, bf...) custom-call(f32[512,1024]{1,0:T(8,128)} %get-tuple-element.244.dy_re, ...), custom_call_target="tpu_custom_call" | custom-call | flops 1 | bytes 1 | tf_op jit(solution)/shard_map/feed_forward_back/pallas_call | solution.py:298
  339.6 4.8 collective-permute-done.13
  344.4 2.6 add_convert_fusion.1
  347.1 9.8 %weight_grad.12 = bf16[16,32,4096]{2,1,0:T(8,128)(2,1)} custom-call(s32[18]{0:T(128)} %pad_add_fusion.1.i_ref, bf16[512,1024]{1,0:T(8,128)(2,1)} %get-tuple-element.251.a_ref.refs_0_.refs_1_, bf16[512,1024]{1,0:T(8,128)(2,1)} %get-tuple-element.251.a_ref.refs_0_.refs_1_, bf16[512,1024]{1,0:T(8,128)(2,1)} %get-tuple-element.252.a_ref.refs_2_.refs_3_, ...), custom_call_target="tpu_custom_call" | custom-call | flops 1 | bytes 1 | tf_op jit(solution)/shard_map/weight_grad/pallas_call | solution.py:445
  356.9 1.6 collective-permute-start.14
  358.5 13.2 %collective-permute-done.14 = bf16[4,128,1024]{2,1,0:T(8,128)(2,1)S(1)} collective-permute-done((bf16[4,128,1024]{2,1,0:T(8,128)(2,1)S(1)}, bf16[4,128,1024]{2,1,0:T(8,128)(2,1)S(1)}, u32[]{:S(2)}, u32[]{:S(2)}) %collective-permute-start.14) | collective-permute-done | bytes 1048608 | tf_op jit(solution)/shard_map/ppermute | solution.py:501
  372.3 10.9 %weight_grad.13 = (bf16[8,32,4096]{2,1,0:T(8,128)(2,1)}, bf16[8,32,4096]{2,1,0:T(8,128)(2,1)}) custom-call(s32[18]{0:T(128)} %pad_add_fusion.i_ref, bf16[512,1024]{1,0:T(8,128)(2,1)} %get-tuple-element.251.a_ref.refs_0_.refs_1_, bf16[512,1024]{1,0:T(8,128)(2,1)} %get-tuple-element.251.a_ref.refs_0_.refs_1_, ...), custom_call_target="tpu_custom_call" | custom-call | flops 1 | bytes 1 | tf_op jit(solution)/shard_map/weight_grad/pallas_call | solution.py:445
  384.2 1.5 collective-permute-done.16
  386.0 4.9 weight_grad.14
  390.9 5.9 %collective-permute-start.18 = (bf16[1,128,1024]{2,1,0:T(8,128)(2,1)S(1)}, bf16[1,128,1024]{2,1,0:T(8,128)(2,1)S(1)}, u32[]{:S(2)}, u32[]{:S(2)}) collective-permute-start(bf16[1,128,1024]{2,1,0:T(8,128)(2,1)S(1)} %get-tuple-element.361), channel_id=1, source_target_pairs={{0,4},{1,5},{2,6},{3,7},{4,0},{5,1},{6,2},{7,3},{8,12},{9,13},{10,... | collective-permute-start | bytes 786440 | tf_op jit(solution)/shard_map/ppermute | solution.py:501
  396.9 8.7 %attention_back.6 = (bf16[3,512,512]{2,1,0:T(8,128)(2,1)}, f32[1,512]{1,0:T(1,128)}, f32[1,512]{1,0:T(1,128)}) custom-call(bf16[512,3072]{1,0:T(8,128)(2,1)} %get-tuple-element.204.q_ref.k_ref.v_ref, bf16[512,3072]{1,0:T(8,128)(2,1)} %get-tuple-element.204.q_ref.k_ref.v_ref, bf16[512,3072]{1,0:T(8,128)(2,1)} %get-tuple-element.204.q_ref.k_ref.v_ref, ...), custom_call_target="tpu_custom_call" | custom-call | flops 1 | bytes 1 | tf_op jit(solution)/shard_map/attention_back/pallas_call | solution.py:145
  406.5 5.2 weight_grad.15
  412.6 6.2 %weight_grad.16 = bf16[16,32,1536]{2,1,0:T(8,128)(2,1)} custom-call(s32[18]{0:T(128)} %pad_add_fusion.1.i_ref, bf16[512,1024]{1,0:T(8,128)(2,1)} %get-tuple-element.281.refs_0_.refs_1_, bf16[512,1024]{1,0:T(8,128)(2,1)} %get-tuple-element.281.refs_0_.refs_1_, bf16[512,1024]{1,0:T(8,128)(2,1)} %get-tuple-element.282.refs_2_.refs_3_, ...), custom_call_target="tpu_custom_call" | custom-call | flops 1 | bytes 1 | tf_op jit(solution)/shard_map/weight_grad/pallas_call | solution.py:445
  419.0 2.4 add_convert_fusion
  421.6 1.7 collective-permute-start.21
  423.3 6.5 %weight_grad.17 = (bf16[8,32,1536]{2,1,0:T(8,128)(2,1)}, bf16[8,32,1536]{2,1,0:T(8,128)(2,1)}) custom-call(s32[18]{0:T(128)} %pad_add_fusion.i_ref, bf16[512,1024]{1,0:T(8,128)(2,1)} %get-tuple-element.281.refs_0_.refs_1_, bf16[512,1024]{1,0:T(8,128)(2,1)} %get-tuple-element.281.refs_0_.refs_1_, bf16[512,1024]{1,0:T(8,128)(2,1)} %get-tuple-element.282.refs_2_.refs_3_, ...), custom_call_target="tpu_custom_call" | custom-call | flops 1 | bytes 1 | tf_op jit(solution)/shard_map/weight_grad/pallas_call | solution.py:445
  429.8 8.5 %attention_back.7 = (bf16[3,512,512]{2,1,0:T(8,128)(2,1)}, f32[1,512]{1,0:T(1,128)}, f32[1,512]{1,0:T(1,128)}) custom-call(bf16[512,3072]{1,0:T(8,128)(2,1)} %get-tuple-element.204.q_ref.k_ref.v_ref, bf16[512,3072]{1,0:T(8,128)(2,1)} %get-tuple-element.204.q_ref.k_ref.v_ref, bf16[512,3072]{1,0:T(8,128)(2,1)} %get-tuple-element.204.q_ref.k_ref.v_ref, ...), custom_call_target="tpu_custom_call" | custom-call | flops 1 | bytes 1 | tf_op jit(solution)/shard_map/attention_back/pallas_call | solution.py:145
  439.5 6.2 %weight_grad.18 = bf16[16,32,1536]{2,1,0:T(8,128)(2,1)} custom-call(s32[18]{0:T(128)} %pad_add_fusion.1.i_ref, bf16[512,1024]{1,0:T(8,128)(2,1)} %get-tuple-element.281.refs_0_.refs_1_, bf16[512,1024]{1,0:T(8,128)(2,1)} %get-tuple-element.281.refs_0_.refs_1_, bf16[512,1024]{1,0:T(8,128)(2,1)} %get-tuple-element.282.refs_2_.refs_3_, ...), custom_call_target="tpu_custom_call" | custom-call | flops 1 | bytes 1 | tf_op jit(solution)/shard_map/weight_grad/pallas_call | solution.py:445
  451.8 6.5 %weight_grad.19 = (bf16[8,32,1536]{2,1,0:T(8,128)(2,1)}, bf16[8,32,1536]{2,1,0:T(8,128)(2,1)}) custom-call(s32[18]{0:T(128)} %pad_add_fusion.i_ref, bf16[512,1024]{1,0:T(8,128)(2,1)} %get-tuple-element.281.refs_0_.refs_1_, bf16[512,1024]{1,0:T(8,128)(2,1)} %get-tuple-element.281.refs_0_.refs_1_, bf16[512,1024]{1,0:T(8,128)(2,1)} %get-tuple-element.282.refs_2_.refs_3_, ...), custom_call_target="tpu_custom_call" | custom-call | flops 1 | bytes 1 | tf_op jit(solution)/shard_map/weight_grad/pallas_call | solution.py:445
  458.3 6.7 %collective-permute-done.23 = bf16[8,32,2560]{2,1,0:T(8,128)(2,1)} collective-permute-done((bf16[8,32,2560]{2,1,0:T(8,128)(2,1)}, bf16[8,32,2560]{2,1,0:T(8,128)(2,1)}, u32[]{:S(2)}, u32[]{:S(2)}) %collective-permute-start.23) | collective-permute-done | bytes 1310752 | tf_op jit(solution)/shard_map/ppermute | solution.py:501
  465.0 1.6 add_convert_fusion.2
  470.6 9.3 %project_back.3 = (bf16[512,1024]{1,0:T(8,128)(2,1)}, f32[1,1024]{1,0:T(1,128)}, f32[1,1024]{1,0:T(1,128)}) custom-call(bf16[3,512,512]{2,1,0:T(8,128)(2,1)} %get-tuple-element.291.refs_4_.refs_0_, bf16[3,512,512]{2,1,0:T(8,128)(2,1)} %get-tuple-element.292.refs_4_.refs_1_, bf16[1024,4096]{1,0:T(8,128)(2,1)} %bitcast.72, bf16[512,1024]{1,0:T(8,128)(2,1)} %bitcast.76, ...), custom_call_target="tpu_custom_call" | custom-call | flops 1 | bytes 1 | tf_op jit(solution)/shard_map/project_back/pallas_call | solution.py:387
  479.9 2.5 pack_sums.1
  483.6 1.2 add_convert_fusion.6
  484.8 2.6 collective-permute-start.28
  488.8 1.8 add_bitcast_fusion
  490.6 4.4 collective-permute-done.28
  495.1 2.7 collective-permute-start.31
  497.9 1.6 collective-permute-start.32
  500.7 4.8 collective-permute-done.31
  508.4 5.4 %collective-permute-done.34 = bf16[1,32,1536]{2,1,0:T(8,128)(2,1)S(1)} collective-permute-done((bf16[1,32,1536]{2,1,0:T(8,128)(2,1)S(1)}, bf16[1,32,1536]{2,1,0:T(8,128)(2,1)S(1)}, u32[]{:S(2)}, u32[]{:S(2)}) %collective-permute-start.34) | collective-permute-done | bytes 98336 | tf_op jit(solution)/shard_map/ppermute | solution.py:501
  514.6 3.1 collective-permute-done.36
  518.8 3.6 collective-permute-done.37
  (211 shorter events, 39.1 us)
Async XLA Ops:
  7.2 3.1 copy-start.26
  7.2 3.1 copy-start.27
  7.2 3.1 copy-start.28
  7.2 3.1 copy-start.29
  7.2 3.1 copy-start.30
  7.3 3.1 copy-start.31
  7.3 4.8 copy-start.32
  7.3 4.9 slice-start
  7.3 171.7 %all-gather.3.cloned.1.call-start = ((), (), s32[]{:S(2)}) async-start(), calls=%async_computation | async-start | bytes 17301504 | tf_op jit(solution)/shard_map/all_gather | solution.py:706
  8.4 35.8 %slice-start.1 = ((bf16[32,3072]{1,0:T(8,128)(2,1)}), bf16[32,1024]{1,0:T(8,128)(2,1)S(1)}, s32[]{:S(2)}) async-start(bf16[32,3072]{1,0:T(8,128)(2,1)} %param.21), calls=%async_computation.2 | async-start | bytes 131072 | tf_op jit(solution)/shard_map/slice | solution.py:703
  8.4 35.8 %copy-start.13 = (bf16[32,1024]{1,0:T(8,128)(2,1)S(1)}, bf16[32,1024]{1,0:T(8,128)(2,1)}, u32[]{:S(2)}) copy-start(bf16[32,1024]{1,0:T(8,128)(2,1)} %param.24) | copy-start | bytes 196612
  12.2 11.8 %collective-permute-start = (bf16[1,40,2048]{2,1,0:T(8,128)(2,1)S(1)}, bf16[1,40,2048]{2,1,0:T(8,128)(2,1)S(1)}, u32[]{:S(2)}, u32[]{:S(2)}) collective-permute-start(bf16[1,40,2048]{2,1,0:T(8,128)(2,1)S(1)} %fusion.2), channel_id=1, source_target_pairs={{0,4},{1,5},{2,6},{3,7},{4,0},{5,1},{6,2},{7,3},{8,12},{9,13},{10,... | collective-permute-start | bytes 491528 | tf_op jit(solution)/shard_map/ppermute | solution.py:501
  24.0 18.8 %collective-permute-start.1 = (bf16[2,40,2048]{2,1,0:T(8,128)(2,1)S(1)}, bf16[2,40,2048]{2,1,0:T(8,128)(2,1)S(1)}, u32[]{:S(2)}, u32[]{:S(2)}) collective-permute-start(bf16[2,40,2048]{2,1,0:T(8,128)(2,1)S(1)} %pad_maximum_fusion.3), channel_id=1, source_target_pairs={{0,2},{1,3},{2,0},{3,1},{4,6},{5,7},{6,4},{7,5},{8,10},{9,11},{10,... | collective-permute-start | bytes 983048 | tf_op jit(solution)/shard_map/ppermute | solution.py:501
  42.8 13.1 %collective-permute-start.3 = (bf16[4,40,2048]{2,1,0:T(8,128)(2,1)S(1)}, bf16[4,40,2048]{2,1,0:T(8,128)(2,1)S(1)}, u32[]{:S(2)}, u32[]{:S(2)}) collective-permute-start(bf16[4,40,2048]{2,1,0:T(8,128)(2,1)S(1)} %constant_dynamic-update-slice_fusion), channel_id=1, source_target_pairs={{0,1},{1,0},{2,3},{3,2},{4,5},{5,4},{6,7},{7,6},{8,24},{9,25},{10,... | collective-permute-start | bytes 1966088 | tf_op jit(solution)/shard_map/ppermute | solution.py:501
  44.2 8.8 %collective-permute-start.2 = (bf16[1,32,2048]{2,1,0:T(8,128)(2,1)S(1)}, bf16[1,32,2048]{2,1,0:T(8,128)(2,1)S(1)}, u32[]{:S(2)}, u32[]{:S(2)}) collective-permute-start(bf16[1,32,2048]{2,1,0:T(8,128)(2,1)S(1)} %maximum_bitcast_fusion), channel_id=1, source_target_pairs={{0,4},{1,5},{2,6},{3,7},{4,0},{5,1},{6,2},{7,3},{8,12},{9,13},{10,... | collective-permute-start | bytes 393224 | tf_op jit(solution)/shard_map/ppermute | solution.py:501
  53.0 22.9 %collective-permute-start.4 = (bf16[2,32,2048]{2,1,0:T(8,128)(2,1)S(1)}, bf16[2,32,2048]{2,1,0:T(8,128)(2,1)S(1)}, u32[]{:S(2)}, u32[]{:S(2)}) collective-permute-start(bf16[2,32,2048]{2,1,0:T(8,128)(2,1)S(1)} %constant_dynamic-update-slice_fusion.2), channel_id=1, source_target_pairs={{0,2},{1,3},{2,0},{3,1},{4,6},{5,7},{6,4},{7,5},{8,10},{9,11},{10,... | collective-permute-start | bytes 786440 | tf_op jit(solution)/shard_map/ppermute | solution.py:501
  56.0 82.1 %copy-start.15 = (s32[1,512]{1,0:T(1,128)S(1)}, s32[1,512]{1,0:T(1,128)}, u32[]{:S(2)}) copy-start(s32[1,512]{1,0:T(1,128)} %param.34) | copy-start | bytes 6148
  56.1 84.8 %copy-start = (bf16[8,40,2048]{2,1,0:T(8,128)(2,1)}, bf16[8,40,2048]{2,1,0:T(8,128)(2,1)S(1)}, u32[]{:S(2)}) copy-start(bf16[8,40,2048]{2,1,0:T(8,128)(2,1)S(1)} %constant_dynamic-update-slice_fusion.4.refs_0_) | copy-start | bytes 3932164
  75.9 16.8 %collective-permute-start.5 = (bf16[4,32,2048]{2,1,0:T(8,128)(2,1)S(1)}, bf16[4,32,2048]{2,1,0:T(8,128)(2,1)S(1)}, u32[]{:S(2)}, u32[]{:S(2)}) collective-permute-start(bf16[4,32,2048]{2,1,0:T(8,128)(2,1)S(1)} %constant_dynamic-update-slice_fusion.6), channel_id=1, source_target_pairs={{0,1},{1,0},{2,3},{3,2},{4,5},{5,4},{6,7},{7,6},{8,24},{9,25},{10,... | collective-permute-start | bytes 1572872 | tf_op jit(solution)/shard_map/ppermute | solution.py:501
  77.1 33.1 %collective-permute-start.6 = (bf16[8,40,2048]{2,1,0:T(8,128)(2,1)S(1)}, bf16[8,40,2048]{2,1,0:T(8,128)(2,1)S(1)}, u32[]{:S(2)}, u32[]{:S(2)}) collective-permute-start(bf16[8,40,2048]{2,1,0:T(8,128)(2,1)S(1)} %constant_dynamic-update-slice_fusion.4.refs_0_), channel_id=1, source_target_pairs={{0,16},{1,17},{2,18},{3,19},{4,20},{5,21},{6,22},{7,23},{8,9},{9,8... | collective-permute-start | bytes 3932168 | tf_op jit(solution)/shard_map/ppermute | solution.py:501
  94.4 42.9 %collective-permute-start.9 = (bf16[8,32,2048]{2,1,0:T(8,128)(2,1)}, bf16[8,32,2048]{2,1,0:T(8,128)(2,1)}, u32[]{:S(2)}, u32[]{:S(2)}) collective-permute-start(bf16[8,32,2048]{2,1,0:T(8,128)(2,1)} %constant_dynamic-update-slice_fusion.8.refs_4_), channel_id=1, source_target_pairs={{0,16},{1,17},{2,18},{3,19},{4,20},{5,21},{6,22},{7,23},{8,9},{9,8... | collective-permute-start | bytes 3145736 | tf_op jit(solution)/shard_map/ppermute | solution.py:501
  95.1 45.8 %collective-permute-start.7 = (bf16[8,40,2048]{2,1,0:T(8,128)(2,1)S(1)}, bf16[8,40,2048]{2,1,0:T(8,128)(2,1)S(1)}, u32[]{:S(2)}, u32[]{:S(2)}) collective-permute-start(bf16[8,40,2048]{2,1,0:T(8,128)(2,1)S(1)} %constant_dynamic-update-slice_fusion.4.refs_0_), channel_id=1, source_target_pairs={{0,8},{1,9},{2,10},{3,11},{4,12},{5,13},{6,14},{7,15},{8,0},{9,1},... | collective-permute-start | bytes 3932168 | tf_op jit(solution)/shard_map/ppermute | solution.py:501
  110.2 32.8 %copy-start.1 = (bf16[8,40,2048]{2,1,0:T(8,128)(2,1)}, bf16[8,40,2048]{2,1,0:T(8,128)(2,1)S(1)}, u32[]{:S(2)}) copy-start(bf16[8,40,2048]{2,1,0:T(8,128)(2,1)S(1)} %collective-permute-done.6.refs_1_) | copy-start | bytes 3932164
  110.2 30.7 %collective-permute-start.8 = (bf16[8,40,2048]{2,1,0:T(8,128)(2,1)S(1)}, bf16[8,40,2048]{2,1,0:T(8,128)(2,1)S(1)}, u32[]{:S(2)}, u32[]{:S(2)}) collective-permute-start(bf16[8,40,2048]{2,1,0:T(8,128)(2,1)S(1)} %collective-permute-done.6.refs_1_), channel_id=1, source_target_pairs={{0,8},{1,9},{2,10},{3,11},{4,12},{5,13},{6,14},{7,15},{8,0},{9,1},... | collective-permute-start | bytes 3932168 | tf_op jit(solution)/shard_map/ppermute | solution.py:501
  110.3 35.8 %collective-permute-start.10 = (bf16[8,32,2048]{2,1,0:T(8,128)(2,1)}, bf16[8,32,2048]{2,1,0:T(8,128)(2,1)}, u32[]{:S(2)}, u32[]{:S(2)}) collective-permute-start(bf16[8,32,2048]{2,1,0:T(8,128)(2,1)} %constant_dynamic-update-slice_fusion.8.refs_4_), channel_id=1, source_target_pairs={{0,8},{1,9},{2,10},{3,11},{4,12},{5,13},{6,14},{7,15},{8,0},{9,1},... | collective-permute-start | bytes 3145736 | tf_op jit(solution)/shard_map/ppermute | solution.py:501
  137.3 8.7 %collective-permute-start.11 = (bf16[8,32,2048]{2,1,0:T(8,128)(2,1)}, bf16[8,32,2048]{2,1,0:T(8,128)(2,1)}, u32[]{:S(2)}, u32[]{:S(2)}) collective-permute-start(bf16[8,32,2048]{2,1,0:T(8,128)(2,1)} %collective-permute-done.9.refs_5_), channel_id=1, source_target_pairs={{0,8},{1,9},{2,10},{3,11},{4,12},{5,13},{6,14},{7,15},{8,0},{9,1},... | collective-permute-start | bytes 3145736 | tf_op jit(solution)/shard_map/ppermute | solution.py:501
  299.8 7.5 %collective-permute-start.12 = (bf16[16,128,1024]{2,1,0:T(8,128)(2,1)}, bf16[16,128,1024]{2,1,0:T(8,128)(2,1)}, u32[]{:S(2)}, u32[]{:S(2)}) collective-permute-start(bf16[16,128,1024]{2,1,0:T(8,128)(2,1)} %weight_grad.10), channel_id=1, source_target_pairs={{0,8},{1,9},{2,10},{3,11},{4,12},{5,13},{6,14},{7,15},{8,0},{9,1},... | collective-permute-start | bytes 12582920 | tf_op jit(solution)/shard_map/ppermute | solution.py:501
  318.1 26.4 %collective-permute-start.13 = (bf16[8,128,1024]{2,1,0:T(8,128)(2,1)}, bf16[8,128,1024]{2,1,0:T(8,128)(2,1)}, u32[]{:S(2)}, u32[]{:S(2)}) collective-permute-start(bf16[8,128,1024]{2,1,0:T(8,128)(2,1)} %get-tuple-element.243), channel_id=1, source_target_pairs={{0,16},{1,17},{2,18},{3,19},{4,20},{5,21},{6,22},{7,23},{8,9},{9,8... | collective-permute-start | bytes 6291464 | tf_op jit(solution)/shard_map/ppermute | solution.py:501
  319.1 25.3 %copy-start.5 = (bf16[8,128,1024]{2,1,0:T(8,128)(2,1)S(1)}, bf16[8,128,1024]{2,1,0:T(8,128)(2,1)}, u32[]{:S(2)}) copy-start(bf16[8,128,1024]{2,1,0:T(8,128)(2,1)} %get-tuple-element.249) | copy-start | bytes 6291460
  356.9 15.4 %collective-permute-start.15 = (bf16[16,32,4096]{2,1,0:T(8,128)(2,1)}, bf16[16,32,4096]{2,1,0:T(8,128)(2,1)}, u32[]{:S(2)}, u32[]{:S(2)}) collective-permute-start(bf16[16,32,4096]{2,1,0:T(8,128)(2,1)} %weight_grad.12), channel_id=1, source_target_pairs={{0,8},{1,9},{2,10},{3,11},{4,12},{5,13},{6,14},{7,15},{8,0},{9,1},... | collective-permute-start | bytes 12582920 | tf_op jit(solution)/shard_map/ppermute | solution.py:501
  356.9 14.8 %collective-permute-start.14 = (bf16[4,128,1024]{2,1,0:T(8,128)(2,1)S(1)}, bf16[4,128,1024]{2,1,0:T(8,128)(2,1)S(1)}, u32[]{:S(2)}, u32[]{:S(2)}) collective-permute-start(bf16[4,128,1024]{2,1,0:T(8,128)(2,1)S(1)} %get-tuple-element.347), channel_id=1, source_target_pairs={{0,1},{1,0},{2,3},{3,2},{4,5},{5,4},{6,7},{7,6},{8,24},{9,25},{10,... | collective-permute-start | bytes 3145736 | tf_op jit(solution)/shard_map/ppermute | solution.py:501
  372.2 13.5 %collective-permute-start.16 = (bf16[2,128,1024]{2,1,0:T(8,128)(2,1)S(1)}, bf16[2,128,1024]{2,1,0:T(8,128)(2,1)S(1)}, u32[]{:S(2)}, u32[]{:S(2)}) collective-permute-start(bf16[2,128,1024]{2,1,0:T(8,128)(2,1)S(1)} %get-tuple-element.353), channel_id=1, source_target_pairs={{0,2},{1,3},{2,0},{3,1},{4,6},{5,7},{6,4},{7,5},{8,10},{9,11},{10,... | collective-permute-start | bytes 1572872 | tf_op jit(solution)/shard_map/ppermute | solution.py:501
  383.1 35.9 %collective-permute-start.19 = (bf16[8,32,4096]{2,1,0:T(8,128)(2,1)}, bf16[8,32,4096]{2,1,0:T(8,128)(2,1)}, u32[]{:S(2)}, u32[]{:S(2)}) collective-permute-start(bf16[8,32,4096]{2,1,0:T(8,128)(2,1)} %get-tuple-element.256), channel_id=1, source_target_pairs={{0,16},{1,17},{2,18},{3,19},{4,20},{5,21},{6,22},{7,23},{8,9},{9,8... | collective-permute-start | bytes 6291464 | tf_op jit(solution)/shard_map/ppermute | solution.py:501
  390.9 14.6 %collective-permute-start.17 = (bf16[16,32,1024]{2,1,0:T(8,128)(2,1)}, bf16[16,32,1024]{2,1,0:T(8,128)(2,1)S(1)}, u32[]{:S(2)}, u32[]{:S(2)}) collective-permute-start(bf16[16,32,1024]{2,1,0:T(8,128)(2,1)} %weight_grad.14), channel_id=1, source_target_pairs={{0,8},{1,9},{2,10},{3,11},{4,12},{5,13},{6,14},{7,15},{8,0},{9,1},... | collective-permute-start | bytes 3145736 | tf_op jit(solution)/shard_map/ppermute | solution.py:501
  390.9 20.9 %collective-permute-start.18 = (bf16[1,128,1024]{2,1,0:T(8,128)(2,1)S(1)}, bf16[1,128,1024]{2,1,0:T(8,128)(2,1)S(1)}, u32[]{:S(2)}, u32[]{:S(2)}) collective-permute-start(bf16[1,128,1024]{2,1,0:T(8,128)(2,1)S(1)} %get-tuple-element.361), channel_id=1, source_target_pairs={{0,4},{1,5},{2,6},{3,7},{4,0},{5,1},{6,2},{7,3},{8,12},{9,13},{10,... | collective-permute-start | bytes 786440 | tf_op jit(solution)/shard_map/ppermute | solution.py:501
  412.6 6.4 %copy-start.4 = (bf16[8,32,4096]{2,1,0:T(8,128)(2,1)S(1)}, bf16[8,32,4096]{2,1,0:T(8,128)(2,1)}, u32[]{:S(2)}) copy-start(bf16[8,32,4096]{2,1,0:T(8,128)(2,1)} %get-tuple-element.273) | copy-start | bytes 6291460
  418.8 4.5 collective-permute-start.20
  421.6 16.7 %collective-permute-start.21 = (bf16[4,32,4096]{2,1,0:T(8,128)(2,1)S(1)}, bf16[4,32,4096]{2,1,0:T(8,128)(2,1)S(1)}, u32[]{:S(2)}, u32[]{:S(2)}) collective-permute-start(bf16[4,32,4096]{2,1,0:T(8,128)(2,1)S(1)} %get-tuple-element.345), channel_id=1, source_target_pairs={{0,1},{1,0},{2,3},{3,2},{4,5},{5,4},{6,7},{7,6},{8,24},{9,25},{10,... | collective-permute-start | bytes 3145736 | tf_op jit(solution)/shard_map/ppermute | solution.py:501
  439.5 6.4 %copy-start.10 = (bf16[8,32,1536]{2,1,0:T(8,128)(2,1)S(1)}, bf16[8,32,1536]{2,1,0:T(8,128)(2,1)}, u32[]{:S(2)}) copy-start(bf16[8,32,1536]{2,1,0:T(8,128)(2,1)} %get-tuple-element.276) | copy-start | bytes 2359300
  439.5 6.4 %copy-start.12 = (bf16[8,32,1024]{2,1,0:T(8,128)(2,1)S(1)}, bf16[8,32,1024]{2,1,0:T(8,128)(2,1)}, u32[]{:S(2)}) copy-start(bf16[8,32,1024]{2,1,0:T(8,128)(2,1)} %get-tuple-element.267) | copy-start | bytes 1572868
  445.7 3.1 copy-start.20
  445.7 3.1 copy-start.21
  445.8 3.1 copy-start.22
  445.8 3.1 copy-start.23
  445.8 3.7 copy-start.9
  445.8 3.7 copy-start.11
  445.8 4.8 collective-permute-start.22
  447.1 17.9 %collective-permute-start.23 = (bf16[8,32,2560]{2,1,0:T(8,128)(2,1)}, bf16[8,32,2560]{2,1,0:T(8,128)(2,1)}, u32[]{:S(2)}, u32[]{:S(2)}) collective-permute-start(bf16[8,32,2560]{2,1,0:T(8,128)(2,1)} %pad_maximum_fusion.1), channel_id=1, source_target_pairs={{0,16},{1,17},{2,18},{3,19},{4,20},{5,21},{6,22},{7,23},{8,9},{9,8... | collective-permute-start | bytes 3932168 | tf_op jit(solution)/shard_map/ppermute | solution.py:501
  449.6 18.4 %collective-permute-start.24 = (bf16[2,32,4096]{2,1,0:T(8,128)(2,1)}, bf16[2,32,4096]{2,1,0:T(8,128)(2,1)}, u32[]{:S(2)}, u32[]{:S(2)}) collective-permute-start(bf16[2,32,4096]{2,1,0:T(8,128)(2,1)} %get-tuple-element.351), channel_id=1, source_target_pairs={{0,2},{1,3},{2,0},{3,1},{4,6},{5,7},{6,4},{7,5},{8,10},{9,11},{10,... | collective-permute-start | bytes 1572872 | tf_op jit(solution)/shard_map/ppermute | solution.py:501
  466.8 16.8 %collective-permute-start.25 = (bf16[4,32,2560]{2,1,0:T(8,128)(2,1)S(1)}, bf16[4,32,2560]{2,1,0:T(8,128)(2,1)}, u32[]{:S(2)}, u32[]{:S(2)}) collective-permute-start(bf16[4,32,2560]{2,1,0:T(8,128)(2,1)S(1)} %get-tuple-element.349), channel_id=1, source_target_pairs={{0,1},{1,0},{2,3},{3,2},{4,5},{5,4},{6,7},{7,6},{8,24},{9,25},{10,... | collective-permute-start | bytes 1966088 | tf_op jit(solution)/shard_map/ppermute | solution.py:501
  469.2 18.3 %collective-permute-start.26 = (bf16[8,32,1536]{2,1,0:T(8,128)(2,1)}, bf16[8,32,1536]{2,1,0:T(8,128)(2,1)S(1)}, u32[]{:S(2)}, u32[]{:S(2)}) collective-permute-start(bf16[8,32,1536]{2,1,0:T(8,128)(2,1)} %get-tuple-element.284), channel_id=1, source_target_pairs={{0,16},{1,17},{2,18},{3,19},{4,20},{5,21},{6,22},{7,23},{8,9},{9,8... | collective-permute-start | bytes 2359304 | tf_op jit(solution)/shard_map/ppermute | solution.py:501
  470.3 18.5 %collective-permute-start.27 = (bf16[1,32,4096]{2,1,0:T(8,128)(2,1)S(1)}, bf16[1,32,4096]{2,1,0:T(8,128)(2,1)}, u32[]{:S(2)}, u32[]{:S(2)}) collective-permute-start(bf16[1,32,4096]{2,1,0:T(8,128)(2,1)S(1)} %get-tuple-element.359), channel_id=1, source_target_pairs={{0,4},{1,5},{2,6},{3,7},{4,0},{5,1},{6,2},{7,3},{8,12},{9,13},{10,... | collective-permute-start | bytes 786440 | tf_op jit(solution)/shard_map/ppermute | solution.py:501
  479.9 7.6 %copy-start.8 = (bf16[8,32,1536]{2,1,0:T(8,128)(2,1)S(1)}, bf16[8,32,1536]{2,1,0:T(8,128)(2,1)}, u32[]{:S(2)}) copy-start(bf16[8,32,1536]{2,1,0:T(8,128)(2,1)} %get-tuple-element.298) | copy-start | bytes 2359300
  483.4 16.1 %collective-permute-start.30 = (f32[16,9,128]{2,1,0:T(8,128)S(1)}, f32[16,9,128]{2,1,0:T(8,128)S(1)}, u32[]{:S(2)}, u32[]{:S(2)}) collective-permute-start(f32[16,9,128]{2,1,0:T(8,128)S(1)} %get-tuple-element.366), channel_id=1, source_target_pairs={{0,8},{1,9},{2,10},{3,11},{4,12},{5,13},{6,14},{7,15},{8,0},{9,1},... | collective-permute-start | bytes 221192 | tf_op jit(solution)/shard_map/ppermute | solution.py:501
  484.8 10.1 %collective-permute-start.28 = (bf16[2,32,2560]{2,1,0:T(8,128)(2,1)S(1)}, bf16[2,32,2560]{2,1,0:T(8,128)(2,1)S(1)}, u32[]{:S(2)}, u32[]{:S(2)}) collective-permute-start(bf16[2,32,2560]{2,1,0:T(8,128)(2,1)S(1)} %get-tuple-element.357), channel_id=1, source_target_pairs={{0,2},{1,3},{2,0},{3,1},{4,6},{5,7},{6,4},{7,5},{8,10},{9,11},{10,... | collective-permute-start | bytes 983048 | tf_op jit(solution)/shard_map/ppermute | solution.py:501
  487.8 10.0 %collective-permute-start.29 = (bf16[4,32,1536]{2,1,0:T(8,128)(2,1)S(1)}, bf16[4,32,1536]{2,1,0:T(8,128)(2,1)S(1)}, u32[]{:S(2)}, u32[]{:S(2)}) collective-permute-start(bf16[4,32,1536]{2,1,0:T(8,128)(2,1)S(1)} %get-tuple-element.355), channel_id=1, source_target_pairs={{0,1},{1,0},{2,3},{3,2},{4,5},{5,4},{6,7},{7,6},{8,24},{9,25},{10,... | collective-permute-start | bytes 1179656 | tf_op jit(solution)/shard_map/ppermute | solution.py:501
  495.1 10.4 %collective-permute-start.31 = (bf16[1,32,2560]{2,1,0:T(8,128)(2,1)S(1)}, bf16[1,32,2560]{2,1,0:T(8,128)(2,1)S(1)}, u32[]{:S(2)}, u32[]{:S(2)}) collective-permute-start(bf16[1,32,2560]{2,1,0:T(8,128)(2,1)S(1)} %get-tuple-element.365), channel_id=1, source_target_pairs={{0,4},{1,5},{2,6},{3,7},{4,0},{5,1},{6,2},{7,3},{8,12},{9,13},{10,... | collective-permute-start | bytes 491528 | tf_op jit(solution)/shard_map/ppermute | solution.py:501
  497.9 8.7 %collective-permute-start.32 = (bf16[2,32,1536]{2,1,0:T(8,128)(2,1)S(1)}, bf16[2,32,1536]{2,1,0:T(8,128)(2,1)S(1)}, u32[]{:S(2)}, u32[]{:S(2)}) collective-permute-start(bf16[2,32,1536]{2,1,0:T(8,128)(2,1)S(1)} %get-tuple-element.363), channel_id=1, source_target_pairs={{0,2},{1,3},{2,0},{3,1},{4,6},{5,7},{6,4},{7,5},{8,10},{9,11},{10,... | collective-permute-start | bytes 589832 | tf_op jit(solution)/shard_map/ppermute | solution.py:501
  499.6 8.2 %collective-permute-start.33 = (f32[8,9,128]{2,1,0:T(8,128)S(1)}, f32[8,9,128]{2,1,0:T(8,128)S(1)}, u32[]{:S(2)}, u32[]{:S(2)}) collective-permute-start(f32[8,9,128]{2,1,0:T(8,128)S(1)} %get-tuple-element.371), channel_id=1, source_target_pairs={{0,16},{1,17},{2,18},{3,19},{4,20},{5,21},{6,22},{7,23},{8,9},{9,8... | collective-permute-start | bytes 110600 | tf_op jit(solution)/shard_map/ppermute | solution.py:501
  506.7 7.1 %collective-permute-start.34 = (bf16[1,32,1536]{2,1,0:T(8,128)(2,1)S(1)}, bf16[1,32,1536]{2,1,0:T(8,128)(2,1)S(1)}, u32[]{:S(2)}, u32[]{:S(2)}) collective-permute-start(bf16[1,32,1536]{2,1,0:T(8,128)(2,1)S(1)} %get-tuple-element.369), channel_id=1, source_target_pairs={{0,4},{1,5},{2,6},{3,7},{4,0},{5,1},{6,2},{7,3},{8,12},{9,13},{10,... | collective-permute-start | bytes 294920 | tf_op jit(solution)/shard_map/ppermute | solution.py:501
  507.8 6.0 %collective-permute-start.35 = (f32[4,9,128]{2,1,0:T(8,128)S(1)}, f32[4,9,128]{2,1,0:T(8,128)S(1)}, u32[]{:S(2)}, u32[]{:S(2)}) collective-permute-start(f32[4,9,128]{2,1,0:T(8,128)S(1)} %get-tuple-element.373), channel_id=1, source_target_pairs={{0,1},{1,0},{2,3},{3,2},{4,5},{5,4},{6,7},{7,6},{8,24},{9,25},{10,... | collective-permute-start | bytes 55304 | tf_op jit(solution)/shard_map/ppermute | solution.py:501
  513.9 3.8 collective-permute-start.36
  517.7 4.7 collective-permute-start.37
  518.8 4.7 copy-start.14
  (10 other events, 20.6 us)
Sparse Core Ops, SparseCore 0:
  11.8 144.8 all-gather.2

commit v6 on v5

--- a/solution.py
+++ b/solution.py
@@ -8,8 +8,9 @@
 from jax.experimental.pallas import tpu as pltpu
 from jax.sharding import PartitionSpec as P
 
-CHEAP = pl.CostEstimate(flops=1, transcendentals=0, bytes_accessed=1)
-call = partial(pl.pallas_call, cost_estimate=CHEAP)
+def call(body, cover=False, **options):
+    cost = pl.CostEstimate(flops=10**11 if cover else 1, transcendentals=0, bytes_accessed=1)
+    return pl.pallas_call(body, cost_estimate=cost, **options)
 
 
 EPSILON = 1e-06
@@ -109,23 +110,22 @@
     )(qkv, qkv, qkv)
 
 
-def attention_back(qkv, logs, o, d_o, first_pair, pairs):
+def attention_back(qkv, logs, d_o, first_pair, pairs, cover=True):
     rows, width = qkv.shape[0], qkv.shape[1] // 3
     every = width // (2 * HEAD_DIM)
     span = 2 * HEAD_DIM
 
-    def body(q_ref, k_ref, v_ref, l_ref, o_ref, do_ref, d_ref, cq_ref, cv_ref):
+    def body(q_ref, k_ref, v_ref, l_ref, do_ref, d_ref, cq_ref, cv_ref):
         q, k, v, do = q_ref[...], k_ref[...], v_ref[...], do_ref[...]
         lane = lax.broadcasted_iota(jnp.int32, (rows, span), 1)
-        turned = (do.astype(jnp.float32) * o_ref[...].astype(jnp.float32)).T
         dqs, dks, dvs = [], [], []
         for h in range(2):
             mine = (lane < HEAD_DIM) if h == 0 else (lane >= HEAD_DIM)
             kh = jnp.where(mine, k, jnp.zeros_like(k))
             vh = jnp.where(mine, v, jnp.zeros_like(v))
             pt = jnp.exp2(dot(kh, q, NT) * SCORE_SCALE - l_ref[0, h : h + 1, :])
-            inner = jnp.sum(turned[h * HEAD_DIM : (h + 1) * HEAD_DIM], axis=0, keepdims=True)
-            dst = (pt * (dot(vh, do, NT) - inner)).astype(jnp.bfloat16)
+            w = pt * dot(vh, do, NT)
+            dst = (w - pt * jnp.sum(w, axis=0, keepdims=True)).astype(jnp.bfloat16)
             dvs.append(dot(pt.astype(jnp.bfloat16), do))
             dks.append(dot(dst, q))
             dqs.append(dot(dst, k, TN))
@@ -151,7 +151,6 @@
             col(2 * every + first_pair),
             pl.BlockSpec((1, 8, rows), lambda j: (first_pair + j, 0, 0)),
             col(first_pair),
-            col(first_pair),
         ],
         out_specs=[pl.BlockSpec((3, rows, span), lambda j: (0, 0, j)), sums, sums],
         out_shape=[
@@ -160,7 +159,8 @@
             vec_shape,
         ],
         name="attention_back",
-    )(qkv, qkv, qkv, logs, o, d_o)
+        cover=cover,
+    )(qkv, qkv, qkv, logs, d_o)
 
 
 def project_norm(o, weight, bias, x, gain, shift, at):
@@ -333,10 +333,11 @@
         ],
         scratch_shapes=[pltpu.VMEM((rows, width), jnp.float32)],
         name="feed_forward_back",
+        cover=True,
     )(dy, gp, packed, packed, x1, gain, w_out)
 
 
-def project_back(grads, weight, x, gain, dx1, extra, out_dtype):
+def project_back(grads, weight, x, gain, dx1, extra, dtypes):
     rows, width = x.shape
     tm = rows // 2
     have = extra is not None
@@ -346,8 +347,9 @@
     def body(*refs):
         d_refs = refs[:count]
         w_ref, x_ref, g_ref, dx_ref = refs[count : count + 4]
-        more = refs[count + 4 : -3]
-        out_ref, cg_ref, cs_ref = refs[-3:]
+        more = refs[count + 4 : -2 - len(dtypes)]
+        out_refs = refs[-2 - len(dtypes) : -2]
+        cg_ref, cs_ref = refs[-2:]
         da = None
         for kind in range(3):
             for i in range(count):
@@ -374,7 +376,8 @@
         dx = dx_ref[...] + inv * (t - m1 - xhat * m2)
         if have:
             dx = more[0][...].astype(jnp.float32) * more[1][...] + dx
-        out_ref[...] = dx.astype(out_dtype)
+        for ref in out_refs:
+            ref[...] = dx.astype(ref.dtype)
 
     rowblk = pl.BlockSpec((tm, width), lambda i: (i, 0))
     vec_spec = whole((1, width))
@@ -388,71 +391,101 @@
         body,
         grid=(rows // tm,),
         in_specs=specs,
-        out_specs=[rowblk, vec_spec, vec_spec],
+        out_specs=[rowblk] * len(dtypes) + [vec_spec, vec_spec],
         out_shape=[
-            jax.ShapeDtypeStruct((rows, width), out_dtype),
+            *[jax.ShapeDtypeStruct((rows, width), d) for d in dtypes],
             jax.ShapeDtypeStruct((1, width), jnp.float32),
             jax.ShapeDtypeStruct((1, width), jnp.float32),
         ],
         name="project_back",
+        cover=True,
     )(*args)
 
 
-def weight_grad_half(lefts, rights, index, blocks, tn, arrived=None):
-    rows, m = lefts[0].shape
-    stacked = rights[0].ndim == 3
-    part = rights[0].shape[-1]
-    cols = part * 3 if stacked else part
+def weight_grad(jobs, index, blocks, chunk, cover=False):
     ndp, nfs, r = blocks
-    tiles = ndp // 2
-    wide = nfs * r
-    count = len(lefts)
-    npos = tiles * nfs
-    final = arrived is not None
-    take = (lambda ref: ref[0]) if stacked else (lambda ref: ref[...])
-    if stacked:
-        right = pl.BlockSpec((1, rows, tn), lambda j, i_ref: (j * tn // part, 0, j % (part // tn)))
-    else:
-        right = pl.BlockSpec((rows, tn), lambda j, i_ref: (0, j))
+    npos = ndp * nfs // 2
+    rows = jobs[0][0][0].shape[0]
+    widths = [rs[0].shape[-1] * (3 if rs[0].ndim == 3 else 1) for _, rs in jobs]
+    starts = [sum(widths[:k]) for k in range(len(jobs))]
+    counts = [len(ls) for ls, _ in jobs]
+    steps = ndp * len(jobs)
 
     def body(i_ref, *refs):
-        a = refs[: count * tiles]
-        b = refs[count * tiles : count * tiles + count]
-        rest = refs[count * tiles + count :]
-        scr = rest[-1]
-        outs = rest[1:-1] if final else rest[:-1]
-        for t in range(tiles):
-            total = dot(a[t][...], take(b[0]), TN)
-            for s in range(1, count):
-                total += dot(a[s * tiles + t][...], take(b[s]), TN)
-            for f in range(nfs):
-                scr[t * nfs + f] = total[f * r : (f + 1) * r]
-        for p in range(npos):
-            value = scr[i_ref[tiles + p]]
-            if final:
-                value += rest[0][p].astype(jnp.float32)
-            share = npos // len(outs)
-            outs[p // share][p % share] = value.astype(jnp.bfloat16)
-
-    left_spec = lambda t: pl.BlockSpec((rows, wide), lambda j, i_ref: (0, i_ref[t]))
-    share = npos // 2 if final else npos
-    specs = [left_spec(t) for _ in range(count) for t in range(tiles)]
-    specs += [right] * count
-    args = [left for left in lefts for _ in range(tiles)] + list(rights)
-    if final:
-        specs.append(pl.BlockSpec((npos, r, tn), lambda j, i_ref: (0, 0, j)))
-        args.append(arrived)
+        sent, kept, buf, sem = refs[-4:]
+        i = pl.program_id(0)
+
+        def copies(step, start):
+            local = step % ndp
+            for k in range(len(jobs)):
+                for which, where in ((local < ndp // 2, sent), (local >= ndp // 2, kept)):
+
+                    @pl.when((step // ndp == k) & which)
+                    def _():
+                        for f in range(nfs):
+                            p = i_ref[ndp + local * nfs + f]
+                            copy = pltpu.make_async_copy(
+                                buf.at[step % 2, f, :, 0 : widths[k]],
+                                where.at[p, :, starts[k] : starts[k] + widths[k]],
+                                sem.at[step % 2, f],
+                            )
+                            copy.start() if start else copy.wait()
+
+        @pl.when(i >= 2)
+        def _():
+            copies(i - 2, False)
+
+        at_ref = 0
+        for k in range(len(jobs)):
+            a = refs[at_ref : at_ref + counts[k]]
+            b = refs[at_ref + counts[k] : at_ref + 2 * counts[k]]
+            at_ref += 2 * counts[k]
+
+            @pl.when(i // ndp == k)
+            def _():
+                for at in range(0, widths[k], chunk):
+                    part = b[0].shape[-1]
+                    if len(b[0].shape) == 3:
+                        take = lambda ref: ref[at // part, :, at % part : at % part + chunk]
+                    else:
+                        take = lambda ref: ref[:, at : at + chunk]
+                    total = dot(a[0][...], take(b[0]), TN)
+                    for x, y in zip(a[1:], b[1:]):
+                        total += dot(x[...], take(y), TN)
+                    total = total.astype(jnp.bfloat16).reshape(nfs, r, chunk)
+                    buf[i % 2, :, :, at : at + chunk] = total
+
+        copies(i, True)
+
+        @pl.when(i == steps - 1)
+        def _():
+            copies(steps - 2, False)
+            copies(steps - 1, False)
+
+    def left_spec(k):
+        step = lambda i: jnp.clip(i - k * ndp, 0, ndp - 1)
+        return pl.BlockSpec((rows, nfs * r), lambda i, i_ref: (0, i_ref[step(i)]))
+
+    anywhere = pl.BlockSpec(memory_space=pl.ANY)
+    specs, args = [], []
+    for k, (ls, rs) in enumerate(jobs):
+        specs += [left_spec(k)] * len(ls) + [whole(rs[0].shape)] * len(rs)
+        args += list(ls) + list(rs)
     return call(
         body,
         grid_spec=pltpu.PrefetchScalarGridSpec(
             num_scalar_prefetch=1,
-            grid=(cols // tn,),
+            grid=(steps,),
             in_specs=specs,
-            out_specs=[pl.BlockSpec((share, r, tn), lambda j, i_ref: (0, 0, j))] * (npos // share),
-            scratch_shapes=[pltpu.VMEM((npos, r, tn), jnp.float32)],
+            out_specs=[anywhere] * 2,
+            scratch_shapes=[
+                pltpu.VMEM((2, nfs, r, max(widths)), jnp.bfloat16),
+                pltpu.SemaphoreType.DMA((2, nfs)),
+            ],
         ),
-        out_shape=[jax.ShapeDtypeStruct((share, r, cols), jnp.bfloat16)] * (npos // share),
+        out_shape=[jax.ShapeDtypeStruct((npos, r, sum(widths)), jnp.bfloat16)] * 2,
         name="weight_grad",
+        cover=cover,
     )(index, *args)
 
 
@@ -632,6 +665,7 @@
         ),
         out_shape=jax.ShapeDtypeStruct((n, rows, 128), jnp.float32),
         name="pack_sums",
+        cover=True,
     )(inverse_row, *flat)
 
 
@@ -643,18 +677,17 @@
 
     def step(self, line, wide=jnp.bfloat16):
         kept, got = line.after(self.kept, self.got)
-        total = kept.astype(jnp.float32) + got.astype(jnp.float32)
+        add = lambda part: kept[part].astype(jnp.float32) + got[part].astype(jnp.float32)
         self.stage += 1
         if self.stage == len(self.perms):
-            self.done = total[0]
+            self.done = add(slice(None))[0]
             line.mark(self.done)
             return
-        total = total.astype(wide)
-        half = total.shape[0] // 2
-        sent = total[half:]
-        self.kept = total[:half]
-        line.mark(sent)
+        half = kept.shape[0] // 2
+        sent = add(slice(half, None)).astype(wide)
         self.got = send(sent, self.perms[self.stage])
+        self.kept = add(slice(0, half)).astype(wide)
+        line.mark(self.kept)
 
 
 def per_device(ndp, nfs,
@@ -773,79 +806,62 @@
         line.mark(outs[0])
         return outs
 
-    def heads_back(saved, d_o, i):
+    def heads_back(saved, d_o, i, cover=True):
         outs = attention_back(
-            saved[2], saved[3], saved[4], *line.after(d_o), i * pairs // parts, pairs // parts
+            saved[2], saved[3], *line.after(d_o), i * pairs // parts, pairs // parts, cover
         )
         line.mark(outs[0])
         return outs
 
-    def qkv_back(heads, saved, dx1, extra, dtype):
-        dx, cg, cs = project_back(
-            [line.after(h[0])[0] for h in heads], w["first"], saved[0], g1, dx1, extra, dtype
+    def qkv_back(heads, saved, dx1, extra, dtypes):
+        outs = project_back(
+            [line.after(h[0])[0] for h in heads], w["first"], saved[0], g1, dx1, extra, dtypes
         )
-        line.mark(dx)
-        return dx, cg, cs
+        line.mark(outs[0])
+        return outs
 
     dm2, du2, dx2, da2, do2, cdm2, cdu2, cda2, cg22, cs22 = ff_back(grad_second, saved_second)
     heads2 = [heads_back(saved_second, do2, i) for i in range(parts)]
-    grad_first, cg12, cs12 = qkv_back(
-        heads2, saved_second, dx2, (cot_first[0], keep_mask), jnp.float32
+    grad_first, dm1, cg12, cs12 = qkv_back(
+        heads2, saved_second, dx2, (cot_first[0], keep_mask), (jnp.float32, jnp.bfloat16)
     )
 
-    local = (row // nfs) // 2 * nfs + row % nfs
     half = n // 2
-    tiles = ndp // 2
     core = (me // nfs) % 2
-    lanes = 2 * jnp.arange(tiles, dtype=jnp.int32)
-    index_keep = jnp.concatenate([lanes + core, local[:half]]).astype(jnp.int32)
-    index_send = jnp.concatenate([lanes + (1 - core), local[half:]]).astype(jnp.int32)
-
-    def grad_send(lefts, rights, r, tn):
-        lefts = line.after(*lefts)
-        (out,) = weight_grad_half(lefts, rights, index_send, (ndp, nfs, r), tn)
-        line.mark(out)
-        return send(out, core_perm)
-
-    def grad_keep(lefts, rights, r, tn, arrived):
-        arrived = line.after(arrived)[0]
-        kept, sent = weight_grad_half(lefts, rights, index_keep, (ndp, nfs, r), tn, arrived)
+    evens = 2 * jnp.arange(ndp // 2, dtype=jnp.int32)
+    lefts_at = jnp.concatenate([evens + (1 - core), evens + core])
+    shards_at = lefts_at[:, None] * nfs + jnp.arange(nfs, dtype=jnp.int32)
+    index = jnp.concatenate([lefts_at, inverse_row[shards_at.reshape(-1)] % half])
+    index = index.astype(jnp.int32)
+
+    def grads(r, *jobs, cover=False):
+        jobs = [(line.after(*ls), rs) for ls, rs in jobs]
+        sent, kept = weight_grad(jobs, index, (ndp, nfs, r), 512, cover)
         line.mark(sent)
-        return kept, sent
-
-    dm1 = grad_first.astype(jnp.bfloat16)
+        return Reduction(perms, kept, sent, 0)
+
     sg = list(zip(saved_first, saved_second))
-    arrived = grad_send(sg[7], (dm1, dm2), r_ff, 256)
-    red_down = Reduction(perms, *grad_keep(sg[7], (dm1, dm2), r_ff, 256, arrived), 1)
+    red_down = grads(r_ff, (sg[7], (dm1, dm2)))
     _, du1, dx1, da1, do1, cdm1, cdu1, cda1, cg21, cs21 = ff_back(grad_first, saved_first)
     red_down.step(line)
-    arrived = grad_send(sg[6], (du1, du2), r_in, 1024)
+    red_up = grads(r_in, (sg[6], (du1, du2)))
     red_down.step(line)
-    red_up = Reduction(perms, *grad_keep(sg[6], (du1, du2), r_in, 1024, arrived), 1)
+    heads1 = [heads_back(saved_first, do1, 0)]
+    rights = lambda i: (heads1[i][0], heads2[i][0])
     red_down.step(line)
-    arrived_out = grad_send(sg[4], (da1, da2), r_in, 1024)
-    heads1 = [heads_back(saved_first, do1, 0)]
-    kept_out, sent_out = grad_keep(sg[4], (da1, da2), r_in, 1024, arrived_out)
+    red_up.step(line)
+    red_one = grads(r_in, (sg[4], (da1, da2)), (sg[1], rights(0)))
+    heads1.append(heads_back(saved_first, do1, 1, False))
+    red_up.step(line)
     red_down.step(line)
-    rights = lambda i: (heads1[i][0], heads2[i][0])
-    arrived = grad_send(sg[1], rights(0), r_in, 512)
-    red_up.step(line)
-    kept_q, sent_q = grad_keep(sg[1], rights(0), r_in, 512, arrived)
-    red_one = Reduction(
-        perms,
-        jnp.concatenate([kept_out, kept_q], axis=2),
-        jnp.concatenate([sent_out, sent_q], axis=2),
-        1,
-    )
-    heads1.append(heads_back(saved_first, do1, 1))
-    red_up.step(line)
-    arrived = grad_send(sg[1], rights(1), r_in, 512)
-    red_two = Reduction(perms, *grad_keep(sg[1], rights(1), r_in, 512, arrived), 1)
+    red_two = grads(r_in, (sg[1], rights(1)), cover=True)
     red_one.step(line)
     red_up.step(line)
-    grad_inputs, cg11, cs11 = qkv_back(heads1, saved_first, dx1, None, jnp.bfloat16)
+    grad_inputs, cg11, cs11 = qkv_back(heads1, saved_first, dx1, None, (jnp.bfloat16,))
+    red_two.step(line)
     red_one.step(line)
-    red_two.step(line)
+    red_up.step(line)
+    red_down.step(line)
     cq = [[h[i][1] for h in (heads1, heads2)] for i in range(parts)]
     cv = [[h[i][2] for h in (heads1, heads2)] for i in range(parts)]
     joined = lambda c: [jnp.concatenate([c[i][s] for i in range(parts)], axis=1) for s in range(2)]
@@ -866,9 +882,8 @@
         len(vectors),
     )
     red_small = Reduction(perms, sums[:half], sums[half:], 0)
-    red_up.step(line)
     for _ in range(stages):
-        for red in (red_one, red_two):
+        for red in (red_two, red_one, red_up, red_down):
             if red.done is None:
                 red.step(line)
         if red_small.done is None:

time: 540 us -> 516 us (0.956)
  Pallas kernels: 269 us -> 246 us
  other arithmetic: 24.1 us -> 42.6 us
  waiting for transfers between devices: 164 us -> 150 us
    pallas_call x12 -> x6, Pallas kernels: 96.2 us -> 72.2 us  [the longest x4 52.4 us: weight_grad(): call(body, grid_spec=pltpu.PrefetchScalarGridSpec(num_scalar_prefetch=1,...]
    convert_element_type x13 -> x16, other arithmetic: 13 us -> 31.3 us  [step(): sent = add(slice(half, None)).astype(wide)]
    ppermute x38 -> x37, waiting for transfers between devices: 164 us -> 150 us  [send(): return lax.ppermute(x, AXES, perm)]
    ppermute x38 -> x37, starting transfers between devices: 42.4 us -> 41.7 us  [send(): return lax.ppermute(x, AXES, perm)]
  transfers between devices with their start and end apart: 39 -> 38, of which waited for: 19 -> 17; matrix products, arithmetic and copies ran while one was open for 5% -> 8% of each run, Pallas kernels for 24% -> 24%
where the time goes in v6:
time: 516 us; the launch traced here: 507 us
  Pallas kernels  246 us (48%)
  waiting for transfers between devices  150 us (29%)
  other arithmetic  42.6 us (8%)
  starting transfers between devices  41.7 us (8%)
  between operations  15.3 us (3%)
  local copies, waits for them, and re-layouts  10.3 us (2%)
    ppermute x37, waiting for transfers between devices, send(): return lax.ppermute(x, AXES, perm)  150 us
    pallas_call x4, Pallas kernels, weight_grad(): call(body, grid_spec=pltpu.PrefetchScalarGridSpec(num_scalar_prefetch=1,...  52.4 us
    ppermute x37, starting transfers between devices, send(): return lax.ppermute(x, AXES, perm)  41.7 us
    pallas_call x2, Pallas kernels, feed_forward_back(): call(body, grid=(steps,), in_specs=[full, pl.BlockSpec((rows, tf), lambda...  40.8 us
    pallas_call x4, Pallas kernels, attention_back(): call(body, grid=(pairs,), in_specs=[col(first_pair), col(every + first_pa...  35.9 us
    pallas_call x2, Pallas kernels, feed_forward(): call(body, grid=(steps,), in_specs=[whole((rows, width)), up_spec(packed,...  35.7 us
    convert_element_type x16, other arithmetic, step(): sent = add(slice(half, None)).astype(wide)  31.3 us
    pallas_call x2, Pallas kernels, attention(): call(body, grid=(pairs,), in_specs=[col(0), col(pairs), col(2 * pairs)],...  21.7 us
  transfers between devices with their start and end apart: 38, of which 17 were waited for; matrix products, arithmetic and copies ran while one was open for 8% of the time, Pallas kernels for 24%

profile of v6, /device:TPU:0, one launch (start us, length us, event | category | flops | bytes accessed | tf_op | source)
XLA Modules:
  0.0 506.5 jit_solution(13720508998446740387)
XLA Ops:
  8.4 1.8 pad_maximum_fusion
  12.2 4.1 collective-permute-start
  16.3 7.7 %collective-permute-done = bf16[1,40,2048]{2,1,0:T(8,128)(2,1)S(1)} collective-permute-done((bf16[1,40,2048]{2,1,0:T(8,128)(2,1)S(1)}, bf16[1,40,2048]{2,1,0:T(8,128)(2,1)S(1)}, u32[]{:S(2)}, u32[]{:S(2)}) %collective-permute-start) | collective-permute-done | bytes 163872 | tf_op jit(solution)/shard_map/ppermute | solution.py:534
  24.8 18.0 %collective-permute-done.1 = bf16[2,40,2048]{2,1,0:T(8,128)(2,1)S(1)} collective-permute-done((bf16[2,40,2048]{2,1,0:T(8,128)(2,1)S(1)}, bf16[2,40,2048]{2,1,0:T(8,128)(2,1)S(1)}, u32[]{:S(2)}, u32[]{:S(2)}) %collective-permute-start.1) | collective-permute-done | bytes 327712 | tf_op jit(solution)/shard_map/ppermute | solution.py:534
  44.2 2.2 collective-permute-start.2
  46.4 6.6 %collective-permute-done.2 = bf16[1,32,2048]{2,1,0:T(8,128)(2,1)S(1)} collective-permute-done((bf16[1,32,2048]{2,1,0:T(8,128)(2,1)S(1)}, bf16[1,32,2048]{2,1,0:T(8,128)(2,1)S(1)}, u32[]{:S(2)}, u32[]{:S(2)}) %collective-permute-start.2) | collective-permute-done | bytes 131104 | tf_op jit(solution)/shard_map/ppermute | solution.py:534
  53.0 3.0 collective-permute-start.4
  56.1 19.8 %collective-permute-done.4 = bf16[2,32,2048]{2,1,0:T(8,128)(2,1)S(1)} collective-permute-done((bf16[2,32,2048]{2,1,0:T(8,128)(2,1)S(1)}, bf16[2,32,2048]{2,1,0:T(8,128)(2,1)S(1)}, u32[]{:S(2)}, u32[]{:S(2)}) %collective-permute-start.4) | collective-permute-done | bytes 262176 | tf_op jit(solution)/shard_map/ppermute | solution.py:534
  77.1 15.7 %collective-permute-done.5 = bf16[4,32,2048]{2,1,0:T(8,128)(2,1)S(1)} collective-permute-done((bf16[4,32,2048]{2,1,0:T(8,128)(2,1)S(1)}, bf16[4,32,2048]{2,1,0:T(8,128)(2,1)S(1)}, u32[]{:S(2)}, u32[]{:S(2)}) %collective-permute-start.5) | collective-permute-done | bytes 524320 | tf_op jit(solution)/shard_map/ppermute | solution.py:534
  94.7 15.6 %collective-permute-done.6.refs_1_ = bf16[8,40,2048]{2,1,0:T(8,128)(2,1)S(1)} collective-permute-done((bf16[8,40,2048]{2,1,0:T(8,128)(2,1)S(1)}, bf16[8,40,2048]{2,1,0:T(8,128)(2,1)S(1)}, u32[]{:S(2)}, u32[]{:S(2)}) %collective-permute-start.6) | collective-permute-done | bytes 1310752 | tf_op jit(solution)/shard_map/ppermute | solution.py:534
  110.8 26.5 %collective-permute-done.9.refs_5_ = bf16[8,32,2048]{2,1,0:T(8,128)(2,1)} collective-permute-done((bf16[8,32,2048]{2,1,0:T(8,128)(2,1)}, bf16[8,32,2048]{2,1,0:T(8,128)(2,1)}, u32[]{:S(2)}, u32[]{:S(2)}) %collective-permute-start.9) | collective-permute-done | bytes 1048608 | tf_op jit(solution)/shard_map/ppermute | solution.py:534
  139.4 2.8 convert_multiply_fusion.dy_ref
  142.3 2.8 unpack_vectors.1
  145.0 8.4 %place_shards.1 = bf16[32,32,4096]{2,1,0:T(8,128)(2,1)} custom-call(s32[32]{0:T(128)} %get-tuple-element.401.t_ref, bf16[8,40,2048]{2,1,0:T(8,128)(2,1)} %copy-done.1, bf16[8,40,2048]{2,1,0:T(8,128)(2,1)} %copy-done.2, bf16[8,40,2048]{2,1,0:T(8,128)(2,1)} %collective-permute-done.7.refs_2_, bf16[8,40,2048]{2,1,0:T(8,128)(2,1)} %collective-permute-done.8.refs_3_, ...), custom_call_target="tpu_custom_call" | custom-call | flops 1 | bytes 1 | tf_op jit(solution)/shard_map/place_shards/pallas_call | solution.py:584
  153.4 8.1 %norm_project.2 = (bf16[512,1024]{1,0:T(8,128)(2,1)}, bf16[512,3072]{1,0:T(8,128)(2,1)}) custom-call(bf16[512,1024]{1,0:T(8,128)(2,1)} %bitcast.73, f32[1,1024]{1,0:T(1,128)} %get-tuple-element.203.g_ref.refs_4_, f32[1,1024]{1,0:T(1,128)} %get-tuple-element.204.s_ref, bf16[1024,4096]{1,0:T(8,128)(2,1)} %bitcast.65, f32[1,3072]{1,0:T(1,128)} %get-tuple-element.205.b_ref), custom_call_target="tpu_custom_call" | custom-call | flops 1 | bytes 1 | tf_op jit(solution)/shard_map/norm_project/pallas_call | solution.py:55
  162.1 10.8 %attention.2 = (bf16[512,1024]{1,0:T(8,128)(2,1)}, f32[8,8,512]{2,1,0:T(8,128)}) custom-call(bf16[512,3072]{1,0:T(8,128)(2,1)} %get-tuple-element.206.q_ref.k_ref.v_ref, bf16[512,3072]{1,0:T(8,128)(2,1)} %get-tuple-element.206.q_ref.k_ref.v_ref, bf16[512,3072]{1,0:T(8,128)(2,1)} %get-tuple-element.206.q_ref.k_ref.v_ref), custom_call_target="tpu_custom_call" | custom-call | flops 1 | bytes 1 | tf_op jit(solution)/shard_map/attention/pallas_call | solution.py:100
  173.0 4.9 project_norm.2
  177.8 17.9 %feed_forward.2 = (bf16[512,4096]{1,0:T(8,128)(2,1)}, bf16[512,4096]{1,0:T(8,128)(2,1)}, bf16[512,1024]{1,0:T(8,128)(2,1)}) custom-call(bf16[512,1024]{1,0:T(8,128)(2,1)} %get-tuple-element.247.a_ref.refs_0_, bf16[32,256,1024]{2,1,0:T(8,128)(2,1)} %bitcast.57, f32[1,4096]{1,0:T(1,128)} %get-tuple-element.213.ub_ref, bf16[32,256,1024]{2,1,0:T(8,128)(2,1)} %bitcast.58, ...), custom_call_target="tpu_custom_call" | custom-call | flops 1 | bytes 1 | tf_op jit(solution)/shard_map/feed_forward/pallas_call | solution.py:229
  195.7 8.3 %norm_project.3 = (bf16[512,1024]{1,0:T(8,128)(2,1)}, bf16[512,3072]{1,0:T(8,128)(2,1)}) custom-call(bf16[512,1024]{1,0:T(8,128)(2,1)} %get-tuple-element.217.x_ref.refs_3_, f32[1,1024]{1,0:T(1,128)} %get-tuple-element.203.g_ref.refs_4_, f32[1,1024]{1,0:T(1,128)} %get-tuple-element.204.s_ref, bf16[1024,4096]{1,0:T(8,128)(2,1)} %bitcast.67, ...), custom_call_target="tpu_custom_call" | custom-call | flops 1 | bytes 1 | tf_op jit(solution)/shard_map/norm_project/pallas_call | solution.py:55
  204.9 10.8 %attention.3 = (bf16[512,1024]{1,0:T(8,128)(2,1)}, f32[8,8,512]{2,1,0:T(8,128)}) custom-call(bf16[512,3072]{1,0:T(8,128)(2,1)} %get-tuple-element.218.q_ref.k_ref.v_ref, bf16[512,3072]{1,0:T(8,128)(2,1)} %get-tuple-element.218.q_ref.k_ref.v_ref, bf16[512,3072]{1,0:T(8,128)(2,1)} %get-tuple-element.218.q_ref.k_ref.v_ref), custom_call_target="tpu_custom_call" | custom-call | flops 1 | bytes 1 | tf_op jit(solution)/shard_map/attention/pallas_call | solution.py:100
  215.7 4.9 project_norm.3
  220.6 17.9 %feed_forward.3 = (bf16[512,4096]{1,0:T(8,128)(2,1)}, bf16[512,4096]{1,0:T(8,128)(2,1)}, bf16[512,1024]{1,0:T(8,128)(2,1)}) custom-call(bf16[512,1024]{1,0:T(8,128)(2,1)} %get-tuple-element.248.a_ref.refs_1_, bf16[32,256,1024]{2,1,0:T(8,128)(2,1)} %bitcast.59, f32[1,4096]{1,0:T(1,128)} %get-tuple-element.213.ub_ref, bf16[32,256,1024]{2,1,0:T(8,128)(2,1)} %bitcast.60, ...), custom_call_target="tpu_custom_call" | custom-call | flops 1 | bytes 1 | tf_op jit(solution)/shard_map/feed_forward/pallas_call | solution.py:229
  238.5 20.3 %feed_forward_back.2 = (bf16[512,1024]{1,0:T(8,128)(2,1)}, bf16[512,4096]{1,0:T(8,128)(2,1)}, f32[512,1024]{1,0:T(8,128)}, bf16[512,1024]{1,0:T(8,128)(2,1)}, bf...) custom-call(f32[512,1024]{1,0:T(8,128)} %convert_multiply_fusion.dy_, ...), custom_call_target="tpu_custom_call" | custom-call | flops 99999997952 | bytes 1 | tf_op jit(solution)/shard_map/feed_forward_back/pallas_call | solution.py:298
  258.8 9.1 %attention_back.4 = (bf16[3,512,512]{2,1,0:T(8,128)(2,1)}, f32[1,512]{1,0:T(1,128)}, f32[1,512]{1,0:T(1,128)}) custom-call(bf16[512,3072]{1,0:T(8,128)(2,1)} %get-tuple-element.218.q_ref.k_ref.v_ref, bf16[512,3072]{1,0:T(8,128)(2,1)} %get-tuple-element.218.q_ref.k_ref.v_ref, bf16[512,3072]{1,0:T(8,128)(2,1)} %get-tuple-element.218.q_ref.k_ref.v_ref, ...), custom_call_target="tpu_custom_call" | custom-call | flops 99999997952 | bytes 1 | tf_op jit(solution)/shard_map/attention_back/pallas_call | solution.py:145
  267.9 8.9 %attention_back.5 = (bf16[3,512,512]{2,1,0:T(8,128)(2,1)}, f32[1,512]{1,0:T(1,128)}, f32[1,512]{1,0:T(1,128)}) custom-call(bf16[512,3072]{1,0:T(8,128)(2,1)} %get-tuple-element.218.q_ref.k_ref.v_ref, bf16[512,3072]{1,0:T(8,128)(2,1)} %get-tuple-element.218.q_ref.k_ref.v_ref, bf16[512,3072]{1,0:T(8,128)(2,1)} %get-tuple-element.218.q_ref.k_ref.v_ref, ...), custom_call_target="tpu_custom_call" | custom-call | flops 99999997952 | bytes 1 | tf_op jit(solution)/shard_map/attention_back/pallas_call | solution.py:145
  276.8 10.2 %project_back.2 = (f32[512,1024]{1,0:T(8,128)}, bf16[512,1024]{1,0:T(8,128)(2,1)}, f32[1,1024]{1,0:T(1,128)}, f32[1,1024]{1,0:T(1,128)}) custom-call(bf16[3,512,512]{2,1,0:T(8,128)(2,1)} %get-tuple-element.234.refs_0_.refs_7_, bf16[3,512,512]{2,1,0:T(8,128)(2,1)} %get-tuple-element.235.refs_1_.refs_3_, bf16[1024,4096]{1,0:T(8,128)(2,1)} %bitcast.70, ...), custom_call_target="tpu_custom_call" | custom-call | flops 99999997952 | bytes 1 | tf_op jit(solution)/shard_map/project_back/pallas_call | solution.py:390
  287.1 14.3 %weight_grad.4 = (bf16[16,128,1024]{2,1,0:T(8,128)(2,1)}, bf16[16,128,1024]{2,1,0:T(8,128)(2,1)}) custom-call(s32[36]{0:T(128)} %pad_add_fusion.i_ref, bf16[512,4096]{1,0:T(8,128)(2,1)} %get-tuple-element.240.refs_0_, bf16[512,4096]{1,0:T(8,128)(2,1)} %get-tuple-element.241.refs_1_, bf16[512,1024]{1,0:T(8,128)(2,1)} %get-tuple-element.242.refs_2_, ...), custom_call_target="tpu_custom_call" | custom-call | flops 1 | bytes 1 | tf_op jit(solution)/shard_map/weight_grad/pallas_call | solution.py:474
  301.6 7.2 %collective-permute-done.12 = bf16[16,128,1024]{2,1,0:T(8,128)(2,1)S(1)} collective-permute-done((bf16[16,128,1024]{2,1,0:T(8,128)(2,1)}, bf16[16,128,1024]{2,1,0:T(8,128)(2,1)S(1)}, u32[]{:S(2)}, u32[]{:S(2)}) %collective-permute-start.12) | collective-permute-done | bytes 4194336 | tf_op jit(solution)/shard_map/ppermute | solution.py:534
  308.8 4.5 add_convert_fusion.2
  313.3 1.4 collective-permute-start.13
  314.8 20.4 %feed_forward_back.3 = (bf16[512,1024]{1,0:T(8,128)(2,1)}, bf16[512,4096]{1,0:T(8,128)(2,1)}, f32[512,1024]{1,0:T(8,128)}, bf16[512,1024]{1,0:T(8,128)(2,1)}, bf...) custom-call(f32[512,1024]{1,0:T(8,128)} %get-tuple-element.249.dy_re, ...), custom_call_target="tpu_custom_call" | custom-call | flops 99999997952 | bytes 1 | tf_op jit(solution)/shard_map/feed_forward_back/pallas_call | solution.py:298
  335.2 15.8 %weight_grad.5 = (bf16[16,32,4096]{2,1,0:T(8,128)(2,1)}, bf16[16,32,4096]{2,1,0:T(8,128)(2,1)}) custom-call(s32[36]{0:T(128)} %pad_add_fusion.i_ref, bf16[512,1024]{1,0:T(8,128)(2,1)} %get-tuple-element.247.a_ref.refs_0_, bf16[512,1024]{1,0:T(8,128)(2,1)} %get-tuple-element.248.a_ref.refs_1_, bf16[512,4096]{1,0:T(8,128)(2,1)} %get-tuple-element.251.refs_2_, ...), custom_call_target="tpu_custom_call" | custom-call | flops 1 | bytes 1 | tf_op jit(solution)/shard_map/weight_grad/pallas_call | solution.py:474
  351.5 3.5 add_convert_fusion.8
  355.0 1.4 collective-permute-start.14
  356.4 9.0 %attention_back.6 = (bf16[3,512,512]{2,1,0:T(8,128)(2,1)}, f32[1,512]{1,0:T(1,128)}, f32[1,512]{1,0:T(1,128)}) custom-call(bf16[512,3072]{1,0:T(8,128)(2,1)} %get-tuple-element.206.q_ref.k_ref.v_ref, bf16[512,3072]{1,0:T(8,128)(2,1)} %get-tuple-element.206.q_ref.k_ref.v_ref, bf16[512,3072]{1,0:T(8,128)(2,1)} %get-tuple-element.206.q_ref.k_ref.v_ref, ...), custom_call_target="tpu_custom_call" | custom-call | flops 99999997952 | bytes 1 | tf_op jit(solution)/shard_map/attention_back/pallas_call | solution.py:145
  365.4 4.6 collective-permute-done.14
  370.0 1.4 add_convert_fusion.16
  371.4 5.2 %add_convert_fusion = (bf16[8,32,4096]{2,1,0:T(8,128)(2,1)}, bf16[8,32,4096]{2,1,0:T(8,128)(2,1)S(1)}) fusion(bf16[16,32,4096]{2,1,0:T(8,128)(2,1)} %collective-permute-done.15, bf16[16,32,4096]{2,1,0:T(8,128)(2,1)} %get-tuple-element.262), kind=kLoop, calls=%fused_computation.1 | loop fusion | flops 8388608 | bytes 12582912 | tf_op jit(solution)/shard_map/convert_element_type | solution.py:687
  376.6 1.5 collective-permute-start.16
  378.7 13.9 %weight_grad.6 = (bf16[16,32,2560]{2,1,0:T(8,128)(2,1)}, bf16[16,32,2560]{2,1,0:T(8,128)(2,1)}) custom-call(s32[36]{0:T(128)} %pad_add_fusion.i_ref, bf16[512,1024]{1,0:T(8,128)(2,1)} %get-tuple-element.264.o_ref.refs_0_, bf16[512,1024]{1,0:T(8,128)(2,1)} %get-tuple-element.265.o_ref.refs_1_, bf16[512,1024]{1,0:T(8,128)(2,1)} %get-tuple-element.266.refs_2_, ...), custom_call_target="tpu_custom_call" | custom-call | flops 1 | bytes 1 | tf_op jit(solution)/shard_map/weight_grad/pallas_call | solution.py:474
  392.7 8.9 %attention_back.7 = (bf16[3,512,512]{2,1,0:T(8,128)(2,1)}, f32[1,512]{1,0:T(1,128)}, f32[1,512]{1,0:T(1,128)}) custom-call(bf16[512,3072]{1,0:T(8,128)(2,1)} %get-tuple-element.206.q_ref.k_ref.v_ref, bf16[512,3072]{1,0:T(8,128)(2,1)} %get-tuple-element.206.q_ref.k_ref.v_ref, bf16[512,3072]{1,0:T(8,128)(2,1)} %get-tuple-element.206.q_ref.k_ref.v_ref, ...), custom_call_target="tpu_custom_call" | custom-call | flops 1 | bytes 1 | tf_op jit(solution)/shard_map/attention_back/pallas_call | solution.py:145
  404.2 3.4 add_convert_fusion.6
  407.5 2.0 add_convert_fusion.23
  410.3 8.3 %weight_grad.7 = (bf16[16,32,1536]{2,1,0:T(8,128)(2,1)}, bf16[16,32,1536]{2,1,0:T(8,128)(2,1)}) custom-call(s32[36]{0:T(128)} %pad_add_fusion.i_ref, bf16[512,1024]{1,0:T(8,128)(2,1)} %get-tuple-element.279.refs_4_.refs_0_, bf16[512,1024]{1,0:T(8,128)(2,1)} %get-tuple-element.280.refs_5_.refs_1_, bf16[3,512,512]{2,1,0:T(8,128)(2,1)} %get-tuple-element.288.refs_2_.refs_1_, ...), custom_call_target="tpu_custom_call" | custom-call | flops 99999997952 | bytes 1 | tf_op jit(solution)/shard_map/weight_grad/pallas_call | solution.py:474
  418.8 7.7 %collective-permute-start.23 = (bf16[1,128,1024]{2,1,0:T(8,128)(2,1)}, bf16[1,128,1024]{2,1,0:T(8,128)(2,1)}, u32[]{:S(2)}, u32[]{:S(2)}) collective-permute-start(bf16[1,128,1024]{2,1,0:T(8,128)(2,1)} %get-tuple-element.372), channel_id=1, source_target_pairs={{0,4},{1,5},{2,6},{3,7},{4,0},{5,1},{6,2},{7,3},{8,12},{9,13},{10,... | collective-permute-start | bytes 786440 | tf_op jit(solution)/shard_map/ppermute | solution.py:534
  426.5 4.8 add_convert_fusion.4
  433.0 9.6 %project_back.3 = (bf16[512,1024]{1,0:T(8,128)(2,1)}, f32[1,1024]{1,0:T(1,128)}, f32[1,1024]{1,0:T(1,128)}) custom-call(bf16[3,512,512]{2,1,0:T(8,128)(2,1)} %get-tuple-element.287.refs_6_.refs_0_, bf16[3,512,512]{2,1,0:T(8,128)(2,1)} %get-tuple-element.288.refs_2_.refs_1_, bf16[1024,4096]{1,0:T(8,128)(2,1)} %bitcast.72, bf16[512,1024]{1,0:T(8,128)(2,1)} %bitcast.75, ...), custom_call_target="tpu_custom_call" | custom-call | flops 99999997952 | bytes 1 | tf_op jit(solution)/shard_map/project_back/pallas_call | solution.py:390
  442.6 2.5 pack_sums.1
  446.2 1.9 add_convert_fusion.10
  448.1 1.7 collective-permute-start.24
  449.8 1.7 add_convert_fusion.12
  453.3 1.8 add_bitcast_fusion.1
  455.1 9.9 %collective-permute-done.24 = bf16[8,32,1536]{2,1,0:T(8,128)(2,1)S(1)} collective-permute-done((bf16[8,32,1536]{2,1,0:T(8,128)(2,1)S(1)}, bf16[8,32,1536]{2,1,0:T(8,128)(2,1)S(1)}, u32[]{:S(2)}, u32[]{:S(2)}) %collective-permute-start.24) | collective-permute-done | bytes 786464 | tf_op jit(solution)/shard_map/ppermute | solution.py:534
  465.2 2.6 collective-permute-start.28
  468.8 2.0 collective-permute-start.29
  471.4 2.8 collective-permute-done.28
  474.4 2.1 collective-permute-start.31
  476.5 3.0 collective-permute-done.29
  479.7 1.5 collective-permute-start.33
  481.2 2.7 collective-permute-done.31
  484.2 4.9 collective-permute-done.32
  491.9 1.7 collective-permute-done.35
  493.6 2.1 collective-permute-start.36
  495.8 2.3 collective-permute-done.36
  (178 shorter events, 27.8 us)
Async XLA Ops:
  7.2 3.1 copy-start.19
  7.2 3.1 copy-start.20
  7.2 3.1 copy-start.21
  7.2 3.1 copy-start.22
  7.2 3.1 copy-start.23
  7.3 3.1 copy-start.24
  7.3 4.8 copy-start.25
  7.3 4.9 slice-start
  7.3 170.6 %all-gather.3.cloned.1.call-start = ((), (), s32[]{:S(2)}) async-start(), calls=%async_computation | async-start | bytes 17301504 | tf_op jit(solution)/shard_map/all_gather | solution.py:739
  8.4 35.8 %slice-start.1 = ((bf16[32,3072]{1,0:T(8,128)(2,1)}), bf16[32,1024]{1,0:T(8,128)(2,1)S(1)}, s32[]{:S(2)}) async-start(bf16[32,3072]{1,0:T(8,128)(2,1)} %param.21), calls=%async_computation.2 | async-start | bytes 131072 | tf_op jit(solution)/shard_map/slice | solution.py:736
  8.4 35.8 %copy-start.8 = (bf16[32,1024]{1,0:T(8,128)(2,1)S(1)}, bf16[32,1024]{1,0:T(8,128)(2,1)}, u32[]{:S(2)}) copy-start(bf16[32,1024]{1,0:T(8,128)(2,1)} %param.24) | copy-start | bytes 196612
  12.2 11.8 %collective-permute-start = (bf16[1,40,2048]{2,1,0:T(8,128)(2,1)S(1)}, bf16[1,40,2048]{2,1,0:T(8,128)(2,1)S(1)}, u32[]{:S(2)}, u32[]{:S(2)}) collective-permute-start(bf16[1,40,2048]{2,1,0:T(8,128)(2,1)S(1)} %fusion.2), channel_id=1, source_target_pairs={{0,4},{1,5},{2,6},{3,7},{4,0},{5,1},{6,2},{7,3},{8,12},{9,13},{10,... | collective-permute-start | bytes 491528 | tf_op jit(solution)/shard_map/ppermute | solution.py:534
  24.0 18.8 %collective-permute-start.1 = (bf16[2,40,2048]{2,1,0:T(8,128)(2,1)S(1)}, bf16[2,40,2048]{2,1,0:T(8,128)(2,1)S(1)}, u32[]{:S(2)}, u32[]{:S(2)}) collective-permute-start(bf16[2,40,2048]{2,1,0:T(8,128)(2,1)S(1)} %pad_maximum_fusion.1), channel_id=1, source_target_pairs={{0,2},{1,3},{2,0},{3,1},{4,6},{5,7},{6,4},{7,5},{8,10},{9,11},{10,... | collective-permute-start | bytes 983048 | tf_op jit(solution)/shard_map/ppermute | solution.py:534
  42.8 13.1 %collective-permute-start.3 = (bf16[4,40,2048]{2,1,0:T(8,128)(2,1)S(1)}, bf16[4,40,2048]{2,1,0:T(8,128)(2,1)S(1)}, u32[]{:S(2)}, u32[]{:S(2)}) collective-permute-start(bf16[4,40,2048]{2,1,0:T(8,128)(2,1)S(1)} %constant_dynamic-update-slice_fusion), channel_id=1, source_target_pairs={{0,1},{1,0},{2,3},{3,2},{4,5},{5,4},{6,7},{7,6},{8,24},{9,25},{10,... | collective-permute-start | bytes 1966088 | tf_op jit(solution)/shard_map/ppermute | solution.py:534
  44.2 8.8 %collective-permute-start.2 = (bf16[1,32,2048]{2,1,0:T(8,128)(2,1)S(1)}, bf16[1,32,2048]{2,1,0:T(8,128)(2,1)S(1)}, u32[]{:S(2)}, u32[]{:S(2)}) collective-permute-start(bf16[1,32,2048]{2,1,0:T(8,128)(2,1)S(1)} %maximum_bitcast_fusion), channel_id=1, source_target_pairs={{0,4},{1,5},{2,6},{3,7},{4,0},{5,1},{6,2},{7,3},{8,12},{9,13},{10,... | collective-permute-start | bytes 393224 | tf_op jit(solution)/shard_map/ppermute | solution.py:534
  53.0 22.9 %collective-permute-start.4 = (bf16[2,32,2048]{2,1,0:T(8,128)(2,1)S(1)}, bf16[2,32,2048]{2,1,0:T(8,128)(2,1)S(1)}, u32[]{:S(2)}, u32[]{:S(2)}) collective-permute-start(bf16[2,32,2048]{2,1,0:T(8,128)(2,1)S(1)} %constant_dynamic-update-slice_fusion.2), channel_id=1, source_target_pairs={{0,2},{1,3},{2,0},{3,1},{4,6},{5,7},{6,4},{7,5},{8,10},{9,11},{10,... | collective-permute-start | bytes 786440 | tf_op jit(solution)/shard_map/ppermute | solution.py:534
  56.1 86.2 %copy-start.1 = (bf16[8,40,2048]{2,1,0:T(8,128)(2,1)}, bf16[8,40,2048]{2,1,0:T(8,128)(2,1)S(1)}, u32[]{:S(2)}) copy-start(bf16[8,40,2048]{2,1,0:T(8,128)(2,1)S(1)} %constant_dynamic-update-slice_fusion.4.refs_0_) | copy-start | bytes 3932164
  56.1 83.3 %copy-start.10 = (s32[1,512]{1,0:T(1,128)S(1)}, s32[1,512]{1,0:T(1,128)}, u32[]{:S(2)}) copy-start(s32[1,512]{1,0:T(1,128)} %param.34) | copy-start | bytes 6148
  75.9 16.8 %collective-permute-start.5 = (bf16[4,32,2048]{2,1,0:T(8,128)(2,1)S(1)}, bf16[4,32,2048]{2,1,0:T(8,128)(2,1)S(1)}, u32[]{:S(2)}, u32[]{:S(2)}) collective-permute-start(bf16[4,32,2048]{2,1,0:T(8,128)(2,1)S(1)} %constant_dynamic-update-slice_fusion.6), channel_id=1, source_target_pairs={{0,1},{1,0},{2,3},{3,2},{4,5},{5,4},{6,7},{7,6},{8,24},{9,25},{10,... | collective-permute-start | bytes 1572872 | tf_op jit(solution)/shard_map/ppermute | solution.py:534
  77.1 33.1 %collective-permute-start.6 = (bf16[8,40,2048]{2,1,0:T(8,128)(2,1)S(1)}, bf16[8,40,2048]{2,1,0:T(8,128)(2,1)S(1)}, u32[]{:S(2)}, u32[]{:S(2)}) collective-permute-start(bf16[8,40,2048]{2,1,0:T(8,128)(2,1)S(1)} %constant_dynamic-update-slice_fusion.4.refs_0_), channel_id=1, source_target_pairs={{0,16},{1,17},{2,18},{3,19},{4,20},{5,21},{6,22},{7,23},{8,9},{9,8... | collective-permute-start | bytes 3932168 | tf_op jit(solution)/shard_map/ppermute | solution.py:534
  94.4 42.9 %collective-permute-start.9 = (bf16[8,32,2048]{2,1,0:T(8,128)(2,1)}, bf16[8,32,2048]{2,1,0:T(8,128)(2,1)}, u32[]{:S(2)}, u32[]{:S(2)}) collective-permute-start(bf16[8,32,2048]{2,1,0:T(8,128)(2,1)} %constant_dynamic-update-slice_fusion.8.refs_4_), channel_id=1, source_target_pairs={{0,16},{1,17},{2,18},{3,19},{4,20},{5,21},{6,22},{7,23},{8,9},{9,8... | collective-permute-start | bytes 3145736 | tf_op jit(solution)/shard_map/ppermute | solution.py:534
  94.7 47.6 %collective-permute-start.7 = (bf16[8,40,2048]{2,1,0:T(8,128)(2,1)S(1)}, bf16[8,40,2048]{2,1,0:T(8,128)(2,1)}, u32[]{:S(2)}, u32[]{:S(2)}) collective-permute-start(bf16[8,40,2048]{2,1,0:T(8,128)(2,1)S(1)} %constant_dynamic-update-slice_fusion.4.refs_0_), channel_id=1, source_target_pairs={{0,8},{1,9},{2,10},{3,11},{4,12},{5,13},{6,14},{7,15},{8,0},{9,1},... | collective-permute-start | bytes 3932168 | tf_op jit(solution)/shard_map/ppermute | solution.py:534
  110.2 32.0 %copy-start.2 = (bf16[8,40,2048]{2,1,0:T(8,128)(2,1)}, bf16[8,40,2048]{2,1,0:T(8,128)(2,1)S(1)}, u32[]{:S(2)}) copy-start(bf16[8,40,2048]{2,1,0:T(8,128)(2,1)S(1)} %collective-permute-done.6.refs_1_) | copy-start | bytes 3932164
  110.2 32.0 %collective-permute-start.8 = (bf16[8,40,2048]{2,1,0:T(8,128)(2,1)S(1)}, bf16[8,40,2048]{2,1,0:T(8,128)(2,1)}, u32[]{:S(2)}, u32[]{:S(2)}) collective-permute-start(bf16[8,40,2048]{2,1,0:T(8,128)(2,1)S(1)} %collective-permute-done.6.refs_1_), channel_id=1, source_target_pairs={{0,8},{1,9},{2,10},{3,11},{4,12},{5,13},{6,14},{7,15},{8,0},{9,1},... | collective-permute-start | bytes 3932168 | tf_op jit(solution)/shard_map/ppermute | solution.py:534
  110.3 34.8 %collective-permute-start.10 = (bf16[8,32,2048]{2,1,0:T(8,128)(2,1)}, bf16[8,32,2048]{2,1,0:T(8,128)(2,1)}, u32[]{:S(2)}, u32[]{:S(2)}) collective-permute-start(bf16[8,32,2048]{2,1,0:T(8,128)(2,1)} %constant_dynamic-update-slice_fusion.8.refs_4_), channel_id=1, source_target_pairs={{0,8},{1,9},{2,10},{3,11},{4,12},{5,13},{6,14},{7,15},{8,0},{9,1},... | collective-permute-start | bytes 3145736 | tf_op jit(solution)/shard_map/ppermute | solution.py:534
  137.3 7.7 %collective-permute-start.11 = (bf16[8,32,2048]{2,1,0:T(8,128)(2,1)}, bf16[8,32,2048]{2,1,0:T(8,128)(2,1)}, u32[]{:S(2)}, u32[]{:S(2)}) collective-permute-start(bf16[8,32,2048]{2,1,0:T(8,128)(2,1)} %collective-permute-done.9.refs_5_), channel_id=1, source_target_pairs={{0,8},{1,9},{2,10},{3,11},{4,12},{5,13},{6,14},{7,15},{8,0},{9,1},... | collective-permute-start | bytes 3145736 | tf_op jit(solution)/shard_map/ppermute | solution.py:534
  138.7 3.6 copy-start
  301.4 7.4 %collective-permute-start.12 = (bf16[16,128,1024]{2,1,0:T(8,128)(2,1)}, bf16[16,128,1024]{2,1,0:T(8,128)(2,1)S(1)}, u32[]{:S(2)}, u32[]{:S(2)}) collective-permute-start(bf16[16,128,1024]{2,1,0:T(8,128)(2,1)} %get-tuple-element.244), channel_id=1, source_target_pairs={{0,8},{1,9},{2,10},{3,11},{4,12},{5,13},{6,14},{7,15},{8,0},{9,1},... | collective-permute-start | bytes 12582920 | tf_op jit(solution)/shard_map/ppermute | solution.py:534
  313.3 38.2 %collective-permute-start.13 = (bf16[8,128,1024]{2,1,0:T(8,128)(2,1)}, bf16[8,128,1024]{2,1,0:T(8,128)(2,1)}, u32[]{:S(2)}, u32[]{:S(2)}) collective-permute-start(bf16[8,128,1024]{2,1,0:T(8,128)(2,1)} %get-tuple-element.350), channel_id=1, source_target_pairs={{0,16},{1,17},{2,18},{3,19},{4,20},{5,21},{6,22},{7,23},{8,9},{9,8... | collective-permute-start | bytes 6291464 | tf_op jit(solution)/shard_map/ppermute | solution.py:534
  351.0 20.4 %collective-permute-start.15 = (bf16[16,32,4096]{2,1,0:T(8,128)(2,1)}, bf16[16,32,4096]{2,1,0:T(8,128)(2,1)}, u32[]{:S(2)}, u32[]{:S(2)}) collective-permute-start(bf16[16,32,4096]{2,1,0:T(8,128)(2,1)} %get-tuple-element.253), channel_id=1, source_target_pairs={{0,8},{1,9},{2,10},{3,11},{4,12},{5,13},{6,14},{7,15},{8,0},{9,1},... | collective-permute-start | bytes 12582920 | tf_op jit(solution)/shard_map/ppermute | solution.py:534
  355.0 15.0 %collective-permute-start.14 = (bf16[4,128,1024]{2,1,0:T(8,128)(2,1)}, bf16[4,128,1024]{2,1,0:T(8,128)(2,1)S(1)}, u32[]{:S(2)}, u32[]{:S(2)}) collective-permute-start(bf16[4,128,1024]{2,1,0:T(8,128)(2,1)} %get-tuple-element.356), channel_id=1, source_target_pairs={{0,1},{1,0},{2,3},{3,2},{4,5},{5,4},{6,7},{7,6},{8,24},{9,25},{10,... | collective-permute-start | bytes 3145736 | tf_op jit(solution)/shard_map/ppermute | solution.py:534
  371.4 6.6 %copy-start.13 = (f32[1,512]{1,0:T(1,128)S(1)}, f32[1,512]{1,0:T(1,128)}, u32[]{:S(2)}) copy-start(f32[1,512]{1,0:T(1,128)} %get-tuple-element.312) | copy-start | bytes 6148
  371.4 6.6 %copy-start.14 = (f32[1,512]{1,0:T(1,128)S(1)}, f32[1,512]{1,0:T(1,128)}, u32[]{:S(2)}) copy-start(f32[1,512]{1,0:T(1,128)} %get-tuple-element.316) | copy-start | bytes 6148
  371.4 6.6 %copy-start.15 = (f32[1,512]{1,0:T(1,128)S(1)}, f32[1,512]{1,0:T(1,128)}, u32[]{:S(2)}) copy-start(f32[1,512]{1,0:T(1,128)} %get-tuple-element.313) | copy-start | bytes 6148
  371.4 6.6 %copy-start.16 = (f32[1,512]{1,0:T(1,128)S(1)}, f32[1,512]{1,0:T(1,128)}, u32[]{:S(2)}) copy-start(f32[1,512]{1,0:T(1,128)} %get-tuple-element.317) | copy-start | bytes 6148
  376.6 27.6 %collective-permute-start.16 = (bf16[8,32,4096]{2,1,0:T(8,128)(2,1)}, bf16[8,32,4096]{2,1,0:T(8,128)(2,1)}, u32[]{:S(2)}, u32[]{:S(2)}) collective-permute-start(bf16[8,32,4096]{2,1,0:T(8,128)(2,1)} %get-tuple-element.348), channel_id=1, source_target_pairs={{0,16},{1,17},{2,18},{3,19},{4,20},{5,21},{6,22},{7,23},{8,9},{9,8... | collective-permute-start | bytes 6291464 | tf_op jit(solution)/shard_map/ppermute | solution.py:534
  378.7 28.9 %collective-permute-start.17 = (bf16[2,128,1024]{2,1,0:T(8,128)(2,1)}, bf16[2,128,1024]{2,1,0:T(8,128)(2,1)}, u32[]{:S(2)}, u32[]{:S(2)}) collective-permute-start(bf16[2,128,1024]{2,1,0:T(8,128)(2,1)} %get-tuple-element.364), channel_id=1, source_target_pairs={{0,2},{1,3},{2,0},{3,1},{4,6},{5,7},{6,4},{7,5},{8,10},{9,11},{10,... | collective-permute-start | bytes 1572872 | tf_op jit(solution)/shard_map/ppermute | solution.py:534
  392.6 9.0 %copy-start.12 = (f32[1,512]{1,0:T(1,128)S(1)}, f32[1,512]{1,0:T(1,128)}, u32[]{:S(2)}) copy-start(f32[1,512]{1,0:T(1,128)} %get-tuple-element.310) | copy-start | bytes 6148
  392.6 10.3 %copy-start.11 = (f32[1,512]{1,0:T(1,128)S(1)}, f32[1,512]{1,0:T(1,128)}, u32[]{:S(2)}) copy-start(f32[1,512]{1,0:T(1,128)} %get-tuple-element.314) | copy-start | bytes 6148
  392.6 33.9 %collective-permute-start.18 = (bf16[16,32,2560]{2,1,0:T(8,128)(2,1)}, bf16[16,32,2560]{2,1,0:T(8,128)(2,1)}, u32[]{:S(2)}, u32[]{:S(2)}) collective-permute-start(bf16[16,32,2560]{2,1,0:T(8,128)(2,1)} %get-tuple-element.272), channel_id=1, source_target_pairs={{0,8},{1,9},{2,10},{3,11},{4,12},{5,13},{6,14},{7,15},{8,0},{9,1},... | collective-permute-start | bytes 7864328 | tf_op jit(solution)/shard_map/ppermute | solution.py:534
  404.2 3.4 copy-start.5
  409.6 22.2 %collective-permute-start.19 = (bf16[4,32,4096]{2,1,0:T(8,128)(2,1)}, bf16[4,32,4096]{2,1,0:T(8,128)(2,1)S(1)}, u32[]{:S(2)}, u32[]{:S(2)}) collective-permute-start(bf16[4,32,4096]{2,1,0:T(8,128)(2,1)} %get-tuple-element.354), channel_id=1, source_target_pairs={{0,1},{1,0},{2,3},{3,2},{4,5},{5,4},{6,7},{7,6},{8,24},{9,25},{10,... | collective-permute-start | bytes 3145736 | tf_op jit(solution)/shard_map/ppermute | solution.py:534
  418.6 27.5 %collective-permute-start.20 = (bf16[16,32,1536]{2,1,0:T(8,128)(2,1)}, bf16[16,32,1536]{2,1,0:T(8,128)(2,1)}, u32[]{:S(2)}, u32[]{:S(2)}) collective-permute-start(bf16[16,32,1536]{2,1,0:T(8,128)(2,1)} %get-tuple-element.281), channel_id=1, source_target_pairs={{0,8},{1,9},{2,10},{3,11},{4,12},{5,13},{6,14},{7,15},{8,0},{9,1},... | collective-permute-start | bytes 4718600 | tf_op jit(solution)/shard_map/ppermute | solution.py:534
  418.8 33.9 %collective-permute-start.23 = (bf16[1,128,1024]{2,1,0:T(8,128)(2,1)}, bf16[1,128,1024]{2,1,0:T(8,128)(2,1)}, u32[]{:S(2)}, u32[]{:S(2)}) collective-permute-start(bf16[1,128,1024]{2,1,0:T(8,128)(2,1)} %get-tuple-element.372), channel_id=1, source_target_pairs={{0,4},{1,5},{2,6},{3,7},{4,0},{5,1},{6,2},{7,3},{8,12},{9,13},{10,... | collective-permute-start | bytes 786440 | tf_op jit(solution)/shard_map/ppermute | solution.py:534
  431.3 18.5 %collective-permute-start.21 = (bf16[8,32,2560]{2,1,0:T(8,128)(2,1)}, bf16[8,32,2560]{2,1,0:T(8,128)(2,1)}, u32[]{:S(2)}, u32[]{:S(2)}) collective-permute-start(bf16[8,32,2560]{2,1,0:T(8,128)(2,1)} %get-tuple-element.352), channel_id=1, source_target_pairs={{0,16},{1,17},{2,18},{3,19},{4,20},{5,21},{6,22},{7,23},{8,9},{9,8... | collective-permute-start | bytes 3932168 | tf_op jit(solution)/shard_map/ppermute | solution.py:534
  433.0 18.6 %collective-permute-start.22 = (bf16[2,32,4096]{2,1,0:T(8,128)(2,1)}, bf16[2,32,4096]{2,1,0:T(8,128)(2,1)}, u32[]{:S(2)}, u32[]{:S(2)}) collective-permute-start(bf16[2,32,4096]{2,1,0:T(8,128)(2,1)} %get-tuple-element.362), channel_id=1, source_target_pairs={{0,2},{1,3},{2,0},{3,1},{4,6},{5,7},{6,4},{7,5},{8,10},{9,11},{10,... | collective-permute-start | bytes 1572872 | tf_op jit(solution)/shard_map/ppermute | solution.py:534
  442.6 3.6 copy-start.6
  446.1 22.8 %collective-permute-start.27 = (f32[16,9,128]{2,1,0:T(8,128)S(1)}, f32[16,9,128]{2,1,0:T(8,128)S(1)}, u32[]{:S(2)}, u32[]{:S(2)}) collective-permute-start(f32[16,9,128]{2,1,0:T(8,128)S(1)} %get-tuple-element.382), channel_id=1, source_target_pairs={{0,8},{1,9},{2,10},{3,11},{4,12},{5,13},{6,14},{7,15},{8,0},{9,1},... | collective-permute-start | bytes 221192 | tf_op jit(solution)/shard_map/ppermute | solution.py:534
  446.2 3.6 copy-start.3
  448.1 3.4 copy-start.4
  448.1 16.9 %collective-permute-start.24 = (bf16[8,32,1536]{2,1,0:T(8,128)(2,1)S(1)}, bf16[8,32,1536]{2,1,0:T(8,128)(2,1)S(1)}, u32[]{:S(2)}, u32[]{:S(2)}) collective-permute-start(bf16[8,32,1536]{2,1,0:T(8,128)(2,1)S(1)} %get-tuple-element.358), channel_id=1, source_target_pairs={{0,16},{1,17},{2,18},{3,19},{4,20},{5,21},{6,22},{7,23},{8,9},{9,8... | collective-permute-start | bytes 2359304 | tf_op jit(solution)/shard_map/ppermute | solution.py:534
  449.8 3.5 copy-start.7
  452.7 15.1 %collective-permute-start.25 = (bf16[4,32,2560]{2,1,0:T(8,128)(2,1)S(1)}, bf16[4,32,2560]{2,1,0:T(8,128)(2,1)S(1)}, u32[]{:S(2)}, u32[]{:S(2)}) collective-permute-start(bf16[4,32,2560]{2,1,0:T(8,128)(2,1)S(1)} %get-tuple-element.360), channel_id=1, source_target_pairs={{0,1},{1,0},{2,3},{3,2},{4,5},{5,4},{6,7},{7,6},{8,24},{9,25},{10,... | collective-permute-start | bytes 1966088 | tf_op jit(solution)/shard_map/ppermute | solution.py:534
  453.3 14.7 %collective-permute-start.26 = (bf16[1,32,4096]{2,1,0:T(8,128)(2,1)S(1)}, bf16[1,32,4096]{2,1,0:T(8,128)(2,1)S(1)}, u32[]{:S(2)}, u32[]{:S(2)}) collective-permute-start(bf16[1,32,4096]{2,1,0:T(8,128)(2,1)S(1)} %get-tuple-element.370), channel_id=1, source_target_pairs={{0,4},{1,5},{2,6},{3,7},{4,0},{5,1},{6,2},{7,3},{8,12},{9,13},{10,... | collective-permute-start | bytes 786440 | tf_op jit(solution)/shard_map/ppermute | solution.py:534
  465.2 9.1 %collective-permute-start.28 = (bf16[4,32,1536]{2,1,0:T(8,128)(2,1)S(1)}, bf16[4,32,1536]{2,1,0:T(8,128)(2,1)S(1)}, u32[]{:S(2)}, u32[]{:S(2)}) collective-permute-start(bf16[4,32,1536]{2,1,0:T(8,128)(2,1)S(1)} %get-tuple-element.366), channel_id=1, source_target_pairs={{0,1},{1,0},{2,3},{3,2},{4,5},{5,4},{6,7},{7,6},{8,24},{9,25},{10,... | collective-permute-start | bytes 1179656 | tf_op jit(solution)/shard_map/ppermute | solution.py:534
  468.8 10.7 %collective-permute-start.29 = (bf16[2,32,2560]{2,1,0:T(8,128)(2,1)S(1)}, bf16[2,32,2560]{2,1,0:T(8,128)(2,1)S(1)}, u32[]{:S(2)}, u32[]{:S(2)}) collective-permute-start(bf16[2,32,2560]{2,1,0:T(8,128)(2,1)S(1)} %get-tuple-element.368), channel_id=1, source_target_pairs={{0,2},{1,3},{2,0},{3,1},{4,6},{5,7},{6,4},{7,5},{8,10},{9,11},{10,... | collective-permute-start | bytes 983048 | tf_op jit(solution)/shard_map/ppermute | solution.py:534
  470.9 8.7 %collective-permute-start.30 = (f32[8,9,128]{2,1,0:T(8,128)S(1)}, f32[8,9,128]{2,1,0:T(8,128)S(1)}, u32[]{:S(2)}, u32[]{:S(2)}) collective-permute-start(f32[8,9,128]{2,1,0:T(8,128)S(1)} %get-tuple-element.380), channel_id=1, source_target_pairs={{0,16},{1,17},{2,18},{3,19},{4,20},{5,21},{6,22},{7,23},{8,9},{9,8... | collective-permute-start | bytes 110600 | tf_op jit(solution)/shard_map/ppermute | solution.py:534
  474.4 9.5 %collective-permute-start.31 = (bf16[2,32,1536]{2,1,0:T(8,128)(2,1)S(1)}, bf16[2,32,1536]{2,1,0:T(8,128)(2,1)S(1)}, u32[]{:S(2)}, u32[]{:S(2)}) collective-permute-start(bf16[2,32,1536]{2,1,0:T(8,128)(2,1)S(1)} %get-tuple-element.374), channel_id=1, source_target_pairs={{0,2},{1,3},{2,0},{3,1},{4,6},{5,7},{6,4},{7,5},{8,10},{9,11},{10,... | collective-permute-start | bytes 589832 | tf_op jit(solution)/shard_map/ppermute | solution.py:534
  479.6 9.5 %collective-permute-start.32 = (bf16[1,32,2560]{2,1,0:T(8,128)(2,1)S(1)}, bf16[1,32,2560]{2,1,0:T(8,128)(2,1)S(1)}, u32[]{:S(2)}, u32[]{:S(2)}) collective-permute-start(bf16[1,32,2560]{2,1,0:T(8,128)(2,1)S(1)} %get-tuple-element.376), channel_id=1, source_target_pairs={{0,4},{1,5},{2,6},{3,7},{4,0},{5,1},{6,2},{7,3},{8,12},{9,13},{10,... | collective-permute-start | bytes 491528 | tf_op jit(solution)/shard_map/ppermute | solution.py:534
  479.7 9.4 %collective-permute-start.33 = (f32[4,9,128]{2,1,0:T(8,128)S(1)}, f32[4,9,128]{2,1,0:T(8,128)S(1)}, u32[]{:S(2)}, u32[]{:S(2)}) collective-permute-start(f32[4,9,128]{2,1,0:T(8,128)S(1)} %get-tuple-element.384), channel_id=1, source_target_pairs={{0,1},{1,0},{2,3},{3,2},{4,5},{5,4},{6,7},{7,6},{8,24},{9,25},{10,... | collective-permute-start | bytes 55304 | tf_op jit(solution)/shard_map/ppermute | solution.py:534
  484.0 7.9 %collective-permute-start.34 = (bf16[1,32,1536]{2,1,0:T(8,128)(2,1)S(1)}, bf16[1,32,1536]{2,1,0:T(8,128)(2,1)S(1)}, u32[]{:S(2)}, u32[]{:S(2)}) collective-permute-start(bf16[1,32,1536]{2,1,0:T(8,128)(2,1)S(1)} %get-tuple-element.378), channel_id=1, source_target_pairs={{0,4},{1,5},{2,6},{3,7},{4,0},{5,1},{6,2},{7,3},{8,12},{9,13},{10,... | collective-permute-start | bytes 294920 | tf_op jit(solution)/shard_map/ppermute | solution.py:534
  489.8 3.7 collective-permute-start.35
  493.6 4.5 collective-permute-start.36
  495.8 3.4 copy-start.9
  (2 other events, 6.1 us)
Sparse Core Ops, SparseCore 0:
  11.8 144.8 all-gather.2

commit v7 on v6

--- a/solution.py
+++ b/solution.py
@@ -252,6 +252,64 @@
     )(a, packed, up_bias, packed, down_bias, x1)
 
 
+def feed_forward_in(a, packed, r_in, up_bias):
+    rows, width = a.shape
+    hidden = up_bias.shape[1]
+
+    def body(a_ref, u_ref, ub_ref, g_ref, gp_ref):
+        u = dot(a_ref[...], flat(u_ref)) + ub_ref[...]
+        phi, bell = normal_cdf(u)
+        g_ref[...] = (u * phi).astype(jnp.bfloat16)
+        gp_ref[...] = (phi + (u * RSQRT_2PI) * bell).astype(jnp.bfloat16)
+
+    block = pl.BlockSpec((rows, width), lambda j: (0, j))
+    return call(
+        body,
+        grid=(hidden // width,),
+        in_specs=[
+            whole((rows, width)),
+            up_spec(packed, r_in),
+            pl.BlockSpec((1, width), lambda j: (0, j)),
+        ],
+        out_specs=[block, block],
+        out_shape=[jax.ShapeDtypeStruct((rows, hidden), jnp.bfloat16)] * 2,
+        name="feed_forward_in",
+    )(a, packed, up_bias)
+
+
+def feed_forward_out(g, packed, r_ff, down_bias, x1):
+    rows, width = x1.shape
+    steps = g.shape[1] // width
+
+    def body(g_ref, d_ref, db_ref, x_ref, y_ref, acc):
+        j = pl.program_id(0)
+
+        @pl.when(j == 0)
+        def _():
+            acc[...] = x_ref[...] + db_ref[...]
+
+        acc[...] += dot(g_ref[...], flat(d_ref))
+
+        @pl.when(j == steps - 1)
+        def _():
+            y_ref[...] = acc[...].astype(jnp.bfloat16)
+
+    return call(
+        body,
+        grid=(steps,),
+        in_specs=[
+            pl.BlockSpec((rows, width), lambda j: (0, j)),
+            down_spec(packed, r_ff),
+            whole((1, width)),
+            whole((rows, width)),
+        ],
+        out_specs=whole((rows, width)),
+        out_shape=jax.ShapeDtypeStruct((rows, width), jnp.bfloat16),
+        scratch_shapes=[pltpu.VMEM((rows, width), jnp.float32)],
+        name="feed_forward_out",
+    )(g, packed, down_bias, x1)
+
+
 def feed_forward_back(dy, gp, packed, r_in, r_ff, x1, gain, w_out, at):
     rows, width = dy.shape
     hidden = gp.shape[1]
@@ -547,30 +605,20 @@
         self.last = array
 
 
-def place_shards(groups, table_row, shapes, slots):
-    n = sum(p.shape[0] for p in groups[0])
-    count = len(groups)
+def place_shards(pieces, table_row, shape, rows_at, rows, into=None, cover=False):
+    count = sum(a.shape[0] for a, _ in pieces)
+    cols = shape[-1]
 
     def body(t_ref, *refs):
-        ins = refs[: 4 * count]
-        outs = refs[4 * count : 4 * count + len(shapes)]
-        bufs = refs[4 * count + len(shapes) : -2]
-        in_sem, out_sem = refs[-2:]
+        ins, out, (buf, in_sem, out_sem) = refs[: len(pieces)], refs[-4], refs[-3:]
         loads, stores = [], []
-        for i in range(count):
-            which, middle, col = slots[i]
-            width = bufs[i].shape[-1]
-            for p in range(n):
-                piece = ins[4 * i + p // (n // 4)].at[p % (n // 4), 0 : bufs[i].shape[1]]
-                loads.append(pltpu.make_async_copy(piece, bufs[i].at[p], in_sem.at[i, p]))
-                target = outs[which].at[t_ref[p]]
-                if middle is not None:
-                    target = target.at[middle]
-                stores.append(
-                    pltpu.make_async_copy(
-                        bufs[i].at[p], target.at[:, col : col + width], out_sem.at[i, p]
-                    )
-                )
+        for ref, (array, first) in zip(ins, pieces):
+            for k in range(array.shape[0]):
+                i = len(loads)
+                source = ref.at[k, :, 0:cols]
+                loads.append(pltpu.make_async_copy(source, buf.at[i], in_sem.at[i]))
+                target = out.at[t_ref[first + k], rows_at : rows_at + rows]
+                stores.append(pltpu.make_async_copy(buf.at[i], target, out_sem.at[i]))
         for c in loads:
             c.start()
         for a, b in zip(loads, stores):
@@ -579,28 +627,58 @@
         for b in stores:
             b.wait()
 
-    flat = [p for g in groups for p in g]
     anywhere = pl.BlockSpec(memory_space=pl.ANY)
-    return call(
-        body,
-        out_shape=[jax.ShapeDtypeStruct(s, jnp.bfloat16) for s in shapes],
+    args = [a for a, _ in pieces] + ([] if into is None else [into])
+    return call(
+        body,
+        out_shape=jax.ShapeDtypeStruct(shape, jnp.bfloat16),
         grid_spec=pltpu.PrefetchScalarGridSpec(
             num_scalar_prefetch=1,
-            in_specs=[anywhere] * len(flat),
-            out_specs=[anywhere] * len(shapes),
-            scratch_shapes=[
-                pltpu.VMEM((n, shapes[s[0]][-2], g[0].shape[-1]), jnp.bfloat16)
-                for g, s in zip(groups, slots)
-            ]
-            + [pltpu.SemaphoreType.DMA((count, n))] * 2,
+            in_specs=[anywhere] * len(args),
+            out_specs=anywhere,
+            scratch_shapes=[pltpu.VMEM((count, rows, cols), jnp.bfloat16)]
+            + [pltpu.SemaphoreType.DMA((count,))] * 2,
         ),
+        input_output_aliases={} if into is None else {len(args): 0},
         name="place_shards",
-    )(table_row, *flat)
+        cover=cover,
+    )(table_row, *args)
+
+
+def pack_shard(matrices, vectors):
+    rows = matrices[0].shape[0]
+    widths = [m.shape[1] for m in matrices]
+    lanes = 128 * -(-len(vectors) // 8)
+
+    def body(*refs):
+        out, scr = refs[-2:]
+        at = 0
+        for ref, width in zip(refs, widths):
+            out[:, at : at + width] = ref[...]
+            at += width
+        scr[...] = jnp.zeros_like(scr)
+        for r, ref in enumerate(refs[len(widths) : -2]):
+            k, col = ref.shape[1], 128 * (r // 8)
+            scr[r % 8 : r % 8 + 1, col : col + k] = ref[...].astype(jnp.float32)
+        out[:, at:] = scr[...].astype(jnp.bfloat16)
+
+    vectors = [v.reshape(1, -1) for v in vectors]
+    cols = sum(widths) + lanes
+    return call(
+        body,
+        grid=(1,),
+        in_specs=[whole(a.shape) for a in (*matrices, *vectors)],
+        out_specs=whole((rows, cols)),
+        out_shape=jax.ShapeDtypeStruct((rows, cols), jnp.bfloat16),
+        scratch_shapes=[pltpu.VMEM((rows, lanes), jnp.float32)],
+        name="pack_shard",
+    )(*matrices, *vectors)
 
 
 def unpack_vectors(pieces, at, inverse_row, sizes, layout):
     per_piece = pieces[0].shape[0]
     n = per_piece * len(pieces)
+    lanes = pieces[0].shape[2] - at
 
     def body(i_ref, *refs):
         ins, outs, scr = refs[: len(pieces)], refs[len(pieces) : -1], refs[-1]
@@ -615,21 +693,24 @@
                     if r is None:
                         value = jnp.zeros((1, per * k), jnp.float32)
                     else:
+                        row, lane = r % 8, 128 * (r // 8)
                         value = jnp.concatenate(
-                            [scr[i_ref[d + e], 0:1, r * 128 : r * 128 + k] for e in range(per)],
+                            [
+                                scr[i_ref[d + e], row : row + 1, lane : lane + k]
+                                for e in range(per)
+                            ],
                             axis=1,
                         )
                     out[0:1, col + d * k : col + (d + per) * k] = value
                 col += n * k
 
     widths = [sum(n * (sizes[0] if r is None else sizes[r]) for r in rows) for rows in layout]
-    lanes = 128 * len(sizes)
     return call(
         body,
         grid_spec=pltpu.PrefetchScalarGridSpec(
             num_scalar_prefetch=1,
             grid=(1,),
-            in_specs=[pl.BlockSpec((per_piece, 8, lanes), lambda i, i_ref: (0, at // 8, 0))]
+            in_specs=[pl.BlockSpec((per_piece, 8, lanes), lambda i, i_ref: (0, 0, at // lanes))]
             * len(pieces),
             out_specs=[pl.BlockSpec((1, w), lambda i, i_ref: (0, 0)) for w in widths],
             scratch_shapes=[pltpu.VMEM((n, 8, lanes), jnp.float32)],
@@ -725,72 +806,108 @@
 
     vectors = (ln1_gain, ln1_bias, bias_q, bias_v, bias_out, ln2_gain, ln2_bias, bias_down, bias_up)
     sizes = [v.shape[0] for v in vectors]
-    lanes_of = lambda v: jnp.pad(v, (0, 128 - v.shape[0]))
-    packed = jnp.concatenate([lanes_of(v) for v in vectors])
-
     line = Line()
-    mid = 2 * width
-    packed = jnp.pad(packed[None], ((0, 7), (0, mid - packed.shape[0])))
-    shards = [
-        jnp.concatenate([w_qkv[:, :mid], packed], axis=0),
-        jnp.concatenate([w_qkv[:, mid:], w_out], axis=1),
-    ]
+    qkv_cols = w_qkv.shape[1]
+    cols = qkv_cols + w_out.shape[1]
+    ahead = pack_shard([w_qkv, w_out], vectors)
     split = w_up.reshape(r_in, hidden // width, width).swapaxes(0, 1).reshape(r_ff, width)
-    w = {"ff": lax.all_gather(jnp.concatenate([split, w_down], axis=0), AXES)}
-    held = [s[None] for s in shards]
-    got = [None] * len(shards)
-    pieces = [None] * len(shards)
-
-    def gather_round(index):
-        for i in range(len(shards)):
-            k = index - i
-            if k < 0 or k > stages:
-                continue
-            if k == 0 and i:
-                (held[i],) = line.after(held[i])
-            if 0 < k < stages:
-                mine, theirs = line.after(held[i], got[i])
-                held[i] = jnp.concatenate([mine, theirs], axis=0)
-                line.mark(held[i])
-            if k < stages:
-                got[i] = send(held[i], gather_perms[k])
-            if k == stages - 1:
-                pieces[i] = [held[i], None, send(held[i], core_perm), None]
-            if k == stages:
-                pieces[i][1] = got[i]
-                pieces[i][3] = send(got[i], core_perm)
-
-    def place(which, shapes, slots):
-        flat = [p for i in which for p in pieces[i]]
-        flat = line.after(*flat)
-        groups = [flat[4 * i : 4 * i + 4] for i in range(len(which))]
-        outs = place_shards(groups, row, shapes, slots)
-        line.mark(outs[0])
-        return outs
-
-    for index in range(stages + 2):
-        gather_round(index)
+
+    class Gather:
+        def __init__(self, shard):
+            self.held, self.stage = shard[None], 0
+            (self.held,) = line.after(self.held)
+            self.got = send(self.held, gather_perms[0])
+
+        def step(self):
+            mine, theirs = line.after(self.held, self.got)
+            self.held = jnp.concatenate([mine, theirs], axis=0)
+            line.mark(self.held)
+            self.stage += 1
+            self.got = send(self.held, gather_perms[self.stage])
+            if self.stage == stages - 1:
+                self.early = send(self.held, core_perm)
+
+        def finish(self):
+            (self.got,) = line.after(self.got)
+            self.late = send(self.got, core_perm)
+
+        def place(self, which, *where, into=None, cover=False):
+            quarter = n // 4
+            pair = (self.got, self.late) if which else (self.held, self.early)
+            pair = line.after(*pair)
+            pieces = [(pair[0], which * quarter), (pair[1], half + which * quarter)]
+            out = place_shards(pieces, row, *where, into=into, cover=cover)
+            line.mark(out)
+            return out
+
+    half = n // 2
+    chain_a = Gather(ahead)
+    for k in range(1, stages - 2):
+        chain_a.step()
+    chain_b = Gather(split)
+    chain_a.step()
+    for k in range(1, stages - 2):
+        chain_b.step()
+    chain_a.step()
+    chain_b.step()
+    chain_c = Gather(w_down)
+    spot_a = ((n, r_in, cols), 0, r_in)
+    first = chain_a.place(0, *spot_a, cover=True)
+    for k in range(1, stages - 2):
+        chain_c.step()
+    chain_b.step()
+    chain_a.finish()
+    first = chain_a.place(1, *spot_a, into=first)
+    w = {"first": first.reshape(n * r_in, cols)}
     g1, s1, bqkv, bo, g2, s2, bd, bu = unpack_vectors(
-        pieces[0], r_in, inverse_row, sizes, [[0], [1], [2, None, 3], [4], [5], [6], [7], [8]]
+        (chain_a.held, chain_a.got, chain_a.early, chain_a.late),
+        cols,
+        inverse_row,
+        sizes,
+        [[0], [1], [2, None, 3], [4], [5], [6], [7], [8]],
     )
-    qkv_cols = w_qkv.shape[1]
-    (first_full,) = place([0, 1], [(n, r_in, 2 * mid)], [(0, None, 0), (0, None, mid)])
-    first_full = first_full.reshape(n * r_in, 2 * mid)
-    w["first"] = first_full
-
-    def forward(x):
+    spot_b = ((n, 2 * r_ff, width), 0, r_ff)
+    spot_c = ((n, 2 * r_ff, width), r_ff, r_ff)
+
+    def more(index):
+        if index == 0:
+            chain_c.step()
+        if index == 1:
+            chain_b.finish()
+        if index == 2:
+            chain_c.step()
+            ff = chain_b.place(0, *spot_b)
+            w["ff"] = chain_b.place(1, *spot_b, into=ff)
+        if index == 3:
+            ff = chain_c.place(0, *spot_c, into=w["ff"])
+            chain_c.finish()
+            w["ff"] = chain_c.place(1, *spot_c, into=ff)
+
+    def forward(x, more=None):
         a1, qkv = norm_project(*line.after(x), g1, s1, w["first"], bqkv, qkv_cols // 2, qkv_cols)
         line.mark(a1)
+        if more:
+            more(0)
         o, logs = attention(*line.after(qkv))
         line.mark(o)
+        if more:
+            more(1)
         x1, a2 = project_norm(*line.after(o), w["first"], bo, x, g2, s2, qkv_cols)
         line.mark(a2)
+        if more:
+            more(2)
         a2 = line.after(a2)[0]
-        g, gp, y = feed_forward(a2, w["ff"], r_in, r_ff, bu, bd, x1)
+        if more is None:
+            g, gp, y = feed_forward(a2, w["ff"], r_in, r_ff, bu, bd, x1)
+        else:
+            g, gp = feed_forward_in(a2, w["ff"], r_in, bu)
+            line.mark(g)
+            more(3)
+            y = feed_forward_out(line.after(g)[0], w["ff"], r_ff, bd, x1)
         line.mark(y)
         return y, (x, a1, qkv, logs, o, x1, a2, g, gp)
 
-    first, saved_first = forward(tokens[0])
+    first, saved_first = forward(tokens[0], more)
     second, saved_second = forward(first)
 
     keep_mask = valid[0].astype(jnp.float32)[:, None]
@@ -826,7 +943,6 @@
         heads2, saved_second, dx2, (cot_first[0], keep_mask), (jnp.float32, jnp.bfloat16)
     )
 
-    half = n // 2
     core = (me // nfs) % 2
     evens = 2 * jnp.arange(ndp // 2, dtype=jnp.int32)
     lefts_at = jnp.concatenate([evens + (1 - core), evens + core])

time: 516 us -> 492 us (0.953)
  waiting for transfers between devices: 150 us -> 115 us
  Pallas kernels: 246 us -> 270 us
  between operations: 15.3 us -> 1.55 us
  local copies, waits for them, and re-layouts: 10.3 us -> 21.8 us
    pallas_call x1 -> x9, Pallas kernels: 8.41 us -> 50.3 us  [the longest x6 27.3 us: place_shards(): call(body, out_shape=jax.ShapeDtypeStruct(shape, jnp.bfloat16), grid_spec...]
    ppermute x37 -> x43, waiting for transfers between devices: 150 us -> 115 us  [send(): return lax.ppermute(x, AXES, perm)]
    pallas_call x2 -> x1, Pallas kernels: 35.7 us -> 17.9 us  [feed_forward(): call(body, grid=(steps,), in_specs=[whole((rows, width)), up_spec(packed,...]
    concatenate x6 -> x8, local copies, waits for them, and re-layouts: 0.94 us -> 7.3 us  [step(): self.held = jnp.concatenate([mine, theirs], axis=0)]
    unnamed x70 -> x59, local copies, waits for them, and re-layouts: 2.76 us -> 8.81 us
    ppermute x37 -> x43, starting transfers between devices: 41.7 us -> 38.9 us  [send(): return lax.ppermute(x, AXES, perm)]
  transfers between devices with their start and end apart: 38 -> 43, of which waited for: 17 -> 20; matrix products, arithmetic and copies ran while one was open for 8% -> 9% of each run, Pallas kernels for 24% -> 30%
where the time goes in v7:
time: 492 us; the launch traced here: 488 us
  Pallas kernels  270 us (55%)
  waiting for transfers between devices  115 us (23%)
  other arithmetic  40.5 us (8%)
  starting transfers between devices  38.9 us (8%)
  local copies, waits for them, and re-layouts  21.8 us (4%)
    ppermute x43, waiting for transfers between devices, send(): return lax.ppermute(x, AXES, perm)  115 us
    pallas_call x4, Pallas kernels, weight_grad(): call(body, grid_spec=pltpu.PrefetchScalarGridSpec(num_scalar_prefetch=1,...  52.6 us
    pallas_call x2, Pallas kernels, feed_forward_back(): call(body, grid=(steps,), in_specs=[full, pl.BlockSpec((rows, tf), lambda...  40.5 us
    ppermute x43, starting transfers between devices, send(): return lax.ppermute(x, AXES, perm)  38.9 us
    pallas_call x4, Pallas kernels, attention_back(): call(body, grid=(pairs,), in_specs=[col(first_pair), col(every + first_pa...  35.7 us
    convert_element_type x16, other arithmetic, step(): sent = add(slice(half, None)).astype(wide)  31.3 us
    pallas_call x6, Pallas kernels, place_shards(): call(body, out_shape=jax.ShapeDtypeStruct(shape, jnp.bfloat16), grid_spec...  27.3 us
    pallas_call x2, Pallas kernels, attention(): call(body, grid=(pairs,), in_specs=[col(0), col(pairs), col(2 * pairs)],...  21.7 us
  transfers between devices with their start and end apart: 43, of which 20 were waited for; matrix products, arithmetic and copies ran while one was open for 9% of the time, Pallas kernels for 30%

profile of v7, /device:TPU:0, one launch (start us, length us, event | category | flops | bytes accessed | tf_op | source)
XLA Modules:
  0.0 487.7 jit_solution(11957414099652220856)
XLA Ops:
  0.7 1.8 pack_shard.1
  2.5 4.0 collective-permute-start
  6.5 12.8 %collective-permute-done = bf16[1,32,4352]{2,1,0:T(8,128)(2,1)S(1)} collective-permute-done((bf16[1,32,4352]{2,1,0:T(8,128)(2,1)}, bf16[1,32,4352]{2,1,0:T(8,128)(2,1)S(1)}, u32[]{:S(2)}, u32[]{:S(2)}) %collective-permute-start) | collective-permute-done | bytes 278560 | tf_op jit(solution)/shard_map/ppermute | solution.py:592
  21.2 13.0 %collective-permute-done.1 = bf16[2,32,4352]{2,1,0:T(8,128)(2,1)S(1)} collective-permute-done((bf16[2,32,4352]{2,1,0:T(8,128)(2,1)S(1)}, bf16[2,32,4352]{2,1,0:T(8,128)(2,1)S(1)}, u32[]{:S(2)}, u32[]{:S(2)}) %collective-permute-start.1) | collective-permute-done | bytes 557088 | tf_op jit(solution)/shard_map/ppermute | solution.py:592
  35.8 3.3 collective-permute-start.2
  39.1 11.3 %collective-permute-done.2 = bf16[1,128,1024]{2,1,0:T(8,128)(2,1)S(1)} collective-permute-done((bf16[1,128,1024]{2,1,0:T(8,128)(2,1)S(1)}, bf16[1,128,1024]{2,1,0:T(8,128)(2,1)S(1)}, u32[]{:S(2)}, u32[]{:S(2)}) %collective-permute-start.2) | collective-permute-done | bytes 262176 | tf_op jit(solution)/shard_map/ppermute | solution.py:592
  56.5 10.7 %collective-permute-done.4 = bf16[2,128,1024]{2,1,0:T(8,128)(2,1)} collective-permute-done((bf16[2,128,1024]{2,1,0:T(8,128)(2,1)S(1)}, bf16[2,128,1024]{2,1,0:T(8,128)(2,1)}, u32[]{:S(2)}, u32[]{:S(2)}) %collective-permute-start.4) | collective-permute-done | bytes 524320 | tf_op jit(solution)/shard_map/ppermute | solution.py:592
  69.3 1.6 collective-permute-start.7
  70.9 2.5 collective-permute-start.6
  73.4 4.5 place_shards.6.refs_2_
  77.9 7.1 %collective-permute-done.6 = bf16[1,128,1024]{2,1,0:T(8,128)(2,1)} collective-permute-done((bf16[1,128,1024]{2,1,0:T(8,128)(2,1)S(1)}, bf16[1,128,1024]{2,1,0:T(8,128)(2,1)}, u32[]{:S(2)}, u32[]{:S(2)}) %collective-permute-start.6) | collective-permute-done | bytes 262176 | tf_op jit(solution)/shard_map/ppermute | solution.py:592
  85.7 1.7 constant_dynamic-update-slice_fusion.8
  87.4 5.8 %collective-permute-done.7 = bf16[4,128,1024]{2,1,0:T(8,128)(2,1)} collective-permute-done((bf16[4,128,1024]{2,1,0:T(8,128)(2,1)S(1)}, bf16[4,128,1024]{2,1,0:T(8,128)(2,1)}, u32[]{:S(2)}, u32[]{:S(2)}) %collective-permute-start.7) | collective-permute-done | bytes 1048608 | tf_op jit(solution)/shard_map/ppermute | solution.py:592
  94.3 2.3 constant_dynamic-update-slice_fusion.10.refs_0_
  98.9 2.3 collective-permute-done.9.refs_1_.refs_3_
  101.2 4.5 place_shards.7
  105.7 2.4 unpack_vectors.1
  108.1 8.1 %norm_project.2 = (bf16[512,1024]{1,0:T(8,128)(2,1)}, bf16[512,3072]{1,0:T(8,128)(2,1)}) custom-call(bf16[512,1024]{1,0:T(8,128)(2,1)} %bitcast.72, f32[1,1024]{1,0:T(1,128)} %get-tuple-element.218.g_ref.refs_4_, f32[1,1024]{1,0:T(1,128)} %get-tuple-element.219.s_ref, bf16[1024,4096]{1,0:T(8,128)(2,1)} %bitcast.63, f32[1,3072]{1,0:T(1,128)} %get-tuple-element.220.b_ref), custom_call_target="tpu_custom_call" | custom-call | flops 1 | bytes 1 | tf_op jit(solution)/shard_map/norm_project/pallas_call | solution.py:55
  118.4 1.6 collective-permute-start.11
  120.0 10.8 %attention.2 = (bf16[512,1024]{1,0:T(8,128)(2,1)}, f32[8,8,512]{2,1,0:T(8,128)}) custom-call(bf16[512,3072]{1,0:T(8,128)(2,1)} %get-tuple-element.225.q_ref.k_ref.v_ref, bf16[512,3072]{1,0:T(8,128)(2,1)} %get-tuple-element.225.q_ref.k_ref.v_ref, bf16[512,3072]{1,0:T(8,128)(2,1)} %get-tuple-element.225.q_ref.k_ref.v_ref), custom_call_target="tpu_custom_call" | custom-call | flops 1 | bytes 1 | tf_op jit(solution)/shard_map/attention/pallas_call | solution.py:100
  131.4 4.9 project_norm.2
  140.0 4.5 place_shards.8.refs_2_
  144.6 4.5 place_shards.9.u_ref.refs_2_
  149.1 11.5 %feed_forward_in.1 = (bf16[512,4096]{1,0:T(8,128)(2,1)}, bf16[512,4096]{1,0:T(8,128)(2,1)}) custom-call(bf16[512,1024]{1,0:T(8,128)(2,1)} %get-tuple-element.279.a_ref.refs_0_, bf16[32,256,1024]{2,1,0:T(8,128)(2,1)} %place_shards.9.u_ref.refs_2_, f32[1,4096]{1,0:T(1,128)} %get-tuple-element.240.ub_ref), custom_call_target="tpu_custom_call" | custom-call | flops 1 | bytes 1 | tf_op jit(solution)/shard_map/feed_forward_in/pallas_call | solution.py:266
  160.7 4.7 place_shards.10.refs_2_
  167.0 1.6 convert_multiply_fusion.dy_ref
  171.1 4.5 place_shards.11.d_ref.u_ref
  175.6 9.7 %feed_forward_out.1.x_ref.refs_3_ = bf16[512,1024]{1,0:T(8,128)(2,1)} custom-call(bf16[512,4096]{1,0:T(8,128)(2,1)} %get-tuple-element.272.g_ref.refs_0_, bf16[32,256,1024]{2,1,0:T(8,128)(2,1)} %place_shards.11.d_ref.u_ref, f32[1,1024]{1,0:T(1,128)} %get-tuple-element.248.db_ref, f32[512,1024]{1,0:T(8,128)} %get-tuple-element.249.x_ref), custom_call_target="tpu_custom_call" | custom-call | flops 1 | bytes 1 | tf_op jit(solution)/shard_map/feed_forward_out/pallas_call | solution.py:297
  185.3 7.8 %norm_project.3 = (bf16[512,1024]{1,0:T(8,128)(2,1)}, bf16[512,3072]{1,0:T(8,128)(2,1)}) custom-call(bf16[512,1024]{1,0:T(8,128)(2,1)} %feed_forward_out.1.x_ref.refs_3_, f32[1,1024]{1,0:T(1,128)} %get-tuple-element.218.g_ref.refs_4_, f32[1,1024]{1,0:T(1,128)} %get-tuple-element.219.s_ref, bf16[1024,4096]{1,0:T(8,128)(2,1)} %bitcast.65, ...), custom_call_target="tpu_custom_call" | custom-call | flops 1 | bytes 1 | tf_op jit(solution)/shard_map/norm_project/pallas_call | solution.py:55
  193.9 10.9 %attention.3 = (bf16[512,1024]{1,0:T(8,128)(2,1)}, f32[8,8,512]{2,1,0:T(8,128)}) custom-call(bf16[512,3072]{1,0:T(8,128)(2,1)} %get-tuple-element.251.q_ref.k_ref.v_ref, bf16[512,3072]{1,0:T(8,128)(2,1)} %get-tuple-element.251.q_ref.k_ref.v_ref, bf16[512,3072]{1,0:T(8,128)(2,1)} %get-tuple-element.251.q_ref.k_ref.v_ref), custom_call_target="tpu_custom_call" | custom-call | flops 1 | bytes 1 | tf_op jit(solution)/shard_map/attention/pallas_call | solution.py:100
  204.8 5.5 %project_norm.3 = (f32[512,1024]{1,0:T(8,128)}, bf16[512,1024]{1,0:T(8,128)(2,1)}) custom-call(bf16[512,1024]{1,0:T(8,128)(2,1)} %get-tuple-element.297.o_ref.refs_1_, bf16[1024,4096]{1,0:T(8,128)(2,1)} %bitcast.66, f32[1,1024]{1,0:T(1,128)} %get-tuple-element.228.b_ref, bf16[512,1024]{1,0:T(8,128)(2,1)} %feed_forward_out.1.x_ref.refs_3_, ...), custom_call_target="tpu_custom_call" | custom-call | flops 1 | bytes 1 | tf_op jit(solution)/shard_map/project_norm/pallas_call | solution.py:178
  210.2 17.9 %feed_forward.1 = (bf16[512,4096]{1,0:T(8,128)(2,1)}, bf16[512,4096]{1,0:T(8,128)(2,1)}, bf16[512,1024]{1,0:T(8,128)(2,1)}) custom-call(bf16[512,1024]{1,0:T(8,128)(2,1)} %get-tuple-element.280.a_ref.refs_1_, bf16[32,256,1024]{2,1,0:T(8,128)(2,1)} %place_shards.11.d_ref.u_ref, f32[1,4096]{1,0:T(1,128)} %get-tuple-element.240.ub_ref, ...), custom_call_target="tpu_custom_call" | custom-call | flops 1 | bytes 1 | tf_op jit(solution)/shard_map/feed_forward/pallas_call | solution.py:229
  228.1 20.3 %feed_forward_back.2 = (bf16[512,1024]{1,0:T(8,128)(2,1)}, bf16[512,4096]{1,0:T(8,128)(2,1)}, f32[512,1024]{1,0:T(8,128)}, bf16[512,1024]{1,0:T(8,128)(2,1)}, bf...) custom-call(f32[512,1024]{1,0:T(8,128)} %convert_multiply_fusion.dy_, ...), custom_call_target="tpu_custom_call" | custom-call | flops 99999997952 | bytes 1 | tf_op jit(solution)/shard_map/feed_forward_back/pallas_call | solution.py:356
  248.4 8.9 %attention_back.4 = (bf16[3,512,512]{2,1,0:T(8,128)(2,1)}, f32[1,512]{1,0:T(1,128)}, f32[1,512]{1,0:T(1,128)}) custom-call(bf16[512,3072]{1,0:T(8,128)(2,1)} %get-tuple-element.251.q_ref.k_ref.v_ref, bf16[512,3072]{1,0:T(8,128)(2,1)} %get-tuple-element.251.q_ref.k_ref.v_ref, bf16[512,3072]{1,0:T(8,128)(2,1)} %get-tuple-element.251.q_ref.k_ref.v_ref, ...), custom_call_target="tpu_custom_call" | custom-call | flops 99999997952 | bytes 1 | tf_op jit(solution)/shard_map/attention_back/pallas_call | solution.py:145
  257.4 8.9 %attention_back.5 = (bf16[3,512,512]{2,1,0:T(8,128)(2,1)}, f32[1,512]{1,0:T(1,128)}, f32[1,512]{1,0:T(1,128)}) custom-call(bf16[512,3072]{1,0:T(8,128)(2,1)} %get-tuple-element.251.q_ref.k_ref.v_ref, bf16[512,3072]{1,0:T(8,128)(2,1)} %get-tuple-element.251.q_ref.k_ref.v_ref, bf16[512,3072]{1,0:T(8,128)(2,1)} %get-tuple-element.251.q_ref.k_ref.v_ref, ...), custom_call_target="tpu_custom_call" | custom-call | flops 99999997952 | bytes 1 | tf_op jit(solution)/shard_map/attention_back/pallas_call | solution.py:145
  266.3 10.4 %project_back.2 = (f32[512,1024]{1,0:T(8,128)}, bf16[512,1024]{1,0:T(8,128)(2,1)}, f32[1,1024]{1,0:T(1,128)}, f32[1,1024]{1,0:T(1,128)}) custom-call(bf16[3,512,512]{2,1,0:T(8,128)(2,1)} %get-tuple-element.267.refs_0_.refs_7_, bf16[3,512,512]{2,1,0:T(8,128)(2,1)} %get-tuple-element.268.refs_1_.refs_3_, bf16[1024,4096]{1,0:T(8,128)(2,1)} %bitcast.68, ...), custom_call_target="tpu_custom_call" | custom-call | flops 99999997952 | bytes 1 | tf_op jit(solution)/shard_map/project_back/pallas_call | solution.py:448
  276.7 14.3 %weight_grad.4 = (bf16[16,128,1024]{2,1,0:T(8,128)(2,1)}, bf16[16,128,1024]{2,1,0:T(8,128)(2,1)}) custom-call(s32[36]{0:T(128)} %pad_add_fusion.i_ref, bf16[512,4096]{1,0:T(8,128)(2,1)} %get-tuple-element.272.g_ref.refs_0_, bf16[512,4096]{1,0:T(8,128)(2,1)} %get-tuple-element.273.refs_1_, bf16[512,1024]{1,0:T(8,128)(2,1)} %get-tuple-element.274.refs_2_, ...), custom_call_target="tpu_custom_call" | custom-call | flops 1 | bytes 1 | tf_op jit(solution)/shard_map/weight_grad/pallas_call | solution.py:532
  291.2 7.2 %collective-permute-done.18 = bf16[16,128,1024]{2,1,0:T(8,128)(2,1)S(1)} collective-permute-done((bf16[16,128,1024]{2,1,0:T(8,128)(2,1)}, bf16[16,128,1024]{2,1,0:T(8,128)(2,1)S(1)}, u32[]{:S(2)}, u32[]{:S(2)}) %collective-permute-start.18) | collective-permute-done | bytes 4194336 | tf_op jit(solution)/shard_map/ppermute | solution.py:592
  298.5 4.5 add_convert_fusion.2
  303.6 20.2 %feed_forward_back.3 = (bf16[512,1024]{1,0:T(8,128)(2,1)}, bf16[512,4096]{1,0:T(8,128)(2,1)}, f32[512,1024]{1,0:T(8,128)}, bf16[512,1024]{1,0:T(8,128)(2,1)}, bf...) custom-call(f32[512,1024]{1,0:T(8,128)} %get-tuple-element.281.dy_re, ...), custom_call_target="tpu_custom_call" | custom-call | flops 99999997952 | bytes 1 | tf_op jit(solution)/shard_map/feed_forward_back/pallas_call | solution.py:356
  323.9 16.0 %weight_grad.5 = (bf16[16,32,4096]{2,1,0:T(8,128)(2,1)}, bf16[16,32,4096]{2,1,0:T(8,128)(2,1)}) custom-call(s32[36]{0:T(128)} %pad_add_fusion.i_ref, bf16[512,1024]{1,0:T(8,128)(2,1)} %get-tuple-element.279.a_ref.refs_0_, bf16[512,1024]{1,0:T(8,128)(2,1)} %get-tuple-element.280.a_ref.refs_1_, bf16[512,4096]{1,0:T(8,128)(2,1)} %get-tuple-element.283.refs_2_, ...), custom_call_target="tpu_custom_call" | custom-call | flops 1 | bytes 1 | tf_op jit(solution)/shard_map/weight_grad/pallas_call | solution.py:532
  340.0 3.5 add_convert_fusion.8
  344.7 8.9 %attention_back.6 = (bf16[3,512,512]{2,1,0:T(8,128)(2,1)}, f32[1,512]{1,0:T(1,128)}, f32[1,512]{1,0:T(1,128)}) custom-call(bf16[512,3072]{1,0:T(8,128)(2,1)} %get-tuple-element.225.q_ref.k_ref.v_ref, bf16[512,3072]{1,0:T(8,128)(2,1)} %get-tuple-element.225.q_ref.k_ref.v_ref, bf16[512,3072]{1,0:T(8,128)(2,1)} %get-tuple-element.225.q_ref.k_ref.v_ref, ...), custom_call_target="tpu_custom_call" | custom-call | flops 99999997952 | bytes 1 | tf_op jit(solution)/shard_map/attention_back/pallas_call | solution.py:145
  353.6 4.8 collective-permute-done.20
  359.9 5.2 %add_convert_fusion = (bf16[8,32,4096]{2,1,0:T(8,128)(2,1)}, bf16[8,32,4096]{2,1,0:T(8,128)(2,1)S(1)}) fusion(bf16[16,32,4096]{2,1,0:T(8,128)(2,1)} %collective-permute-done.21, bf16[16,32,4096]{2,1,0:T(8,128)(2,1)} %get-tuple-element.294), kind=kLoop, calls=%fused_computation.1 | loop fusion | flops 8388608 | bytes 12582912 | tf_op jit(solution)/shard_map/convert_element_type | solution.py:768
  367.5 13.7 %weight_grad.6 = (bf16[16,32,2560]{2,1,0:T(8,128)(2,1)}, bf16[16,32,2560]{2,1,0:T(8,128)(2,1)}) custom-call(s32[36]{0:T(128)} %pad_add_fusion.i_ref, bf16[512,1024]{1,0:T(8,128)(2,1)} %get-tuple-element.296.o_ref.refs_0_, bf16[512,1024]{1,0:T(8,128)(2,1)} %get-tuple-element.297.o_ref.refs_1_, bf16[512,1024]{1,0:T(8,128)(2,1)} %get-tuple-element.298.refs_2_, ...), custom_call_target="tpu_custom_call" | custom-call | flops 1 | bytes 1 | tf_op jit(solution)/shard_map/weight_grad/pallas_call | solution.py:532
  381.3 8.9 %attention_back.7 = (bf16[3,512,512]{2,1,0:T(8,128)(2,1)}, f32[1,512]{1,0:T(1,128)}, f32[1,512]{1,0:T(1,128)}) custom-call(bf16[512,3072]{1,0:T(8,128)(2,1)} %get-tuple-element.225.q_ref.k_ref.v_ref, bf16[512,3072]{1,0:T(8,128)(2,1)} %get-tuple-element.225.q_ref.k_ref.v_ref, bf16[512,3072]{1,0:T(8,128)(2,1)} %get-tuple-element.225.q_ref.k_ref.v_ref, ...), custom_call_target="tpu_custom_call" | custom-call | flops 1 | bytes 1 | tf_op jit(solution)/shard_map/attention_back/pallas_call | solution.py:145
  392.7 3.4 add_convert_fusion.6
  396.1 2.0 add_convert_fusion.23
  399.4 8.6 %weight_grad.7 = (bf16[16,32,1536]{2,1,0:T(8,128)(2,1)}, bf16[16,32,1536]{2,1,0:T(8,128)(2,1)}) custom-call(s32[36]{0:T(128)} %pad_add_fusion.i_ref, bf16[512,1024]{1,0:T(8,128)(2,1)} %get-tuple-element.310.refs_4_.refs_0_, bf16[512,1024]{1,0:T(8,128)(2,1)} %get-tuple-element.311.refs_5_.refs_1_, bf16[3,512,512]{2,1,0:T(8,128)(2,1)} %get-tuple-element.319.refs_2_.refs_1_, ...), custom_call_target="tpu_custom_call" | custom-call | flops 99999997952 | bytes 1 | tf_op jit(solution)/shard_map/weight_grad/pallas_call | solution.py:532
  408.3 2.7 collective-permute-start.29
  411.0 4.8 add_convert_fusion.4
  419.8 9.3 %project_back.3 = (bf16[512,1024]{1,0:T(8,128)(2,1)}, f32[1,1024]{1,0:T(1,128)}, f32[1,1024]{1,0:T(1,128)}) custom-call(bf16[3,512,512]{2,1,0:T(8,128)(2,1)} %get-tuple-element.318.refs_6_.refs_0_, bf16[3,512,512]{2,1,0:T(8,128)(2,1)} %get-tuple-element.319.refs_2_.refs_1_, bf16[1024,4096]{1,0:T(8,128)(2,1)} %bitcast.70, bf16[512,1024]{1,0:T(8,128)(2,1)} %bitcast.74, ...), custom_call_target="tpu_custom_call" | custom-call | flops 99999997952 | bytes 1 | tf_op jit(solution)/shard_map/project_back/pallas_call | solution.py:448
  429.1 2.5 pack_sums.1
  432.7 1.9 add_convert_fusion.10
  435.5 1.7 add_convert_fusion.12
  439.7 1.8 add_bitcast_fusion.1
  441.5 10.6 %collective-permute-done.30 = bf16[8,32,1536]{2,1,0:T(8,128)(2,1)S(1)} collective-permute-done((bf16[8,32,1536]{2,1,0:T(8,128)(2,1)S(1)}, bf16[8,32,1536]{2,1,0:T(8,128)(2,1)S(1)}, u32[]{:S(2)}, u32[]{:S(2)}) %collective-permute-start.30) | collective-permute-done | bytes 786464 | tf_op jit(solution)/shard_map/ppermute | solution.py:592
  456.1 4.7 collective-permute-done.34
  461.4 4.3 collective-permute-done.35
  466.7 2.8 collective-permute-done.37
  469.7 7.5 %collective-permute-done.38 = bf16[1,32,2560]{2,1,0:T(8,128)(2,1)S(1)} collective-permute-done((bf16[1,32,2560]{2,1,0:T(8,128)(2,1)S(1)}, bf16[1,32,2560]{2,1,0:T(8,128)(2,1)S(1)}, u32[]{:S(2)}, u32[]{:S(2)}) %collective-permute-start.38) | collective-permute-done | bytes 163872 | tf_op jit(solution)/shard_map/ppermute | solution.py:592
  478.9 2.9 collective-permute-done.41
  482.5 3.9 collective-permute-done.42
  (168 shorter events, 54.8 us)
Async XLA Ops:
  0.7 35.1 %copy-start.13 = (bf16[32,4096]{1,0:T(8,128)(2,1)S(1)}, bf16[32,4096]{1,0:T(8,128)(2,1)}, u32[]{:S(2)}) copy-start(bf16[32,4096]{1,0:T(8,128)(2,1)} %param.28) | copy-start | bytes 786436
  2.5 16.9 %collective-permute-start = (bf16[1,32,4352]{2,1,0:T(8,128)(2,1)}, bf16[1,32,4352]{2,1,0:T(8,128)(2,1)S(1)}, u32[]{:S(2)}, u32[]{:S(2)}) collective-permute-start(bf16[1,32,4352]{2,1,0:T(8,128)(2,1)} %bitcast.75), channel_id=1, source_target_pairs={{0,4},{1,5},{2,6},{3,7},{4,0},{5,1},{6,2},{7,3},{8,12},{9,13},{10,... | collective-permute-start | bytes 835592 | tf_op jit(solution)/shard_map/ppermute | solution.py:592
  20.4 13.9 %collective-permute-start.1 = (bf16[2,32,4352]{2,1,0:T(8,128)(2,1)S(1)}, bf16[2,32,4352]{2,1,0:T(8,128)(2,1)S(1)}, u32[]{:S(2)}, u32[]{:S(2)}) collective-permute-start(bf16[2,32,4352]{2,1,0:T(8,128)(2,1)S(1)} %pad_maximum_fusion), channel_id=1, source_target_pairs={{0,2},{1,3},{2,0},{3,1},{4,6},{5,7},{6,4},{7,5},{8,10},{9,11},{10,... | collective-permute-start | bytes 1671176 | tf_op jit(solution)/shard_map/ppermute | solution.py:592
  34.3 16.1 %collective-permute-start.3 = (bf16[4,32,4352]{2,1,0:T(8,128)(2,1)S(1)}, bf16[4,32,4352]{2,1,0:T(8,128)(2,1)S(1)}, u32[]{:S(2)}, u32[]{:S(2)}) collective-permute-start(bf16[4,32,4352]{2,1,0:T(8,128)(2,1)S(1)} %constant_dynamic-update-slice_fusion), channel_id=1, source_target_pairs={{0,1},{1,0},{2,3},{3,2},{4,5},{5,4},{6,7},{7,6},{8,24},{9,25},{10,... | collective-permute-start | bytes 3342344 | tf_op jit(solution)/shard_map/ppermute | solution.py:592
  35.8 14.6 %collective-permute-start.2 = (bf16[1,128,1024]{2,1,0:T(8,128)(2,1)S(1)}, bf16[1,128,1024]{2,1,0:T(8,128)(2,1)S(1)}, u32[]{:S(2)}, u32[]{:S(2)}) collective-permute-start(bf16[1,128,1024]{2,1,0:T(8,128)(2,1)S(1)} %bitcast.77), channel_id=1, source_target_pairs={{0,4},{1,5},{2,6},{3,7},{4,0},{5,1},{6,2},{7,3},{8,12},{9,13},{10,... | collective-permute-start | bytes 786440 | tf_op jit(solution)/shard_map/ppermute | solution.py:592
  50.4 6.0 %copy-start.8 = (bf16[2,128,1024]{2,1,0:T(8,128)(2,1)}, bf16[2,128,1024]{2,1,0:T(8,128)(2,1)S(1)}, u32[]{:S(2)}) copy-start(bf16[2,128,1024]{2,1,0:T(8,128)(2,1)S(1)} %constant_dynamic-update-slice_fusion.2) | copy-start | bytes 1572868
  51.7 19.3 %copy-start.14 = (bf16[128,1024]{1,0:T(8,128)(2,1)S(1)}, bf16[128,1024]{1,0:T(8,128)(2,1)}, u32[]{:S(2)}) copy-start(bf16[128,1024]{1,0:T(8,128)(2,1)} %param.30) | copy-start | bytes 786436
  52.7 20.7 %collective-permute-start.5 = (bf16[8,32,4352]{2,1,0:T(8,128)(2,1)}, bf16[8,32,4352]{2,1,0:T(8,128)(2,1)}, u32[]{:S(2)}, u32[]{:S(2)}) collective-permute-start(bf16[8,32,4352]{2,1,0:T(8,128)(2,1)} %constant_dynamic-update-slice_fusion.4.refs_0_), channel_id=1, source_target_pairs={{0,8},{1,9},{2,10},{3,11},{4,12},{5,13},{6,14},{7,15},{8,0},{9,1},... | collective-permute-start | bytes 6684680 | tf_op jit(solution)/shard_map/ppermute | solution.py:592
  52.7 14.4 %collective-permute-start.4 = (bf16[2,128,1024]{2,1,0:T(8,128)(2,1)S(1)}, bf16[2,128,1024]{2,1,0:T(8,128)(2,1)}, u32[]{:S(2)}, u32[]{:S(2)}) collective-permute-start(bf16[2,128,1024]{2,1,0:T(8,128)(2,1)S(1)} %constant_dynamic-update-slice_fusion.2), channel_id=1, source_target_pairs={{0,2},{1,3},{2,0},{3,1},{4,6},{5,7},{6,4},{7,5},{8,10},{9,11},{10,... | collective-permute-start | bytes 1572872 | tf_op jit(solution)/shard_map/ppermute | solution.py:592
  55.0 41.6 %collective-permute-start.8 = (bf16[8,32,4352]{2,1,0:T(8,128)(2,1)}, bf16[8,32,4352]{2,1,0:T(8,128)(2,1)S(1)}, u32[]{:S(2)}, u32[]{:S(2)}) collective-permute-start(bf16[8,32,4352]{2,1,0:T(8,128)(2,1)} %constant_dynamic-update-slice_fusion.4.refs_0_), channel_id=1, source_target_pairs={{0,16},{1,17},{2,18},{3,19},{4,20},{5,21},{6,22},{7,23},{8,9},{9,8... | collective-permute-start | bytes 6684680 | tf_op jit(solution)/shard_map/ppermute | solution.py:592
  69.3 23.9 %collective-permute-start.7 = (bf16[4,128,1024]{2,1,0:T(8,128)(2,1)S(1)}, bf16[4,128,1024]{2,1,0:T(8,128)(2,1)}, u32[]{:S(2)}, u32[]{:S(2)}) collective-permute-start(bf16[4,128,1024]{2,1,0:T(8,128)(2,1)S(1)} %constant_dynamic-update-slice_fusion.6), channel_id=1, source_target_pairs={{0,1},{1,0},{2,3},{3,2},{4,5},{5,4},{6,7},{7,6},{8,24},{9,25},{10,... | collective-permute-start | bytes 3145736 | tf_op jit(solution)/shard_map/ppermute | solution.py:592
  70.9 14.1 %collective-permute-start.6 = (bf16[1,128,1024]{2,1,0:T(8,128)(2,1)S(1)}, bf16[1,128,1024]{2,1,0:T(8,128)(2,1)}, u32[]{:S(2)}, u32[]{:S(2)}) collective-permute-start(bf16[1,128,1024]{2,1,0:T(8,128)(2,1)S(1)} %bitcast.80), channel_id=1, source_target_pairs={{0,4},{1,5},{2,6},{3,7},{4,0},{5,1},{6,2},{7,3},{8,12},{9,13},{10,... | collective-permute-start | bytes 786440 | tf_op jit(solution)/shard_map/ppermute | solution.py:592
  96.5 4.7 copy-start.1
  96.5 4.7 collective-permute-start.9
  97.1 33.7 %collective-permute-start.13 = (bf16[8,128,1024]{2,1,0:T(8,128)(2,1)}, bf16[8,128,1024]{2,1,0:T(8,128)(2,1)}, u32[]{:S(2)}, u32[]{:S(2)}) collective-permute-start(bf16[8,128,1024]{2,1,0:T(8,128)(2,1)} %constant_dynamic-update-slice_fusion.10.refs_0_), channel_id=1, source_target_pairs={{0,16},{1,17},{2,18},{3,19},{4,20},{5,21},{6,22},{7,23},{8,9},{9,8... | collective-permute-start | bytes 6291464 | tf_op jit(solution)/shard_map/ppermute | solution.py:592
  98.4 17.8 %collective-permute-start.10 = (bf16[2,128,1024]{2,1,0:T(8,128)(2,1)}, bf16[2,128,1024]{2,1,0:T(8,128)(2,1)}, u32[]{:S(2)}, u32[]{:S(2)}) collective-permute-start(bf16[2,128,1024]{2,1,0:T(8,128)(2,1)} %constant_dynamic-update-slice_fusion.8), channel_id=1, source_target_pairs={{0,2},{1,3},{2,0},{3,1},{4,6},{5,7},{6,4},{7,5},{8,10},{9,11},{10,... | collective-permute-start | bytes 1572872 | tf_op jit(solution)/shard_map/ppermute | solution.py:592
  118.4 17.9 %collective-permute-start.11 = (bf16[4,128,1024]{2,1,0:T(8,128)(2,1)S(1)}, bf16[4,128,1024]{2,1,0:T(8,128)(2,1)S(1)}, u32[]{:S(2)}, u32[]{:S(2)}) collective-permute-start(bf16[4,128,1024]{2,1,0:T(8,128)(2,1)S(1)} %constant_dynamic-update-slice_fusion.12), channel_id=1, source_target_pairs={{0,1},{1,0},{2,3},{3,2},{4,5},{5,4},{6,7},{7,6},{8,24},{9,25},{10,... | collective-permute-start | bytes 3145736 | tf_op jit(solution)/shard_map/ppermute | solution.py:592
  120.0 20.0 %collective-permute-start.12 = (bf16[8,128,1024]{2,1,0:T(8,128)(2,1)}, bf16[8,128,1024]{2,1,0:T(8,128)(2,1)}, u32[]{:S(2)}, u32[]{:S(2)}) collective-permute-start(bf16[8,128,1024]{2,1,0:T(8,128)(2,1)} %constant_dynamic-update-slice_fusion.10.refs_0_), channel_id=1, source_target_pairs={{0,8},{1,9},{2,10},{3,11},{4,12},{5,13},{6,14},{7,15},{8,0},{9,1},... | collective-permute-start | bytes 6291464 | tf_op jit(solution)/shard_map/ppermute | solution.py:592
  130.8 13.7 %collective-permute-start.14 = (bf16[8,128,1024]{2,1,0:T(8,128)(2,1)}, bf16[8,128,1024]{2,1,0:T(8,128)(2,1)}, u32[]{:S(2)}, u32[]{:S(2)}) collective-permute-start(bf16[8,128,1024]{2,1,0:T(8,128)(2,1)} %collective-permute-done.13.refs_0_), channel_id=1, source_target_pairs={{0,8},{1,9},{2,10},{3,11},{4,12},{5,13},{6,14},{7,15},{8,0},{9,1},... | collective-permute-start | bytes 6291464 | tf_op jit(solution)/shard_map/ppermute | solution.py:592
  138.5 6.0 %copy-start.3 = (bf16[8,128,1024]{2,1,0:T(8,128)(2,1)}, bf16[8,128,1024]{2,1,0:T(8,128)(2,1)S(1)}, u32[]{:S(2)}) copy-start(bf16[8,128,1024]{2,1,0:T(8,128)(2,1)S(1)} %constant_dynamic-update-slice_fusion.14.refs_0_) | copy-start | bytes 6291460
  138.6 22.1 %collective-permute-start.15 = (bf16[8,128,1024]{2,1,0:T(8,128)(2,1)S(1)}, bf16[8,128,1024]{2,1,0:T(8,128)(2,1)}, u32[]{:S(2)}, u32[]{:S(2)}) collective-permute-start(bf16[8,128,1024]{2,1,0:T(8,128)(2,1)S(1)} %constant_dynamic-update-slice_fusion.14.refs_0_), channel_id=1, source_target_pairs={{0,8},{1,9},{2,10},{3,11},{4,12},{5,13},{6,14},{7,15},{8,0},{9,1},... | collective-permute-start | bytes 6291464 | tf_op jit(solution)/shard_map/ppermute | solution.py:592
  138.7 26.7 %collective-permute-start.16 = (bf16[8,128,1024]{2,1,0:T(8,128)(2,1)S(1)}, bf16[8,128,1024]{2,1,0:T(8,128)(2,1)}, u32[]{:S(2)}, u32[]{:S(2)}) collective-permute-start(bf16[8,128,1024]{2,1,0:T(8,128)(2,1)S(1)} %constant_dynamic-update-slice_fusion.14.refs_0_), channel_id=1, source_target_pairs={{0,16},{1,17},{2,18},{3,19},{4,20},{5,21},{6,22},{7,23},{8,9},{9,8... | collective-permute-start | bytes 6291464 | tf_op jit(solution)/shard_map/ppermute | solution.py:592
  160.6 5.1 %copy-start = (s32[32]{0:T(128)S(1)}, s32[32]{0:T(128)}, u32[]{:S(2)}) copy-start(s32[32]{0:T(128)} %get-tuple-element.431.i_ref) | copy-start | bytes 388
  160.6 6.4 %copy-start.16 = (s32[1,512]{1,0:T(1,128)S(1)}, s32[1,512]{1,0:T(1,128)}, u32[]{:S(2)}) copy-start(s32[1,512]{1,0:T(1,128)} %param.34) | copy-start | bytes 6148
  160.6 6.4 %copy-start.11 = (bf16[1,512,1024]{2,1,0:T(8,128)(2,1)S(1)}, bf16[1,512,1024]{2,1,0:T(8,128)(2,1)}, u32[]{:S(2)}) copy-start(bf16[1,512,1024]{2,1,0:T(8,128)(2,1)} %param.33) | copy-start | bytes 3145732
  165.3 4.4 collective-permute-start.17
  169.8 1.3 copy-start.4
  291.0 7.4 %collective-permute-start.18 = (bf16[16,128,1024]{2,1,0:T(8,128)(2,1)}, bf16[16,128,1024]{2,1,0:T(8,128)(2,1)S(1)}, u32[]{:S(2)}, u32[]{:S(2)}) collective-permute-start(bf16[16,128,1024]{2,1,0:T(8,128)(2,1)} %get-tuple-element.276), channel_id=1, source_target_pairs={{0,8},{1,9},{2,10},{3,11},{4,12},{5,13},{6,14},{7,15},{8,0},{9,1},... | collective-permute-start | bytes 12582920 | tf_op jit(solution)/shard_map/ppermute | solution.py:592
  303.0 37.0 %collective-permute-start.19 = (bf16[8,128,1024]{2,1,0:T(8,128)(2,1)}, bf16[8,128,1024]{2,1,0:T(8,128)(2,1)}, u32[]{:S(2)}, u32[]{:S(2)}) collective-permute-start(bf16[8,128,1024]{2,1,0:T(8,128)(2,1)} %get-tuple-element.381), channel_id=1, source_target_pairs={{0,16},{1,17},{2,18},{3,19},{4,20},{5,21},{6,22},{7,23},{8,9},{9,8... | collective-permute-start | bytes 6291464 | tf_op jit(solution)/shard_map/ppermute | solution.py:592
  339.9 20.0 %collective-permute-start.21 = (bf16[16,32,4096]{2,1,0:T(8,128)(2,1)}, bf16[16,32,4096]{2,1,0:T(8,128)(2,1)}, u32[]{:S(2)}, u32[]{:S(2)}) collective-permute-start(bf16[16,32,4096]{2,1,0:T(8,128)(2,1)} %get-tuple-element.285), channel_id=1, source_target_pairs={{0,8},{1,9},{2,10},{3,11},{4,12},{5,13},{6,14},{7,15},{8,0},{9,1},... | collective-permute-start | bytes 12582920 | tf_op jit(solution)/shard_map/ppermute | solution.py:592
  343.4 15.0 %collective-permute-start.20 = (bf16[4,128,1024]{2,1,0:T(8,128)(2,1)}, bf16[4,128,1024]{2,1,0:T(8,128)(2,1)S(1)}, u32[]{:S(2)}, u32[]{:S(2)}) collective-permute-start(bf16[4,128,1024]{2,1,0:T(8,128)(2,1)} %get-tuple-element.387), channel_id=1, source_target_pairs={{0,1},{1,0},{2,3},{3,2},{4,5},{5,4},{6,7},{7,6},{8,24},{9,25},{10,... | collective-permute-start | bytes 3145736 | tf_op jit(solution)/shard_map/ppermute | solution.py:592
  359.8 6.5 %copy-start.19 = (f32[1,512]{1,0:T(1,128)S(1)}, f32[1,512]{1,0:T(1,128)}, u32[]{:S(2)}) copy-start(f32[1,512]{1,0:T(1,128)} %get-tuple-element.343) | copy-start | bytes 6148
  359.8 6.5 %copy-start.20 = (f32[1,512]{1,0:T(1,128)S(1)}, f32[1,512]{1,0:T(1,128)}, u32[]{:S(2)}) copy-start(f32[1,512]{1,0:T(1,128)} %get-tuple-element.347) | copy-start | bytes 6148
  359.8 6.5 %copy-start.21 = (f32[1,512]{1,0:T(1,128)S(1)}, f32[1,512]{1,0:T(1,128)}, u32[]{:S(2)}) copy-start(f32[1,512]{1,0:T(1,128)} %get-tuple-element.344) | copy-start | bytes 6148
  359.8 6.5 %copy-start.22 = (f32[1,512]{1,0:T(1,128)S(1)}, f32[1,512]{1,0:T(1,128)}, u32[]{:S(2)}) copy-start(f32[1,512]{1,0:T(1,128)} %get-tuple-element.348) | copy-start | bytes 6148
  365.0 27.7 %collective-permute-start.22 = (bf16[8,32,4096]{2,1,0:T(8,128)(2,1)}, bf16[8,32,4096]{2,1,0:T(8,128)(2,1)}, u32[]{:S(2)}, u32[]{:S(2)}) collective-permute-start(bf16[8,32,4096]{2,1,0:T(8,128)(2,1)} %get-tuple-element.379), channel_id=1, source_target_pairs={{0,16},{1,17},{2,18},{3,19},{4,20},{5,21},{6,22},{7,23},{8,9},{9,8... | collective-permute-start | bytes 6291464 | tf_op jit(solution)/shard_map/ppermute | solution.py:592
  366.9 29.2 %collective-permute-start.23 = (bf16[2,128,1024]{2,1,0:T(8,128)(2,1)}, bf16[2,128,1024]{2,1,0:T(8,128)(2,1)}, u32[]{:S(2)}, u32[]{:S(2)}) collective-permute-start(bf16[2,128,1024]{2,1,0:T(8,128)(2,1)} %get-tuple-element.395), channel_id=1, source_target_pairs={{0,2},{1,3},{2,0},{3,1},{4,6},{5,7},{6,4},{7,5},{8,10},{9,11},{10,... | collective-permute-start | bytes 1572872 | tf_op jit(solution)/shard_map/ppermute | solution.py:592
  381.2 9.0 %copy-start.18 = (f32[1,512]{1,0:T(1,128)S(1)}, f32[1,512]{1,0:T(1,128)}, u32[]{:S(2)}) copy-start(f32[1,512]{1,0:T(1,128)} %get-tuple-element.341) | copy-start | bytes 6148
  381.2 10.3 %copy-start.17 = (f32[1,512]{1,0:T(1,128)S(1)}, f32[1,512]{1,0:T(1,128)}, u32[]{:S(2)}) copy-start(f32[1,512]{1,0:T(1,128)} %get-tuple-element.345) | copy-start | bytes 6148
  381.2 29.8 %collective-permute-start.24 = (bf16[16,32,2560]{2,1,0:T(8,128)(2,1)}, bf16[16,32,2560]{2,1,0:T(8,128)(2,1)}, u32[]{:S(2)}, u32[]{:S(2)}) collective-permute-start(bf16[16,32,2560]{2,1,0:T(8,128)(2,1)} %get-tuple-element.303), channel_id=1, source_target_pairs={{0,8},{1,9},{2,10},{3,11},{4,12},{5,13},{6,14},{7,15},{8,0},{9,1},... | collective-permute-start | bytes 7864328 | tf_op jit(solution)/shard_map/ppermute | solution.py:592
  392.7 3.4 copy-start.6
  398.2 18.8 %collective-permute-start.25 = (bf16[4,32,4096]{2,1,0:T(8,128)(2,1)}, bf16[4,32,4096]{2,1,0:T(8,128)(2,1)S(1)}, u32[]{:S(2)}, u32[]{:S(2)}) collective-permute-start(bf16[4,32,4096]{2,1,0:T(8,128)(2,1)} %get-tuple-element.385), channel_id=1, source_target_pairs={{0,1},{1,0},{2,3},{3,2},{4,5},{5,4},{6,7},{7,6},{8,24},{9,25},{10,... | collective-permute-start | bytes 3145736 | tf_op jit(solution)/shard_map/ppermute | solution.py:592
  408.0 24.7 %collective-permute-start.26 = (bf16[16,32,1536]{2,1,0:T(8,128)(2,1)}, bf16[16,32,1536]{2,1,0:T(8,128)(2,1)}, u32[]{:S(2)}, u32[]{:S(2)}) collective-permute-start(bf16[16,32,1536]{2,1,0:T(8,128)(2,1)} %get-tuple-element.312), channel_id=1, source_target_pairs={{0,8},{1,9},{2,10},{3,11},{4,12},{5,13},{6,14},{7,15},{8,0},{9,1},... | collective-permute-start | bytes 4718600 | tf_op jit(solution)/shard_map/ppermute | solution.py:592
  408.3 30.1 %collective-permute-start.29 = (bf16[1,128,1024]{2,1,0:T(8,128)(2,1)}, bf16[1,128,1024]{2,1,0:T(8,128)(2,1)}, u32[]{:S(2)}, u32[]{:S(2)}) collective-permute-start(bf16[1,128,1024]{2,1,0:T(8,128)(2,1)} %get-tuple-element.403), channel_id=1, source_target_pairs={{0,4},{1,5},{2,6},{3,7},{4,0},{5,1},{6,2},{7,3},{8,12},{9,13},{10,... | collective-permute-start | bytes 786440 | tf_op jit(solution)/shard_map/ppermute | solution.py:592
  415.7 19.7 %collective-permute-start.27 = (bf16[8,32,2560]{2,1,0:T(8,128)(2,1)}, bf16[8,32,2560]{2,1,0:T(8,128)(2,1)}, u32[]{:S(2)}, u32[]{:S(2)}) collective-permute-start(bf16[8,32,2560]{2,1,0:T(8,128)(2,1)} %get-tuple-element.383), channel_id=1, source_target_pairs={{0,16},{1,17},{2,18},{3,19},{4,20},{5,21},{6,22},{7,23},{8,9},{9,8... | collective-permute-start | bytes 3932168 | tf_op jit(solution)/shard_map/ppermute | solution.py:592
  418.2 19.0 %collective-permute-start.28 = (bf16[2,32,4096]{2,1,0:T(8,128)(2,1)}, bf16[2,32,4096]{2,1,0:T(8,128)(2,1)}, u32[]{:S(2)}, u32[]{:S(2)}) collective-permute-start(bf16[2,32,4096]{2,1,0:T(8,128)(2,1)} %get-tuple-element.393), channel_id=1, source_target_pairs={{0,2},{1,3},{2,0},{3,1},{4,6},{5,7},{6,4},{7,5},{8,10},{9,11},{10,... | collective-permute-start | bytes 1572872 | tf_op jit(solution)/shard_map/ppermute | solution.py:592
  429.1 3.6 copy-start.7
  432.6 22.6 %collective-permute-start.33 = (f32[16,9,128]{2,1,0:T(8,128)S(1)}, f32[16,9,128]{2,1,0:T(8,128)S(1)}, u32[]{:S(2)}, u32[]{:S(2)}) collective-permute-start(f32[16,9,128]{2,1,0:T(8,128)S(1)} %get-tuple-element.413), channel_id=1, source_target_pairs={{0,8},{1,9},{2,10},{3,11},{4,12},{5,13},{6,14},{7,15},{8,0},{9,1},... | collective-permute-start | bytes 221192 | tf_op jit(solution)/shard_map/ppermute | solution.py:592
  432.7 2.8 copy-start.2
  434.6 2.5 copy-start.5
  434.6 17.5 %collective-permute-start.30 = (bf16[8,32,1536]{2,1,0:T(8,128)(2,1)S(1)}, bf16[8,32,1536]{2,1,0:T(8,128)(2,1)S(1)}, u32[]{:S(2)}, u32[]{:S(2)}) collective-permute-start(bf16[8,32,1536]{2,1,0:T(8,128)(2,1)S(1)} %get-tuple-element.389), channel_id=1, source_target_pairs={{0,16},{1,17},{2,18},{3,19},{4,20},{5,21},{6,22},{7,23},{8,9},{9,8... | collective-permute-start | bytes 2359304 | tf_op jit(solution)/shard_map/ppermute | solution.py:592
  435.5 4.2 copy-start.12
  438.4 14.9 %collective-permute-start.31 = (bf16[4,32,2560]{2,1,0:T(8,128)(2,1)S(1)}, bf16[4,32,2560]{2,1,0:T(8,128)(2,1)S(1)}, u32[]{:S(2)}, u32[]{:S(2)}) collective-permute-start(bf16[4,32,2560]{2,1,0:T(8,128)(2,1)S(1)} %get-tuple-element.391), channel_id=1, source_target_pairs={{0,1},{1,0},{2,3},{3,2},{4,5},{5,4},{6,7},{7,6},{8,24},{9,25},{10,... | collective-permute-start | bytes 1966088 | tf_op jit(solution)/shard_map/ppermute | solution.py:592
  439.7 14.6 %collective-permute-start.32 = (bf16[1,32,4096]{2,1,0:T(8,128)(2,1)S(1)}, bf16[1,32,4096]{2,1,0:T(8,128)(2,1)S(1)}, u32[]{:S(2)}, u32[]{:S(2)}) collective-permute-start(bf16[1,32,4096]{2,1,0:T(8,128)(2,1)S(1)} %get-tuple-element.401), channel_id=1, source_target_pairs={{0,4},{1,5},{2,6},{3,7},{4,0},{5,1},{6,2},{7,3},{8,12},{9,13},{10,... | collective-permute-start | bytes 786440 | tf_op jit(solution)/shard_map/ppermute | solution.py:592
  452.3 8.5 %collective-permute-start.34 = (bf16[4,32,1536]{2,1,0:T(8,128)(2,1)S(1)}, bf16[4,32,1536]{2,1,0:T(8,128)(2,1)S(1)}, u32[]{:S(2)}, u32[]{:S(2)}) collective-permute-start(bf16[4,32,1536]{2,1,0:T(8,128)(2,1)S(1)} %get-tuple-element.397), channel_id=1, source_target_pairs={{0,1},{1,0},{2,3},{3,2},{4,5},{5,4},{6,7},{7,6},{8,24},{9,25},{10,... | collective-permute-start | bytes 1179656 | tf_op jit(solution)/shard_map/ppermute | solution.py:592
  455.2 10.6 %collective-permute-start.35 = (bf16[2,32,2560]{2,1,0:T(8,128)(2,1)S(1)}, bf16[2,32,2560]{2,1,0:T(8,128)(2,1)S(1)}, u32[]{:S(2)}, u32[]{:S(2)}) collective-permute-start(bf16[2,32,2560]{2,1,0:T(8,128)(2,1)S(1)} %get-tuple-element.399), channel_id=1, source_target_pairs={{0,2},{1,3},{2,0},{3,1},{4,6},{5,7},{6,4},{7,5},{8,10},{9,11},{10,... | collective-permute-start | bytes 983048 | tf_op jit(solution)/shard_map/ppermute | solution.py:592
  455.2 10.6 %collective-permute-start.36 = (f32[8,9,128]{2,1,0:T(8,128)S(1)}, f32[8,9,128]{2,1,0:T(8,128)S(1)}, u32[]{:S(2)}, u32[]{:S(2)}) collective-permute-start(f32[8,9,128]{2,1,0:T(8,128)S(1)} %get-tuple-element.411), channel_id=1, source_target_pairs={{0,16},{1,17},{2,18},{3,19},{4,20},{5,21},{6,22},{7,23},{8,9},{9,8... | collective-permute-start | bytes 110600 | tf_op jit(solution)/shard_map/ppermute | solution.py:592
  460.9 8.6 %collective-permute-start.37 = (bf16[2,32,1536]{2,1,0:T(8,128)(2,1)S(1)}, bf16[2,32,1536]{2,1,0:T(8,128)(2,1)S(1)}, u32[]{:S(2)}, u32[]{:S(2)}) collective-permute-start(bf16[2,32,1536]{2,1,0:T(8,128)(2,1)S(1)} %get-tuple-element.405), channel_id=1, source_target_pairs={{0,2},{1,3},{2,0},{3,1},{4,6},{5,7},{6,4},{7,5},{8,10},{9,11},{10,... | collective-permute-start | bytes 589832 | tf_op jit(solution)/shard_map/ppermute | solution.py:592
  465.8 11.5 %collective-permute-start.38 = (bf16[1,32,2560]{2,1,0:T(8,128)(2,1)S(1)}, bf16[1,32,2560]{2,1,0:T(8,128)(2,1)S(1)}, u32[]{:S(2)}, u32[]{:S(2)}) collective-permute-start(bf16[1,32,2560]{2,1,0:T(8,128)(2,1)S(1)} %get-tuple-element.407), channel_id=1, source_target_pairs={{0,4},{1,5},{2,6},{3,7},{4,0},{5,1},{6,2},{7,3},{8,12},{9,13},{10,... | collective-permute-start | bytes 491528 | tf_op jit(solution)/shard_map/ppermute | solution.py:592
  465.9 11.4 %collective-permute-start.39 = (f32[4,9,128]{2,1,0:T(8,128)S(1)}, f32[4,9,128]{2,1,0:T(8,128)S(1)}, u32[]{:S(2)}, u32[]{:S(2)}) collective-permute-start(f32[4,9,128]{2,1,0:T(8,128)S(1)} %get-tuple-element.415), channel_id=1, source_target_pairs={{0,1},{1,0},{2,3},{3,2},{4,5},{5,4},{6,7},{7,6},{8,24},{9,25},{10,... | collective-permute-start | bytes 55304 | tf_op jit(solution)/shard_map/ppermute | solution.py:592
  469.5 9.3 %collective-permute-start.40 = (bf16[1,32,1536]{2,1,0:T(8,128)(2,1)S(1)}, bf16[1,32,1536]{2,1,0:T(8,128)(2,1)S(1)}, u32[]{:S(2)}, u32[]{:S(2)}) collective-permute-start(bf16[1,32,1536]{2,1,0:T(8,128)(2,1)S(1)} %get-tuple-element.409), channel_id=1, source_target_pairs={{0,4},{1,5},{2,6},{3,7},{4,0},{5,1},{6,2},{7,3},{8,12},{9,13},{10,... | collective-permute-start | bytes 294920 | tf_op jit(solution)/shard_map/ppermute | solution.py:592
  478.0 3.7 collective-permute-start.41
  481.8 4.5 collective-permute-start.42
  482.4 4.9 %copy-start.15 = (f32[32,3072]{1,0:T(8,128)}, f32[32,3072]{1,0:T(8,128)S(1)}, u32[]{:S(2)}) copy-start(f32[32,3072]{1,0:T(8,128)S(1)} %slice_dynamic-update-slice_fusion) | copy-start | bytes 1179652
  (2 other events, 2.2 us)

commit v8 on v7

--- a/solution.py
+++ b/solution.py
@@ -456,7 +456,6 @@
             jax.ShapeDtypeStruct((1, width), jnp.float32),
         ],
         name="project_back",
-        cover=True,
     )(*args)
 
 
@@ -547,6 +546,53 @@
     )(index, *args)
 
 
+def weight_grad_half(lefts, rights, index, blocks):
+    ndp, nfs, r = blocks
+    steps = ndp // 2
+    rows = lefts[0].shape[0]
+    cols = rights[0].shape[1]
+    count = len(lefts)
+
+    def body(i_ref, *refs):
+        a, b = refs[:count], refs[count : 2 * count]
+        out, buf, sem = refs[2 * count :]
+        i = pl.program_id(0)
+
+        def copies(step, start):
+            for f in range(nfs):
+                where = out.at[i_ref[steps + step * nfs + f]]
+                copy = pltpu.make_async_copy(buf.at[step, f], where, sem.at[step, f])
+                copy.start() if start else copy.wait()
+
+        total = dot(a[0][...], b[0][...], TN)
+        for x, y in zip(a[1:], b[1:]):
+            total += dot(x[...], y[...], TN)
+        buf[i] = total.astype(jnp.bfloat16).reshape(nfs, r, cols)
+        copies(i, True)
+
+        @pl.when(i == steps - 1)
+        def _():
+            for step in range(steps):
+                copies(step, False)
+
+    return call(
+        body,
+        grid_spec=pltpu.PrefetchScalarGridSpec(
+            num_scalar_prefetch=1,
+            grid=(steps,),
+            in_specs=[pl.BlockSpec((rows, nfs * r), lambda i, i_ref: (0, i_ref[i]))] * count
+            + [whole((rows, cols))] * count,
+            out_specs=pl.BlockSpec(memory_space=pl.ANY),
+            scratch_shapes=[
+                pltpu.VMEM((steps, nfs, r, cols), jnp.bfloat16),
+                pltpu.SemaphoreType.DMA((steps, nfs)),
+            ],
+        ),
+        out_shape=jax.ShapeDtypeStruct((steps * nfs, r, cols), jnp.bfloat16),
+        name="weight_grad_half",
+    )(index, *lefts, *rights)
+
+
 def bits_of(ndp, nfs):
     core = nfs
     outer = [nfs << i for i in range(1, ndp.bit_length() - 1)]
@@ -594,15 +640,13 @@
 
 class Line:
     def __init__(self):
-        self.last = None
+        self.last = ()
 
     def after(self, *arrays):
-        if self.last is not None:
-            arrays = lax.optimization_barrier((self.last,) + arrays)[1:]
-        return arrays
-
-    def mark(self, array):
-        self.last = array
+        return lax.optimization_barrier(self.last + arrays)[len(self.last) :]
+
+    def mark(self, *arrays):
+        self.last = arrays
 
 
 def place_shards(pieces, table_row, shape, rows_at, rows, into=None, cover=False):
@@ -721,33 +765,34 @@
 
 
 def pack_sums(parts, inverse_row, n, rows):
-    flat = [a for group in parts for a in group]
+    flat_parts = [a for pieces in parts for group in pieces for a in group]
 
     def body(i_ref, *refs):
         out = refs[-1]
         out[...] = jnp.zeros_like(out)
         at = 0
-        for r, group in enumerate(parts):
-            total = refs[at][...]
-            for k in range(1, len(group)):
-                total += refs[at + k][...]
-            at += len(group)
-            k = total.shape[1] // n
-            for d in range(n):
-                out[i_ref[d], r : r + 1, 0:k] = total[:, d * k : (d + 1) * k]
+        for r, pieces in enumerate(parts):
+            per = n // len(pieces)
+            for piece, group in enumerate(pieces):
+                total = refs[at][...]
+                for k in range(1, len(group)):
+                    total += refs[at + k][...]
+                at += len(group)
+                k = total.shape[1] // per
+                for d in range(per):
+                    out[i_ref[piece * per + d], r : r + 1, 0:k] = total[:, d * k : (d + 1) * k]
 
     return call(
         body,
         grid_spec=pltpu.PrefetchScalarGridSpec(
             num_scalar_prefetch=1,
             grid=(1,),
-            in_specs=[whole(a.shape) for a in flat],
+            in_specs=[whole(a.shape) for a in flat_parts],
             out_specs=whole((n, rows, 128)),
         ),
         out_shape=jax.ShapeDtypeStruct((n, rows, 128), jnp.float32),
         name="pack_sums",
-        cover=True,
-    )(inverse_row, *flat)
+    )(inverse_row, *flat_parts)
 
 
 class Reduction:
@@ -768,7 +813,7 @@
         sent = add(slice(half, None)).astype(wide)
         self.got = send(sent, self.perms[self.stage])
         self.kept = add(slice(0, half)).astype(wide)
-        line.mark(self.kept)
+        line.mark(sent, self.kept)
 
 
 def per_device(ndp, nfs,
@@ -956,8 +1001,18 @@
         line.mark(sent)
         return Reduction(perms, kept, sent, 0)
 
+    def grads_split(r, lefts, rights):
+        lefts = line.after(*lefts)
+        parts_at = index[:ndp].reshape(2, -1), index[ndp:].reshape(2, -1)
+        made = []
+        for k in range(2):
+            at = jnp.concatenate([parts_at[0][k], parts_at[1][k]])
+            made.append(weight_grad_half(line.after(*lefts), rights, at, (ndp, nfs, r)))
+            line.mark(made[k])
+        return Reduction(perms, made[1], made[0], 0)
+
     sg = list(zip(saved_first, saved_second))
-    red_down = grads(r_ff, (sg[7], (dm1, dm2)))
+    red_down = grads_split(r_ff, sg[7], (dm1, dm2))
     _, du1, dx1, da1, do1, cdm1, cdu1, cda1, cg21, cs21 = ff_back(grad_first, saved_first)
     red_down.step(line)
     red_up = grads(r_in, (sg[6], (du1, du2)))
@@ -973,42 +1028,37 @@
     red_two = grads(r_in, (sg[1], rights(1)), cover=True)
     red_one.step(line)
     red_up.step(line)
+    red_two.step(line)
     grad_inputs, cg11, cs11 = qkv_back(heads1, saved_first, dx1, None, (jnp.bfloat16,))
-    red_two.step(line)
-    red_one.step(line)
-    red_up.step(line)
-    red_down.step(line)
-    cq = [[h[i][1] for h in (heads1, heads2)] for i in range(parts)]
-    cv = [[h[i][2] for h in (heads1, heads2)] for i in range(parts)]
-    joined = lambda c: [jnp.concatenate([c[i][s] for i in range(parts)], axis=1) for s in range(2)]
+    halves = lambda k: [[h[i][k] for h in (heads1, heads2)] for i in range(parts)]
+    cg11 = line.after(cg11)[0]
     sums = pack_sums(
         [
-            [cg11, cg12],
-            [cs11, cs12],
-            joined(cq),
-            joined(cv),
-            [cda1, cda2],
-            [cg21, cg22],
-            [cs21, cs22],
-            [cdm1, cdm2],
-            [cdu1, cdu2],
+            [[cg11, cg12]],
+            [[cs11, cs12]],
+            halves(1),
+            halves(2),
+            [[cda1, cda2]],
+            [[cg21, cg22]],
+            [[cs21, cs22]],
+            [[cdm1, cdm2]],
+            [[cdu1, cdu2]],
         ],
         inverse_row,
         n,
         len(vectors),
     )
+    line.mark(sums)
     red_small = Reduction(perms, sums[:half], sums[half:], 0)
-    for _ in range(stages):
-        for red in (red_two, red_one, red_up, red_down):
-            if red.done is None:
-                red.step(line)
-        if red_small.done is None:
-            red_small.step(line, jnp.float32)
-    for red in (red_down, red_up, red_one, red_two):
-        while red.done is None:
+    red_one.step(line)
+    red_up.step(line)
+    todo = [red_two, red_one, red_up, red_down]
+    while todo:
+        for red in todo:
             red.step(line)
-    while red_small.done is None:
-        red_small.step(line, jnp.float32)
+            if red_small.done is None and red not in (red_up, red_down):
+                red_small.step(line, jnp.float32)
+        todo = [red for red in todo if red.done is None]
     outs = [red_small.done[i, : sizes[i]] for i in range(len(vectors))]
     o_g1, o_s1, o_bq, o_bv, o_bo, o_g2, o_s2, o_bd, o_bu = outs
     one = red_one.done

time: 492 us -> 478 us (0.972)
  waiting for transfers between devices: 115 us -> 90.6 us
  starting transfers between devices: 38.9 us -> 44.4 us
    ppermute x43, waiting for transfers between devices: 115 us -> 90.6 us  [send(): return lax.ppermute(x, AXES, perm)]
    pallas_call x0 -> x2, Pallas kernels: none -> 18.4 us  [weight_grad_half(): call(body, grid_spec=pltpu.PrefetchScalarGridSpec(num_scalar_prefetch=1,...]
    pallas_call x4 -> x3, Pallas kernels: 52.6 us -> 38.3 us  [weight_grad(): call(body, grid_spec=pltpu.PrefetchScalarGridSpec(num_scalar_prefetch=1,...]
    ppermute x43, starting transfers between devices: 38.9 us -> 44.4 us  [send(): return lax.ppermute(x, AXES, perm)]
    unnamed x59 -> x60, local copies, waits for them, and re-layouts: 8.81 us -> 11.8 us
  transfers between devices with their start and end apart: 43 -> 43, of which waited for: 20 -> 17; matrix products, arithmetic and copies ran while one was open for 9% -> 9% of each run, Pallas kernels for 30% -> 33%
where the time goes in v8:
time: 478 us; the launch traced here: 474 us
  Pallas kernels  273 us (57%)
  waiting for transfers between devices  90.6 us (19%)
  starting transfers between devices  44.4 us (9%)
  other arithmetic  38.8 us (8%)
  local copies, waits for them, and re-layouts  25.4 us (5%)
    ppermute x43, waiting for transfers between devices, send(): return lax.ppermute(x, AXES, perm)  90.6 us
    ppermute x43, starting transfers between devices, send(): return lax.ppermute(x, AXES, perm)  44.4 us
    pallas_call x2, Pallas kernels, feed_forward_back(): call(body, grid=(steps,), in_specs=[full, pl.BlockSpec((rows, tf), lambda...  40.4 us
    pallas_call x3, Pallas kernels, weight_grad(): call(body, grid_spec=pltpu.PrefetchScalarGridSpec(num_scalar_prefetch=1,...  38.3 us
    pallas_call x4, Pallas kernels, attention_back(): call(body, grid=(pairs,), in_specs=[col(first_pair), col(every + first_pa...  35.7 us
    convert_element_type x16, other arithmetic, step(): self.kept = add(slice(0, half)).astype(wide)  32.6 us
    pallas_call x6, Pallas kernels, place_shards(): call(body, out_shape=jax.ShapeDtypeStruct(shape, jnp.bfloat16), grid_spec...  27.3 us
    pallas_call x2, Pallas kernels, attention(): call(body, grid=(pairs,), in_specs=[col(0), col(pairs), col(2 * pairs)],...  21.6 us
  transfers between devices with their start and end apart: 43, of which 17 were waited for; matrix products, arithmetic and copies ran while one was open for 9% of the time, Pallas kernels for 33%

profile of v8, /device:TPU:0, one launch (start us, length us, event | category | flops | bytes accessed | tf_op | source)
XLA Modules:
  0.0 473.8 jit_solution(7283315857254998287)
XLA Ops:
  0.7 1.8 pack_shard.1
  2.5 4.0 collective-permute-start
  6.5 12.8 %collective-permute-done = bf16[1,32,4352]{2,1,0:T(8,128)(2,1)S(1)} collective-permute-done((bf16[1,32,4352]{2,1,0:T(8,128)(2,1)}, bf16[1,32,4352]{2,1,0:T(8,128)(2,1)S(1)}, u32[]{:S(2)}, u32[]{:S(2)}) %collective-permute-start) | collective-permute-done | bytes 278560 | tf_op jit(solution)/shard_map/ppermute | solution.py:638
  21.2 13.0 %collective-permute-done.1 = bf16[2,32,4352]{2,1,0:T(8,128)(2,1)S(1)} collective-permute-done((bf16[2,32,4352]{2,1,0:T(8,128)(2,1)S(1)}, bf16[2,32,4352]{2,1,0:T(8,128)(2,1)S(1)}, u32[]{:S(2)}, u32[]{:S(2)}) %collective-permute-start.1) | collective-permute-done | bytes 557088 | tf_op jit(solution)/shard_map/ppermute | solution.py:638
  35.7 3.3 collective-permute-start.2
  39.1 11.3 %collective-permute-done.2 = bf16[1,128,1024]{2,1,0:T(8,128)(2,1)S(1)} collective-permute-done((bf16[1,128,1024]{2,1,0:T(8,128)(2,1)S(1)}, bf16[1,128,1024]{2,1,0:T(8,128)(2,1)S(1)}, u32[]{:S(2)}, u32[]{:S(2)}) %collective-permute-start.2) | collective-permute-done | bytes 262176 | tf_op jit(solution)/shard_map/ppermute | solution.py:638
  56.4 10.7 %collective-permute-done.4 = bf16[2,128,1024]{2,1,0:T(8,128)(2,1)} collective-permute-done((bf16[2,128,1024]{2,1,0:T(8,128)(2,1)S(1)}, bf16[2,128,1024]{2,1,0:T(8,128)(2,1)}, u32[]{:S(2)}, u32[]{:S(2)}) %collective-permute-start.4) | collective-permute-done | bytes 524320 | tf_op jit(solution)/shard_map/ppermute | solution.py:638
  69.3 1.6 collective-permute-start.7
  70.9 2.5 collective-permute-start.6
  73.4 4.5 place_shards.6.refs_2_
  77.9 7.1 %collective-permute-done.6 = bf16[1,128,1024]{2,1,0:T(8,128)(2,1)} collective-permute-done((bf16[1,128,1024]{2,1,0:T(8,128)(2,1)S(1)}, bf16[1,128,1024]{2,1,0:T(8,128)(2,1)}, u32[]{:S(2)}, u32[]{:S(2)}) %collective-permute-start.6) | collective-permute-done | bytes 262176 | tf_op jit(solution)/shard_map/ppermute | solution.py:638
  85.7 1.7 constant_dynamic-update-slice_fusion.10
  87.4 5.8 %collective-permute-done.7 = bf16[4,128,1024]{2,1,0:T(8,128)(2,1)} collective-permute-done((bf16[4,128,1024]{2,1,0:T(8,128)(2,1)S(1)}, bf16[4,128,1024]{2,1,0:T(8,128)(2,1)}, u32[]{:S(2)}, u32[]{:S(2)}) %collective-permute-start.7) | collective-permute-done | bytes 1048608 | tf_op jit(solution)/shard_map/ppermute | solution.py:638
  94.2 2.3 constant_dynamic-update-slice_fusion.12.refs_0_
  98.9 2.3 collective-permute-done.9.refs_1_.refs_3_
  101.2 4.5 place_shards.7
  105.7 2.4 unpack_vectors.1
  108.1 8.4 %norm_project.2 = (bf16[512,1024]{1,0:T(8,128)(2,1)}, bf16[512,3072]{1,0:T(8,128)(2,1)}) custom-call(bf16[512,1024]{1,0:T(8,128)(2,1)} %bitcast.72, f32[1,1024]{1,0:T(1,128)} %get-tuple-element.225.g_ref.refs_4_, f32[1,1024]{1,0:T(1,128)} %get-tuple-element.226.s_ref, bf16[1024,4096]{1,0:T(8,128)(2,1)} %bitcast.63, f32[1,3072]{1,0:T(1,128)} %get-tuple-element.227.b_ref), custom_call_target="tpu_custom_call" | custom-call | flops 1 | bytes 1 | tf_op jit(solution)/shard_map/norm_project/pallas_call | solution.py:55
  119.4 1.6 collective-permute-start.11
  121.0 10.8 %attention.2 = (bf16[512,1024]{1,0:T(8,128)(2,1)}, f32[8,8,512]{2,1,0:T(8,128)}) custom-call(bf16[512,3072]{1,0:T(8,128)(2,1)} %get-tuple-element.232.q_ref.k_ref.v_ref, bf16[512,3072]{1,0:T(8,128)(2,1)} %get-tuple-element.232.q_ref.k_ref.v_ref, bf16[512,3072]{1,0:T(8,128)(2,1)} %get-tuple-element.232.q_ref.k_ref.v_ref), custom_call_target="tpu_custom_call" | custom-call | flops 1 | bytes 1 | tf_op jit(solution)/shard_map/attention/pallas_call | solution.py:100
  132.4 4.9 %project_norm.2 = (f32[512,1024]{1,0:T(8,128)}, bf16[512,1024]{1,0:T(8,128)(2,1)}) custom-call(bf16[512,1024]{1,0:T(8,128)(2,1)} %get-tuple-element.305.o_ref.refs_0_, bf16[1024,4096]{1,0:T(8,128)(2,1)} %bitcast.64, f32[1,1024]{1,0:T(1,128)} %get-tuple-element.235.b_ref, bf16[512,1024]{1,0:T(8,128)(2,1)} %bitcast.73, f32[1,1024]{1,0:T(1,128)} %get-tuple-element.236.g_ref, ...), custom_call_target="tpu_custom_call" | custom-call | flops 1 | bytes 1 | tf_op jit(solution)/shard_map/project_norm/pallas_call | solution.py:178
  141.0 4.5 place_shards.8.refs_2_
  145.6 4.5 place_shards.9.u_ref.refs_2_
  150.1 11.4 %feed_forward_in.1 = (bf16[512,4096]{1,0:T(8,128)(2,1)}, bf16[512,4096]{1,0:T(8,128)(2,1)}) custom-call(bf16[512,1024]{1,0:T(8,128)(2,1)} %get-tuple-element.288.a_ref.refs_0_, bf16[32,256,1024]{2,1,0:T(8,128)(2,1)} %place_shards.9.u_ref.refs_2_, f32[1,4096]{1,0:T(1,128)} %get-tuple-element.247.ub_ref), custom_call_target="tpu_custom_call" | custom-call | flops 1 | bytes 1 | tf_op jit(solution)/shard_map/feed_forward_in/pallas_call | solution.py:266
  161.6 4.7 place_shards.10.refs_2_
  169.1 1.5 convert_multiply_fusion.dy_ref
  172.0 4.5 place_shards.11.d_ref.u_ref
  176.6 9.7 %feed_forward_out.1.x_ref.refs_3_ = bf16[512,1024]{1,0:T(8,128)(2,1)} custom-call(bf16[512,4096]{1,0:T(8,128)(2,1)} %get-tuple-element.284.g_ref.refs_0_, bf16[32,256,1024]{2,1,0:T(8,128)(2,1)} %place_shards.11.d_ref.u_ref, f32[1,1024]{1,0:T(1,128)} %get-tuple-element.255.db_ref, f32[512,1024]{1,0:T(8,128)} %get-tuple-element.256.x_ref), custom_call_target="tpu_custom_call" | custom-call | flops 1 | bytes 1 | tf_op jit(solution)/shard_map/feed_forward_out/pallas_call | solution.py:297
  186.2 7.8 %norm_project.3 = (bf16[512,1024]{1,0:T(8,128)(2,1)}, bf16[512,3072]{1,0:T(8,128)(2,1)}) custom-call(bf16[512,1024]{1,0:T(8,128)(2,1)} %feed_forward_out.1.x_ref.refs_3_, f32[1,1024]{1,0:T(1,128)} %get-tuple-element.225.g_ref.refs_4_, f32[1,1024]{1,0:T(1,128)} %get-tuple-element.226.s_ref, bf16[1024,4096]{1,0:T(8,128)(2,1)} %bitcast.65, ...), custom_call_target="tpu_custom_call" | custom-call | flops 1 | bytes 1 | tf_op jit(solution)/shard_map/norm_project/pallas_call | solution.py:55
  194.9 10.8 %attention.3 = (bf16[512,1024]{1,0:T(8,128)(2,1)}, f32[8,8,512]{2,1,0:T(8,128)}) custom-call(bf16[512,3072]{1,0:T(8,128)(2,1)} %get-tuple-element.258.q_ref.k_ref.v_ref, bf16[512,3072]{1,0:T(8,128)(2,1)} %get-tuple-element.258.q_ref.k_ref.v_ref, bf16[512,3072]{1,0:T(8,128)(2,1)} %get-tuple-element.258.q_ref.k_ref.v_ref), custom_call_target="tpu_custom_call" | custom-call | flops 1 | bytes 1 | tf_op jit(solution)/shard_map/attention/pallas_call | solution.py:100
  205.7 5.1 %project_norm.3 = (f32[512,1024]{1,0:T(8,128)}, bf16[512,1024]{1,0:T(8,128)(2,1)}) custom-call(bf16[512,1024]{1,0:T(8,128)(2,1)} %get-tuple-element.306.o_ref.refs_1_, bf16[1024,4096]{1,0:T(8,128)(2,1)} %bitcast.66, f32[1,1024]{1,0:T(1,128)} %get-tuple-element.235.b_ref, bf16[512,1024]{1,0:T(8,128)(2,1)} %feed_forward_out.1.x_ref.refs_3_, ...), custom_call_target="tpu_custom_call" | custom-call | flops 1 | bytes 1 | tf_op jit(solution)/shard_map/project_norm/pallas_call | solution.py:178
  210.8 17.9 %feed_forward.1 = (bf16[512,4096]{1,0:T(8,128)(2,1)}, bf16[512,4096]{1,0:T(8,128)(2,1)}, bf16[512,1024]{1,0:T(8,128)(2,1)}) custom-call(bf16[512,1024]{1,0:T(8,128)(2,1)} %get-tuple-element.289.a_ref.refs_1_, bf16[32,256,1024]{2,1,0:T(8,128)(2,1)} %place_shards.11.d_ref.u_ref, f32[1,4096]{1,0:T(1,128)} %get-tuple-element.247.ub_ref, ...), custom_call_target="tpu_custom_call" | custom-call | flops 1 | bytes 1 | tf_op jit(solution)/shard_map/feed_forward/pallas_call | solution.py:229
  228.7 20.2 %feed_forward_back.2 = (bf16[512,1024]{1,0:T(8,128)(2,1)}, bf16[512,4096]{1,0:T(8,128)(2,1)}, f32[512,1024]{1,0:T(8,128)}, bf16[512,1024]{1,0:T(8,128)(2,1)}, bf...) custom-call(f32[512,1024]{1,0:T(8,128)} %convert_multiply_fusion.dy_, ...), custom_call_target="tpu_custom_call" | custom-call | flops 99999997952 | bytes 1 | tf_op jit(solution)/shard_map/feed_forward_back/pallas_call | solution.py:356
  248.9 8.9 %attention_back.4 = (bf16[3,512,512]{2,1,0:T(8,128)(2,1)}, f32[1,512]{1,0:T(1,128)}, f32[1,512]{1,0:T(1,128)}) custom-call(bf16[512,3072]{1,0:T(8,128)(2,1)} %get-tuple-element.258.q_ref.k_ref.v_ref, bf16[512,3072]{1,0:T(8,128)(2,1)} %get-tuple-element.258.q_ref.k_ref.v_ref, bf16[512,3072]{1,0:T(8,128)(2,1)} %get-tuple-element.258.q_ref.k_ref.v_ref, ...), custom_call_target="tpu_custom_call" | custom-call | flops 99999997952 | bytes 1 | tf_op jit(solution)/shard_map/attention_back/pallas_call | solution.py:145
  257.8 8.9 %attention_back.5 = (bf16[3,512,512]{2,1,0:T(8,128)(2,1)}, f32[1,512]{1,0:T(1,128)}, f32[1,512]{1,0:T(1,128)}) custom-call(bf16[512,3072]{1,0:T(8,128)(2,1)} %get-tuple-element.258.q_ref.k_ref.v_ref, bf16[512,3072]{1,0:T(8,128)(2,1)} %get-tuple-element.258.q_ref.k_ref.v_ref, bf16[512,3072]{1,0:T(8,128)(2,1)} %get-tuple-element.258.q_ref.k_ref.v_ref, ...), custom_call_target="tpu_custom_call" | custom-call | flops 99999997952 | bytes 1 | tf_op jit(solution)/shard_map/attention_back/pallas_call | solution.py:145
  266.8 10.4 %project_back.2 = (f32[512,1024]{1,0:T(8,128)}, bf16[512,1024]{1,0:T(8,128)(2,1)}, f32[1,1024]{1,0:T(1,128)}, f32[1,1024]{1,0:T(1,128)}) custom-call(bf16[3,512,512]{2,1,0:T(8,128)(2,1)} %get-tuple-element.274.refs_0_.refs_7_, bf16[3,512,512]{2,1,0:T(8,128)(2,1)} %get-tuple-element.275.refs_1_.refs_3_, bf16[1024,4096]{1,0:T(8,128)(2,1)} %bitcast.68, ...), custom_call_target="tpu_custom_call" | custom-call | flops 1 | bytes 1 | tf_op jit(solution)/shard_map/project_back/pallas_call | solution.py:448
  277.2 9.3 %weight_grad_half.2 = bf16[16,128,1024]{2,1,0:T(8,128)(2,1)} custom-call(s32[18]{0:T(128)} %pad_add_fusion.2.i_ref, bf16[512,4096]{1,0:T(8,128)(2,1)} %get-tuple-element.284.g_ref.refs_0_, bf16[512,4096]{1,0:T(8,128)(2,1)} %get-tuple-element.285.refs_1_, bf16[512,1024]{1,0:T(8,128)(2,1)} %get-tuple-element.283.refs_2_, ...), custom_call_target="tpu_custom_call" | custom-call | flops 1 | bytes 1 | tf_op jit(solution)/shard_map/weight_grad_half/pallas_call | solution.py:578
  288.1 9.1 %weight_grad_half.3 = bf16[16,128,1024]{2,1,0:T(8,128)(2,1)} custom-call(s32[18]{0:T(128)} %pad_add_fusion.1.i_ref, bf16[512,4096]{1,0:T(8,128)(2,1)} %get-tuple-element.284.g_ref.refs_0_, bf16[512,4096]{1,0:T(8,128)(2,1)} %get-tuple-element.285.refs_1_, bf16[512,1024]{1,0:T(8,128)(2,1)} %get-tuple-element.283.refs_2_, ...), custom_call_target="tpu_custom_call" | custom-call | flops 1 | bytes 1 | tf_op jit(solution)/shard_map/weight_grad_half/pallas_call | solution.py:578
  297.2 5.5 %add_convert_fusion.2 = (bf16[8,128,1024]{2,1,0:T(8,128)(2,1)S(1)}, bf16[8,128,1024]{2,1,0:T(8,128)(2,1)}) fusion(bf16[16,128,1024]{2,1,0:T(8,128)(2,1)} %collective-permute-done.18, bf16[16,128,1024]{2,1,0:T(8,128)(2,1)} %weight_grad_half.3), kind=kLoop, calls=%fused_computation.3 | loop fusion | flops 8388608 | bytes 12582912 | tf_op jit(solution)/shard_map/convert_element_type | solution.py:815
  303.6 20.2 %feed_forward_back.3 = (bf16[512,1024]{1,0:T(8,128)(2,1)}, bf16[512,4096]{1,0:T(8,128)(2,1)}, f32[512,1024]{1,0:T(8,128)}, bf16[512,1024]{1,0:T(8,128)(2,1)}, bf...) custom-call(f32[512,1024]{1,0:T(8,128)} %get-tuple-element.290.dy_re, ...), custom_call_target="tpu_custom_call" | custom-call | flops 99999997952 | bytes 1 | tf_op jit(solution)/shard_map/feed_forward_back/pallas_call | solution.py:356
  323.8 16.2 %weight_grad.3 = (bf16[16,32,4096]{2,1,0:T(8,128)(2,1)}, bf16[16,32,4096]{2,1,0:T(8,128)(2,1)}) custom-call(s32[36]{0:T(128)} %pad_add_fusion.i_ref, bf16[512,1024]{1,0:T(8,128)(2,1)} %get-tuple-element.288.a_ref.refs_0_, bf16[512,1024]{1,0:T(8,128)(2,1)} %get-tuple-element.289.a_ref.refs_1_, bf16[512,4096]{1,0:T(8,128)(2,1)} %get-tuple-element.292.refs_2_, ...), custom_call_target="tpu_custom_call" | custom-call | flops 1 | bytes 1 | tf_op jit(solution)/shard_map/weight_grad/pallas_call | solution.py:531
  340.1 3.5 add_convert_fusion.8
  344.8 8.9 %attention_back.6 = (bf16[3,512,512]{2,1,0:T(8,128)(2,1)}, f32[1,512]{1,0:T(1,128)}, f32[1,512]{1,0:T(1,128)}) custom-call(bf16[512,3072]{1,0:T(8,128)(2,1)} %get-tuple-element.232.q_ref.k_ref.v_ref, bf16[512,3072]{1,0:T(8,128)(2,1)} %get-tuple-element.232.q_ref.k_ref.v_ref, bf16[512,3072]{1,0:T(8,128)(2,1)} %get-tuple-element.232.q_ref.k_ref.v_ref, ...), custom_call_target="tpu_custom_call" | custom-call | flops 99999997952 | bytes 1 | tf_op jit(solution)/shard_map/attention_back/pallas_call | solution.py:145
  353.7 4.8 %collective-permute-done.20 = bf16[4,128,1024]{2,1,0:T(8,128)(2,1)S(1)} collective-permute-done((bf16[4,128,1024]{2,1,0:T(8,128)(2,1)}, bf16[4,128,1024]{2,1,0:T(8,128)(2,1)S(1)}, u32[]{:S(2)}, u32[]{:S(2)}) %collective-permute-start.20) | collective-permute-done | bytes 1048608 | tf_op jit(solution)/shard_map/ppermute | solution.py:638
  359.9 5.2 %add_convert_fusion = (bf16[8,32,4096]{2,1,0:T(8,128)(2,1)S(1)}, bf16[8,32,4096]{2,1,0:T(8,128)(2,1)}) fusion(bf16[16,32,4096]{2,1,0:T(8,128)(2,1)} %collective-permute-done.21, bf16[16,32,4096]{2,1,0:T(8,128)(2,1)} %get-tuple-element.303), kind=kLoop, calls=%fused_computation.1 | loop fusion | flops 8388608 | bytes 12582912 | tf_op jit(solution)/shard_map/convert_element_type | solution.py:815
  366.8 13.6 %weight_grad.4 = (bf16[16,32,2560]{2,1,0:T(8,128)(2,1)}, bf16[16,32,2560]{2,1,0:T(8,128)(2,1)}) custom-call(s32[36]{0:T(128)} %pad_add_fusion.i_ref, bf16[512,1024]{1,0:T(8,128)(2,1)} %get-tuple-element.305.o_ref.refs_0_, bf16[512,1024]{1,0:T(8,128)(2,1)} %get-tuple-element.306.o_ref.refs_1_, bf16[512,1024]{1,0:T(8,128)(2,1)} %get-tuple-element.307.refs_2_, ...), custom_call_target="tpu_custom_call" | custom-call | flops 1 | bytes 1 | tf_op jit(solution)/shard_map/weight_grad/pallas_call | solution.py:531
  380.6 8.9 %attention_back.7 = (bf16[3,512,512]{2,1,0:T(8,128)(2,1)}, f32[1,512]{1,0:T(1,128)}, f32[1,512]{1,0:T(1,128)}) custom-call(bf16[512,3072]{1,0:T(8,128)(2,1)} %get-tuple-element.232.q_ref.k_ref.v_ref, bf16[512,3072]{1,0:T(8,128)(2,1)} %get-tuple-element.232.q_ref.k_ref.v_ref, bf16[512,3072]{1,0:T(8,128)(2,1)} %get-tuple-element.232.q_ref.k_ref.v_ref, ...), custom_call_target="tpu_custom_call" | custom-call | flops 1 | bytes 1 | tf_op jit(solution)/shard_map/attention_back/pallas_call | solution.py:145
  389.5 2.0 collective-permute-done.22
  391.5 3.4 add_convert_fusion.6
  396.1 1.9 add_convert_fusion.24
  398.0 3.2 collective-permute-start.34
  401.2 8.5 %weight_grad.5 = (bf16[16,32,1536]{2,1,0:T(8,128)(2,1)}, bf16[16,32,1536]{2,1,0:T(8,128)(2,1)}) custom-call(s32[36]{0:T(128)} %pad_add_fusion.i_ref, bf16[512,1024]{1,0:T(8,128)(2,1)} %get-tuple-element.319.refs_4_.refs_0_, bf16[512,1024]{1,0:T(8,128)(2,1)} %get-tuple-element.320.refs_5_.refs_1_, bf16[3,512,512]{2,1,0:T(8,128)(2,1)} %get-tuple-element.331.refs_2_.refs_1_, ...), custom_call_target="tpu_custom_call" | custom-call | flops 99999997952 | bytes 1 | tf_op jit(solution)/shard_map/weight_grad/pallas_call | solution.py:531
  409.8 4.4 add_convert_fusion.4
  414.9 2.4 add_convert_fusion.14
  419.7 9.3 %project_back.3 = (bf16[512,1024]{1,0:T(8,128)(2,1)}, f32[1,1024]{1,0:T(1,128)}, f32[1,1024]{1,0:T(1,128)}) custom-call(bf16[3,512,512]{2,1,0:T(8,128)(2,1)} %get-tuple-element.330.refs_6_.refs_0_, bf16[3,512,512]{2,1,0:T(8,128)(2,1)} %get-tuple-element.331.refs_2_.refs_1_, bf16[1024,4096]{1,0:T(8,128)(2,1)} %bitcast.70, bf16[512,1024]{1,0:T(8,128)(2,1)} %bitcast.74, ...), custom_call_target="tpu_custom_call" | custom-call | flops 1 | bytes 1 | tf_op jit(solution)/shard_map/project_back/pallas_call | solution.py:448
  428.9 2.4 pack_sums.1
  432.5 1.7 add_convert_fusion.12
  436.4 7.2 %collective-permute-done.29 = bf16[8,32,1536]{2,1,0:T(8,128)(2,1)} collective-permute-done((bf16[8,32,1536]{2,1,0:T(8,128)(2,1)S(1)}, bf16[8,32,1536]{2,1,0:T(8,128)(2,1)}, u32[]{:S(2)}, u32[]{:S(2)}) %collective-permute-start.29) | collective-permute-done | bytes 786464 | tf_op jit(solution)/shard_map/ppermute | solution.py:638
  448.4 2.6 collective-permute-done.32
  453.1 1.8 add_bitcast_fusion
  455.1 2.1 collective-permute-start.38
  458.3 4.5 collective-permute-done.38
  463.0 2.8 collective-permute-start.42
  465.8 4.9 %collective-permute-done.40 = f32[1,9,128]{2,1,0:T(8,128)S(1)} collective-permute-done((f32[1,9,128]{2,1,0:T(8,128)S(1)}, f32[1,9,128]{2,1,0:T(8,128)S(1)}, u32[]{:S(2)}, u32[]{:S(2)}) %collective-permute-start.40) | collective-permute-done | bytes 4640 | tf_op jit(solution)/shard_map/ppermute | solution.py:638
  (170 shorter events, 53.8 us)
Async XLA Ops:
  0.7 35.1 %copy-start.12 = (bf16[32,4096]{1,0:T(8,128)(2,1)S(1)}, bf16[32,4096]{1,0:T(8,128)(2,1)}, u32[]{:S(2)}) copy-start(bf16[32,4096]{1,0:T(8,128)(2,1)} %param.28) | copy-start | bytes 786436
  2.5 16.9 %collective-permute-start = (bf16[1,32,4352]{2,1,0:T(8,128)(2,1)}, bf16[1,32,4352]{2,1,0:T(8,128)(2,1)S(1)}, u32[]{:S(2)}, u32[]{:S(2)}) collective-permute-start(bf16[1,32,4352]{2,1,0:T(8,128)(2,1)} %bitcast.75), channel_id=1, source_target_pairs={{0,4},{1,5},{2,6},{3,7},{4,0},{5,1},{6,2},{7,3},{8,12},{9,13},{10,... | collective-permute-start | bytes 835592 | tf_op jit(solution)/shard_map/ppermute | solution.py:638
  20.3 13.9 %collective-permute-start.1 = (bf16[2,32,4352]{2,1,0:T(8,128)(2,1)S(1)}, bf16[2,32,4352]{2,1,0:T(8,128)(2,1)S(1)}, u32[]{:S(2)}, u32[]{:S(2)}) collective-permute-start(bf16[2,32,4352]{2,1,0:T(8,128)(2,1)S(1)} %constant_dynamic-update-slice_fusion), channel_id=1, source_target_pairs={{0,2},{1,3},{2,0},{3,1},{4,6},{5,7},{6,4},{7,5},{8,10},{9,11},{10,... | collective-permute-start | bytes 1671176 | tf_op jit(solution)/shard_map/ppermute | solution.py:638
  34.3 16.1 %collective-permute-start.3 = (bf16[4,32,4352]{2,1,0:T(8,128)(2,1)S(1)}, bf16[4,32,4352]{2,1,0:T(8,128)(2,1)S(1)}, u32[]{:S(2)}, u32[]{:S(2)}) collective-permute-start(bf16[4,32,4352]{2,1,0:T(8,128)(2,1)S(1)} %constant_dynamic-update-slice_fusion.2), channel_id=1, source_target_pairs={{0,1},{1,0},{2,3},{3,2},{4,5},{5,4},{6,7},{7,6},{8,24},{9,25},{10,... | collective-permute-start | bytes 3342344 | tf_op jit(solution)/shard_map/ppermute | solution.py:638
  35.7 14.6 %collective-permute-start.2 = (bf16[1,128,1024]{2,1,0:T(8,128)(2,1)S(1)}, bf16[1,128,1024]{2,1,0:T(8,128)(2,1)S(1)}, u32[]{:S(2)}, u32[]{:S(2)}) collective-permute-start(bf16[1,128,1024]{2,1,0:T(8,128)(2,1)S(1)} %bitcast.78), channel_id=1, source_target_pairs={{0,4},{1,5},{2,6},{3,7},{4,0},{5,1},{6,2},{7,3},{8,12},{9,13},{10,... | collective-permute-start | bytes 786440 | tf_op jit(solution)/shard_map/ppermute | solution.py:638
  50.4 6.0 %copy-start.7 = (bf16[2,128,1024]{2,1,0:T(8,128)(2,1)}, bf16[2,128,1024]{2,1,0:T(8,128)(2,1)S(1)}, u32[]{:S(2)}) copy-start(bf16[2,128,1024]{2,1,0:T(8,128)(2,1)S(1)} %constant_dynamic-update-slice_fusion.4) | copy-start | bytes 1572868
  51.7 19.3 %copy-start.13 = (bf16[128,1024]{1,0:T(8,128)(2,1)S(1)}, bf16[128,1024]{1,0:T(8,128)(2,1)}, u32[]{:S(2)}) copy-start(bf16[128,1024]{1,0:T(8,128)(2,1)} %param.30) | copy-start | bytes 786436
  52.7 20.7 %collective-permute-start.5 = (bf16[8,32,4352]{2,1,0:T(8,128)(2,1)}, bf16[8,32,4352]{2,1,0:T(8,128)(2,1)}, u32[]{:S(2)}, u32[]{:S(2)}) collective-permute-start(bf16[8,32,4352]{2,1,0:T(8,128)(2,1)} %constant_dynamic-update-slice_fusion.6.refs_0_), channel_id=1, source_target_pairs={{0,8},{1,9},{2,10},{3,11},{4,12},{5,13},{6,14},{7,15},{8,0},{9,1},... | collective-permute-start | bytes 6684680 | tf_op jit(solution)/shard_map/ppermute | solution.py:638
  52.7 14.4 %collective-permute-start.4 = (bf16[2,128,1024]{2,1,0:T(8,128)(2,1)S(1)}, bf16[2,128,1024]{2,1,0:T(8,128)(2,1)}, u32[]{:S(2)}, u32[]{:S(2)}) collective-permute-start(bf16[2,128,1024]{2,1,0:T(8,128)(2,1)S(1)} %constant_dynamic-update-slice_fusion.4), channel_id=1, source_target_pairs={{0,2},{1,3},{2,0},{3,1},{4,6},{5,7},{6,4},{7,5},{8,10},{9,11},{10,... | collective-permute-start | bytes 1572872 | tf_op jit(solution)/shard_map/ppermute | solution.py:638
  54.9 41.6 %collective-permute-start.8 = (bf16[8,32,4352]{2,1,0:T(8,128)(2,1)}, bf16[8,32,4352]{2,1,0:T(8,128)(2,1)S(1)}, u32[]{:S(2)}, u32[]{:S(2)}) collective-permute-start(bf16[8,32,4352]{2,1,0:T(8,128)(2,1)} %constant_dynamic-update-slice_fusion.6.refs_0_), channel_id=1, source_target_pairs={{0,16},{1,17},{2,18},{3,19},{4,20},{5,21},{6,22},{7,23},{8,9},{9,8... | collective-permute-start | bytes 6684680 | tf_op jit(solution)/shard_map/ppermute | solution.py:638
  69.3 23.9 %collective-permute-start.7 = (bf16[4,128,1024]{2,1,0:T(8,128)(2,1)S(1)}, bf16[4,128,1024]{2,1,0:T(8,128)(2,1)}, u32[]{:S(2)}, u32[]{:S(2)}) collective-permute-start(bf16[4,128,1024]{2,1,0:T(8,128)(2,1)S(1)} %constant_dynamic-update-slice_fusion.8), channel_id=1, source_target_pairs={{0,1},{1,0},{2,3},{3,2},{4,5},{5,4},{6,7},{7,6},{8,24},{9,25},{10,... | collective-permute-start | bytes 3145736 | tf_op jit(solution)/shard_map/ppermute | solution.py:638
  70.9 14.1 %collective-permute-start.6 = (bf16[1,128,1024]{2,1,0:T(8,128)(2,1)S(1)}, bf16[1,128,1024]{2,1,0:T(8,128)(2,1)}, u32[]{:S(2)}, u32[]{:S(2)}) collective-permute-start(bf16[1,128,1024]{2,1,0:T(8,128)(2,1)S(1)} %bitcast.81), channel_id=1, source_target_pairs={{0,4},{1,5},{2,6},{3,7},{4,0},{5,1},{6,2},{7,3},{8,12},{9,13},{10,... | collective-permute-start | bytes 786440 | tf_op jit(solution)/shard_map/ppermute | solution.py:638
  96.5 4.7 copy-start.1
  96.5 4.7 collective-permute-start.9
  97.1 34.7 %collective-permute-start.13 = (bf16[8,128,1024]{2,1,0:T(8,128)(2,1)}, bf16[8,128,1024]{2,1,0:T(8,128)(2,1)}, u32[]{:S(2)}, u32[]{:S(2)}) collective-permute-start(bf16[8,128,1024]{2,1,0:T(8,128)(2,1)} %constant_dynamic-update-slice_fusion.12.refs_0_), channel_id=1, source_target_pairs={{0,16},{1,17},{2,18},{3,19},{4,20},{5,21},{6,22},{7,23},{8,9},{9,8... | collective-permute-start | bytes 6291464 | tf_op jit(solution)/shard_map/ppermute | solution.py:638
  98.4 18.1 %collective-permute-start.10 = (bf16[2,128,1024]{2,1,0:T(8,128)(2,1)}, bf16[2,128,1024]{2,1,0:T(8,128)(2,1)S(1)}, u32[]{:S(2)}, u32[]{:S(2)}) collective-permute-start(bf16[2,128,1024]{2,1,0:T(8,128)(2,1)} %constant_dynamic-update-slice_fusion.10), channel_id=1, source_target_pairs={{0,2},{1,3},{2,0},{3,1},{4,6},{5,7},{6,4},{7,5},{8,10},{9,11},{10,... | collective-permute-start | bytes 1572872 | tf_op jit(solution)/shard_map/ppermute | solution.py:638
  116.5 0.8 copy-start.11
  119.4 17.9 %collective-permute-start.11 = (bf16[4,128,1024]{2,1,0:T(8,128)(2,1)S(1)}, bf16[4,128,1024]{2,1,0:T(8,128)(2,1)S(1)}, u32[]{:S(2)}, u32[]{:S(2)}) collective-permute-start(bf16[4,128,1024]{2,1,0:T(8,128)(2,1)S(1)} %constant_dynamic-update-slice_fusion.14), channel_id=1, source_target_pairs={{0,1},{1,0},{2,3},{3,2},{4,5},{5,4},{6,7},{7,6},{8,24},{9,25},{10,... | collective-permute-start | bytes 3145736 | tf_op jit(solution)/shard_map/ppermute | solution.py:638
  121.0 20.0 %collective-permute-start.12 = (bf16[8,128,1024]{2,1,0:T(8,128)(2,1)}, bf16[8,128,1024]{2,1,0:T(8,128)(2,1)}, u32[]{:S(2)}, u32[]{:S(2)}) collective-permute-start(bf16[8,128,1024]{2,1,0:T(8,128)(2,1)} %constant_dynamic-update-slice_fusion.12.refs_0_), channel_id=1, source_target_pairs={{0,8},{1,9},{2,10},{3,11},{4,12},{5,13},{6,14},{7,15},{8,0},{9,1},... | collective-permute-start | bytes 6291464 | tf_op jit(solution)/shard_map/ppermute | solution.py:638
  131.8 13.7 %collective-permute-start.14 = (bf16[8,128,1024]{2,1,0:T(8,128)(2,1)}, bf16[8,128,1024]{2,1,0:T(8,128)(2,1)}, u32[]{:S(2)}, u32[]{:S(2)}) collective-permute-start(bf16[8,128,1024]{2,1,0:T(8,128)(2,1)} %collective-permute-done.13.refs_0_), channel_id=1, source_target_pairs={{0,8},{1,9},{2,10},{3,11},{4,12},{5,13},{6,14},{7,15},{8,0},{9,1},... | collective-permute-start | bytes 6291464 | tf_op jit(solution)/shard_map/ppermute | solution.py:638
  137.3 1.0 copy-start.8
  138.2 1.2 copy-start.9
  139.5 6.0 %copy-start.2 = (bf16[8,128,1024]{2,1,0:T(8,128)(2,1)}, bf16[8,128,1024]{2,1,0:T(8,128)(2,1)S(1)}, u32[]{:S(2)}) copy-start(bf16[8,128,1024]{2,1,0:T(8,128)(2,1)S(1)} %constant_dynamic-update-slice_fusion.16.refs_0_) | copy-start | bytes 6291460
  139.6 22.0 %collective-permute-start.15 = (bf16[8,128,1024]{2,1,0:T(8,128)(2,1)S(1)}, bf16[8,128,1024]{2,1,0:T(8,128)(2,1)}, u32[]{:S(2)}, u32[]{:S(2)}) collective-permute-start(bf16[8,128,1024]{2,1,0:T(8,128)(2,1)S(1)} %constant_dynamic-update-slice_fusion.16.refs_0_), channel_id=1, source_target_pairs={{0,8},{1,9},{2,10},{3,11},{4,12},{5,13},{6,14},{7,15},{8,0},{9,1},... | collective-permute-start | bytes 6291464 | tf_op jit(solution)/shard_map/ppermute | solution.py:638
  139.7 26.6 %collective-permute-start.16 = (bf16[8,128,1024]{2,1,0:T(8,128)(2,1)S(1)}, bf16[8,128,1024]{2,1,0:T(8,128)(2,1)}, u32[]{:S(2)}, u32[]{:S(2)}) collective-permute-start(bf16[8,128,1024]{2,1,0:T(8,128)(2,1)S(1)} %constant_dynamic-update-slice_fusion.16.refs_0_), channel_id=1, source_target_pairs={{0,16},{1,17},{2,18},{3,19},{4,20},{5,21},{6,22},{7,23},{8,9},{9,8... | collective-permute-start | bytes 6291464 | tf_op jit(solution)/shard_map/ppermute | solution.py:638
  161.5 5.6 %copy-start = (s32[32]{0:T(128)S(1)}, s32[32]{0:T(128)}, u32[]{:S(2)}) copy-start(s32[32]{0:T(128)} %get-tuple-element.443.i_ref) | copy-start | bytes 388
  161.5 7.5 %copy-start.17 = (s32[1,512]{1,0:T(1,128)S(1)}, s32[1,512]{1,0:T(1,128)}, u32[]{:S(2)}) copy-start(s32[1,512]{1,0:T(1,128)} %param.34) | copy-start | bytes 6148
  161.6 7.5 %copy-start.10 = (bf16[1,512,1024]{2,1,0:T(8,128)(2,1)S(1)}, bf16[1,512,1024]{2,1,0:T(8,128)(2,1)}, u32[]{:S(2)}) copy-start(bf16[1,512,1024]{2,1,0:T(8,128)(2,1)} %param.33) | copy-start | bytes 3145732
  166.3 4.4 collective-permute-start.17
  166.4 10.2 %copy-start.20 = (s32[2]{0:T(128)}, s32[2]{0:T(128)S(1)}, u32[]{:S(2)}) copy-start(s32[2]{0:T(128)S(1)} %get-tuple-element.446) | copy-start | bytes 28
  170.7 1.3 copy-start.3
  277.2 9.7 %copy-start.16 = (s32[32]{0:T(128)S(1)}, s32[32]{0:T(128)}, u32[]{:S(2)}) copy-start(s32[32]{0:T(128)} %copy-done.15) | copy-start | bytes 388
  277.2 9.7 %copy-start.19 = (s32[2]{0:T(128)S(1)}, s32[2]{0:T(128)}, u32[]{:S(2)}) copy-start(s32[2]{0:T(128)} %copy-done.18) | copy-start | bytes 28
  277.2 9.7 %copy-start.21 = (s32[2]{0:T(128)S(1)}, s32[2]{0:T(128)}, u32[]{:S(2)}) copy-start(s32[2]{0:T(128)} %copy-done.20) | copy-start | bytes 28
  277.2 10.3 %copy-start.22 = (s32[16]{0:T(128)S(1)}, s32[16]{0:T(128)}, u32[]{:S(2)}) copy-start(s32[16]{0:T(128)} %get-tuple-element.442) | copy-start | bytes 196
  286.5 10.7 %collective-permute-start.18 = (bf16[16,128,1024]{2,1,0:T(8,128)(2,1)}, bf16[16,128,1024]{2,1,0:T(8,128)(2,1)}, u32[]{:S(2)}, u32[]{:S(2)}) collective-permute-start(bf16[16,128,1024]{2,1,0:T(8,128)(2,1)} %weight_grad_half.2), channel_id=1, source_target_pairs={{0,8},{1,9},{2,10},{3,11},{4,12},{5,13},{6,14},{7,15},{8,0},{9,1},... | collective-permute-start | bytes 12582920 | tf_op jit(solution)/shard_map/ppermute | solution.py:638
  302.6 37.4 %collective-permute-start.19 = (bf16[8,128,1024]{2,1,0:T(8,128)(2,1)}, bf16[8,128,1024]{2,1,0:T(8,128)(2,1)}, u32[]{:S(2)}, u32[]{:S(2)}) collective-permute-start(bf16[8,128,1024]{2,1,0:T(8,128)(2,1)} %get-tuple-element.392), channel_id=1, source_target_pairs={{0,16},{1,17},{2,18},{3,19},{4,20},{5,21},{6,22},{7,23},{8,9},{9,8... | collective-permute-start | bytes 6291464 | tf_op jit(solution)/shard_map/ppermute | solution.py:638
  340.0 20.0 %collective-permute-start.21 = (bf16[16,32,4096]{2,1,0:T(8,128)(2,1)}, bf16[16,32,4096]{2,1,0:T(8,128)(2,1)}, u32[]{:S(2)}, u32[]{:S(2)}) collective-permute-start(bf16[16,32,4096]{2,1,0:T(8,128)(2,1)} %get-tuple-element.294), channel_id=1, source_target_pairs={{0,8},{1,9},{2,10},{3,11},{4,12},{5,13},{6,14},{7,15},{8,0},{9,1},... | collective-permute-start | bytes 12582920 | tf_op jit(solution)/shard_map/ppermute | solution.py:638
  343.5 15.0 %collective-permute-start.20 = (bf16[4,128,1024]{2,1,0:T(8,128)(2,1)}, bf16[4,128,1024]{2,1,0:T(8,128)(2,1)S(1)}, u32[]{:S(2)}, u32[]{:S(2)}) collective-permute-start(bf16[4,128,1024]{2,1,0:T(8,128)(2,1)} %get-tuple-element.398), channel_id=1, source_target_pairs={{0,1},{1,0},{2,3},{3,2},{4,5},{5,4},{6,7},{7,6},{8,24},{9,25},{10,... | collective-permute-start | bytes 3145736 | tf_op jit(solution)/shard_map/ppermute | solution.py:638
  365.1 26.4 %collective-permute-start.22 = (bf16[8,32,4096]{2,1,0:T(8,128)(2,1)}, bf16[8,32,4096]{2,1,0:T(8,128)(2,1)}, u32[]{:S(2)}, u32[]{:S(2)}) collective-permute-start(bf16[8,32,4096]{2,1,0:T(8,128)(2,1)} %get-tuple-element.390), channel_id=1, source_target_pairs={{0,16},{1,17},{2,18},{3,19},{4,20},{5,21},{6,22},{7,23},{8,9},{9,8... | collective-permute-start | bytes 6291464 | tf_op jit(solution)/shard_map/ppermute | solution.py:638
  366.2 29.8 %collective-permute-start.23 = (bf16[2,128,1024]{2,1,0:T(8,128)(2,1)}, bf16[2,128,1024]{2,1,0:T(8,128)(2,1)}, u32[]{:S(2)}, u32[]{:S(2)}) collective-permute-start(bf16[2,128,1024]{2,1,0:T(8,128)(2,1)} %get-tuple-element.406), channel_id=1, source_target_pairs={{0,2},{1,3},{2,0},{3,1},{4,6},{5,7},{6,4},{7,5},{8,10},{9,11},{10,... | collective-permute-start | bytes 1572872 | tf_op jit(solution)/shard_map/ppermute | solution.py:638
  380.5 29.3 %collective-permute-start.24 = (bf16[16,32,2560]{2,1,0:T(8,128)(2,1)}, bf16[16,32,2560]{2,1,0:T(8,128)(2,1)}, u32[]{:S(2)}, u32[]{:S(2)}) collective-permute-start(bf16[16,32,2560]{2,1,0:T(8,128)(2,1)} %get-tuple-element.312), channel_id=1, source_target_pairs={{0,8},{1,9},{2,10},{3,11},{4,12},{5,13},{6,14},{7,15},{8,0},{9,1},... | collective-permute-start | bytes 7864328 | tf_op jit(solution)/shard_map/ppermute | solution.py:638
  391.5 4.6 copy-start.5
  394.8 20.1 %collective-permute-start.25 = (bf16[4,32,4096]{2,1,0:T(8,128)(2,1)}, bf16[4,32,4096]{2,1,0:T(8,128)(2,1)}, u32[]{:S(2)}, u32[]{:S(2)}) collective-permute-start(bf16[4,32,4096]{2,1,0:T(8,128)(2,1)} %get-tuple-element.396), channel_id=1, source_target_pairs={{0,1},{1,0},{2,3},{3,2},{4,5},{5,4},{6,7},{7,6},{8,24},{9,25},{10,... | collective-permute-start | bytes 3145736 | tf_op jit(solution)/shard_map/ppermute | solution.py:638
  398.0 55.1 %collective-permute-start.34 = (bf16[1,128,1024]{2,1,0:T(8,128)(2,1)}, bf16[1,128,1024]{2,1,0:T(8,128)(2,1)}, u32[]{:S(2)}, u32[]{:S(2)}) collective-permute-start(bf16[1,128,1024]{2,1,0:T(8,128)(2,1)} %get-tuple-element.414), channel_id=1, source_target_pairs={{0,4},{1,5},{2,6},{3,7},{4,0},{5,1},{6,2},{7,3},{8,12},{9,13},{10,... | collective-permute-start | bytes 786440 | tf_op jit(solution)/shard_map/ppermute | solution.py:638
  409.7 8.2 %collective-permute-start.26 = (bf16[16,32,1536]{2,1,0:T(8,128)(2,1)}, bf16[16,32,1536]{2,1,0:T(8,128)(2,1)S(1)}, u32[]{:S(2)}, u32[]{:S(2)}) collective-permute-start(bf16[16,32,1536]{2,1,0:T(8,128)(2,1)} %get-tuple-element.321), channel_id=1, source_target_pairs={{0,8},{1,9},{2,10},{3,11},{4,12},{5,13},{6,14},{7,15},{8,0},{9,1},... | collective-permute-start | bytes 4718600 | tf_op jit(solution)/shard_map/ppermute | solution.py:638
  414.2 3.7 copy-start.6
  414.2 18.3 %collective-permute-start.27 = (bf16[8,32,2560]{2,1,0:T(8,128)(2,1)}, bf16[8,32,2560]{2,1,0:T(8,128)(2,1)}, u32[]{:S(2)}, u32[]{:S(2)}) collective-permute-start(bf16[8,32,2560]{2,1,0:T(8,128)(2,1)} %get-tuple-element.394), channel_id=1, source_target_pairs={{0,16},{1,17},{2,18},{3,19},{4,20},{5,21},{6,22},{7,23},{8,9},{9,8... | collective-permute-start | bytes 3932168 | tf_op jit(solution)/shard_map/ppermute | solution.py:638
  417.3 17.6 %collective-permute-start.28 = (bf16[2,32,4096]{2,1,0:T(8,128)(2,1)}, bf16[2,32,4096]{2,1,0:T(8,128)(2,1)}, u32[]{:S(2)}, u32[]{:S(2)}) collective-permute-start(bf16[2,32,4096]{2,1,0:T(8,128)(2,1)} %get-tuple-element.404), channel_id=1, source_target_pairs={{0,2},{1,3},{2,0},{3,1},{4,6},{5,7},{6,4},{7,5},{8,10},{9,11},{10,... | collective-permute-start | bytes 1572872 | tf_op jit(solution)/shard_map/ppermute | solution.py:638
  418.4 25.3 %collective-permute-start.29 = (bf16[8,32,1536]{2,1,0:T(8,128)(2,1)S(1)}, bf16[8,32,1536]{2,1,0:T(8,128)(2,1)}, u32[]{:S(2)}, u32[]{:S(2)}) collective-permute-start(bf16[8,32,1536]{2,1,0:T(8,128)(2,1)S(1)} %get-tuple-element.400), channel_id=1, source_target_pairs={{0,16},{1,17},{2,18},{3,19},{4,20},{5,21},{6,22},{7,23},{8,9},{9,8... | collective-permute-start | bytes 2359304 | tf_op jit(solution)/shard_map/ppermute | solution.py:638
  432.3 2.6 copy-start.4
  432.4 13.5 %collective-permute-start.30 = (f32[16,9,128]{2,1,0:T(8,128)S(1)}, f32[16,9,128]{2,1,0:T(8,128)S(1)}, u32[]{:S(2)}, u32[]{:S(2)}) collective-permute-start(f32[16,9,128]{2,1,0:T(8,128)S(1)} %get-tuple-element.423), channel_id=1, source_target_pairs={{0,8},{1,9},{2,10},{3,11},{4,12},{5,13},{6,14},{7,15},{8,0},{9,1},... | collective-permute-start | bytes 221192 | tf_op jit(solution)/shard_map/ppermute | solution.py:638
  434.1 13.0 %collective-permute-start.31 = (bf16[4,32,2560]{2,1,0:T(8,128)(2,1)S(1)}, bf16[4,32,2560]{2,1,0:T(8,128)(2,1)S(1)}, u32[]{:S(2)}, u32[]{:S(2)}) collective-permute-start(bf16[4,32,2560]{2,1,0:T(8,128)(2,1)S(1)} %get-tuple-element.402), channel_id=1, source_target_pairs={{0,1},{1,0},{2,3},{3,2},{4,5},{5,4},{6,7},{7,6},{8,24},{9,25},{10,... | collective-permute-start | bytes 1966088 | tf_op jit(solution)/shard_map/ppermute | solution.py:638
  436.1 16.2 %collective-permute-start.33 = (bf16[1,32,4096]{2,1,0:T(8,128)(2,1)S(1)}, bf16[1,32,4096]{2,1,0:T(8,128)(2,1)S(1)}, u32[]{:S(2)}, u32[]{:S(2)}) collective-permute-start(bf16[1,32,4096]{2,1,0:T(8,128)(2,1)S(1)} %get-tuple-element.412), channel_id=1, source_target_pairs={{0,4},{1,5},{2,6},{3,7},{4,0},{5,1},{6,2},{7,3},{8,12},{9,13},{10,... | collective-permute-start | bytes 786440 | tf_op jit(solution)/shard_map/ppermute | solution.py:638
  445.0 10.0 %collective-permute-start.35 = (bf16[4,32,1536]{2,1,0:T(8,128)(2,1)S(1)}, bf16[4,32,1536]{2,1,0:T(8,128)(2,1)S(1)}, u32[]{:S(2)}, u32[]{:S(2)}) collective-permute-start(bf16[4,32,1536]{2,1,0:T(8,128)(2,1)S(1)} %get-tuple-element.408), channel_id=1, source_target_pairs={{0,1},{1,0},{2,3},{3,2},{4,5},{5,4},{6,7},{7,6},{8,24},{9,25},{10,... | collective-permute-start | bytes 1179656 | tf_op jit(solution)/shard_map/ppermute | solution.py:638
  445.9 5.1 %collective-permute-start.32 = (f32[8,9,128]{2,1,0:T(8,128)S(1)}, f32[8,9,128]{2,1,0:T(8,128)S(1)}, u32[]{:S(2)}, u32[]{:S(2)}) collective-permute-start(f32[8,9,128]{2,1,0:T(8,128)S(1)} %get-tuple-element.422), channel_id=1, source_target_pairs={{0,16},{1,17},{2,18},{3,19},{4,20},{5,21},{6,22},{7,23},{8,9},{9,8... | collective-permute-start | bytes 110600 | tf_op jit(solution)/shard_map/ppermute | solution.py:638
  447.3 10.9 %collective-permute-start.37 = (bf16[2,32,2560]{2,1,0:T(8,128)(2,1)S(1)}, bf16[2,32,2560]{2,1,0:T(8,128)(2,1)S(1)}, u32[]{:S(2)}, u32[]{:S(2)}) collective-permute-start(bf16[2,32,2560]{2,1,0:T(8,128)(2,1)S(1)} %get-tuple-element.410), channel_id=1, source_target_pairs={{0,2},{1,3},{2,0},{3,1},{4,6},{5,7},{6,4},{7,5},{8,10},{9,11},{10,... | collective-permute-start | bytes 983048 | tf_op jit(solution)/shard_map/ppermute | solution.py:638
  451.0 4.1 collective-permute-start.36
  455.0 7.9 %collective-permute-start.39 = (bf16[2,32,1536]{2,1,0:T(8,128)(2,1)S(1)}, bf16[2,32,1536]{2,1,0:T(8,128)(2,1)S(1)}, u32[]{:S(2)}, u32[]{:S(2)}) collective-permute-start(bf16[2,32,1536]{2,1,0:T(8,128)(2,1)S(1)} %get-tuple-element.416), channel_id=1, source_target_pairs={{0,2},{1,3},{2,0},{3,1},{4,6},{5,7},{6,4},{7,5},{8,10},{9,11},{10,... | collective-permute-start | bytes 589832 | tf_op jit(solution)/shard_map/ppermute | solution.py:638
  455.1 7.7 %collective-permute-start.38 = (f32[2,9,128]{2,1,0:T(8,128)S(1)}, f32[2,9,128]{2,1,0:T(8,128)S(1)}, u32[]{:S(2)}, u32[]{:S(2)}) collective-permute-start(f32[2,9,128]{2,1,0:T(8,128)S(1)} %get-tuple-element.428), channel_id=1, source_target_pairs={{0,2},{1,3},{2,0},{3,1},{4,6},{5,7},{6,4},{7,5},{8,10},{9,11},{10,... | collective-permute-start | bytes 27656 | tf_op jit(solution)/shard_map/ppermute | solution.py:638
  458.3 13.5 %collective-permute-start.41 = (bf16[1,32,2560]{2,1,0:T(8,128)(2,1)S(1)}, bf16[1,32,2560]{2,1,0:T(8,128)(2,1)S(1)}, u32[]{:S(2)}, u32[]{:S(2)}) collective-permute-start(bf16[1,32,2560]{2,1,0:T(8,128)(2,1)S(1)} %get-tuple-element.418), channel_id=1, source_target_pairs={{0,4},{1,5},{2,6},{3,7},{4,0},{5,1},{6,2},{7,3},{8,12},{9,13},{10,... | collective-permute-start | bytes 491528 | tf_op jit(solution)/shard_map/ppermute | solution.py:638
  462.8 7.9 %collective-permute-start.40 = (f32[1,9,128]{2,1,0:T(8,128)S(1)}, f32[1,9,128]{2,1,0:T(8,128)S(1)}, u32[]{:S(2)}, u32[]{:S(2)}) collective-permute-start(f32[1,9,128]{2,1,0:T(8,128)S(1)} %get-tuple-element.430), channel_id=1, source_target_pairs={{0,4},{1,5},{2,6},{3,7},{4,0},{5,1},{6,2},{7,3},{8,12},{9,13},{10,... | collective-permute-start | bytes 13832 | tf_op jit(solution)/shard_map/ppermute | solution.py:638
  463.0 9.7 %collective-permute-start.42 = (bf16[1,32,1536]{2,1,0:T(8,128)(2,1)S(1)}, bf16[1,32,1536]{2,1,0:T(8,128)(2,1)S(1)}, u32[]{:S(2)}, u32[]{:S(2)}) collective-permute-start(bf16[1,32,1536]{2,1,0:T(8,128)(2,1)S(1)} %get-tuple-element.420), channel_id=1, source_target_pairs={{0,4},{1,5},{2,6},{3,7},{4,0},{5,1},{6,2},{7,3},{8,12},{9,13},{10,... | collective-permute-start | bytes 294920 | tf_op jit(solution)/shard_map/ppermute | solution.py:638
  472.8 0.7 copy-start.14
  (2 other events, 1.1 us)

commit v9 on v8

--- a/solution.py
+++ b/solution.py
@@ -41,6 +41,23 @@
     return centre * inv, inv
 
 
+def masked(values, mask):
+    rows, width = values.shape
+
+    def body(v_ref, m_ref, o_ref):
+        o_ref[...] = v_ref[...].astype(jnp.float32) * m_ref[...]
+
+    return call(
+        body,
+        grid=(1,),
+        in_specs=[whole((rows, width)), whole((rows, 1))],
+        out_specs=whole((rows, width)),
+        out_shape=jax.ShapeDtypeStruct((rows, width), jnp.float32),
+        name="masked",
+        cover=True,
+    )(values, mask)
+
+
 def norm_project(x, gain, shift, weight, bias, tn, cols):
     rows, width = x.shape
 
@@ -71,7 +88,7 @@
     )(x, gain, shift, weight, bias)
 
 
-def attention(qkv):
+def attention(qkv, mover=None):
     rows, width = qkv.shape[0], qkv.shape[1] // 3
     pairs = width // (2 * HEAD_DIM)
     span = 2 * HEAD_DIM
@@ -96,18 +113,20 @@
         l_ref[0, 0:1, :] = turned[0:1, :]
         l_ref[0, 1:2, :] = turned[HEAD_DIM : HEAD_DIM + 1, :]
 
-    col = lambda base: pl.BlockSpec((rows, span), lambda j: (0, base + j))
-    return call(
-        body,
-        grid=(pairs,),
-        in_specs=[col(0), col(pairs), col(2 * pairs)],
-        out_specs=[col(0), pl.BlockSpec((1, 8, rows), lambda j: (j, 0, 0))],
-        out_shape=[
+    col = lambda base: pl.BlockSpec((rows, span), lambda j, *_: (0, base + j))
+    return riding(
+        body,
+        mover,
+        (pairs,),
+        [col(0), col(pairs), col(2 * pairs)],
+        [col(0), pl.BlockSpec((1, 8, rows), lambda j, *_: (j, 0, 0))],
+        [
             jax.ShapeDtypeStruct((rows, width), jnp.bfloat16),
             jax.ShapeDtypeStruct((pairs, 8, rows), jnp.float32),
         ],
-        name="attention",
-    )(qkv, qkv, qkv)
+        "attention",
+        (qkv, qkv, qkv),
+    )
 
 
 def attention_back(qkv, logs, d_o, first_pair, pairs, cover=True):
@@ -163,12 +182,12 @@
     )(qkv, qkv, qkv, logs, d_o)
 
 
-def project_norm(o, weight, bias, x, gain, shift, at):
+def project_norm(o, packed, r_in, block, bias, x, gain, shift):
     rows, width = o.shape
     tm = rows // 2
 
     def body(o_ref, w_ref, b_ref, x_ref, g_ref, s_ref, x1_ref, a_ref):
-        x1 = x_ref[...].astype(jnp.float32) + (dot(o_ref[...], w_ref[...]) + b_ref[...])
+        x1 = x_ref[...].astype(jnp.float32) + (dot(o_ref[...], flat(w_ref)) + b_ref[...])
         x1_ref[...] = x1
         xhat, _ = row_stats(x1)
         a_ref[...] = (xhat * g_ref[...] + s_ref[...]).astype(jnp.bfloat16)
@@ -178,31 +197,36 @@
     return call(
         body,
         grid=(rows // tm,),
-        in_specs=[rowblk, pl.BlockSpec((width, width), lambda i: (0, at // width)), vec, rowblk, vec, vec],
+        in_specs=[rowblk, rows_spec(packed, r_in, block), vec, rowblk, vec, vec],
         out_specs=[rowblk, rowblk],
         out_shape=[
             jax.ShapeDtypeStruct((rows, width), jnp.float32),
             jax.ShapeDtypeStruct((rows, width), jnp.bfloat16),
         ],
         name="project_norm",
-    )(o, weight, bias, x, gain, shift)
+    )(o, packed, bias, x, gain, shift)
 
 
 def flat(ref):
     return ref[...].reshape(-1, ref.shape[-1])
 
 
+def rows_spec(packed, r_in, block):
+    n, _, width = packed.shape
+    return pl.BlockSpec((n, r_in, width), lambda *_: (0, block, 0))
+
+
 def up_spec(packed, r_in):
     n, _, width = packed.shape
-    return pl.BlockSpec((n, r_in, width), lambda j: (0, j, 0))
-
-
-def down_spec(packed, r_ff):
-    width = packed.shape[2]
-    return pl.BlockSpec((width // r_ff, r_ff, width), lambda j: (j, 1, 0))
-
-
-def feed_forward(a, packed, r_in, r_ff, up_bias, down_bias, x1):
+    return pl.BlockSpec((n, r_in, width), lambda j, *_: (0, j, 0))
+
+
+def down_spec(packed):
+    _, r_ff, width = packed.shape
+    return pl.BlockSpec((width // r_ff, r_ff, width), lambda j: (j, 0, 0))
+
+
+def feed_forward(a, up, down, r_in, up_bias, down_bias, x1):
     rows, width = a.shape
     hidden = up_bias.shape[1]
     tf = width
@@ -231,9 +255,9 @@
         grid=(steps,),
         in_specs=[
             whole((rows, width)),
-            up_spec(packed, r_in),
+            up_spec(up, r_in),
             pl.BlockSpec((1, tf), lambda j: (0, j)),
-            down_spec(packed, r_ff),
+            down_spec(down),
             whole((1, width)),
             whole((rows, width)),
         ],
@@ -249,10 +273,10 @@
         ],
         scratch_shapes=[pltpu.VMEM((rows, width), jnp.float32)],
         name="feed_forward",
-    )(a, packed, up_bias, packed, down_bias, x1)
-
-
-def feed_forward_in(a, packed, r_in, up_bias):
+    )(a, up, up_bias, down, down_bias, x1)
+
+
+def feed_forward_in(a, up, r_in, up_bias, mover=None):
     rows, width = a.shape
     hidden = up_bias.shape[1]
 
@@ -262,22 +286,24 @@
         g_ref[...] = (u * phi).astype(jnp.bfloat16)
         gp_ref[...] = (phi + (u * RSQRT_2PI) * bell).astype(jnp.bfloat16)
 
-    block = pl.BlockSpec((rows, width), lambda j: (0, j))
-    return call(
-        body,
-        grid=(hidden // width,),
-        in_specs=[
+    block = pl.BlockSpec((rows, width), lambda j, *_: (0, j))
+    return riding(
+        body,
+        mover,
+        (hidden // width,),
+        [
             whole((rows, width)),
-            up_spec(packed, r_in),
-            pl.BlockSpec((1, width), lambda j: (0, j)),
-        ],
-        out_specs=[block, block],
-        out_shape=[jax.ShapeDtypeStruct((rows, hidden), jnp.bfloat16)] * 2,
-        name="feed_forward_in",
-    )(a, packed, up_bias)
-
-
-def feed_forward_out(g, packed, r_ff, down_bias, x1):
+            up_spec(up, r_in),
+            pl.BlockSpec((1, width), lambda j, *_: (0, j)),
+        ],
+        [block, block],
+        [jax.ShapeDtypeStruct((rows, hidden), jnp.bfloat16)] * 2,
+        "feed_forward_in",
+        (a, up, up_bias),
+    )
+
+
+def feed_forward_out(g, down, down_bias, x1):
     rows, width = x1.shape
     steps = g.shape[1] // width
 
@@ -299,7 +325,7 @@
         grid=(steps,),
         in_specs=[
             pl.BlockSpec((rows, width), lambda j: (0, j)),
-            down_spec(packed, r_ff),
+            down_spec(down),
             whole((1, width)),
             whole((rows, width)),
         ],
@@ -307,10 +333,10 @@
         out_shape=jax.ShapeDtypeStruct((rows, width), jnp.bfloat16),
         scratch_shapes=[pltpu.VMEM((rows, width), jnp.float32)],
         name="feed_forward_out",
-    )(g, packed, down_bias, x1)
-
-
-def feed_forward_back(dy, gp, packed, r_in, r_ff, x1, gain, w_out, at):
+    )(g, down, down_bias, x1)
+
+
+def feed_forward_back(dy, gp, up, down, r_in, x1, gain, block):
     rows, width = dy.shape
     hidden = gp.shape[1]
     tf = width
@@ -348,7 +374,7 @@
             low = dx1.astype(jnp.bfloat16)
             da_ref[...] = low
             cda_ref[...] = jnp.sum(low.astype(jnp.float32), axis=0, keepdims=True)
-            do_ref[...] = dot(low, w_ref[...], NT).astype(jnp.bfloat16)
+            do_ref[...] = dot(low, flat(w_ref), NT).astype(jnp.bfloat16)
 
     full = whole((rows, width))
     vec = whole((1, width))
@@ -359,11 +385,11 @@
         in_specs=[
             full,
             pl.BlockSpec((rows, tf), lambda j: (0, j)),
-            down_spec(packed, r_ff),
-            up_spec(packed, r_in),
+            down_spec(down),
+            up_spec(up, r_in),
             full,
             vec,
-            pl.BlockSpec((width, width), lambda j: (0, at // width)),
+            rows_spec(up, r_in, block),
         ],
         out_specs=[
             full,
@@ -392,7 +418,7 @@
         scratch_shapes=[pltpu.VMEM((rows, width), jnp.float32)],
         name="feed_forward_back",
         cover=True,
-    )(dy, gp, packed, packed, x1, gain, w_out)
+    )(dy, gp, down, up, x1, gain, up)
 
 
 def project_back(grads, weight, x, gain, dx1, extra, dtypes):
@@ -456,6 +482,7 @@
             jax.ShapeDtypeStruct((1, width), jnp.float32),
         ],
         name="project_back",
+        cover=True,
     )(*args)
 
 
@@ -649,20 +676,55 @@
         self.last = arrays
 
 
-def place_shards(pieces, table_row, shape, rows_at, rows, into=None, cover=False):
-    count = sum(a.shape[0] for a, _ in pieces)
-    cols = shape[-1]
-
-    def body(t_ref, *refs):
-        ins, out, (buf, in_sem, out_sem) = refs[: len(pieces)], refs[-4], refs[-3:]
+class Mover:
+    def __init__(self, pieces, table, shape, into=None):
+        self.pieces, self.table, self.into = pieces, table, into
+        self.args = [p[0] for p in pieces] + ([] if into is None else [into])
+        self.specs = [pl.BlockSpec(memory_space=pl.ANY)] * len(self.args)
+        self.out_spec = pl.BlockSpec(memory_space=pl.ANY)
+        self.out_shape = jax.ShapeDtypeStruct(shape, jnp.bfloat16)
+        counts = [p[0].shape[0] for p in pieces]
+        self.scratch = [
+            pltpu.VMEM((k, p[3], shape[-1]), jnp.bfloat16) for k, p in zip(counts, pieces)
+        ] + [pltpu.SemaphoreType.DMA((sum(counts),))] * 2
+
+    def copies(self, t_ref, ins, out, scratch):
         loads, stores = [], []
-        for ref, (array, first) in zip(ins, pieces):
+        in_sem, out_sem = scratch[-2:]
+        for ref, buf, (array, first, rows_at, rows) in zip(ins, scratch, self.pieces):
             for k in range(array.shape[0]):
                 i = len(loads)
-                source = ref.at[k, :, 0:cols]
-                loads.append(pltpu.make_async_copy(source, buf.at[i], in_sem.at[i]))
+                source = ref.at[k, :, 0 : buf.shape[-1]]
+                loads.append(pltpu.make_async_copy(source, buf.at[k], in_sem.at[i]))
                 target = out.at[t_ref[first + k], rows_at : rows_at + rows]
-                stores.append(pltpu.make_async_copy(buf.at[i], target, out_sem.at[i]))
+                stores.append(pltpu.make_async_copy(buf.at[k], target, out_sem.at[i]))
+        return loads, stores
+
+    def ride(self, step, last, *refs):
+        loads, stores = self.copies(*refs)
+
+        @pl.when(step == 0)
+        def _():
+            for c in loads:
+                c.start()
+
+        @pl.when(step == 1)
+        def _():
+            for a, b in zip(loads, stores):
+                a.wait()
+                b.start()
+
+        @pl.when(step == last)
+        def _():
+            for c in stores:
+                c.wait()
+
+
+def place_shards(mover, cover=False):
+    count = len(mover.args)
+
+    def body(t_ref, *refs):
+        loads, stores = mover.copies(t_ref, refs, refs[count], refs[count + 1 :])
         for c in loads:
             c.start()
         for a, b in zip(loads, stores):
@@ -671,22 +733,47 @@
         for b in stores:
             b.wait()
 
-    anywhere = pl.BlockSpec(memory_space=pl.ANY)
-    args = [a for a, _ in pieces] + ([] if into is None else [into])
-    return call(
-        body,
-        out_shape=jax.ShapeDtypeStruct(shape, jnp.bfloat16),
+    return call(
+        body,
+        out_shape=mover.out_shape,
         grid_spec=pltpu.PrefetchScalarGridSpec(
             num_scalar_prefetch=1,
-            in_specs=[anywhere] * len(args),
-            out_specs=anywhere,
-            scratch_shapes=[pltpu.VMEM((count, rows, cols), jnp.bfloat16)]
-            + [pltpu.SemaphoreType.DMA((count,))] * 2,
+            in_specs=mover.specs,
+            out_specs=mover.out_spec,
+            scratch_shapes=mover.scratch,
         ),
-        input_output_aliases={} if into is None else {len(args): 0},
+        input_output_aliases={} if mover.into is None else {count: 0},
         name="place_shards",
         cover=cover,
-    )(table_row, *args)
+    )(mover.table, *mover.args)
+
+
+def riding(body, mover, grid, in_specs, out_specs, out_shape, name, args):
+    if mover is None:
+        return call(
+            body, grid=grid, in_specs=in_specs, out_specs=out_specs, out_shape=out_shape, name=name
+        )(*args)
+    ins, outs, extra = len(in_specs), len(out_specs), len(mover.args)
+
+    def both(t_ref, *refs):
+        own = refs[:ins] + refs[ins + extra : ins + extra + outs]
+        moved = refs[ins : ins + extra], refs[ins + extra + outs], refs[ins + extra + outs + 1 :]
+        mover.ride(pl.program_id(0), grid[0] - 1, t_ref, *moved)
+        body(*own)
+
+    return call(
+        both,
+        grid_spec=pltpu.PrefetchScalarGridSpec(
+            num_scalar_prefetch=1,
+            grid=grid,
+            in_specs=in_specs + mover.specs,
+            out_specs=out_specs + [mover.out_spec],
+            scratch_shapes=mover.scratch,
+        ),
+        out_shape=out_shape + [mover.out_shape],
+        input_output_aliases={} if mover.into is None else {ins + extra: outs},
+        name=name,
+    )(mover.table, *args, *mover.args)
 
 
 def pack_shard(matrices, vectors):
@@ -853,22 +940,24 @@
     sizes = [v.shape[0] for v in vectors]
     line = Line()
     qkv_cols = w_qkv.shape[1]
-    cols = qkv_cols + w_out.shape[1]
-    ahead = pack_shard([w_qkv, w_out], vectors)
+    ahead = pack_shard([w_qkv], vectors)
     split = w_up.reshape(r_in, hidden // width, width).swapaxes(0, 1).reshape(r_ff, width)
+    split = jnp.concatenate([split, w_out], axis=0)
+    out_at = hidden // width
 
     class Gather:
         def __init__(self, shard):
+            self.perms, self.rows = gather_perms, shard.shape[0]
             self.held, self.stage = shard[None], 0
             (self.held,) = line.after(self.held)
-            self.got = send(self.held, gather_perms[0])
+            self.got = send(self.held, self.perms[0])
 
         def step(self):
             mine, theirs = line.after(self.held, self.got)
             self.held = jnp.concatenate([mine, theirs], axis=0)
             line.mark(self.held)
             self.stage += 1
-            self.got = send(self.held, gather_perms[self.stage])
+            self.got = send(self.held, self.perms[self.stage])
             if self.stage == stages - 1:
                 self.early = send(self.held, core_perm)
 
@@ -876,94 +965,94 @@
             (self.got,) = line.after(self.got)
             self.late = send(self.got, core_perm)
 
-        def place(self, which, *where, into=None, cover=False):
+        def pieces(self, which):
             quarter = n // 4
             pair = (self.got, self.late) if which else (self.held, self.early)
             pair = line.after(*pair)
-            pieces = [(pair[0], which * quarter), (pair[1], half + which * quarter)]
-            out = place_shards(pieces, row, *where, into=into, cover=cover)
-            line.mark(out)
-            return out
+            firsts = which * quarter, half + which * quarter
+            return [(a, f, 0, self.rows) for a, f in zip(pair, firsts)]
+
+    def place(pieces, shape, into=None, cover=False):
+        out = place_shards(Mover(pieces, row, shape, into), cover)
+        line.mark(out)
+        return out
 
     half = n // 2
+    ff_shape, first_shape = (n, r_ff, width), (n, r_in, qkv_cols)
+    mid_shape = (n, r_ff + r_in, width)
     chain_a = Gather(ahead)
     for k in range(1, stages - 2):
         chain_a.step()
     chain_b = Gather(split)
     chain_a.step()
+    keep_mask = valid[0].astype(jnp.float32)[:, None]
+    grad_second = masked(*line.after(cot_second[0]), keep_mask)
+    line.mark(grad_second)
     for k in range(1, stages - 2):
         chain_b.step()
     chain_a.step()
     chain_b.step()
     chain_c = Gather(w_down)
-    spot_a = ((n, r_in, cols), 0, r_in)
-    first = chain_a.place(0, *spot_a, cover=True)
+    chain_a.finish()
+    first = place(chain_a.pieces(0), first_shape)
+    first = place(chain_a.pieces(1), first_shape, first)
     for k in range(1, stages - 2):
         chain_c.step()
     chain_b.step()
-    chain_a.finish()
-    first = chain_a.place(1, *spot_a, into=first)
-    w = {"first": first.reshape(n * r_in, cols)}
+    w = {"qkv": first.reshape(n * r_in, qkv_cols)}
     g1, s1, bqkv, bo, g2, s2, bd, bu = unpack_vectors(
         (chain_a.held, chain_a.got, chain_a.early, chain_a.late),
-        cols,
+        qkv_cols,
         inverse_row,
         sizes,
         [[0], [1], [2, None, 3], [4], [5], [6], [7], [8]],
     )
-    spot_b = ((n, 2 * r_ff, width), 0, r_ff)
-    spot_c = ((n, 2 * r_ff, width), r_ff, r_ff)
-
-    def more(index):
-        if index == 0:
-            chain_c.step()
-        if index == 1:
-            chain_b.finish()
-        if index == 2:
-            chain_c.step()
-            ff = chain_b.place(0, *spot_b)
-            w["ff"] = chain_b.place(1, *spot_b, into=ff)
-        if index == 3:
-            ff = chain_c.place(0, *spot_c, into=w["ff"])
-            chain_c.finish()
-            w["ff"] = chain_c.place(1, *spot_c, into=ff)
-
-    def forward(x, more=None):
-        a1, qkv = norm_project(*line.after(x), g1, s1, w["first"], bqkv, qkv_cols // 2, qkv_cols)
-        line.mark(a1)
-        if more:
-            more(0)
+    def attend(qkv):
+        chain_c.step()
         o, logs = attention(*line.after(qkv))
         line.mark(o)
-        if more:
-            more(1)
-        x1, a2 = project_norm(*line.after(o), w["first"], bo, x, g2, s2, qkv_cols)
+        up = place(chain_b.pieces(0), mid_shape)
+        chain_b.finish()
+        chain_c.step()
+        w["up"] = place(chain_b.pieces(1), mid_shape, up)
+        return o, logs
+
+    def feed(a2, x1):
+        g, gp = feed_forward_in(*line.after(a2), w["up"], r_in, bu)
+        line.mark(g)
+        down = place(chain_c.pieces(0), ff_shape)
+        chain_c.finish()
+        w["down"] = place(chain_c.pieces(1), ff_shape, down)
+        y = feed_forward_out(line.after(g)[0], w["down"], bd, x1)
+        return g, gp, y
+
+    def forward(x, gathering=False):
+        a1, qkv = norm_project(
+            *line.after(x), g1, s1, w["qkv"], bqkv, qkv_cols // 2, qkv_cols
+        )
+        line.mark(a1)
+        o, logs = attend(qkv) if gathering else attention(*line.after(qkv))
+        if not gathering:
+            line.mark(o)
+        x1, a2 = project_norm(*line.after(o), w["up"], r_in, out_at, bo, x, g2, s2)
         line.mark(a2)
-        if more:
-            more(2)
-        a2 = line.after(a2)[0]
-        if more is None:
-            g, gp, y = feed_forward(a2, w["ff"], r_in, r_ff, bu, bd, x1)
+        if gathering:
+            g, gp, y = feed(a2, x1)
         else:
-            g, gp = feed_forward_in(a2, w["ff"], r_in, bu)
-            line.mark(g)
-            more(3)
-            y = feed_forward_out(line.after(g)[0], w["ff"], r_ff, bd, x1)
+            g, gp, y = feed_forward(*line.after(a2), w["up"], w["down"], r_in, bu, bd, x1)
         line.mark(y)
         return y, (x, a1, qkv, logs, o, x1, a2, g, gp)
 
-    first, saved_first = forward(tokens[0], more)
+    first, saved_first = forward(tokens[0], True)
     second, saved_second = forward(first)
 
-    keep_mask = valid[0].astype(jnp.float32)[:, None]
-    grad_second = cot_second[0].astype(jnp.float32) * keep_mask
     pairs = width // (2 * HEAD_DIM)
     parts = 2
 
     def ff_back(dy, saved):
         x, a1, qkv, logs, o, x1, a2, g, gp = saved
         outs = feed_forward_back(
-            *line.after(dy), gp, w["ff"], r_in, r_ff, x1, g2, w["first"], qkv_cols
+            *line.after(dy), gp, w["up"], w["down"], r_in, x1, g2, out_at
         )
         line.mark(outs[0])
         return outs
@@ -977,7 +1066,7 @@
 
     def qkv_back(heads, saved, dx1, extra, dtypes):
         outs = project_back(
-            [line.after(h[0])[0] for h in heads], w["first"], saved[0], g1, dx1, extra, dtypes
+            [line.after(h[0])[0] for h in heads], w["qkv"], saved[0], g1, dx1, extra, dtypes
         )
         line.mark(outs[0])
         return outs

time: 478 us -> 475 us (level)
    pallas_call x12 -> x13, Pallas kernels: 88.3 us -> 92 us  [the longest x3 33.1 us: riding(): call(body, grid=grid, in_specs=in_specs, out_specs=out_specs, out_shape=o...]
    unnamed x60 -> x54, local copies, waits for them, and re-layouts: 11.8 us -> 8.66 us
  transfers between devices with their start and end apart: 43 -> 43, of which waited for: 17 -> 20; matrix products, arithmetic and copies ran while one was open for 9% -> 9% of each run, Pallas kernels for 33% -> 34%
where the time goes in v9:
time: 475 us; the launch traced here: 471 us
  Pallas kernels  277 us (58%)
  waiting for transfers between devices  89 us (19%)
  starting transfers between devices  44.4 us (9%)
  other arithmetic  37.1 us (8%)
  local copies, waits for them, and re-layouts  22.4 us (5%)
    ppermute x43, waiting for transfers between devices, send(): return lax.ppermute(x, AXES, perm)  89 us
    ppermute x43, starting transfers between devices, send(): return lax.ppermute(x, AXES, perm)  44.4 us
    pallas_call x2, Pallas kernels, feed_forward_back(): call(body, grid=(steps,), in_specs=[full, pl.BlockSpec((rows, tf), lambda...  40.5 us
    pallas_call x3, Pallas kernels, weight_grad(): call(body, grid_spec=pltpu.PrefetchScalarGridSpec(num_scalar_prefetch=1,...  38.4 us
    pallas_call x4, Pallas kernels, attention_back(): call(body, grid=(pairs,), in_specs=[col(first_pair), col(every + first_pa...  35.7 us
    pallas_call x3, Pallas kernels, riding(): call(body, grid=grid, in_specs=in_specs, out_specs=out_specs, out_shape=o...  33.1 us
    convert_element_type x16, other arithmetic, step(): self.kept = add(slice(0, half)).astype(wide)  31.7 us
    pallas_call x6, Pallas kernels, place_shards(): call(body, out_shape=mover.out_shape, grid_spec=pltpu.PrefetchScalarGridS...  28.2 us
  transfers between devices with their start and end apart: 43, of which 20 were waited for; matrix products, arithmetic and copies ran while one was open for 9% of the time, Pallas kernels for 34%

profile of v9, /device:TPU:0, one launch (start us, length us, event | category | flops | bytes accessed | tf_op | source)
XLA Modules:
  0.0 471.2 jit_solution(9334645569587401481)
XLA Ops:
  0.7 1.7 pack_shard.1
  2.4 4.0 collective-permute-start
  6.4 10.0 %collective-permute-done = bf16[1,32,3328]{2,1,0:T(8,128)(2,1)S(1)} collective-permute-done((bf16[1,32,3328]{2,1,0:T(8,128)(2,1)}, bf16[1,32,3328]{2,1,0:T(8,128)(2,1)S(1)}, u32[]{:S(2)}, u32[]{:S(2)}) %collective-permute-start) | collective-permute-done | bytes 213024 | tf_op jit(solution)/shard_map/ppermute | solution.py:665
  20.9 3.3 collective-permute-start.2
  24.2 10.6 %collective-permute-done.1 = bf16[2,32,3328]{2,1,0:T(8,128)(2,1)S(1)} collective-permute-done((bf16[2,32,3328]{2,1,0:T(8,128)(2,1)S(1)}, bf16[2,32,3328]{2,1,0:T(8,128)(2,1)S(1)}, u32[]{:S(2)}, u32[]{:S(2)}) %collective-permute-start.1) | collective-permute-done | bytes 426016 | tf_op jit(solution)/shard_map/ppermute | solution.py:665
  36.3 2.8 masked.1.dy_ref
  39.1 8.5 %collective-permute-done.3 = bf16[4,32,3328]{2,1,0:T(8,128)(2,1)S(1)} collective-permute-done((bf16[4,32,3328]{2,1,0:T(8,128)(2,1)S(1)}, bf16[4,32,3328]{2,1,0:T(8,128)(2,1)S(1)}, u32[]{:S(2)}, u32[]{:S(2)}) %collective-permute-start.3) | collective-permute-done | bytes 852000 | tf_op jit(solution)/shard_map/ppermute | solution.py:665
  49.1 13.7 %collective-permute-done.4 = bf16[2,160,1024]{2,1,0:T(8,128)(2,1)S(1)} collective-permute-done((bf16[2,160,1024]{2,1,0:T(8,128)(2,1)S(1)}, bf16[2,160,1024]{2,1,0:T(8,128)(2,1)S(1)}, u32[]{:S(2)}, u32[]{:S(2)}) %collective-permute-start.4) | collective-permute-done | bytes 655392 | tf_op jit(solution)/shard_map/ppermute | solution.py:665
  64.5 5.1 %collective-permute-done.6.refs_0_.refs_1_ = bf16[8,32,3328]{2,1,0:T(8,128)(2,1)S(1)} collective-permute-done((bf16[8,32,3328]{2,1,0:T(8,128)(2,1)S(1)}, bf16[8,32,3328]{2,1,0:T(8,128)(2,1)S(1)}, u32[]{:S(2)}, u32[]{:S(2)}) %collective-permute-start.6) | collective-permute-done | bytes 1703968 | tf_op jit(solution)/shard_map/ppermute | solution.py:665
  73.3 3.8 place_shards.6.refs_2_
  77.1 4.0 place_shards.7
  81.1 5.1 %collective-permute-done.8 = bf16[1,128,1024]{2,1,0:T(8,128)(2,1)} collective-permute-done((bf16[1,128,1024]{2,1,0:T(8,128)(2,1)}, bf16[1,128,1024]{2,1,0:T(8,128)(2,1)}, u32[]{:S(2)}, u32[]{:S(2)}) %collective-permute-start.8) | collective-permute-done | bytes 262176 | tf_op jit(solution)/shard_map/ppermute | solution.py:665
  91.9 2.4 unpack_vectors.1
  94.2 8.3 %norm_project.2 = (bf16[512,1024]{1,0:T(8,128)(2,1)}, bf16[512,3072]{1,0:T(8,128)(2,1)}) custom-call(bf16[512,1024]{1,0:T(8,128)(2,1)} %bitcast.67, f32[1,1024]{1,0:T(1,128)} %get-tuple-element.228.g_ref.refs_4_, f32[1,1024]{1,0:T(1,128)} %get-tuple-element.229.s_ref, bf16[1024,3072]{1,0:T(8,128)(2,1)} %bitcast.62, f32[1,3072]{1,0:T(1,128)} %get-tuple-element.230.b_ref), custom_call_target="tpu_custom_call" | custom-call | flops 1 | bytes 1 | tf_op jit(solution)/shard_map/norm_project/pallas_call | solution.py:72
  102.5 3.4 collective-permute-done.10
  106.8 1.9 constant_dynamic-update-slice_fusion.14
  109.4 10.8 %attention.2 = (bf16[512,1024]{1,0:T(8,128)(2,1)}, f32[8,8,512]{2,1,0:T(8,128)}) custom-call(bf16[512,3072]{1,0:T(8,128)(2,1)} %get-tuple-element.235.q_ref.k_ref.v_ref, bf16[512,3072]{1,0:T(8,128)(2,1)} %get-tuple-element.235.q_ref.k_ref.v_ref, bf16[512,3072]{1,0:T(8,128)(2,1)} %get-tuple-element.235.q_ref.k_ref.v_ref), custom_call_target="tpu_custom_call" | custom-call | flops 1 | bytes 1 | tf_op jit(solution)/shard_map/attention/pallas_call | solution.py:753
  120.2 5.6 %place_shards.8.refs_2_ = bf16[32,160,1024]{2,1,0:T(8,128)(2,1)} custom-call(s32[32]{0:T(128)} %get-tuple-element.446.t_ref, bf16[8,160,1024]{2,1,0:T(8,128)(2,1)} %copy-done.3, bf16[8,160,1024]{2,1,0:T(8,128)(2,1)} %collective-permute-done.11.refs_1_), custom_call_target="tpu_custom_call" | custom-call | flops 1 | bytes 1 | tf_op jit(solution)/shard_map/place_shards/pallas_call | solution.py:736
  125.8 7.3 %collective-permute-done.13.refs_0_ = bf16[8,160,1024]{2,1,0:T(8,128)(2,1)} collective-permute-done((bf16[8,160,1024]{2,1,0:T(8,128)(2,1)S(1)}, bf16[8,160,1024]{2,1,0:T(8,128)(2,1)}, u32[]{:S(2)}, u32[]{:S(2)}) %collective-permute-start.13) | collective-permute-done | bytes 2621472 | tf_op jit(solution)/shard_map/ppermute | solution.py:665
  138.4 5.6 %place_shards.9.w_ref.u_ref = bf16[32,160,1024]{2,1,0:T(8,128)(2,1)} custom-call(s32[32]{0:T(128)} %get-tuple-element.446.t_ref, bf16[8,160,1024]{2,1,0:T(8,128)(2,1)} %collective-permute-done.13.refs_0_, bf16[8,160,1024]{2,1,0:T(8,128)(2,1)} %collective-permute-done.14.refs_1_, ...), custom_call_target="tpu_custom_call", output_to_operand_aliasing={{}: (3, {})} | custom-call | flops 1 | bytes 1 | tf_op jit(solution)/shard_map/place_shards/pallas_call | solution.py:736
  144.0 4.9 %project_norm.2 = (f32[512,1024]{1,0:T(8,128)}, bf16[512,1024]{1,0:T(8,128)(2,1)}) custom-call(bf16[512,1024]{1,0:T(8,128)(2,1)} %get-tuple-element.309.o_ref.refs_0_, bf16[32,160,1024]{2,1,0:T(8,128)(2,1)} %place_shards.9.w_ref.u_ref, f32[1,1024]{1,0:T(1,128)} %get-tuple-element.245.b_ref, bf16[512,1024]{1,0:T(8,128)(2,1)} %bitcast.68, ...), custom_call_target="tpu_custom_call" | custom-call | flops 1 | bytes 1 | tf_op jit(solution)/shard_map/project_norm/pallas_call | solution.py:197
  148.9 11.4 %feed_forward_in.1 = (bf16[512,4096]{1,0:T(8,128)(2,1)}, bf16[512,4096]{1,0:T(8,128)(2,1)}) custom-call(bf16[512,1024]{1,0:T(8,128)(2,1)} %get-tuple-element.292.a_ref.refs_0_, bf16[32,160,1024]{2,1,0:T(8,128)(2,1)} %place_shards.9.w_ref.u_ref, f32[1,4096]{1,0:T(1,128)} %get-tuple-element.250.ub_ref), custom_call_target="tpu_custom_call" | custom-call | flops 1 | bytes 1 | tf_op jit(solution)/shard_map/feed_forward_in/pallas_call | solution.py:753
  160.3 4.7 place_shards.10.refs_2_
  167.8 1.6 collective-permute-done.17.refs_1_
  170.7 4.5 place_shards.11.d_ref
  175.3 9.7 %feed_forward_out.1.x_ref.refs_3_ = bf16[512,1024]{1,0:T(8,128)(2,1)} custom-call(bf16[512,4096]{1,0:T(8,128)(2,1)} %get-tuple-element.288.g_ref.refs_0_, bf16[32,128,1024]{2,1,0:T(8,128)(2,1)} %place_shards.11.d_ref, f32[1,1024]{1,0:T(1,128)} %get-tuple-element.258.db_ref, f32[512,1024]{1,0:T(8,128)} %get-tuple-element.259.x_ref), custom_call_target="tpu_custom_call" | custom-call | flops 1 | bytes 1 | tf_op jit(solution)/shard_map/feed_forward_out/pallas_call | solution.py:323
  184.9 7.7 %norm_project.3 = (bf16[512,1024]{1,0:T(8,128)(2,1)}, bf16[512,3072]{1,0:T(8,128)(2,1)}) custom-call(bf16[512,1024]{1,0:T(8,128)(2,1)} %feed_forward_out.1.x_ref.refs_3_, f32[1,1024]{1,0:T(1,128)} %get-tuple-element.228.g_ref.refs_4_, f32[1,1024]{1,0:T(1,128)} %get-tuple-element.229.s_ref, bf16[1024,3072]{1,0:T(8,128)(2,1)} %bitcast.63, ...), custom_call_target="tpu_custom_call" | custom-call | flops 1 | bytes 1 | tf_op jit(solution)/shard_map/norm_project/pallas_call | solution.py:72
  193.2 10.8 %attention.3 = (bf16[512,1024]{1,0:T(8,128)(2,1)}, f32[8,8,512]{2,1,0:T(8,128)}) custom-call(bf16[512,3072]{1,0:T(8,128)(2,1)} %get-tuple-element.261.q_ref.k_ref.v_ref, bf16[512,3072]{1,0:T(8,128)(2,1)} %get-tuple-element.261.q_ref.k_ref.v_ref, bf16[512,3072]{1,0:T(8,128)(2,1)} %get-tuple-element.261.q_ref.k_ref.v_ref), custom_call_target="tpu_custom_call" | custom-call | flops 1 | bytes 1 | tf_op jit(solution)/shard_map/attention/pallas_call | solution.py:753
  204.1 5.1 %project_norm.3 = (f32[512,1024]{1,0:T(8,128)}, bf16[512,1024]{1,0:T(8,128)(2,1)}) custom-call(bf16[512,1024]{1,0:T(8,128)(2,1)} %get-tuple-element.310.o_ref.refs_1_, bf16[32,160,1024]{2,1,0:T(8,128)(2,1)} %place_shards.9.w_ref.u_ref, f32[1,1024]{1,0:T(1,128)} %get-tuple-element.245.b_ref, bf16[512,1024]{1,0:T(8,128)(2,1)} %feed_forward_out.1.x_ref.refs_3_, ...), custom_call_target="tpu_custom_call" | custom-call | flops 1 | bytes 1 | tf_op jit(solution)/shard_map/project_norm/pallas_call | solution.py:197
  209.2 18.0 %feed_forward.1 = (bf16[512,4096]{1,0:T(8,128)(2,1)}, bf16[512,4096]{1,0:T(8,128)(2,1)}, bf16[512,1024]{1,0:T(8,128)(2,1)}) custom-call(bf16[512,1024]{1,0:T(8,128)(2,1)} %get-tuple-element.293.a_ref.refs_1_, bf16[32,160,1024]{2,1,0:T(8,128)(2,1)} %place_shards.9.w_ref.u_ref, f32[1,4096]{1,0:T(1,128)} %get-tuple-element.250.ub_ref, ...), custom_call_target="tpu_custom_call" | custom-call | flops 1 | bytes 1 | tf_op jit(solution)/shard_map/feed_forward/pallas_call | solution.py:253
  227.2 20.3 %feed_forward_back.2 = (bf16[512,1024]{1,0:T(8,128)(2,1)}, bf16[512,4096]{1,0:T(8,128)(2,1)}, f32[512,1024]{1,0:T(8,128)}, bf16[512,1024]{1,0:T(8,128)(2,1)}, bf...) custom-call(f32[512,1024]{1,0:T(8,128)} %masked.1.dy_ref, ...), custom_call_target="tpu_custom_call" | custom-call | flops 99999997952 | bytes 1 | tf_op jit(solution)/shard_map/feed_forward_back/pallas_call | solution.py:382
  247.4 8.9 %attention_back.4 = (bf16[3,512,512]{2,1,0:T(8,128)(2,1)}, f32[1,512]{1,0:T(1,128)}, f32[1,512]{1,0:T(1,128)}) custom-call(bf16[512,3072]{1,0:T(8,128)(2,1)} %get-tuple-element.261.q_ref.k_ref.v_ref, bf16[512,3072]{1,0:T(8,128)(2,1)} %get-tuple-element.261.q_ref.k_ref.v_ref, bf16[512,3072]{1,0:T(8,128)(2,1)} %get-tuple-element.261.q_ref.k_ref.v_ref, ...), custom_call_target="tpu_custom_call" | custom-call | flops 99999997952 | bytes 1 | tf_op jit(solution)/shard_map/attention_back/pallas_call | solution.py:164
  256.4 8.9 %attention_back.5 = (bf16[3,512,512]{2,1,0:T(8,128)(2,1)}, f32[1,512]{1,0:T(1,128)}, f32[1,512]{1,0:T(1,128)}) custom-call(bf16[512,3072]{1,0:T(8,128)(2,1)} %get-tuple-element.261.q_ref.k_ref.v_ref, bf16[512,3072]{1,0:T(8,128)(2,1)} %get-tuple-element.261.q_ref.k_ref.v_ref, bf16[512,3072]{1,0:T(8,128)(2,1)} %get-tuple-element.261.q_ref.k_ref.v_ref, ...), custom_call_target="tpu_custom_call" | custom-call | flops 99999997952 | bytes 1 | tf_op jit(solution)/shard_map/attention_back/pallas_call | solution.py:164
  265.3 10.4 %project_back.2 = (f32[512,1024]{1,0:T(8,128)}, bf16[512,1024]{1,0:T(8,128)(2,1)}, f32[1,1024]{1,0:T(1,128)}, f32[1,1024]{1,0:T(1,128)}) custom-call(bf16[3,512,512]{2,1,0:T(8,128)(2,1)} %get-tuple-element.278.refs_0_.refs_7_, bf16[3,512,512]{2,1,0:T(8,128)(2,1)} %get-tuple-element.279.refs_1_.refs_3_, bf16[1024,3072]{1,0:T(8,128)(2,1)} %bitcast.64, ...), custom_call_target="tpu_custom_call" | custom-call | flops 99999997952 | bytes 1 | tf_op jit(solution)/shard_map/project_back/pallas_call | solution.py:474
  275.7 9.3 %weight_grad_half.2 = bf16[16,128,1024]{2,1,0:T(8,128)(2,1)} custom-call(s32[18]{0:T(128)} %pad_add_fusion.2.i_ref, bf16[512,4096]{1,0:T(8,128)(2,1)} %get-tuple-element.288.g_ref.refs_0_, bf16[512,4096]{1,0:T(8,128)(2,1)} %get-tuple-element.289.refs_1_, bf16[512,1024]{1,0:T(8,128)(2,1)} %get-tuple-element.287.refs_2_, ...), custom_call_target="tpu_custom_call" | custom-call | flops 1 | bytes 1 | tf_op jit(solution)/shard_map/weight_grad_half/pallas_call | solution.py:605
  286.4 9.1 %weight_grad_half.3 = bf16[16,128,1024]{2,1,0:T(8,128)(2,1)} custom-call(s32[18]{0:T(128)} %pad_add_fusion.1.i_ref, bf16[512,4096]{1,0:T(8,128)(2,1)} %get-tuple-element.288.g_ref.refs_0_, bf16[512,4096]{1,0:T(8,128)(2,1)} %get-tuple-element.289.refs_1_, bf16[512,1024]{1,0:T(8,128)(2,1)} %get-tuple-element.287.refs_2_, ...), custom_call_target="tpu_custom_call" | custom-call | flops 1 | bytes 1 | tf_op jit(solution)/shard_map/weight_grad_half/pallas_call | solution.py:605
  295.5 5.5 %add_convert_fusion.2 = (bf16[8,128,1024]{2,1,0:T(8,128)(2,1)S(1)}, bf16[8,128,1024]{2,1,0:T(8,128)(2,1)}) fusion(bf16[16,128,1024]{2,1,0:T(8,128)(2,1)} %collective-permute-done.18, bf16[16,128,1024]{2,1,0:T(8,128)(2,1)} %weight_grad_half.3), kind=kLoop, calls=%fused_computation.3 | loop fusion | flops 8388608 | bytes 12582912 | tf_op jit(solution)/shard_map/convert_element_type | solution.py:902
  301.9 20.2 %feed_forward_back.3 = (bf16[512,1024]{1,0:T(8,128)(2,1)}, bf16[512,4096]{1,0:T(8,128)(2,1)}, f32[512,1024]{1,0:T(8,128)}, bf16[512,1024]{1,0:T(8,128)(2,1)}, bf...) custom-call(f32[512,1024]{1,0:T(8,128)} %get-tuple-element.294.dy_re, ...), custom_call_target="tpu_custom_call" | custom-call | flops 99999997952 | bytes 1 | tf_op jit(solution)/shard_map/feed_forward_back/pallas_call | solution.py:382
  322.1 16.2 %weight_grad.3 = (bf16[16,32,4096]{2,1,0:T(8,128)(2,1)}, bf16[16,32,4096]{2,1,0:T(8,128)(2,1)}) custom-call(s32[36]{0:T(128)} %pad_add_fusion.i_ref, bf16[512,1024]{1,0:T(8,128)(2,1)} %get-tuple-element.292.a_ref.refs_0_, bf16[512,1024]{1,0:T(8,128)(2,1)} %get-tuple-element.293.a_ref.refs_1_, bf16[512,4096]{1,0:T(8,128)(2,1)} %get-tuple-element.296.refs_2_, ...), custom_call_target="tpu_custom_call" | custom-call | flops 1 | bytes 1 | tf_op jit(solution)/shard_map/weight_grad/pallas_call | solution.py:558
  339.3 3.5 add_convert_fusion.8
  344.3 8.9 %attention_back.6 = (bf16[3,512,512]{2,1,0:T(8,128)(2,1)}, f32[1,512]{1,0:T(1,128)}, f32[1,512]{1,0:T(1,128)}) custom-call(bf16[512,3072]{1,0:T(8,128)(2,1)} %get-tuple-element.235.q_ref.k_ref.v_ref, bf16[512,3072]{1,0:T(8,128)(2,1)} %get-tuple-element.235.q_ref.k_ref.v_ref, bf16[512,3072]{1,0:T(8,128)(2,1)} %get-tuple-element.235.q_ref.k_ref.v_ref, ...), custom_call_target="tpu_custom_call" | custom-call | flops 99999997952 | bytes 1 | tf_op jit(solution)/shard_map/attention_back/pallas_call | solution.py:164
  353.2 4.6 collective-permute-done.20
  359.2 5.2 %add_convert_fusion = (bf16[8,32,4096]{2,1,0:T(8,128)(2,1)S(1)}, bf16[8,32,4096]{2,1,0:T(8,128)(2,1)}) fusion(bf16[16,32,4096]{2,1,0:T(8,128)(2,1)} %collective-permute-done.21, bf16[16,32,4096]{2,1,0:T(8,128)(2,1)} %get-tuple-element.307), kind=kLoop, calls=%fused_computation.1 | loop fusion | flops 8388608 | bytes 12582912 | tf_op jit(solution)/shard_map/convert_element_type | solution.py:902
  364.4 1.6 collective-permute-start.22
  365.9 13.7 %weight_grad.4 = (bf16[16,32,2560]{2,1,0:T(8,128)(2,1)}, bf16[16,32,2560]{2,1,0:T(8,128)(2,1)}) custom-call(s32[36]{0:T(128)} %pad_add_fusion.i_ref, bf16[512,1024]{1,0:T(8,128)(2,1)} %get-tuple-element.309.o_ref.refs_0_, bf16[512,1024]{1,0:T(8,128)(2,1)} %get-tuple-element.310.o_ref.refs_1_, bf16[512,1024]{1,0:T(8,128)(2,1)} %get-tuple-element.311.refs_2_, ...), custom_call_target="tpu_custom_call" | custom-call | flops 1 | bytes 1 | tf_op jit(solution)/shard_map/weight_grad/pallas_call | solution.py:558
  379.8 8.9 %attention_back.7 = (bf16[3,512,512]{2,1,0:T(8,128)(2,1)}, f32[1,512]{1,0:T(1,128)}, f32[1,512]{1,0:T(1,128)}) custom-call(bf16[512,3072]{1,0:T(8,128)(2,1)} %get-tuple-element.235.q_ref.k_ref.v_ref, bf16[512,3072]{1,0:T(8,128)(2,1)} %get-tuple-element.235.q_ref.k_ref.v_ref, bf16[512,3072]{1,0:T(8,128)(2,1)} %get-tuple-element.235.q_ref.k_ref.v_ref, ...), custom_call_target="tpu_custom_call" | custom-call | flops 1 | bytes 1 | tf_op jit(solution)/shard_map/attention_back/pallas_call | solution.py:164
  388.7 2.0 collective-permute-done.22
  390.7 3.4 add_convert_fusion.6
  395.6 2.0 add_convert_fusion.24
  398.5 8.5 %weight_grad.5 = (bf16[16,32,1536]{2,1,0:T(8,128)(2,1)}, bf16[16,32,1536]{2,1,0:T(8,128)(2,1)}) custom-call(s32[36]{0:T(128)} %pad_add_fusion.i_ref, bf16[512,1024]{1,0:T(8,128)(2,1)} %get-tuple-element.323.refs_4_.refs_0_, bf16[512,1024]{1,0:T(8,128)(2,1)} %get-tuple-element.324.refs_5_.refs_1_, bf16[3,512,512]{2,1,0:T(8,128)(2,1)} %get-tuple-element.335.refs_2_.refs_1_, ...), custom_call_target="tpu_custom_call" | custom-call | flops 99999997952 | bytes 1 | tf_op jit(solution)/shard_map/weight_grad/pallas_call | solution.py:558
  407.1 4.4 add_convert_fusion.4
  412.4 2.4 add_convert_fusion.14
  414.8 2.2 collective-permute-start.28
  419.0 9.3 %project_back.3 = (bf16[512,1024]{1,0:T(8,128)(2,1)}, f32[1,1024]{1,0:T(1,128)}, f32[1,1024]{1,0:T(1,128)}) custom-call(bf16[3,512,512]{2,1,0:T(8,128)(2,1)} %get-tuple-element.334.refs_6_.refs_0_, bf16[3,512,512]{2,1,0:T(8,128)(2,1)} %get-tuple-element.335.refs_2_.refs_1_, bf16[1024,3072]{1,0:T(8,128)(2,1)} %bitcast.65, bf16[512,1024]{1,0:T(8,128)(2,1)} %bitcast.69, ...), custom_call_target="tpu_custom_call" | custom-call | flops 99999997952 | bytes 1 | tf_op jit(solution)/shard_map/project_back/pallas_call | solution.py:474
  428.2 2.4 pack_sums.1
  431.8 1.7 add_convert_fusion.12
  434.4 4.5 collective-permute-done.29
  442.5 2.4 collective-permute-done.31
  445.1 2.8 collective-permute-start.37
  449.5 1.8 add_bitcast_fusion
  451.4 4.0 collective-permute-start.39
  457.6 4.7 %collective-permute-done.38 = f32[2,9,128]{2,1,0:T(8,128)S(1)} collective-permute-done((f32[2,9,128]{2,1,0:T(8,128)S(1)}, f32[2,9,128]{2,1,0:T(8,128)S(1)}, u32[]{:S(2)}, u32[]{:S(2)}) %collective-permute-start.38) | collective-permute-done | bytes 9248 | tf_op jit(solution)/shard_map/ppermute | solution.py:665
  462.7 2.7 collective-permute-start.42
  465.4 2.6 collective-permute-done.40
  (165 shorter events, 54.5 us)
Async XLA Ops:
  0.7 20.2 %copy-start.11 = (bf16[32,1024]{1,0:T(8,128)(2,1)S(1)}, bf16[32,1024]{1,0:T(8,128)(2,1)}, u32[]{:S(2)}) copy-start(bf16[32,1024]{1,0:T(8,128)(2,1)} %param.24) | copy-start | bytes 196612
  2.4 14.1 %collective-permute-start = (bf16[1,32,3328]{2,1,0:T(8,128)(2,1)}, bf16[1,32,3328]{2,1,0:T(8,128)(2,1)S(1)}, u32[]{:S(2)}, u32[]{:S(2)}) collective-permute-start(bf16[1,32,3328]{2,1,0:T(8,128)(2,1)} %bitcast.71), channel_id=1, source_target_pairs={{0,4},{1,5},{2,6},{3,7},{4,0},{5,1},{6,2},{7,3},{8,12},{9,13},{10,... | collective-permute-start | bytes 638984 | tf_op jit(solution)/shard_map/ppermute | solution.py:665
  17.4 17.3 %collective-permute-start.1 = (bf16[2,32,3328]{2,1,0:T(8,128)(2,1)S(1)}, bf16[2,32,3328]{2,1,0:T(8,128)(2,1)S(1)}, u32[]{:S(2)}, u32[]{:S(2)}) collective-permute-start(bf16[2,32,3328]{2,1,0:T(8,128)(2,1)S(1)} %constant_dynamic-update-slice_fusion), channel_id=1, source_target_pairs={{0,2},{1,3},{2,0},{3,1},{4,6},{5,7},{6,4},{7,5},{8,10},{9,11},{10,... | collective-permute-start | bytes 1277960 | tf_op jit(solution)/shard_map/ppermute | solution.py:665
  20.9 18.2 %collective-permute-start.2 = (bf16[1,160,1024]{2,1,0:T(8,128)(2,1)S(1)}, bf16[1,160,1024]{2,1,0:T(8,128)(2,1)S(1)}, u32[]{:S(2)}, u32[]{:S(2)}) collective-permute-start(bf16[1,160,1024]{2,1,0:T(8,128)(2,1)S(1)} %maximum_bitcast_fusion), channel_id=1, source_target_pairs={{0,4},{1,5},{2,6},{3,7},{4,0},{5,1},{6,2},{7,3},{8,12},{9,13},{10,... | collective-permute-start | bytes 983048 | tf_op jit(solution)/shard_map/ppermute | solution.py:665
  34.9 12.8 %collective-permute-start.3 = (bf16[4,32,3328]{2,1,0:T(8,128)(2,1)S(1)}, bf16[4,32,3328]{2,1,0:T(8,128)(2,1)S(1)}, u32[]{:S(2)}, u32[]{:S(2)}) collective-permute-start(bf16[4,32,3328]{2,1,0:T(8,128)(2,1)S(1)} %constant_dynamic-update-slice_fusion.2), channel_id=1, source_target_pairs={{0,1},{1,0},{2,3},{3,2},{4,5},{5,4},{6,7},{7,6},{8,24},{9,25},{10,... | collective-permute-start | bytes 2555912 | tf_op jit(solution)/shard_map/ppermute | solution.py:665
  47.7 25.5 %copy-start.1 = (bf16[8,32,3328]{2,1,0:T(8,128)(2,1)}, bf16[8,32,3328]{2,1,0:T(8,128)(2,1)S(1)}, u32[]{:S(2)}) copy-start(bf16[8,32,3328]{2,1,0:T(8,128)(2,1)S(1)} %constant_dynamic-update-slice_fusion.6.refs_0_) | copy-start | bytes 5111812
  47.7 21.9 %collective-permute-start.6 = (bf16[8,32,3328]{2,1,0:T(8,128)(2,1)S(1)}, bf16[8,32,3328]{2,1,0:T(8,128)(2,1)S(1)}, u32[]{:S(2)}, u32[]{:S(2)}) collective-permute-start(bf16[8,32,3328]{2,1,0:T(8,128)(2,1)S(1)} %constant_dynamic-update-slice_fusion.6.refs_0_), channel_id=1, source_target_pairs={{0,16},{1,17},{2,18},{3,19},{4,20},{5,21},{6,22},{7,23},{8,9},{9,8... | collective-permute-start | bytes 5111816 | tf_op jit(solution)/shard_map/ppermute | solution.py:665
  49.1 13.7 %collective-permute-start.4 = (bf16[2,160,1024]{2,1,0:T(8,128)(2,1)S(1)}, bf16[2,160,1024]{2,1,0:T(8,128)(2,1)S(1)}, u32[]{:S(2)}, u32[]{:S(2)}) collective-permute-start(bf16[2,160,1024]{2,1,0:T(8,128)(2,1)S(1)} %constant_dynamic-update-slice_fusion.4), channel_id=1, source_target_pairs={{0,2},{1,3},{2,0},{3,1},{4,6},{5,7},{6,4},{7,5},{8,10},{9,11},{10,... | collective-permute-start | bytes 1966088 | tf_op jit(solution)/shard_map/ppermute | solution.py:665
  49.1 24.1 %collective-permute-start.5 = (bf16[8,32,3328]{2,1,0:T(8,128)(2,1)S(1)}, bf16[8,32,3328]{2,1,0:T(8,128)(2,1)}, u32[]{:S(2)}, u32[]{:S(2)}) collective-permute-start(bf16[8,32,3328]{2,1,0:T(8,128)(2,1)S(1)} %constant_dynamic-update-slice_fusion.6.refs_0_), channel_id=1, source_target_pairs={{0,8},{1,9},{2,10},{3,11},{4,12},{5,13},{6,14},{7,15},{8,0},{9,1},... | collective-permute-start | bytes 5111816 | tf_op jit(solution)/shard_map/ppermute | solution.py:665
  69.6 7.5 %copy-start.2 = (bf16[8,32,3328]{2,1,0:T(8,128)(2,1)}, bf16[8,32,3328]{2,1,0:T(8,128)(2,1)S(1)}, u32[]{:S(2)}) copy-start(bf16[8,32,3328]{2,1,0:T(8,128)(2,1)S(1)} %collective-permute-done.6.refs_0_.refs_1_) | copy-start | bytes 5111812
  69.6 7.5 %collective-permute-start.7 = (bf16[8,32,3328]{2,1,0:T(8,128)(2,1)S(1)}, bf16[8,32,3328]{2,1,0:T(8,128)(2,1)}, u32[]{:S(2)}, u32[]{:S(2)}) collective-permute-start(bf16[8,32,3328]{2,1,0:T(8,128)(2,1)S(1)} %collective-permute-done.6.refs_0_.refs_1_), channel_id=1, source_target_pairs={{0,8},{1,9},{2,10},{3,11},{4,12},{5,13},{6,14},{7,15},{8,0},{9,1},... | collective-permute-start | bytes 5111816 | tf_op jit(solution)/shard_map/ppermute | solution.py:665
  69.6 17.9 %collective-permute-start.9 = (bf16[4,160,1024]{2,1,0:T(8,128)(2,1)}, bf16[4,160,1024]{2,1,0:T(8,128)(2,1)}, u32[]{:S(2)}, u32[]{:S(2)}) collective-permute-start(bf16[4,160,1024]{2,1,0:T(8,128)(2,1)} %constant_dynamic-update-slice_fusion.8), channel_id=1, source_target_pairs={{0,1},{1,0},{2,3},{3,2},{4,5},{5,4},{6,7},{7,6},{8,24},{9,25},{10,... | collective-permute-start | bytes 3932168 | tf_op jit(solution)/shard_map/ppermute | solution.py:665
  71.0 15.2 %collective-permute-start.8 = (bf16[1,128,1024]{2,1,0:T(8,128)(2,1)}, bf16[1,128,1024]{2,1,0:T(8,128)(2,1)}, u32[]{:S(2)}, u32[]{:S(2)}) collective-permute-start(bf16[1,128,1024]{2,1,0:T(8,128)(2,1)} %bitcast.74), channel_id=1, source_target_pairs={{0,4},{1,5},{2,6},{3,7},{4,0},{5,1},{6,2},{7,3},{8,12},{9,13},{10,... | collective-permute-start | bytes 786440 | tf_op jit(solution)/shard_map/ppermute | solution.py:665
  77.1 9.1 %copy-start.10 = (bf16[128,1024]{1,0:T(8,128)(2,1)S(1)}, bf16[128,1024]{1,0:T(8,128)(2,1)}, u32[]{:S(2)}) copy-start(bf16[128,1024]{1,0:T(8,128)(2,1)} %param.30) | copy-start | bytes 786436
  90.4 3.8 copy-start.3
  90.4 29.8 %collective-permute-start.11 = (bf16[8,160,1024]{2,1,0:T(8,128)(2,1)S(1)}, bf16[8,160,1024]{2,1,0:T(8,128)(2,1)}, u32[]{:S(2)}, u32[]{:S(2)}) collective-permute-start(bf16[8,160,1024]{2,1,0:T(8,128)(2,1)S(1)} %constant_dynamic-update-slice_fusion.12.refs_0_), channel_id=1, source_target_pairs={{0,8},{1,9},{2,10},{3,11},{4,12},{5,13},{6,14},{7,15},{8,0},{9,1},... | collective-permute-start | bytes 7864328 | tf_op jit(solution)/shard_map/ppermute | solution.py:665
  90.5 42.6 %collective-permute-start.13 = (bf16[8,160,1024]{2,1,0:T(8,128)(2,1)S(1)}, bf16[8,160,1024]{2,1,0:T(8,128)(2,1)}, u32[]{:S(2)}, u32[]{:S(2)}) collective-permute-start(bf16[8,160,1024]{2,1,0:T(8,128)(2,1)S(1)} %constant_dynamic-update-slice_fusion.12.refs_0_), channel_id=1, source_target_pairs={{0,16},{1,17},{2,18},{3,19},{4,20},{5,21},{6,22},{7,23},{8,9},{9,8... | collective-permute-start | bytes 7864328 | tf_op jit(solution)/shard_map/ppermute | solution.py:665
  91.9 14.1 %collective-permute-start.10 = (bf16[2,128,1024]{2,1,0:T(8,128)(2,1)S(1)}, bf16[2,128,1024]{2,1,0:T(8,128)(2,1)}, u32[]{:S(2)}, u32[]{:S(2)}) collective-permute-start(bf16[2,128,1024]{2,1,0:T(8,128)(2,1)S(1)} %constant_dynamic-update-slice_fusion.10), channel_id=1, source_target_pairs={{0,2},{1,3},{2,0},{3,1},{4,6},{5,7},{6,4},{7,5},{8,10},{9,11},{10,... | collective-permute-start | bytes 1572872 | tf_op jit(solution)/shard_map/ppermute | solution.py:665
  108.7 24.4 %collective-permute-start.12 = (bf16[4,128,1024]{2,1,0:T(8,128)(2,1)}, bf16[4,128,1024]{2,1,0:T(8,128)(2,1)}, u32[]{:S(2)}, u32[]{:S(2)}) collective-permute-start(bf16[4,128,1024]{2,1,0:T(8,128)(2,1)} %constant_dynamic-update-slice_fusion.14), channel_id=1, source_target_pairs={{0,1},{1,0},{2,3},{3,2},{4,5},{5,4},{6,7},{7,6},{8,24},{9,25},{10,... | collective-permute-start | bytes 3145736 | tf_op jit(solution)/shard_map/ppermute | solution.py:665
  133.1 5.3 %collective-permute-start.14 = (bf16[8,160,1024]{2,1,0:T(8,128)(2,1)}, bf16[8,160,1024]{2,1,0:T(8,128)(2,1)}, u32[]{:S(2)}, u32[]{:S(2)}) collective-permute-start(bf16[8,160,1024]{2,1,0:T(8,128)(2,1)} %collective-permute-done.13.refs_0_), channel_id=1, source_target_pairs={{0,8},{1,9},{2,10},{3,11},{4,12},{5,13},{6,14},{7,15},{8,0},{9,1},... | collective-permute-start | bytes 7864328 | tf_op jit(solution)/shard_map/ppermute | solution.py:665
  135.7 8.3 %copy-start.4 = (bf16[8,128,1024]{2,1,0:T(8,128)(2,1)}, bf16[8,128,1024]{2,1,0:T(8,128)(2,1)S(1)}, u32[]{:S(2)}) copy-start(bf16[8,128,1024]{2,1,0:T(8,128)(2,1)S(1)} %constant_dynamic-update-slice_fusion.16.refs_0_) | copy-start | bytes 6291460
  135.7 24.6 %collective-permute-start.15 = (bf16[8,128,1024]{2,1,0:T(8,128)(2,1)S(1)}, bf16[8,128,1024]{2,1,0:T(8,128)(2,1)}, u32[]{:S(2)}, u32[]{:S(2)}) collective-permute-start(bf16[8,128,1024]{2,1,0:T(8,128)(2,1)S(1)} %constant_dynamic-update-slice_fusion.16.refs_0_), channel_id=1, source_target_pairs={{0,8},{1,9},{2,10},{3,11},{4,12},{5,13},{6,14},{7,15},{8,0},{9,1},... | collective-permute-start | bytes 6291464 | tf_op jit(solution)/shard_map/ppermute | solution.py:665
  136.3 28.6 %collective-permute-start.16 = (bf16[8,128,1024]{2,1,0:T(8,128)(2,1)S(1)}, bf16[8,128,1024]{2,1,0:T(8,128)(2,1)}, u32[]{:S(2)}, u32[]{:S(2)}) collective-permute-start(bf16[8,128,1024]{2,1,0:T(8,128)(2,1)S(1)} %constant_dynamic-update-slice_fusion.16.refs_0_), channel_id=1, source_target_pairs={{0,16},{1,17},{2,18},{3,19},{4,20},{5,21},{6,22},{7,23},{8,9},{9,8... | collective-permute-start | bytes 6291464 | tf_op jit(solution)/shard_map/ppermute | solution.py:665
  160.3 5.7 %copy-start = (s32[32]{0:T(128)S(1)}, s32[32]{0:T(128)}, u32[]{:S(2)}) copy-start(s32[32]{0:T(128)} %get-tuple-element.445.i_ref) | copy-start | bytes 388
  164.9 4.4 collective-permute-start.17
  165.2 0.5 copy-start.15
  165.2 27.5 %copy-start.17 = (s32[2]{0:T(128)}, s32[2]{0:T(128)S(1)}, u32[]{:S(2)}) copy-start(s32[2]{0:T(128)S(1)} %get-tuple-element.448) | copy-start | bytes 28
  166.7 0.5 copy-start.13
  169.4 1.3 copy-start.5
  275.7 9.5 %copy-start.14 = (s32[32]{0:T(128)S(1)}, s32[32]{0:T(128)}, u32[]{:S(2)}) copy-start(s32[32]{0:T(128)} %copy-done.13) | copy-start | bytes 388
  275.7 9.5 %copy-start.16 = (s32[2]{0:T(128)S(1)}, s32[2]{0:T(128)}, u32[]{:S(2)}) copy-start(s32[2]{0:T(128)} %copy-done.15) | copy-start | bytes 28
  275.7 9.5 %copy-start.18 = (s32[2]{0:T(128)S(1)}, s32[2]{0:T(128)}, u32[]{:S(2)}) copy-start(s32[2]{0:T(128)} %copy-done.17) | copy-start | bytes 28
  275.7 10.1 %copy-start.19 = (s32[16]{0:T(128)S(1)}, s32[16]{0:T(128)}, u32[]{:S(2)}) copy-start(s32[16]{0:T(128)} %get-tuple-element.444) | copy-start | bytes 196
  285.0 10.5 %collective-permute-start.18 = (bf16[16,128,1024]{2,1,0:T(8,128)(2,1)}, bf16[16,128,1024]{2,1,0:T(8,128)(2,1)}, u32[]{:S(2)}, u32[]{:S(2)}) collective-permute-start(bf16[16,128,1024]{2,1,0:T(8,128)(2,1)} %weight_grad_half.2), channel_id=1, source_target_pairs={{0,8},{1,9},{2,10},{3,11},{4,12},{5,13},{6,14},{7,15},{8,0},{9,1},... | collective-permute-start | bytes 12582920 | tf_op jit(solution)/shard_map/ppermute | solution.py:665
  301.0 38.3 %collective-permute-start.19 = (bf16[8,128,1024]{2,1,0:T(8,128)(2,1)}, bf16[8,128,1024]{2,1,0:T(8,128)(2,1)}, u32[]{:S(2)}, u32[]{:S(2)}) collective-permute-start(bf16[8,128,1024]{2,1,0:T(8,128)(2,1)} %get-tuple-element.396), channel_id=1, source_target_pairs={{0,16},{1,17},{2,18},{3,19},{4,20},{5,21},{6,22},{7,23},{8,9},{9,8... | collective-permute-start | bytes 6291464 | tf_op jit(solution)/shard_map/ppermute | solution.py:665
  338.3 20.9 %collective-permute-start.21 = (bf16[16,32,4096]{2,1,0:T(8,128)(2,1)}, bf16[16,32,4096]{2,1,0:T(8,128)(2,1)}, u32[]{:S(2)}, u32[]{:S(2)}) collective-permute-start(bf16[16,32,4096]{2,1,0:T(8,128)(2,1)} %get-tuple-element.298), channel_id=1, source_target_pairs={{0,8},{1,9},{2,10},{3,11},{4,12},{5,13},{6,14},{7,15},{8,0},{9,1},... | collective-permute-start | bytes 12582920 | tf_op jit(solution)/shard_map/ppermute | solution.py:665
  342.8 15.0 %collective-permute-start.20 = (bf16[4,128,1024]{2,1,0:T(8,128)(2,1)}, bf16[4,128,1024]{2,1,0:T(8,128)(2,1)S(1)}, u32[]{:S(2)}, u32[]{:S(2)}) collective-permute-start(bf16[4,128,1024]{2,1,0:T(8,128)(2,1)} %get-tuple-element.402), channel_id=1, source_target_pairs={{0,1},{1,0},{2,3},{3,2},{4,5},{5,4},{6,7},{7,6},{8,24},{9,25},{10,... | collective-permute-start | bytes 3145736 | tf_op jit(solution)/shard_map/ppermute | solution.py:665
  364.4 26.4 %collective-permute-start.22 = (bf16[8,32,4096]{2,1,0:T(8,128)(2,1)}, bf16[8,32,4096]{2,1,0:T(8,128)(2,1)}, u32[]{:S(2)}, u32[]{:S(2)}) collective-permute-start(bf16[8,32,4096]{2,1,0:T(8,128)(2,1)} %get-tuple-element.394), channel_id=1, source_target_pairs={{0,16},{1,17},{2,18},{3,19},{4,20},{5,21},{6,22},{7,23},{8,9},{9,8... | collective-permute-start | bytes 6291464 | tf_op jit(solution)/shard_map/ppermute | solution.py:665
  365.9 29.7 %collective-permute-start.23 = (bf16[2,128,1024]{2,1,0:T(8,128)(2,1)}, bf16[2,128,1024]{2,1,0:T(8,128)(2,1)}, u32[]{:S(2)}, u32[]{:S(2)}) collective-permute-start(bf16[2,128,1024]{2,1,0:T(8,128)(2,1)} %get-tuple-element.410), channel_id=1, source_target_pairs={{0,2},{1,3},{2,0},{3,1},{4,6},{5,7},{6,4},{7,5},{8,10},{9,11},{10,... | collective-permute-start | bytes 1572872 | tf_op jit(solution)/shard_map/ppermute | solution.py:665
  379.7 27.4 %collective-permute-start.24 = (bf16[16,32,2560]{2,1,0:T(8,128)(2,1)}, bf16[16,32,2560]{2,1,0:T(8,128)(2,1)}, u32[]{:S(2)}, u32[]{:S(2)}) collective-permute-start(bf16[16,32,2560]{2,1,0:T(8,128)(2,1)} %get-tuple-element.316), channel_id=1, source_target_pairs={{0,8},{1,9},{2,10},{3,11},{4,12},{5,13},{6,14},{7,15},{8,0},{9,1},... | collective-permute-start | bytes 7864328 | tf_op jit(solution)/shard_map/ppermute | solution.py:665
  390.7 4.9 %copy-start.7 = (bf16[2,128,1024]{2,1,0:T(8,128)(2,1)S(1)}, bf16[2,128,1024]{2,1,0:T(8,128)(2,1)}, u32[]{:S(2)}) copy-start(bf16[2,128,1024]{2,1,0:T(8,128)(2,1)} %get-tuple-element.321) | copy-start | bytes 1572868
  394.1 18.3 %collective-permute-start.25 = (bf16[4,32,4096]{2,1,0:T(8,128)(2,1)}, bf16[4,32,4096]{2,1,0:T(8,128)(2,1)}, u32[]{:S(2)}, u32[]{:S(2)}) collective-permute-start(bf16[4,32,4096]{2,1,0:T(8,128)(2,1)} %get-tuple-element.400), channel_id=1, source_target_pairs={{0,1},{1,0},{2,3},{3,2},{4,5},{5,4},{6,7},{7,6},{8,24},{9,25},{10,... | collective-permute-start | bytes 3145736 | tf_op jit(solution)/shard_map/ppermute | solution.py:665
  397.6 51.9 %collective-permute-start.34 = (bf16[1,128,1024]{2,1,0:T(8,128)(2,1)}, bf16[1,128,1024]{2,1,0:T(8,128)(2,1)}, u32[]{:S(2)}, u32[]{:S(2)}) collective-permute-start(bf16[1,128,1024]{2,1,0:T(8,128)(2,1)} %get-tuple-element.418), channel_id=1, source_target_pairs={{0,4},{1,5},{2,6},{3,7},{4,0},{5,1},{6,2},{7,3},{8,12},{9,13},{10,... | collective-permute-start | bytes 786440 | tf_op jit(solution)/shard_map/ppermute | solution.py:665
  407.0 10.0 %collective-permute-start.26 = (bf16[16,32,1536]{2,1,0:T(8,128)(2,1)}, bf16[16,32,1536]{2,1,0:T(8,128)(2,1)S(1)}, u32[]{:S(2)}, u32[]{:S(2)}) collective-permute-start(bf16[16,32,1536]{2,1,0:T(8,128)(2,1)} %get-tuple-element.325), channel_id=1, source_target_pairs={{0,8},{1,9},{2,10},{3,11},{4,12},{5,13},{6,14},{7,15},{8,0},{9,1},... | collective-permute-start | bytes 4718600 | tf_op jit(solution)/shard_map/ppermute | solution.py:665
  411.4 5.6 %copy-start.8 = (bf16[16,32,1536]{2,1,0:T(8,128)(2,1)S(1)}, bf16[16,32,1536]{2,1,0:T(8,128)(2,1)}, u32[]{:S(2)}) copy-start(bf16[16,32,1536]{2,1,0:T(8,128)(2,1)} %get-tuple-element.332) | copy-start | bytes 4718596
  411.4 20.3 %collective-permute-start.27 = (bf16[8,32,2560]{2,1,0:T(8,128)(2,1)}, bf16[8,32,2560]{2,1,0:T(8,128)(2,1)}, u32[]{:S(2)}, u32[]{:S(2)}) collective-permute-start(bf16[8,32,2560]{2,1,0:T(8,128)(2,1)} %get-tuple-element.398), channel_id=1, source_target_pairs={{0,16},{1,17},{2,18},{3,19},{4,20},{5,21},{6,22},{7,23},{8,9},{9,8... | collective-permute-start | bytes 3932168 | tf_op jit(solution)/shard_map/ppermute | solution.py:665
  414.8 19.3 %collective-permute-start.28 = (bf16[2,32,4096]{2,1,0:T(8,128)(2,1)}, bf16[2,32,4096]{2,1,0:T(8,128)(2,1)S(1)}, u32[]{:S(2)}, u32[]{:S(2)}) collective-permute-start(bf16[2,32,4096]{2,1,0:T(8,128)(2,1)} %get-tuple-element.408), channel_id=1, source_target_pairs={{0,2},{1,3},{2,0},{3,1},{4,6},{5,7},{6,4},{7,5},{8,10},{9,11},{10,... | collective-permute-start | bytes 1572872 | tf_op jit(solution)/shard_map/ppermute | solution.py:665
  417.5 21.4 %collective-permute-start.29 = (bf16[8,32,1536]{2,1,0:T(8,128)(2,1)S(1)}, bf16[8,32,1536]{2,1,0:T(8,128)(2,1)}, u32[]{:S(2)}, u32[]{:S(2)}) collective-permute-start(bf16[8,32,1536]{2,1,0:T(8,128)(2,1)S(1)} %get-tuple-element.404), channel_id=1, source_target_pairs={{0,16},{1,17},{2,18},{3,19},{4,20},{5,21},{6,22},{7,23},{8,9},{9,8... | collective-permute-start | bytes 2359304 | tf_op jit(solution)/shard_map/ppermute | solution.py:665
  431.7 2.5 copy-start.6
  431.7 10.1 %collective-permute-start.30 = (f32[16,9,128]{2,1,0:T(8,128)S(1)}, f32[16,9,128]{2,1,0:T(8,128)S(1)}, u32[]{:S(2)}, u32[]{:S(2)}) collective-permute-start(f32[16,9,128]{2,1,0:T(8,128)S(1)} %get-tuple-element.427), channel_id=1, source_target_pairs={{0,8},{1,9},{2,10},{3,11},{4,12},{5,13},{6,14},{7,15},{8,0},{9,1},... | collective-permute-start | bytes 221192 | tf_op jit(solution)/shard_map/ppermute | solution.py:665
  433.4 11.5 %collective-permute-start.31 = (bf16[4,32,2560]{2,1,0:T(8,128)(2,1)S(1)}, bf16[4,32,2560]{2,1,0:T(8,128)(2,1)S(1)}, u32[]{:S(2)}, u32[]{:S(2)}) collective-permute-start(bf16[4,32,2560]{2,1,0:T(8,128)(2,1)S(1)} %get-tuple-element.406), channel_id=1, source_target_pairs={{0,1},{1,0},{2,3},{3,2},{4,5},{5,4},{6,7},{7,6},{8,24},{9,25},{10,... | collective-permute-start | bytes 1966088 | tf_op jit(solution)/shard_map/ppermute | solution.py:665
  434.3 14.4 %collective-permute-start.33 = (bf16[1,32,4096]{2,1,0:T(8,128)(2,1)S(1)}, bf16[1,32,4096]{2,1,0:T(8,128)(2,1)S(1)}, u32[]{:S(2)}, u32[]{:S(2)}) collective-permute-start(bf16[1,32,4096]{2,1,0:T(8,128)(2,1)S(1)} %get-tuple-element.416), channel_id=1, source_target_pairs={{0,4},{1,5},{2,6},{3,7},{4,0},{5,1},{6,2},{7,3},{8,12},{9,13},{10,... | collective-permute-start | bytes 786440 | tf_op jit(solution)/shard_map/ppermute | solution.py:665
  440.2 9.3 %copy-start.9 = (bf16[1,128,1024]{2,1,0:T(8,128)(2,1)S(1)}, bf16[1,128,1024]{2,1,0:T(8,128)(2,1)}, u32[]{:S(2)}) copy-start(bf16[1,128,1024]{2,1,0:T(8,128)(2,1)} %get-tuple-element.375) | copy-start | bytes 786436
  440.2 11.1 %collective-permute-start.35 = (bf16[4,32,1536]{2,1,0:T(8,128)(2,1)S(1)}, bf16[4,32,1536]{2,1,0:T(8,128)(2,1)S(1)}, u32[]{:S(2)}, u32[]{:S(2)}) collective-permute-start(bf16[4,32,1536]{2,1,0:T(8,128)(2,1)S(1)} %get-tuple-element.412), channel_id=1, source_target_pairs={{0,1},{1,0},{2,3},{3,2},{4,5},{5,4},{6,7},{7,6},{8,24},{9,25},{10,... | collective-permute-start | bytes 1179656 | tf_op jit(solution)/shard_map/ppermute | solution.py:665
  441.8 6.1 %collective-permute-start.32 = (f32[8,9,128]{2,1,0:T(8,128)S(1)}, f32[8,9,128]{2,1,0:T(8,128)S(1)}, u32[]{:S(2)}, u32[]{:S(2)}) collective-permute-start(f32[8,9,128]{2,1,0:T(8,128)S(1)} %get-tuple-element.426), channel_id=1, source_target_pairs={{0,16},{1,17},{2,18},{3,19},{4,20},{5,21},{6,22},{7,23},{8,9},{9,8... | collective-permute-start | bytes 110600 | tf_op jit(solution)/shard_map/ppermute | solution.py:665
  445.1 11.4 %collective-permute-start.37 = (bf16[2,32,2560]{2,1,0:T(8,128)(2,1)S(1)}, bf16[2,32,2560]{2,1,0:T(8,128)(2,1)S(1)}, u32[]{:S(2)}, u32[]{:S(2)}) collective-permute-start(bf16[2,32,2560]{2,1,0:T(8,128)(2,1)S(1)} %get-tuple-element.414), channel_id=1, source_target_pairs={{0,2},{1,3},{2,0},{3,1},{4,6},{5,7},{6,4},{7,5},{8,10},{9,11},{10,... | collective-permute-start | bytes 983048 | tf_op jit(solution)/shard_map/ppermute | solution.py:665
  447.9 7.6 %collective-permute-start.36 = (f32[4,9,128]{2,1,0:T(8,128)S(1)}, f32[4,9,128]{2,1,0:T(8,128)S(1)}, u32[]{:S(2)}, u32[]{:S(2)}) collective-permute-start(f32[4,9,128]{2,1,0:T(8,128)S(1)} %get-tuple-element.430), channel_id=1, source_target_pairs={{0,1},{1,0},{2,3},{3,2},{4,5},{5,4},{6,7},{7,6},{8,24},{9,25},{10,... | collective-permute-start | bytes 55304 | tf_op jit(solution)/shard_map/ppermute | solution.py:665
  451.4 11.2 %collective-permute-start.39 = (bf16[2,32,1536]{2,1,0:T(8,128)(2,1)S(1)}, bf16[2,32,1536]{2,1,0:T(8,128)(2,1)S(1)}, u32[]{:S(2)}, u32[]{:S(2)}) collective-permute-start(bf16[2,32,1536]{2,1,0:T(8,128)(2,1)S(1)} %get-tuple-element.420), channel_id=1, source_target_pairs={{0,2},{1,3},{2,0},{3,1},{4,6},{5,7},{6,4},{7,5},{8,10},{9,11},{10,... | collective-permute-start | bytes 589832 | tf_op jit(solution)/shard_map/ppermute | solution.py:665
  455.4 6.9 %collective-permute-start.38 = (f32[2,9,128]{2,1,0:T(8,128)S(1)}, f32[2,9,128]{2,1,0:T(8,128)S(1)}, u32[]{:S(2)}, u32[]{:S(2)}) collective-permute-start(f32[2,9,128]{2,1,0:T(8,128)S(1)} %get-tuple-element.432), channel_id=1, source_target_pairs={{0,2},{1,3},{2,0},{3,1},{4,6},{5,7},{6,4},{7,5},{8,10},{9,11},{10,... | collective-permute-start | bytes 27656 | tf_op jit(solution)/shard_map/ppermute | solution.py:665
  456.5 12.6 %collective-permute-start.41 = (bf16[1,32,2560]{2,1,0:T(8,128)(2,1)S(1)}, bf16[1,32,2560]{2,1,0:T(8,128)(2,1)S(1)}, u32[]{:S(2)}, u32[]{:S(2)}) collective-permute-start(bf16[1,32,2560]{2,1,0:T(8,128)(2,1)S(1)} %get-tuple-element.422), channel_id=1, source_target_pairs={{0,4},{1,5},{2,6},{3,7},{4,0},{5,1},{6,2},{7,3},{8,12},{9,13},{10,... | collective-permute-start | bytes 491528 | tf_op jit(solution)/shard_map/ppermute | solution.py:665
  462.4 5.7 %collective-permute-start.40 = (f32[1,9,128]{2,1,0:T(8,128)S(1)}, f32[1,9,128]{2,1,0:T(8,128)S(1)}, u32[]{:S(2)}, u32[]{:S(2)}) collective-permute-start(f32[1,9,128]{2,1,0:T(8,128)S(1)} %get-tuple-element.434), channel_id=1, source_target_pairs={{0,4},{1,5},{2,6},{3,7},{4,0},{5,1},{6,2},{7,3},{8,12},{9,13},{10,... | collective-permute-start | bytes 13832 | tf_op jit(solution)/shard_map/ppermute | solution.py:665
  462.7 7.5 %collective-permute-start.42 = (bf16[1,32,1536]{2,1,0:T(8,128)(2,1)S(1)}, bf16[1,32,1536]{2,1,0:T(8,128)(2,1)S(1)}, u32[]{:S(2)}, u32[]{:S(2)}) collective-permute-start(bf16[1,32,1536]{2,1,0:T(8,128)(2,1)S(1)} %get-tuple-element.424), channel_id=1, source_target_pairs={{0,4},{1,5},{2,6},{3,7},{4,0},{5,1},{6,2},{7,3},{8,12},{9,13},{10,... | collective-permute-start | bytes 294920 | tf_op jit(solution)/shard_map/ppermute | solution.py:665
  470.3 0.7 copy-start.12

commit v10 on v9

--- a/solution.py
+++ b/solution.py
@@ -1018,9 +1018,9 @@
         return o, logs
 
     def feed(a2, x1):
-        g, gp = feed_forward_in(*line.after(a2), w["up"], r_in, bu)
+        mover = Mover(chain_c.pieces(0), row, ff_shape)
+        g, gp, down = feed_forward_in(*line.after(a2), w["up"], r_in, bu, mover)
         line.mark(g)
-        down = place(chain_c.pieces(0), ff_shape)
         chain_c.finish()
         w["down"] = place(chain_c.pieces(1), ff_shape, down)
         y = feed_forward_out(line.after(g)[0], w["down"], bd, x1)

time: 475 us -> 473 us (level)
    pallas_call x0 -> x1, Pallas kernels: none -> 13.4 us  [riding(): call(both, grid_spec=pltpu.PrefetchScalarGridSpec(num_scalar_prefetch=1,...]
    pallas_call x3 -> x2, Pallas kernels: 33.1 us -> 21.7 us  [riding(): call(body, grid=grid, in_specs=in_specs, out_specs=out_specs, out_shape=o...]
    pallas_call x6 -> x5, Pallas kernels: 28.2 us -> 23.6 us  [place_shards(): call(body, out_shape=mover.out_shape, grid_spec=pltpu.PrefetchScalarGridS...]
  transfers between devices with their start and end apart: 43 -> 43, of which waited for: 20 -> 21; matrix products, arithmetic and copies ran while one was open for 9% -> 9% of each run, Pallas kernels for 34% -> 34%
where the time goes in v10:
time: 473 us; the launch traced here: 469 us
  Pallas kernels  274 us (58%)
  waiting for transfers between devices  89.8 us (19%)
  starting transfers between devices  44.2 us (9%)
  other arithmetic  37.1 us (8%)
  local copies, waits for them, and re-layouts  21.9 us (5%)
    ppermute x43, waiting for transfers between devices, send(): return lax.ppermute(x, AXES, perm)  89.8 us
    ppermute x43, starting transfers between devices, send(): return lax.ppermute(x, AXES, perm)  44.2 us
    pallas_call x2, Pallas kernels, feed_forward_back(): call(body, grid=(steps,), in_specs=[full, pl.BlockSpec((rows, tf), lambda...  40.5 us
    pallas_call x3, Pallas kernels, weight_grad(): call(body, grid_spec=pltpu.PrefetchScalarGridSpec(num_scalar_prefetch=1,...  38.4 us
    pallas_call x4, Pallas kernels, attention_back(): call(body, grid=(pairs,), in_specs=[col(first_pair), col(every + first_pa...  35.7 us
    convert_element_type x16, other arithmetic, step(): self.kept = add(slice(0, half)).astype(wide)  31.7 us
    pallas_call x5, Pallas kernels, place_shards(): call(body, out_shape=mover.out_shape, grid_spec=pltpu.PrefetchScalarGridS...  23.6 us
    pallas_call x2, Pallas kernels, riding(): call(body, grid=grid, in_specs=in_specs, out_specs=out_specs, out_shape=o...  21.7 us
  transfers between devices with their start and end apart: 43, of which 21 were waited for; matrix products, arithmetic and copies ran while one was open for 9% of the time, Pallas kernels for 34%

profile of v10, /device:TPU:0, one launch (start us, length us, event | category | flops | bytes accessed | tf_op | source)
XLA Modules:
  0.0 468.6 jit_solution(7658763521863616503)
XLA Ops:
  0.7 1.7 pack_shard.1
  2.4 4.0 collective-permute-start
  6.4 10.0 %collective-permute-done = bf16[1,32,3328]{2,1,0:T(8,128)(2,1)S(1)} collective-permute-done((bf16[1,32,3328]{2,1,0:T(8,128)(2,1)}, bf16[1,32,3328]{2,1,0:T(8,128)(2,1)S(1)}, u32[]{:S(2)}, u32[]{:S(2)}) %collective-permute-start) | collective-permute-done | bytes 213024 | tf_op jit(solution)/shard_map/ppermute | solution.py:665
  20.9 3.3 collective-permute-start.2
  24.2 10.6 %collective-permute-done.1 = bf16[2,32,3328]{2,1,0:T(8,128)(2,1)S(1)} collective-permute-done((bf16[2,32,3328]{2,1,0:T(8,128)(2,1)S(1)}, bf16[2,32,3328]{2,1,0:T(8,128)(2,1)S(1)}, u32[]{:S(2)}, u32[]{:S(2)}) %collective-permute-start.1) | collective-permute-done | bytes 426016 | tf_op jit(solution)/shard_map/ppermute | solution.py:665
  36.3 2.8 masked.1.dy_ref
  39.1 8.5 %collective-permute-done.3 = bf16[4,32,3328]{2,1,0:T(8,128)(2,1)S(1)} collective-permute-done((bf16[4,32,3328]{2,1,0:T(8,128)(2,1)S(1)}, bf16[4,32,3328]{2,1,0:T(8,128)(2,1)S(1)}, u32[]{:S(2)}, u32[]{:S(2)}) %collective-permute-start.3) | collective-permute-done | bytes 852000 | tf_op jit(solution)/shard_map/ppermute | solution.py:665
  49.1 13.7 %collective-permute-done.4 = bf16[2,160,1024]{2,1,0:T(8,128)(2,1)S(1)} collective-permute-done((bf16[2,160,1024]{2,1,0:T(8,128)(2,1)S(1)}, bf16[2,160,1024]{2,1,0:T(8,128)(2,1)S(1)}, u32[]{:S(2)}, u32[]{:S(2)}) %collective-permute-start.4) | collective-permute-done | bytes 655392 | tf_op jit(solution)/shard_map/ppermute | solution.py:665
  64.5 5.1 %collective-permute-done.6.refs_0_.refs_1_ = bf16[8,32,3328]{2,1,0:T(8,128)(2,1)S(1)} collective-permute-done((bf16[8,32,3328]{2,1,0:T(8,128)(2,1)S(1)}, bf16[8,32,3328]{2,1,0:T(8,128)(2,1)S(1)}, u32[]{:S(2)}, u32[]{:S(2)}) %collective-permute-start.6) | collective-permute-done | bytes 1703968 | tf_op jit(solution)/shard_map/ppermute | solution.py:665
  73.3 3.8 place_shards.5.refs_2_
  77.1 4.0 place_shards.6
  81.1 5.1 %collective-permute-done.8 = bf16[1,128,1024]{2,1,0:T(8,128)(2,1)} collective-permute-done((bf16[1,128,1024]{2,1,0:T(8,128)(2,1)}, bf16[1,128,1024]{2,1,0:T(8,128)(2,1)}, u32[]{:S(2)}, u32[]{:S(2)}) %collective-permute-start.8) | collective-permute-done | bytes 262176 | tf_op jit(solution)/shard_map/ppermute | solution.py:665
  91.9 2.4 unpack_vectors.1
  94.2 8.3 %norm_project.2 = (bf16[512,1024]{1,0:T(8,128)(2,1)}, bf16[512,3072]{1,0:T(8,128)(2,1)}) custom-call(bf16[512,1024]{1,0:T(8,128)(2,1)} %bitcast.67, f32[1,1024]{1,0:T(1,128)} %get-tuple-element.229.g_ref.refs_4_, f32[1,1024]{1,0:T(1,128)} %get-tuple-element.230.s_ref, bf16[1024,3072]{1,0:T(8,128)(2,1)} %bitcast.62, f32[1,3072]{1,0:T(1,128)} %get-tuple-element.231.b_ref), custom_call_target="tpu_custom_call" | custom-call | flops 1 | bytes 1 | tf_op jit(solution)/shard_map/norm_project/pallas_call | solution.py:72
  102.5 3.4 collective-permute-done.10
  106.8 1.9 constant_dynamic-update-slice_fusion.14
  109.4 10.8 %attention.2 = (bf16[512,1024]{1,0:T(8,128)(2,1)}, f32[8,8,512]{2,1,0:T(8,128)}) custom-call(bf16[512,3072]{1,0:T(8,128)(2,1)} %get-tuple-element.236.q_ref.k_ref.v_ref, bf16[512,3072]{1,0:T(8,128)(2,1)} %get-tuple-element.236.q_ref.k_ref.v_ref, bf16[512,3072]{1,0:T(8,128)(2,1)} %get-tuple-element.236.q_ref.k_ref.v_ref), custom_call_target="tpu_custom_call" | custom-call | flops 1 | bytes 1 | tf_op jit(solution)/shard_map/attention/pallas_call | solution.py:753
  120.2 5.6 %place_shards.7.refs_2_ = bf16[32,160,1024]{2,1,0:T(8,128)(2,1)} custom-call(s32[32]{0:T(128)} %get-tuple-element.448.t_ref, bf16[8,160,1024]{2,1,0:T(8,128)(2,1)} %copy-done.3, bf16[8,160,1024]{2,1,0:T(8,128)(2,1)} %collective-permute-done.11.refs_1_), custom_call_target="tpu_custom_call" | custom-call | flops 1 | bytes 1 | tf_op jit(solution)/shard_map/place_shards/pallas_call | solution.py:736
  125.8 7.3 %collective-permute-done.13.refs_0_ = bf16[8,160,1024]{2,1,0:T(8,128)(2,1)} collective-permute-done((bf16[8,160,1024]{2,1,0:T(8,128)(2,1)S(1)}, bf16[8,160,1024]{2,1,0:T(8,128)(2,1)}, u32[]{:S(2)}, u32[]{:S(2)}) %collective-permute-start.13) | collective-permute-done | bytes 2621472 | tf_op jit(solution)/shard_map/ppermute | solution.py:665
  138.4 5.6 %place_shards.8.w_ref.refs_1_.u_ref = bf16[32,160,1024]{2,1,0:T(8,128)(2,1)} custom-call(s32[32]{0:T(128)} %get-tuple-element.448.t_ref, bf16[8,160,1024]{2,1,0:T(8,128)(2,1)} %collective-permute-done.13.refs_0_, bf16[8,160,1024]{2,1,0:T(8,128)(2,1)} %collective-permute-done.14.refs_1_, ...), custom_call_target="tpu_custom_call", output_to_operand_aliasing={{}: (3, {})} | custom-call | flops 1 | bytes 1 | tf_op jit(solution)/shard_map/place_shards/pallas_call | solution.py:736
  144.0 4.9 %project_norm.2 = (f32[512,1024]{1,0:T(8,128)}, bf16[512,1024]{1,0:T(8,128)(2,1)}) custom-call(bf16[512,1024]{1,0:T(8,128)(2,1)} %get-tuple-element.311.o_ref.refs_0_, bf16[32,160,1024]{2,1,0:T(8,128)(2,1)} %place_shards.8.w_ref.refs_1_.u_ref, f32[1,1024]{1,0:T(1,128)} %get-tuple-element.246.b_ref, bf16[512,1024]{1,0:T(8,128)(2,1)} %bitcast.68, ...), custom_call_target="tpu_custom_call" | custom-call | flops 1 | bytes 1 | tf_op jit(solution)/shard_map/project_norm/pallas_call | solution.py:197
  148.9 13.4 %feed_forward_in.1 = (bf16[512,4096]{1,0:T(8,128)(2,1)}, bf16[512,4096]{1,0:T(8,128)(2,1)}, bf16[32,128,1024]{2,1,0:T(8,128)(2,1)}) custom-call(s32[32]{0:T(128)} %get-tuple-element.448.t_ref, bf16[512,1024]{1,0:T(8,128)(2,1)} %get-tuple-element.294.refs_0_, bf16[32,160,1024]{2,1,0:T(8,128)(2,1)} %place_shards.8.w_ref.refs_1_.u_ref, ...), custom_call_target="tpu_custom_call" | custom-call | flops 1 | bytes 1 | tf_op jit(solution)/shard_map/feed_forward_in/pallas_call | solution.py:764
  164.6 2.2 collective-permute-done.17.refs_1_
  168.1 4.5 place_shards.9.d_ref
  172.7 9.7 %feed_forward_out.1.x_ref.refs_3_ = bf16[512,1024]{1,0:T(8,128)(2,1)} custom-call(bf16[512,4096]{1,0:T(8,128)(2,1)} %get-tuple-element.290.g_ref.refs_0_, bf16[32,128,1024]{2,1,0:T(8,128)(2,1)} %place_shards.9.d_ref, f32[1,1024]{1,0:T(1,128)} %get-tuple-element.260.db_ref, f32[512,1024]{1,0:T(8,128)} %get-tuple-element.261.x_ref), custom_call_target="tpu_custom_call" | custom-call | flops 1 | bytes 1 | tf_op jit(solution)/shard_map/feed_forward_out/pallas_call | solution.py:323
  182.3 7.7 %norm_project.3 = (bf16[512,1024]{1,0:T(8,128)(2,1)}, bf16[512,3072]{1,0:T(8,128)(2,1)}) custom-call(bf16[512,1024]{1,0:T(8,128)(2,1)} %feed_forward_out.1.x_ref.refs_3_, f32[1,1024]{1,0:T(1,128)} %get-tuple-element.229.g_ref.refs_4_, f32[1,1024]{1,0:T(1,128)} %get-tuple-element.230.s_ref, bf16[1024,3072]{1,0:T(8,128)(2,1)} %bitcast.63, ...), custom_call_target="tpu_custom_call" | custom-call | flops 1 | bytes 1 | tf_op jit(solution)/shard_map/norm_project/pallas_call | solution.py:72
  190.7 10.8 %attention.3 = (bf16[512,1024]{1,0:T(8,128)(2,1)}, f32[8,8,512]{2,1,0:T(8,128)}) custom-call(bf16[512,3072]{1,0:T(8,128)(2,1)} %get-tuple-element.263.q_ref.k_ref.v_ref, bf16[512,3072]{1,0:T(8,128)(2,1)} %get-tuple-element.263.q_ref.k_ref.v_ref, bf16[512,3072]{1,0:T(8,128)(2,1)} %get-tuple-element.263.q_ref.k_ref.v_ref), custom_call_target="tpu_custom_call" | custom-call | flops 1 | bytes 1 | tf_op jit(solution)/shard_map/attention/pallas_call | solution.py:753
  201.5 5.1 %project_norm.3 = (f32[512,1024]{1,0:T(8,128)}, bf16[512,1024]{1,0:T(8,128)(2,1)}) custom-call(bf16[512,1024]{1,0:T(8,128)(2,1)} %get-tuple-element.312.o_ref.refs_1_, bf16[32,160,1024]{2,1,0:T(8,128)(2,1)} %place_shards.8.w_ref.refs_1_.u_ref, f32[1,1024]{1,0:T(1,128)} %get-tuple-element.246.b_ref, bf16[512,1024]{1,0:T(8,128)(2,1)} %feed_forward_out.1.x_ref.refs_3_, ...), custom_call_target="tpu_custom_call" | custom-call | flops 1 | bytes 1 | tf_op jit(solution)/shard_map/project_norm/pallas_call | solution.py:197
  206.6 18.0 %feed_forward.1 = (bf16[512,4096]{1,0:T(8,128)(2,1)}, bf16[512,4096]{1,0:T(8,128)(2,1)}, bf16[512,1024]{1,0:T(8,128)(2,1)}) custom-call(bf16[512,1024]{1,0:T(8,128)(2,1)} %get-tuple-element.295.a_ref.refs_1_, bf16[32,160,1024]{2,1,0:T(8,128)(2,1)} %place_shards.8.w_ref.refs_1_.u_ref, f32[1,4096]{1,0:T(1,128)} %get-tuple-element.251.refs_2_.ub_ref, ...), custom_call_target="tpu_custom_call" | custom-call | flops 1 | bytes 1 | tf_op jit(solution)/shard_map/feed_forward/pallas_call | solution.py:253
  224.6 20.3 %feed_forward_back.2 = (bf16[512,1024]{1,0:T(8,128)(2,1)}, bf16[512,4096]{1,0:T(8,128)(2,1)}, f32[512,1024]{1,0:T(8,128)}, bf16[512,1024]{1,0:T(8,128)(2,1)}, bf...) custom-call(f32[512,1024]{1,0:T(8,128)} %masked.1.dy_ref, ...), custom_call_target="tpu_custom_call" | custom-call | flops 99999997952 | bytes 1 | tf_op jit(solution)/shard_map/feed_forward_back/pallas_call | solution.py:382
  244.8 8.9 %attention_back.4 = (bf16[3,512,512]{2,1,0:T(8,128)(2,1)}, f32[1,512]{1,0:T(1,128)}, f32[1,512]{1,0:T(1,128)}) custom-call(bf16[512,3072]{1,0:T(8,128)(2,1)} %get-tuple-element.263.q_ref.k_ref.v_ref, bf16[512,3072]{1,0:T(8,128)(2,1)} %get-tuple-element.263.q_ref.k_ref.v_ref, bf16[512,3072]{1,0:T(8,128)(2,1)} %get-tuple-element.263.q_ref.k_ref.v_ref, ...), custom_call_target="tpu_custom_call" | custom-call | flops 99999997952 | bytes 1 | tf_op jit(solution)/shard_map/attention_back/pallas_call | solution.py:164
  253.8 8.9 %attention_back.5 = (bf16[3,512,512]{2,1,0:T(8,128)(2,1)}, f32[1,512]{1,0:T(1,128)}, f32[1,512]{1,0:T(1,128)}) custom-call(bf16[512,3072]{1,0:T(8,128)(2,1)} %get-tuple-element.263.q_ref.k_ref.v_ref, bf16[512,3072]{1,0:T(8,128)(2,1)} %get-tuple-element.263.q_ref.k_ref.v_ref, bf16[512,3072]{1,0:T(8,128)(2,1)} %get-tuple-element.263.q_ref.k_ref.v_ref, ...), custom_call_target="tpu_custom_call" | custom-call | flops 99999997952 | bytes 1 | tf_op jit(solution)/shard_map/attention_back/pallas_call | solution.py:164
  262.7 10.4 %project_back.2 = (f32[512,1024]{1,0:T(8,128)}, bf16[512,1024]{1,0:T(8,128)(2,1)}, f32[1,1024]{1,0:T(1,128)}, f32[1,1024]{1,0:T(1,128)}) custom-call(bf16[3,512,512]{2,1,0:T(8,128)(2,1)} %get-tuple-element.280.refs_0_.refs_7_, bf16[3,512,512]{2,1,0:T(8,128)(2,1)} %get-tuple-element.281.refs_1_.refs_3_, bf16[1024,3072]{1,0:T(8,128)(2,1)} %bitcast.64, ...), custom_call_target="tpu_custom_call" | custom-call | flops 99999997952 | bytes 1 | tf_op jit(solution)/shard_map/project_back/pallas_call | solution.py:474
  273.2 9.3 %weight_grad_half.2 = bf16[16,128,1024]{2,1,0:T(8,128)(2,1)} custom-call(s32[18]{0:T(128)} %pad_add_fusion.2.i_ref, bf16[512,4096]{1,0:T(8,128)(2,1)} %get-tuple-element.290.g_ref.refs_0_, bf16[512,4096]{1,0:T(8,128)(2,1)} %get-tuple-element.291.refs_1_, bf16[512,1024]{1,0:T(8,128)(2,1)} %get-tuple-element.289.refs_2_, ...), custom_call_target="tpu_custom_call" | custom-call | flops 1 | bytes 1 | tf_op jit(solution)/shard_map/weight_grad_half/pallas_call | solution.py:605
  283.8 9.1 %weight_grad_half.3 = bf16[16,128,1024]{2,1,0:T(8,128)(2,1)} custom-call(s32[18]{0:T(128)} %pad_add_fusion.1.i_ref, bf16[512,4096]{1,0:T(8,128)(2,1)} %get-tuple-element.290.g_ref.refs_0_, bf16[512,4096]{1,0:T(8,128)(2,1)} %get-tuple-element.291.refs_1_, bf16[512,1024]{1,0:T(8,128)(2,1)} %get-tuple-element.289.refs_2_, ...), custom_call_target="tpu_custom_call" | custom-call | flops 1 | bytes 1 | tf_op jit(solution)/shard_map/weight_grad_half/pallas_call | solution.py:605
  292.9 5.5 %add_convert_fusion.2 = (bf16[8,128,1024]{2,1,0:T(8,128)(2,1)S(1)}, bf16[8,128,1024]{2,1,0:T(8,128)(2,1)}) fusion(bf16[16,128,1024]{2,1,0:T(8,128)(2,1)} %collective-permute-done.18, bf16[16,128,1024]{2,1,0:T(8,128)(2,1)} %weight_grad_half.3), kind=kLoop, calls=%fused_computation.3 | loop fusion | flops 8388608 | bytes 12582912 | tf_op jit(solution)/shard_map/convert_element_type | solution.py:902
  299.5 20.2 %feed_forward_back.3 = (bf16[512,1024]{1,0:T(8,128)(2,1)}, bf16[512,4096]{1,0:T(8,128)(2,1)}, f32[512,1024]{1,0:T(8,128)}, bf16[512,1024]{1,0:T(8,128)(2,1)}, bf...) custom-call(f32[512,1024]{1,0:T(8,128)} %get-tuple-element.296.dy_re, ...), custom_call_target="tpu_custom_call" | custom-call | flops 99999997952 | bytes 1 | tf_op jit(solution)/shard_map/feed_forward_back/pallas_call | solution.py:382
  319.7 16.2 %weight_grad.3 = (bf16[16,32,4096]{2,1,0:T(8,128)(2,1)}, bf16[16,32,4096]{2,1,0:T(8,128)(2,1)}) custom-call(s32[36]{0:T(128)} %pad_add_fusion.i_ref, bf16[512,1024]{1,0:T(8,128)(2,1)} %get-tuple-element.294.refs_0_, bf16[512,1024]{1,0:T(8,128)(2,1)} %get-tuple-element.295.a_ref.refs_1_, bf16[512,4096]{1,0:T(8,128)(2,1)} %get-tuple-element.298.refs_2_, ...), custom_call_target="tpu_custom_call" | custom-call | flops 1 | bytes 1 | tf_op jit(solution)/shard_map/weight_grad/pallas_call | solution.py:558
  336.7 3.5 add_convert_fusion.8
  341.6 8.9 %attention_back.6 = (bf16[3,512,512]{2,1,0:T(8,128)(2,1)}, f32[1,512]{1,0:T(1,128)}, f32[1,512]{1,0:T(1,128)}) custom-call(bf16[512,3072]{1,0:T(8,128)(2,1)} %get-tuple-element.236.q_ref.k_ref.v_ref, bf16[512,3072]{1,0:T(8,128)(2,1)} %get-tuple-element.236.q_ref.k_ref.v_ref, bf16[512,3072]{1,0:T(8,128)(2,1)} %get-tuple-element.236.q_ref.k_ref.v_ref, ...), custom_call_target="tpu_custom_call" | custom-call | flops 99999997952 | bytes 1 | tf_op jit(solution)/shard_map/attention_back/pallas_call | solution.py:164
  350.6 4.6 collective-permute-done.20
  356.6 5.2 %add_convert_fusion = (bf16[8,32,4096]{2,1,0:T(8,128)(2,1)S(1)}, bf16[8,32,4096]{2,1,0:T(8,128)(2,1)}) fusion(bf16[16,32,4096]{2,1,0:T(8,128)(2,1)} %collective-permute-done.21, bf16[16,32,4096]{2,1,0:T(8,128)(2,1)} %get-tuple-element.309), kind=kLoop, calls=%fused_computation.1 | loop fusion | flops 8388608 | bytes 12582912 | tf_op jit(solution)/shard_map/convert_element_type | solution.py:902
  361.8 1.5 collective-permute-start.22
  363.3 13.7 %weight_grad.4 = (bf16[16,32,2560]{2,1,0:T(8,128)(2,1)}, bf16[16,32,2560]{2,1,0:T(8,128)(2,1)}) custom-call(s32[36]{0:T(128)} %pad_add_fusion.i_ref, bf16[512,1024]{1,0:T(8,128)(2,1)} %get-tuple-element.311.o_ref.refs_0_, bf16[512,1024]{1,0:T(8,128)(2,1)} %get-tuple-element.312.o_ref.refs_1_, bf16[512,1024]{1,0:T(8,128)(2,1)} %get-tuple-element.313.refs_2_, ...), custom_call_target="tpu_custom_call" | custom-call | flops 1 | bytes 1 | tf_op jit(solution)/shard_map/weight_grad/pallas_call | solution.py:558
  377.1 8.9 %attention_back.7 = (bf16[3,512,512]{2,1,0:T(8,128)(2,1)}, f32[1,512]{1,0:T(1,128)}, f32[1,512]{1,0:T(1,128)}) custom-call(bf16[512,3072]{1,0:T(8,128)(2,1)} %get-tuple-element.236.q_ref.k_ref.v_ref, bf16[512,3072]{1,0:T(8,128)(2,1)} %get-tuple-element.236.q_ref.k_ref.v_ref, bf16[512,3072]{1,0:T(8,128)(2,1)} %get-tuple-element.236.q_ref.k_ref.v_ref, ...), custom_call_target="tpu_custom_call" | custom-call | flops 1 | bytes 1 | tf_op jit(solution)/shard_map/attention_back/pallas_call | solution.py:164
  386.1 2.1 collective-permute-done.22
  388.1 3.4 add_convert_fusion.6
  393.0 2.0 add_convert_fusion.24
  395.9 8.5 %weight_grad.5 = (bf16[16,32,1536]{2,1,0:T(8,128)(2,1)}, bf16[16,32,1536]{2,1,0:T(8,128)(2,1)}) custom-call(s32[36]{0:T(128)} %pad_add_fusion.i_ref, bf16[512,1024]{1,0:T(8,128)(2,1)} %get-tuple-element.325.refs_4_.refs_0_, bf16[512,1024]{1,0:T(8,128)(2,1)} %get-tuple-element.326.refs_5_.refs_1_, bf16[3,512,512]{2,1,0:T(8,128)(2,1)} %get-tuple-element.337.refs_2_.refs_1_, ...), custom_call_target="tpu_custom_call" | custom-call | flops 99999997952 | bytes 1 | tf_op jit(solution)/shard_map/weight_grad/pallas_call | solution.py:558
  404.5 4.4 add_convert_fusion.4
  409.8 2.4 add_convert_fusion.14
  412.2 2.1 collective-permute-start.28
  416.4 9.3 %project_back.3 = (bf16[512,1024]{1,0:T(8,128)(2,1)}, f32[1,1024]{1,0:T(1,128)}, f32[1,1024]{1,0:T(1,128)}) custom-call(bf16[3,512,512]{2,1,0:T(8,128)(2,1)} %get-tuple-element.336.refs_6_.refs_0_, bf16[3,512,512]{2,1,0:T(8,128)(2,1)} %get-tuple-element.337.refs_2_.refs_1_, bf16[1024,3072]{1,0:T(8,128)(2,1)} %bitcast.65, bf16[512,1024]{1,0:T(8,128)(2,1)} %bitcast.69, ...), custom_call_target="tpu_custom_call" | custom-call | flops 99999997952 | bytes 1 | tf_op jit(solution)/shard_map/project_back/pallas_call | solution.py:474
  425.7 2.4 pack_sums.1
  429.2 1.7 add_convert_fusion.12
  431.8 4.5 collective-permute-done.29
  437.6 1.6 collective-permute-start.35
  439.9 2.4 collective-permute-done.31
  442.5 2.8 collective-permute-start.37
  446.9 1.8 add_bitcast_fusion
  448.8 4.0 collective-permute-start.39
  455.0 4.8 %collective-permute-done.38 = f32[2,9,128]{2,1,0:T(8,128)S(1)} collective-permute-done((f32[2,9,128]{2,1,0:T(8,128)S(1)}, f32[2,9,128]{2,1,0:T(8,128)S(1)}, u32[]{:S(2)}, u32[]{:S(2)}) %collective-permute-start.38) | collective-permute-done | bytes 9248 | tf_op jit(solution)/shard_map/ppermute | solution.py:665
  460.0 2.8 collective-permute-start.42
  462.8 2.6 collective-permute-done.40
  (164 shorter events, 52.3 us)
Async XLA Ops:
  0.7 20.2 %copy-start.11 = (bf16[32,1024]{1,0:T(8,128)(2,1)S(1)}, bf16[32,1024]{1,0:T(8,128)(2,1)}, u32[]{:S(2)}) copy-start(bf16[32,1024]{1,0:T(8,128)(2,1)} %param.24) | copy-start | bytes 196612
  2.4 14.1 %collective-permute-start = (bf16[1,32,3328]{2,1,0:T(8,128)(2,1)}, bf16[1,32,3328]{2,1,0:T(8,128)(2,1)S(1)}, u32[]{:S(2)}, u32[]{:S(2)}) collective-permute-start(bf16[1,32,3328]{2,1,0:T(8,128)(2,1)} %bitcast.71), channel_id=1, source_target_pairs={{0,4},{1,5},{2,6},{3,7},{4,0},{5,1},{6,2},{7,3},{8,12},{9,13},{10,... | collective-permute-start | bytes 638984 | tf_op jit(solution)/shard_map/ppermute | solution.py:665
  17.4 17.3 %collective-permute-start.1 = (bf16[2,32,3328]{2,1,0:T(8,128)(2,1)S(1)}, bf16[2,32,3328]{2,1,0:T(8,128)(2,1)S(1)}, u32[]{:S(2)}, u32[]{:S(2)}) collective-permute-start(bf16[2,32,3328]{2,1,0:T(8,128)(2,1)S(1)} %constant_dynamic-update-slice_fusion), channel_id=1, source_target_pairs={{0,2},{1,3},{2,0},{3,1},{4,6},{5,7},{6,4},{7,5},{8,10},{9,11},{10,... | collective-permute-start | bytes 1277960 | tf_op jit(solution)/shard_map/ppermute | solution.py:665
  20.9 18.2 %collective-permute-start.2 = (bf16[1,160,1024]{2,1,0:T(8,128)(2,1)S(1)}, bf16[1,160,1024]{2,1,0:T(8,128)(2,1)S(1)}, u32[]{:S(2)}, u32[]{:S(2)}) collective-permute-start(bf16[1,160,1024]{2,1,0:T(8,128)(2,1)S(1)} %maximum_bitcast_fusion), channel_id=1, source_target_pairs={{0,4},{1,5},{2,6},{3,7},{4,0},{5,1},{6,2},{7,3},{8,12},{9,13},{10,... | collective-permute-start | bytes 983048 | tf_op jit(solution)/shard_map/ppermute | solution.py:665
  34.9 12.8 %collective-permute-start.3 = (bf16[4,32,3328]{2,1,0:T(8,128)(2,1)S(1)}, bf16[4,32,3328]{2,1,0:T(8,128)(2,1)S(1)}, u32[]{:S(2)}, u32[]{:S(2)}) collective-permute-start(bf16[4,32,3328]{2,1,0:T(8,128)(2,1)S(1)} %constant_dynamic-update-slice_fusion.2), channel_id=1, source_target_pairs={{0,1},{1,0},{2,3},{3,2},{4,5},{5,4},{6,7},{7,6},{8,24},{9,25},{10,... | collective-permute-start | bytes 2555912 | tf_op jit(solution)/shard_map/ppermute | solution.py:665
  47.7 25.5 %copy-start.1 = (bf16[8,32,3328]{2,1,0:T(8,128)(2,1)}, bf16[8,32,3328]{2,1,0:T(8,128)(2,1)S(1)}, u32[]{:S(2)}) copy-start(bf16[8,32,3328]{2,1,0:T(8,128)(2,1)S(1)} %constant_dynamic-update-slice_fusion.6.refs_0_) | copy-start | bytes 5111812
  47.7 21.9 %collective-permute-start.6 = (bf16[8,32,3328]{2,1,0:T(8,128)(2,1)S(1)}, bf16[8,32,3328]{2,1,0:T(8,128)(2,1)S(1)}, u32[]{:S(2)}, u32[]{:S(2)}) collective-permute-start(bf16[8,32,3328]{2,1,0:T(8,128)(2,1)S(1)} %constant_dynamic-update-slice_fusion.6.refs_0_), channel_id=1, source_target_pairs={{0,16},{1,17},{2,18},{3,19},{4,20},{5,21},{6,22},{7,23},{8,9},{9,8... | collective-permute-start | bytes 5111816 | tf_op jit(solution)/shard_map/ppermute | solution.py:665
  49.1 13.7 %collective-permute-start.4 = (bf16[2,160,1024]{2,1,0:T(8,128)(2,1)S(1)}, bf16[2,160,1024]{2,1,0:T(8,128)(2,1)S(1)}, u32[]{:S(2)}, u32[]{:S(2)}) collective-permute-start(bf16[2,160,1024]{2,1,0:T(8,128)(2,1)S(1)} %constant_dynamic-update-slice_fusion.4), channel_id=1, source_target_pairs={{0,2},{1,3},{2,0},{3,1},{4,6},{5,7},{6,4},{7,5},{8,10},{9,11},{10,... | collective-permute-start | bytes 1966088 | tf_op jit(solution)/shard_map/ppermute | solution.py:665
  49.1 24.1 %collective-permute-start.5 = (bf16[8,32,3328]{2,1,0:T(8,128)(2,1)S(1)}, bf16[8,32,3328]{2,1,0:T(8,128)(2,1)}, u32[]{:S(2)}, u32[]{:S(2)}) collective-permute-start(bf16[8,32,3328]{2,1,0:T(8,128)(2,1)S(1)} %constant_dynamic-update-slice_fusion.6.refs_0_), channel_id=1, source_target_pairs={{0,8},{1,9},{2,10},{3,11},{4,12},{5,13},{6,14},{7,15},{8,0},{9,1},... | collective-permute-start | bytes 5111816 | tf_op jit(solution)/shard_map/ppermute | solution.py:665
  69.6 7.5 %copy-start.2 = (bf16[8,32,3328]{2,1,0:T(8,128)(2,1)}, bf16[8,32,3328]{2,1,0:T(8,128)(2,1)S(1)}, u32[]{:S(2)}) copy-start(bf16[8,32,3328]{2,1,0:T(8,128)(2,1)S(1)} %collective-permute-done.6.refs_0_.refs_1_) | copy-start | bytes 5111812
  69.6 7.5 %collective-permute-start.7 = (bf16[8,32,3328]{2,1,0:T(8,128)(2,1)S(1)}, bf16[8,32,3328]{2,1,0:T(8,128)(2,1)}, u32[]{:S(2)}, u32[]{:S(2)}) collective-permute-start(bf16[8,32,3328]{2,1,0:T(8,128)(2,1)S(1)} %collective-permute-done.6.refs_0_.refs_1_), channel_id=1, source_target_pairs={{0,8},{1,9},{2,10},{3,11},{4,12},{5,13},{6,14},{7,15},{8,0},{9,1},... | collective-permute-start | bytes 5111816 | tf_op jit(solution)/shard_map/ppermute | solution.py:665
  69.6 17.9 %collective-permute-start.9 = (bf16[4,160,1024]{2,1,0:T(8,128)(2,1)}, bf16[4,160,1024]{2,1,0:T(8,128)(2,1)}, u32[]{:S(2)}, u32[]{:S(2)}) collective-permute-start(bf16[4,160,1024]{2,1,0:T(8,128)(2,1)} %constant_dynamic-update-slice_fusion.8), channel_id=1, source_target_pairs={{0,1},{1,0},{2,3},{3,2},{4,5},{5,4},{6,7},{7,6},{8,24},{9,25},{10,... | collective-permute-start | bytes 3932168 | tf_op jit(solution)/shard_map/ppermute | solution.py:665
  71.0 15.2 %collective-permute-start.8 = (bf16[1,128,1024]{2,1,0:T(8,128)(2,1)}, bf16[1,128,1024]{2,1,0:T(8,128)(2,1)}, u32[]{:S(2)}, u32[]{:S(2)}) collective-permute-start(bf16[1,128,1024]{2,1,0:T(8,128)(2,1)} %bitcast.74), channel_id=1, source_target_pairs={{0,4},{1,5},{2,6},{3,7},{4,0},{5,1},{6,2},{7,3},{8,12},{9,13},{10,... | collective-permute-start | bytes 786440 | tf_op jit(solution)/shard_map/ppermute | solution.py:665
  77.1 9.1 %copy-start.10 = (bf16[128,1024]{1,0:T(8,128)(2,1)S(1)}, bf16[128,1024]{1,0:T(8,128)(2,1)}, u32[]{:S(2)}) copy-start(bf16[128,1024]{1,0:T(8,128)(2,1)} %param.30) | copy-start | bytes 786436
  90.4 3.8 copy-start.3
  90.4 29.8 %collective-permute-start.11 = (bf16[8,160,1024]{2,1,0:T(8,128)(2,1)S(1)}, bf16[8,160,1024]{2,1,0:T(8,128)(2,1)}, u32[]{:S(2)}, u32[]{:S(2)}) collective-permute-start(bf16[8,160,1024]{2,1,0:T(8,128)(2,1)S(1)} %constant_dynamic-update-slice_fusion.12.refs_0_), channel_id=1, source_target_pairs={{0,8},{1,9},{2,10},{3,11},{4,12},{5,13},{6,14},{7,15},{8,0},{9,1},... | collective-permute-start | bytes 7864328 | tf_op jit(solution)/shard_map/ppermute | solution.py:665
  90.5 42.6 %collective-permute-start.13 = (bf16[8,160,1024]{2,1,0:T(8,128)(2,1)S(1)}, bf16[8,160,1024]{2,1,0:T(8,128)(2,1)}, u32[]{:S(2)}, u32[]{:S(2)}) collective-permute-start(bf16[8,160,1024]{2,1,0:T(8,128)(2,1)S(1)} %constant_dynamic-update-slice_fusion.12.refs_0_), channel_id=1, source_target_pairs={{0,16},{1,17},{2,18},{3,19},{4,20},{5,21},{6,22},{7,23},{8,9},{9,8... | collective-permute-start | bytes 7864328 | tf_op jit(solution)/shard_map/ppermute | solution.py:665
  91.9 14.1 %collective-permute-start.10 = (bf16[2,128,1024]{2,1,0:T(8,128)(2,1)S(1)}, bf16[2,128,1024]{2,1,0:T(8,128)(2,1)}, u32[]{:S(2)}, u32[]{:S(2)}) collective-permute-start(bf16[2,128,1024]{2,1,0:T(8,128)(2,1)S(1)} %constant_dynamic-update-slice_fusion.10), channel_id=1, source_target_pairs={{0,2},{1,3},{2,0},{3,1},{4,6},{5,7},{6,4},{7,5},{8,10},{9,11},{10,... | collective-permute-start | bytes 1572872 | tf_op jit(solution)/shard_map/ppermute | solution.py:665
  108.7 24.4 %collective-permute-start.12 = (bf16[4,128,1024]{2,1,0:T(8,128)(2,1)}, bf16[4,128,1024]{2,1,0:T(8,128)(2,1)}, u32[]{:S(2)}, u32[]{:S(2)}) collective-permute-start(bf16[4,128,1024]{2,1,0:T(8,128)(2,1)} %constant_dynamic-update-slice_fusion.14), channel_id=1, source_target_pairs={{0,1},{1,0},{2,3},{3,2},{4,5},{5,4},{6,7},{7,6},{8,24},{9,25},{10,... | collective-permute-start | bytes 3145736 | tf_op jit(solution)/shard_map/ppermute | solution.py:665
  133.1 5.3 %collective-permute-start.14 = (bf16[8,160,1024]{2,1,0:T(8,128)(2,1)}, bf16[8,160,1024]{2,1,0:T(8,128)(2,1)}, u32[]{:S(2)}, u32[]{:S(2)}) collective-permute-start(bf16[8,160,1024]{2,1,0:T(8,128)(2,1)} %collective-permute-done.13.refs_0_), channel_id=1, source_target_pairs={{0,8},{1,9},{2,10},{3,11},{4,12},{5,13},{6,14},{7,15},{8,0},{9,1},... | collective-permute-start | bytes 7864328 | tf_op jit(solution)/shard_map/ppermute | solution.py:665
  135.7 8.3 %copy-start.4 = (bf16[8,128,1024]{2,1,0:T(8,128)(2,1)}, bf16[8,128,1024]{2,1,0:T(8,128)(2,1)S(1)}, u32[]{:S(2)}) copy-start(bf16[8,128,1024]{2,1,0:T(8,128)(2,1)S(1)} %constant_dynamic-update-slice_fusion.16.refs_3_) | copy-start | bytes 6291460
  135.7 13.1 %collective-permute-start.15 = (bf16[8,128,1024]{2,1,0:T(8,128)(2,1)S(1)}, bf16[8,128,1024]{2,1,0:T(8,128)(2,1)}, u32[]{:S(2)}, u32[]{:S(2)}) collective-permute-start(bf16[8,128,1024]{2,1,0:T(8,128)(2,1)S(1)} %constant_dynamic-update-slice_fusion.16.refs_3_), channel_id=1, source_target_pairs={{0,8},{1,9},{2,10},{3,11},{4,12},{5,13},{6,14},{7,15},{8,0},{9,1},... | collective-permute-start | bytes 6291464 | tf_op jit(solution)/shard_map/ppermute | solution.py:665
  136.3 26.1 %collective-permute-start.16 = (bf16[8,128,1024]{2,1,0:T(8,128)(2,1)S(1)}, bf16[8,128,1024]{2,1,0:T(8,128)(2,1)}, u32[]{:S(2)}, u32[]{:S(2)}) collective-permute-start(bf16[8,128,1024]{2,1,0:T(8,128)(2,1)S(1)} %constant_dynamic-update-slice_fusion.16.refs_3_), channel_id=1, source_target_pairs={{0,16},{1,17},{2,18},{3,19},{4,20},{5,21},{6,22},{7,23},{8,9},{9,8... | collective-permute-start | bytes 6291464 | tf_op jit(solution)/shard_map/ppermute | solution.py:665
  148.9 14.4 %copy-start = (s32[32]{0:T(128)S(1)}, s32[32]{0:T(128)}, u32[]{:S(2)}) copy-start(s32[32]{0:T(128)} %get-tuple-element.447.i_ref) | copy-start | bytes 388
  162.4 4.4 collective-permute-start.17
  162.5 0.5 copy-start.15
  162.5 27.5 %copy-start.17 = (s32[2]{0:T(128)}, s32[2]{0:T(128)S(1)}, u32[]{:S(2)}) copy-start(s32[2]{0:T(128)S(1)} %get-tuple-element.450) | copy-start | bytes 28
  164.0 2.8 copy-start.13
  166.8 1.3 copy-start.5
  273.1 9.5 %copy-start.14 = (s32[32]{0:T(128)S(1)}, s32[32]{0:T(128)}, u32[]{:S(2)}) copy-start(s32[32]{0:T(128)} %copy-done.13) | copy-start | bytes 388
  273.1 9.5 %copy-start.16 = (s32[2]{0:T(128)S(1)}, s32[2]{0:T(128)}, u32[]{:S(2)}) copy-start(s32[2]{0:T(128)} %copy-done.15) | copy-start | bytes 28
  273.1 9.5 %copy-start.18 = (s32[2]{0:T(128)S(1)}, s32[2]{0:T(128)}, u32[]{:S(2)}) copy-start(s32[2]{0:T(128)} %copy-done.17) | copy-start | bytes 28
  273.1 10.0 %copy-start.19 = (s32[16]{0:T(128)S(1)}, s32[16]{0:T(128)}, u32[]{:S(2)}) copy-start(s32[16]{0:T(128)} %get-tuple-element.446) | copy-start | bytes 196
  282.4 10.5 %collective-permute-start.18 = (bf16[16,128,1024]{2,1,0:T(8,128)(2,1)}, bf16[16,128,1024]{2,1,0:T(8,128)(2,1)}, u32[]{:S(2)}, u32[]{:S(2)}) collective-permute-start(bf16[16,128,1024]{2,1,0:T(8,128)(2,1)} %weight_grad_half.2), channel_id=1, source_target_pairs={{0,8},{1,9},{2,10},{3,11},{4,12},{5,13},{6,14},{7,15},{8,0},{9,1},... | collective-permute-start | bytes 12582920 | tf_op jit(solution)/shard_map/ppermute | solution.py:665
  298.4 38.3 %collective-permute-start.19 = (bf16[8,128,1024]{2,1,0:T(8,128)(2,1)}, bf16[8,128,1024]{2,1,0:T(8,128)(2,1)}, u32[]{:S(2)}, u32[]{:S(2)}) collective-permute-start(bf16[8,128,1024]{2,1,0:T(8,128)(2,1)} %get-tuple-element.398), channel_id=1, source_target_pairs={{0,16},{1,17},{2,18},{3,19},{4,20},{5,21},{6,22},{7,23},{8,9},{9,8... | collective-permute-start | bytes 6291464 | tf_op jit(solution)/shard_map/ppermute | solution.py:665
  335.9 20.7 %collective-permute-start.21 = (bf16[16,32,4096]{2,1,0:T(8,128)(2,1)}, bf16[16,32,4096]{2,1,0:T(8,128)(2,1)}, u32[]{:S(2)}, u32[]{:S(2)}) collective-permute-start(bf16[16,32,4096]{2,1,0:T(8,128)(2,1)} %get-tuple-element.300), channel_id=1, source_target_pairs={{0,8},{1,9},{2,10},{3,11},{4,12},{5,13},{6,14},{7,15},{8,0},{9,1},... | collective-permute-start | bytes 12582920 | tf_op jit(solution)/shard_map/ppermute | solution.py:665
  340.2 15.0 %collective-permute-start.20 = (bf16[4,128,1024]{2,1,0:T(8,128)(2,1)}, bf16[4,128,1024]{2,1,0:T(8,128)(2,1)S(1)}, u32[]{:S(2)}, u32[]{:S(2)}) collective-permute-start(bf16[4,128,1024]{2,1,0:T(8,128)(2,1)} %get-tuple-element.404), channel_id=1, source_target_pairs={{0,1},{1,0},{2,3},{3,2},{4,5},{5,4},{6,7},{7,6},{8,24},{9,25},{10,... | collective-permute-start | bytes 3145736 | tf_op jit(solution)/shard_map/ppermute | solution.py:665
  361.8 26.4 %collective-permute-start.22 = (bf16[8,32,4096]{2,1,0:T(8,128)(2,1)}, bf16[8,32,4096]{2,1,0:T(8,128)(2,1)}, u32[]{:S(2)}, u32[]{:S(2)}) collective-permute-start(bf16[8,32,4096]{2,1,0:T(8,128)(2,1)} %get-tuple-element.396), channel_id=1, source_target_pairs={{0,16},{1,17},{2,18},{3,19},{4,20},{5,21},{6,22},{7,23},{8,9},{9,8... | collective-permute-start | bytes 6291464 | tf_op jit(solution)/shard_map/ppermute | solution.py:665
  363.3 29.7 %collective-permute-start.23 = (bf16[2,128,1024]{2,1,0:T(8,128)(2,1)}, bf16[2,128,1024]{2,1,0:T(8,128)(2,1)}, u32[]{:S(2)}, u32[]{:S(2)}) collective-permute-start(bf16[2,128,1024]{2,1,0:T(8,128)(2,1)} %get-tuple-element.412), channel_id=1, source_target_pairs={{0,2},{1,3},{2,0},{3,1},{4,6},{5,7},{6,4},{7,5},{8,10},{9,11},{10,... | collective-permute-start | bytes 1572872 | tf_op jit(solution)/shard_map/ppermute | solution.py:665
  377.1 27.4 %collective-permute-start.24 = (bf16[16,32,2560]{2,1,0:T(8,128)(2,1)}, bf16[16,32,2560]{2,1,0:T(8,128)(2,1)}, u32[]{:S(2)}, u32[]{:S(2)}) collective-permute-start(bf16[16,32,2560]{2,1,0:T(8,128)(2,1)} %get-tuple-element.318), channel_id=1, source_target_pairs={{0,8},{1,9},{2,10},{3,11},{4,12},{5,13},{6,14},{7,15},{8,0},{9,1},... | collective-permute-start | bytes 7864328 | tf_op jit(solution)/shard_map/ppermute | solution.py:665
  388.1 4.9 %copy-start.7 = (bf16[2,128,1024]{2,1,0:T(8,128)(2,1)S(1)}, bf16[2,128,1024]{2,1,0:T(8,128)(2,1)}, u32[]{:S(2)}) copy-start(bf16[2,128,1024]{2,1,0:T(8,128)(2,1)} %get-tuple-element.323) | copy-start | bytes 1572868
  391.5 18.3 %collective-permute-start.25 = (bf16[4,32,4096]{2,1,0:T(8,128)(2,1)}, bf16[4,32,4096]{2,1,0:T(8,128)(2,1)}, u32[]{:S(2)}, u32[]{:S(2)}) collective-permute-start(bf16[4,32,4096]{2,1,0:T(8,128)(2,1)} %get-tuple-element.402), channel_id=1, source_target_pairs={{0,1},{1,0},{2,3},{3,2},{4,5},{5,4},{6,7},{7,6},{8,24},{9,25},{10,... | collective-permute-start | bytes 3145736 | tf_op jit(solution)/shard_map/ppermute | solution.py:665
  395.0 51.9 %collective-permute-start.34 = (bf16[1,128,1024]{2,1,0:T(8,128)(2,1)}, bf16[1,128,1024]{2,1,0:T(8,128)(2,1)}, u32[]{:S(2)}, u32[]{:S(2)}) collective-permute-start(bf16[1,128,1024]{2,1,0:T(8,128)(2,1)} %get-tuple-element.420), channel_id=1, source_target_pairs={{0,4},{1,5},{2,6},{3,7},{4,0},{5,1},{6,2},{7,3},{8,12},{9,13},{10,... | collective-permute-start | bytes 786440 | tf_op jit(solution)/shard_map/ppermute | solution.py:665
  404.4 10.0 %collective-permute-start.26 = (bf16[16,32,1536]{2,1,0:T(8,128)(2,1)}, bf16[16,32,1536]{2,1,0:T(8,128)(2,1)S(1)}, u32[]{:S(2)}, u32[]{:S(2)}) collective-permute-start(bf16[16,32,1536]{2,1,0:T(8,128)(2,1)} %get-tuple-element.327), channel_id=1, source_target_pairs={{0,8},{1,9},{2,10},{3,11},{4,12},{5,13},{6,14},{7,15},{8,0},{9,1},... | collective-permute-start | bytes 4718600 | tf_op jit(solution)/shard_map/ppermute | solution.py:665
  408.8 5.6 %copy-start.8 = (bf16[16,32,1536]{2,1,0:T(8,128)(2,1)S(1)}, bf16[16,32,1536]{2,1,0:T(8,128)(2,1)}, u32[]{:S(2)}) copy-start(bf16[16,32,1536]{2,1,0:T(8,128)(2,1)} %get-tuple-element.334) | copy-start | bytes 4718596
  408.8 20.3 %collective-permute-start.27 = (bf16[8,32,2560]{2,1,0:T(8,128)(2,1)}, bf16[8,32,2560]{2,1,0:T(8,128)(2,1)}, u32[]{:S(2)}, u32[]{:S(2)}) collective-permute-start(bf16[8,32,2560]{2,1,0:T(8,128)(2,1)} %get-tuple-element.400), channel_id=1, source_target_pairs={{0,16},{1,17},{2,18},{3,19},{4,20},{5,21},{6,22},{7,23},{8,9},{9,8... | collective-permute-start | bytes 3932168 | tf_op jit(solution)/shard_map/ppermute | solution.py:665
  412.2 19.3 %collective-permute-start.28 = (bf16[2,32,4096]{2,1,0:T(8,128)(2,1)}, bf16[2,32,4096]{2,1,0:T(8,128)(2,1)S(1)}, u32[]{:S(2)}, u32[]{:S(2)}) collective-permute-start(bf16[2,32,4096]{2,1,0:T(8,128)(2,1)} %get-tuple-element.410), channel_id=1, source_target_pairs={{0,2},{1,3},{2,0},{3,1},{4,6},{5,7},{6,4},{7,5},{8,10},{9,11},{10,... | collective-permute-start | bytes 1572872 | tf_op jit(solution)/shard_map/ppermute | solution.py:665
  414.9 21.4 %collective-permute-start.29 = (bf16[8,32,1536]{2,1,0:T(8,128)(2,1)S(1)}, bf16[8,32,1536]{2,1,0:T(8,128)(2,1)}, u32[]{:S(2)}, u32[]{:S(2)}) collective-permute-start(bf16[8,32,1536]{2,1,0:T(8,128)(2,1)S(1)} %get-tuple-element.406), channel_id=1, source_target_pairs={{0,16},{1,17},{2,18},{3,19},{4,20},{5,21},{6,22},{7,23},{8,9},{9,8... | collective-permute-start | bytes 2359304 | tf_op jit(solution)/shard_map/ppermute | solution.py:665
  429.1 2.5 copy-start.6
  429.1 10.1 %collective-permute-start.30 = (f32[16,9,128]{2,1,0:T(8,128)S(1)}, f32[16,9,128]{2,1,0:T(8,128)S(1)}, u32[]{:S(2)}, u32[]{:S(2)}) collective-permute-start(f32[16,9,128]{2,1,0:T(8,128)S(1)} %get-tuple-element.429), channel_id=1, source_target_pairs={{0,8},{1,9},{2,10},{3,11},{4,12},{5,13},{6,14},{7,15},{8,0},{9,1},... | collective-permute-start | bytes 221192 | tf_op jit(solution)/shard_map/ppermute | solution.py:665
  430.8 11.5 %collective-permute-start.31 = (bf16[4,32,2560]{2,1,0:T(8,128)(2,1)S(1)}, bf16[4,32,2560]{2,1,0:T(8,128)(2,1)S(1)}, u32[]{:S(2)}, u32[]{:S(2)}) collective-permute-start(bf16[4,32,2560]{2,1,0:T(8,128)(2,1)S(1)} %get-tuple-element.408), channel_id=1, source_target_pairs={{0,1},{1,0},{2,3},{3,2},{4,5},{5,4},{6,7},{7,6},{8,24},{9,25},{10,... | collective-permute-start | bytes 1966088 | tf_op jit(solution)/shard_map/ppermute | solution.py:665
  431.7 14.3 %collective-permute-start.33 = (bf16[1,32,4096]{2,1,0:T(8,128)(2,1)S(1)}, bf16[1,32,4096]{2,1,0:T(8,128)(2,1)S(1)}, u32[]{:S(2)}, u32[]{:S(2)}) collective-permute-start(bf16[1,32,4096]{2,1,0:T(8,128)(2,1)S(1)} %get-tuple-element.418), channel_id=1, source_target_pairs={{0,4},{1,5},{2,6},{3,7},{4,0},{5,1},{6,2},{7,3},{8,12},{9,13},{10,... | collective-permute-start | bytes 786440 | tf_op jit(solution)/shard_map/ppermute | solution.py:665
  437.5 9.3 %copy-start.9 = (bf16[1,128,1024]{2,1,0:T(8,128)(2,1)S(1)}, bf16[1,128,1024]{2,1,0:T(8,128)(2,1)}, u32[]{:S(2)}) copy-start(bf16[1,128,1024]{2,1,0:T(8,128)(2,1)} %get-tuple-element.377) | copy-start | bytes 786436
  437.6 11.1 %collective-permute-start.35 = (bf16[4,32,1536]{2,1,0:T(8,128)(2,1)S(1)}, bf16[4,32,1536]{2,1,0:T(8,128)(2,1)S(1)}, u32[]{:S(2)}, u32[]{:S(2)}) collective-permute-start(bf16[4,32,1536]{2,1,0:T(8,128)(2,1)S(1)} %get-tuple-element.414), channel_id=1, source_target_pairs={{0,1},{1,0},{2,3},{3,2},{4,5},{5,4},{6,7},{7,6},{8,24},{9,25},{10,... | collective-permute-start | bytes 1179656 | tf_op jit(solution)/shard_map/ppermute | solution.py:665
  439.2 6.1 %collective-permute-start.32 = (f32[8,9,128]{2,1,0:T(8,128)S(1)}, f32[8,9,128]{2,1,0:T(8,128)S(1)}, u32[]{:S(2)}, u32[]{:S(2)}) collective-permute-start(f32[8,9,128]{2,1,0:T(8,128)S(1)} %get-tuple-element.428), channel_id=1, source_target_pairs={{0,16},{1,17},{2,18},{3,19},{4,20},{5,21},{6,22},{7,23},{8,9},{9,8... | collective-permute-start | bytes 110600 | tf_op jit(solution)/shard_map/ppermute | solution.py:665
  442.5 11.4 %collective-permute-start.37 = (bf16[2,32,2560]{2,1,0:T(8,128)(2,1)S(1)}, bf16[2,32,2560]{2,1,0:T(8,128)(2,1)S(1)}, u32[]{:S(2)}, u32[]{:S(2)}) collective-permute-start(bf16[2,32,2560]{2,1,0:T(8,128)(2,1)S(1)} %get-tuple-element.416), channel_id=1, source_target_pairs={{0,2},{1,3},{2,0},{3,1},{4,6},{5,7},{6,4},{7,5},{8,10},{9,11},{10,... | collective-permute-start | bytes 983048 | tf_op jit(solution)/shard_map/ppermute | solution.py:665
  445.3 7.6 %collective-permute-start.36 = (f32[4,9,128]{2,1,0:T(8,128)S(1)}, f32[4,9,128]{2,1,0:T(8,128)S(1)}, u32[]{:S(2)}, u32[]{:S(2)}) collective-permute-start(f32[4,9,128]{2,1,0:T(8,128)S(1)} %get-tuple-element.432), channel_id=1, source_target_pairs={{0,1},{1,0},{2,3},{3,2},{4,5},{5,4},{6,7},{7,6},{8,24},{9,25},{10,... | collective-permute-start | bytes 55304 | tf_op jit(solution)/shard_map/ppermute | solution.py:665
  448.8 11.2 %collective-permute-start.39 = (bf16[2,32,1536]{2,1,0:T(8,128)(2,1)S(1)}, bf16[2,32,1536]{2,1,0:T(8,128)(2,1)S(1)}, u32[]{:S(2)}, u32[]{:S(2)}) collective-permute-start(bf16[2,32,1536]{2,1,0:T(8,128)(2,1)S(1)} %get-tuple-element.422), channel_id=1, source_target_pairs={{0,2},{1,3},{2,0},{3,1},{4,6},{5,7},{6,4},{7,5},{8,10},{9,11},{10,... | collective-permute-start | bytes 589832 | tf_op jit(solution)/shard_map/ppermute | solution.py:665
  452.8 6.9 %collective-permute-start.38 = (f32[2,9,128]{2,1,0:T(8,128)S(1)}, f32[2,9,128]{2,1,0:T(8,128)S(1)}, u32[]{:S(2)}, u32[]{:S(2)}) collective-permute-start(f32[2,9,128]{2,1,0:T(8,128)S(1)} %get-tuple-element.434), channel_id=1, source_target_pairs={{0,2},{1,3},{2,0},{3,1},{4,6},{5,7},{6,4},{7,5},{8,10},{9,11},{10,... | collective-permute-start | bytes 27656 | tf_op jit(solution)/shard_map/ppermute | solution.py:665
  453.9 12.6 %collective-permute-start.41 = (bf16[1,32,2560]{2,1,0:T(8,128)(2,1)S(1)}, bf16[1,32,2560]{2,1,0:T(8,128)(2,1)S(1)}, u32[]{:S(2)}, u32[]{:S(2)}) collective-permute-start(bf16[1,32,2560]{2,1,0:T(8,128)(2,1)S(1)} %get-tuple-element.424), channel_id=1, source_target_pairs={{0,4},{1,5},{2,6},{3,7},{4,0},{5,1},{6,2},{7,3},{8,12},{9,13},{10,... | collective-permute-start | bytes 491528 | tf_op jit(solution)/shard_map/ppermute | solution.py:665
  459.8 5.7 %collective-permute-start.40 = (f32[1,9,128]{2,1,0:T(8,128)S(1)}, f32[1,9,128]{2,1,0:T(8,128)S(1)}, u32[]{:S(2)}, u32[]{:S(2)}) collective-permute-start(f32[1,9,128]{2,1,0:T(8,128)S(1)} %get-tuple-element.436), channel_id=1, source_target_pairs={{0,4},{1,5},{2,6},{3,7},{4,0},{5,1},{6,2},{7,3},{8,12},{9,13},{10,... | collective-permute-start | bytes 13832 | tf_op jit(solution)/shard_map/ppermute | solution.py:665
  460.0 7.5 %collective-permute-start.42 = (bf16[1,32,1536]{2,1,0:T(8,128)(2,1)S(1)}, bf16[1,32,1536]{2,1,0:T(8,128)(2,1)S(1)}, u32[]{:S(2)}, u32[]{:S(2)}) collective-permute-start(bf16[1,32,1536]{2,1,0:T(8,128)(2,1)S(1)} %get-tuple-element.426), channel_id=1, source_target_pairs={{0,4},{1,5},{2,6},{3,7},{4,0},{5,1},{6,2},{7,3},{8,12},{9,13},{10,... | collective-permute-start | bytes 294920 | tf_op jit(solution)/shard_map/ppermute | solution.py:665
  467.6 0.7 copy-start.12
